TPU v7x, 32 devices: a whole 2x2x4 slice. The times are simulated.
32 devices in a mesh: sec: 4 (over y, x), blk: 4 (over z), case: 2 (over core).
Axes of the slice: x: 2, y: 2, z: 4, core: 2. Of those that a mesh axis runs over, the one named last changes fastest.
Arguments:
- vertex_costate: float32 [512, 128, 128], P(('sec', 'blk'), 'case'), may hold values from -6 to 6
- inverter_costate: float32 [512, 128, 128], P(('sec', 'blk'), 'case'), may hold values from -6 to 6
- highvoltage_costate: float32 [128, 4096], P('case', ('sec', 'blk')), may hold values from -6 to 6
- derivative_tiles: bfloat16 [3072, 128, 128], P(('sec', 'blk', 'case')), may hold values from -0.25 to 0.25
- tile_source_index: int32 [3072], P(('sec', 'blk', 'case')), may hold values from 0 to 31
- tile_target_index: int32 [3072], P(('sec', 'blk', 'case')), may hold values from 0 to 47
- inverter_decay_factor: float32 [512, 128], P(('sec', 'blk')), may hold values from 0.05 to 0.95
- costate_to_inverter_factor: float32 [512, 128], P(('sec', 'blk')), may hold values from 0.2 to 1
- inverter_to_costate_factor: float32 [512, 128], P(('sec', 'blk')), may hold values from -1 to 1
- distribution_entry_vertex: int32 [2048], P(('sec', 'blk')), may hold values from 0 to 4095
- distribution_entry_holder: int32 [2048, 1], P(('sec', 'blk')), may hold values from 0 to 15; in each aligned block of 128 rows (0 to 127, 128 to 255, ...) at most 16 rows name the same one
- distribution_entry_substation: int32 [2048], P(('sec', 'blk')), may hold values from 0 to 255
- highvoltage_derivative_matrix: bfloat16 [4096, 256], P(('sec', 'blk')), may hold values from -0.375 to 0.375
Outputs:
- adjoint_out: float32 [512, 128, 128], P(('sec', 'blk'), 'case')
- droop_out: float32 [512, 128, 128], P(('sec', 'blk'), 'case')
- trans_out: float32 [128, 4096], P('case', ('sec', 'blk'))
Inputs may be any that keep to these rules, and one draw needn't show every extreme that they name: `distribution_entry_holder`: in each aligned block of 128 rows (the feeder heads of one network device) no owner is named by more than 16 rows, a bound that some block reaches.
All inputs are finite; a program needn't handle non-finite values.
Results may differ from a plain program's by a relative error of at most 0.0047.
Values may be sent and summed in bfloat16 or wider, within the bound.
No kernel may reach another device: no remote copies, remote signals or barrier semaphores. Data moves between devices by JAX's collectives and lax.ppermute only.
A program may use at most 64 MiB of HBM per device.

v0:
```python
import jax
import jax.numpy as jnp
from jax import lax
from jax.sharding import PartitionSpec as P

STEPS = 3


def shifted(block, axis, distance):
    devices = range(lax.axis_size(axis))
    route = [(i - distance, i) for i in devices if i - distance in devices]
    return lax.ppermute(block, axis, route)


def block_terms(lam_rows, mats, row_ids, col_ids, targets):
    picked = jnp.take(lam_rows, row_ids, axis=0)
    prods = jnp.einsum("ecn,enm->ecm", picked, mats, preferred_element_type=jnp.float32)
    return jax.ops.segment_sum(prods, col_ids, num_segments=targets)


def local(
    vertex_costate,
    inverter_costate,
    highvoltage_costate,
    derivative_tiles,
    tile_source_index,
    tile_target_index,
    inverter_decay_factor,
    costate_to_inverter_factor,
    inverter_to_costate_factor,
    distribution_entry_vertex,
    distribution_entry_holder,
    distribution_entry_substation,
    highvoltage_derivative_matrix,
):
    owned_blocks = vertex_costate.shape[0]
    nodes = vertex_costate.shape[2]
    cases_here = vertex_costate.shape[1]
    rim_blocks = owned_blocks // 2
    targets = owned_blocks + rim_blocks
    sections = lax.axis_size("sec")
    owners_blk = lax.axis_size("blk")
    network = sections * owners_blk
    heads = distribution_entry_vertex.shape[0]
    slots = max(2, 2 * heads // network)
    buses = highvoltage_derivative_matrix.shape[1]
    decay_triple = inverter_decay_factor[:, None, :]
    inflow_factor = costate_to_inverter_factor[:, None, :]
    outflow_factor = inverter_to_costate_factor[:, None, :]
    owner_ids = distribution_entry_holder[:, 0]
    owner_hot = (owner_ids[:, None] == jnp.arange(network, dtype=jnp.int32)[None, :]).astype(
        jnp.int32
    )
    earlier = jnp.cumsum(owner_hot, axis=0) - owner_hot
    slot_ids = jnp.sum(earlier * owner_hot, axis=1)
    dest_ids = owner_ids * slots + slot_ids
    place_int = (dest_ids[:, None] == jnp.arange(network * slots, dtype=jnp.int32)[None, :]).astype(
        jnp.int32
    )
    place = place_int.astype(jnp.float32)
    bus_sent = jnp.dot(place_int.T, distribution_entry_substation + 1)
    head_block = distribution_entry_vertex // nodes
    head_pos = distribution_entry_vertex % nodes
    all_mats, all_rows, all_cols = (
        lax.all_gather(derivative_tiles, "case", axis=0, tiled=True),
        lax.all_gather(tile_source_index, "case", axis=0, tiled=True),
        lax.all_gather(tile_target_index, "case", axis=0, tiled=True),
    )
    lam = vertex_costate
    iteration_carry = inverter_costate
    trans = highvoltage_costate
    for step in range(STEPS):
        lam_bf = lam.astype(jnp.bfloat16)
        partial_sum = block_terms(lam_bf, all_mats, all_rows, all_cols, targets)
        arriving = shifted(partial_sum[owned_blocks:], "blk", 1)
        summed = partial_sum[:owned_blocks]
        summed = jnp.concatenate([summed[:rim_blocks] + arriving, summed[rim_blocks:]], axis=0)
        head_vals = lam[head_block, :, head_pos]
        send_vals = jnp.dot(place.T, head_vals, precision=lax.Precision.HIGHEST)
        recv_vals, recv_bus = (
            lax.all_to_all(
                send_vals.reshape(network, slots, cases_here),
                ("sec", "blk"),
                split_axis=0,
                concat_axis=0,
                tiled=True,
            ),
            lax.all_to_all(
                bus_sent.reshape(network, slots),
                ("sec", "blk"),
                split_axis=0,
                concat_axis=0,
                tiled=True,
            ),
        )
        recv_vals = recv_vals.reshape(network * slots, cases_here)
        recv_bus = recv_bus.reshape(network * slots)
        bus_hot = (recv_bus[:, None] - 1 == jnp.arange(buses, dtype=jnp.int32)[None, :]).astype(
            jnp.float32
        )
        inj = jnp.dot(recv_vals.T, bus_hot, precision=lax.Precision.HIGHEST)
        trans_next = (
            jnp.dot(
                trans.astype(jnp.bfloat16),
                highvoltage_derivative_matrix,
                preferred_element_type=jnp.float32,
            )
            + inj
        )
        state_next = decay_triple * iteration_carry + inflow_factor * lam
        lam_next = summed + outflow_factor * iteration_carry
        lam, iteration_carry, trans = (lam_next, state_next, trans_next)
    return (lam, iteration_carry, trans)


def solution(mesh):
    placed = (
        P(("sec", "blk"), "case", None),
        P(("sec", "blk"), "case", None),
        P("case", ("sec", "blk")),
        P(("sec", "blk", "case"), None, None),
        P(("sec", "blk", "case")),
        P(("sec", "blk", "case")),
        P(("sec", "blk"), None),
        P(("sec", "blk"), None),
        P(("sec", "blk"), None),
        P(("sec", "blk")),
        P(("sec", "blk"), None),
        P(("sec", "blk")),
        P(("sec", "blk"), None),
    )
    return jax.shard_map(
        local,
        mesh=mesh,
        in_specs=placed,
        out_specs=(
            P(("sec", "blk"), "case", None),
            P(("sec", "blk"), "case", None),
            P("case", ("sec", "blk")),
        ),
        check_vma=False,
    )
```

profile of v0, /device:TPU:0, one launch (start us, length us, event | category | flops | bytes accessed | tf_op | source)
XLA Modules:
  0.0 199.0 jit_solution(4722228548900247049)
XLA Ops:
  7.3 0.7 all-gather.2.cloned.1.call-update
  8.1 0.2 reduce_window_sum.11
  8.3 0.2 select_reduce_fusion
  8.5 0.2 fusion.26
  8.6 0.7 all_to_all.18
  9.4 8.3 %all-to-all-start.1 = ((s32[16,1,16]{2,1,0:T(1,128)}), s32[16,1,16]{2,1,0:T(1,128)S(1)}, u32[]{:S(2)}, u32[]{:S(2)}) async-start(s32[16,1,16]{2,1,0:T(1,128)} %all_to_all.18), calls=%async_computation.1 | async-start | bytes 16384 | tf_op jit(solution)/shard_map/all_to_all | solution.py:88
  17.8 2.0 copy.30
  19.8 2.1 %gather_fusion = f32[128,64]{1,0:T(8,128)S(1)} fusion(f32[32,64,128]{1,2,0:T(8,128)} %copy.30, s32[128]{0:T(128)S(1)} %fusion.36), kind=kCustom, calls=%fused_computation.3 | custom fusion | bytes 66560 | tf_op jit(solution)/shard_map/gather | solution.py:78
  21.9 0.4 fusion.21
  22.2 0.8 reshape.164
  23.0 0.6 dynamic-slice
  24.3 0.2 dynamic-update-slice
  24.5 0.2 dynamic-update-slice.1
  24.7 1.8 all-reduce.2
  26.6 2.7 %gather_fusion.3 = bf16[192,64,128]{2,1,0:T(8,128)(2,1)} fusion(bf16[32,64,128]{2,1,0:T(8,128)(2,1)S(1)} %convert_element_type.30, s32[1024]{0:T(1024)S(1)} %pad_clamp_fusion), kind=kCustom, calls=%fused_computation.clone | custom fusion | bytes 6292224 | tf_op jit(solution)/shard_map/jit(_take)/gather | solution.py:16
  29.3 8.2 %fusion.4 = f32[192,64,128]{2,1,0:T(8,128)} fusion(bf16[192,128,128]{2,1,0:T(8,128)(2,1)} %all-gather.2.cloned.1.call-done, bf16[192,64,128]{2,1,0:T(8,128)(2,1)} %gather_fusion.3, pred[192]{0:T(512)(128)(4,1)S(1)} %compare_and_fusion), kind=kOutput, calls=%fused_computation.13 | convolution fusion | flops 404226048 | bytes 15728832 | tf_op jit(solution)/shard_map/ecn,enm->ecm/dot_general | solution.py:17
  37.5 0.2 broadcast.44.clone
  37.7 19.9 %scatter_fusion = f32[48,64,128]{2,1,0:T(8,128)S(1)} fusion(f32[48,64,128]{2,1,0:T(8,128)S(1)} %broadcast.44.clone, s32[192]{0:T(256)S(1)} %get-tuple-element.7, f32[192,64,128]{2,1,0:T(8,128)} %fusion.4), kind=kCustom, calls=%fused_computation.6 | custom fusion | flops 1572864 | bytes 18875136 | tf_op jit(solution)/shard_map/scatter-add | solution.py:18
  57.7 3.9 %collective-permute-start = (f32[16,64,128]{2,1,0:T(8,128)S(1)}, f32[16,64,128]{2,1,0:T(8,128)S(1)}, u32[]{:S(2)}, u32[]{:S(2)}) collective-permute-start(f32[16,64,128]{2,1,0:T(8,128)S(1)} %slice.58), channel_id=1, source_target_pairs={{0,2},{2,4},{4,6},{1,3},{3,5},{5,7},{8,10},{10,12},{12,14},{9,11},... | collective-permute-start | bytes 1572872 | tf_op jit(solution)/shard_map/ppermute | solution.py:12
  61.6 5.5 %all-to-all-start = ((f32[16,1,1024]{2,1,0:T(1,128)}), f32[16,1,1024]{2,1,0:T(1,128)S(1)}, u32[]{:S(2)}, u32[]{:S(2)}) async-start(f32[16,1,1024]{2,1,0:T(1,128)} %reshape.164), calls=%async_computation | async-start | bytes 131072 | tf_op jit(solution)/shard_map/all_to_all | solution.py:81
  67.2 0.1 fusion.32
  67.4 7.2 %all-to-all-done = f32[16,1,1024]{2,1,0:T(1,128)S(1)} async-done(((f32[16,1,1024]{2,1,0:T(1,128)}), f32[16,1,1024]{2,1,0:T(1,128)S(1)}, u32[]{:S(2)}, u32[]{:S(2)}) %all-to-all-start) | async-done | bytes 65568 | tf_op jit(solution)/shard_map/all_to_all | solution.py:81
  74.6 0.5 broadcast.124
  75.1 0.8 reduce.4
  76.0 0.3 fusion.12
  76.3 0.1 slice_add_fusion.2
  76.4 1.4 fusion.47
  77.9 2.7 %gather_fusion.4 = bf16[192,64,128]{2,1,0:T(8,128)(2,1)} fusion(bf16[32,64,128]{2,1,0:T(8,128)(2,1)S(1)} %get-tuple-element.11, s32[1024]{0:T(1024)S(1)} %pad_clamp_fusion), kind=kCustom, calls=%fused_computation.1.clone | custom fusion | bytes 6292224 | tf_op jit(solution)/shard_map/jit(_take)/gather | solution.py:16
  80.6 8.2 %fusion.2 = f32[192,64,128]{2,1,0:T(8,128)} fusion(bf16[192,128,128]{2,1,0:T(8,128)(2,1)} %all-gather.2.cloned.1.call-done, bf16[192,64,128]{2,1,0:T(8,128)(2,1)} %gather_fusion.4, pred[192]{0:T(512)(128)(4,1)S(1)} %compare_and_fusion), kind=kOutput, calls=%fused_computation.11 | convolution fusion | flops 404226048 | bytes 15728832 | tf_op jit(solution)/shard_map/ecn,enm->ecm/dot_general | solution.py:17
  88.8 0.2 broadcast.44.clone.1
  89.0 20.0 %scatter_fusion.1 = f32[48,64,128]{2,1,0:T(8,128)S(1)} fusion(f32[48,64,128]{2,1,0:T(8,128)S(1)} %broadcast.44.clone.1, s32[192]{0:T(256)S(1)} %get-tuple-element.7, f32[192,64,128]{2,1,0:T(8,128)} %fusion.2), kind=kCustom, calls=%fused_computation.7 | custom fusion | flops 1572864 | bytes 18875136 | tf_op jit(solution)/shard_map/scatter-add | solution.py:18
  108.9 0.8 slice.61
  109.8 5.5 %collective-permute-start.1 = (f32[16,64,128]{2,1,0:T(8,128)}, f32[16,64,128]{2,1,0:T(8,128)S(1)}, u32[]{:S(2)}, u32[]{:S(2)}) collective-permute-start(f32[16,64,128]{2,1,0:T(8,128)} %slice.61), channel_id=1, source_target_pairs={{0,2},{2,4},{4,6},{1,3},{3,5},{5,7},{8,10},{10,12},{12,14},{9,11},... | collective-permute-start | bytes 1572872 | tf_op jit(solution)/shard_map/ppermute | solution.py:12
  115.2 2.0 copy.32
  117.2 1.8 gather_fusion.1
  119.0 0.4 fusion.19
  119.4 0.8 reshape.166
  120.1 4.3 %all-to-all-start.2 = ((f32[16,1,1024]{2,1,0:T(1,128)}), f32[16,1,1024]{2,1,0:T(1,128)S(1)}, u32[]{:S(2)}, u32[]{:S(2)}) async-start(f32[16,1,1024]{2,1,0:T(1,128)} %reshape.166), calls=%async_computation.2 | async-start | bytes 131072 | tf_op jit(solution)/shard_map/all_to_all | solution.py:81
  124.5 0.1 fusion.48
  124.6 7.3 %all-to-all-done.2 = f32[16,1,1024]{2,1,0:T(1,128)S(1)} async-done(((f32[16,1,1024]{2,1,0:T(1,128)}), f32[16,1,1024]{2,1,0:T(1,128)S(1)}, u32[]{:S(2)}, u32[]{:S(2)}) %all-to-all-start.2) | async-done | bytes 65568 | tf_op jit(solution)/shard_map/all_to_all | solution.py:81
  131.9 0.8 reduce.5
  132.8 0.9 fusion.13
  133.7 0.1 slice_add_fusion.1
  133.9 0.1 copy-done.2
  134.0 0.3 copy-done.4
  134.4 2.4 %multiply_add_fusion = (f32[32,64,128]{2,1,0:T(8,128)}, f32[32,64,128]{2,1,0:T(8,128)S(1)}) fusion(f32[32,128]{1,0:T(8,128)} %param.22, f32[32,128]{1,0:T(8,128)} %param.21, f32[32,64,128]{2,1,0:T(8,128)S(1)} %get-tuple-element.12, f32[32,64,128]{2,1,0:T(8,128)S(1)} %copy-done.2, f32[32,64,128]{2,1,0:T(8,128)S(1)} %copy-done.4, f32[32,128]{1,0:T(8,128)} %param.23, ...), kind=kLoop, calls=%fused_computation.29 | loop fusion | flops 3145728 | bytes 6340608 | tf_op jit(solution)/shard_map/add | solution.py:110
  136.7 2.0 copy.34
  138.8 1.8 gather_fusion.2
  140.5 2.7 %gather_fusion.5 = bf16[192,64,128]{2,1,0:T(8,128)(2,1)} fusion(bf16[32,64,128]{2,1,0:T(8,128)(2,1)S(1)} %convert_element_type.32, s32[1024]{0:T(1024)S(1)} %pad_clamp_fusion), kind=kCustom, calls=%fused_computation.2.clone | custom fusion | bytes 6292224 | tf_op jit(solution)/shard_map/jit(_take)/gather | solution.py:16
  143.2 8.2 %fusion = f32[192,64,128]{2,1,0:T(8,128)} fusion(bf16[192,128,128]{2,1,0:T(8,128)(2,1)} %all-gather.2.cloned.1.call-done, bf16[192,64,128]{2,1,0:T(8,128)(2,1)} %gather_fusion.5, pred[192]{0:T(512)(128)(4,1)S(1)} %copy-done.9), kind=kOutput, calls=%fused_computation.9 | convolution fusion | flops 404226048 | bytes 15728832 | tf_op jit(solution)/shard_map/ecn,enm->ecm/dot_general | solution.py:17
  151.4 0.2 broadcast.44
  151.6 19.9 %scatter_fusion.2 = f32[48,64,128]{2,1,0:T(8,128)S(1)} fusion(f32[48,64,128]{2,1,0:T(8,128)S(1)} %broadcast.44, s32[192]{0:T(256)S(1)} %get-tuple-element.7, f32[192,64,128]{2,1,0:T(8,128)} %fusion), kind=kCustom, calls=%fused_computation.8 | custom fusion | flops 1572864 | bytes 18875136 | tf_op jit(solution)/shard_map/scatter-add | solution.py:18
  171.6 0.8 slice.64
  172.4 2.8 %collective-permute-start.2 = (f32[16,64,128]{2,1,0:T(8,128)}, f32[16,64,128]{2,1,0:T(8,128)S(1)}, u32[]{:S(2)}, u32[]{:S(2)}) collective-permute-start(f32[16,64,128]{2,1,0:T(8,128)} %slice.64), channel_id=1, source_target_pairs={{0,2},{2,4},{4,6},{1,3},{3,5},{5,7},{8,10},{10,12},{12,14},{9,11},... | collective-permute-start | bytes 1572872 | tf_op jit(solution)/shard_map/ppermute | solution.py:12
  175.3 0.4 fusion.17
  175.7 0.8 reshape.168
  176.4 3.5 %all-to-all-start.3 = ((f32[16,1,1024]{2,1,0:T(1,128)}), f32[16,1,1024]{2,1,0:T(1,128)S(1)}, u32[]{:S(2)}, u32[]{:S(2)}) async-start(f32[16,1,1024]{2,1,0:T(1,128)} %reshape.168), calls=%async_computation.3 | async-start | bytes 131072 | tf_op jit(solution)/shard_map/all_to_all | solution.py:81
  179.9 0.9 fusion.49
  180.8 6.5 %all-to-all-done.3 = f32[16,1,1024]{2,1,0:T(1,128)S(1)} async-done(((f32[16,1,1024]{2,1,0:T(1,128)}), f32[16,1,1024]{2,1,0:T(1,128)S(1)}, u32[]{:S(2)}, u32[]{:S(2)}) %all-to-all-start.3) | async-done | bytes 65568 | tf_op jit(solution)/shard_map/all_to_all | solution.py:81
  187.3 0.8 reduce.6
  188.2 1.0 convolution_add_fusion
  189.3 0.2 copy-done.3
  189.4 0.3 copy-done.5
  189.8 2.3 %maximum_add_fusion.2 = f32[32,64,128]{2,1,0:T(8,128)} fusion(f32[16,64,128]{2,1,0:T(8,128)S(1)} %get-tuple-element.14, f32[16,64,128]{2,1,0:T(8,128)S(1)} %get-tuple-element.13, f32[32,128]{1,0:T(8,128)} %param.23, f32[32,64,128]{2,1,0:T(8,128)S(1)} %get-tuple-element.12, f32[32,64,128]{2,1,0:T(8,128)S(1)} %copy-done.3, f32[32,128]{1,0:T(8,128)} %param.22, ...), kind=kLoop, calls=%fused_computation.28 | loop fusion | flops 2359296 | bytes 5292032 | tf_op jit(solution)/shard_map/add | solution.py:111
  (55 shorter events, 0.9 us)
Async XLA Ops:
  7.2 60.0 %copy-start = (bf16[256,256]{1,0:T(8,128)(2,1)S(1)}, bf16[256,256]{1,0:T(8,128)(2,1)}, u32[]{:S(2)}) copy-start(bf16[256,256]{1,0:T(8,128)(2,1)} %param.27) | copy-start | bytes 393220
  7.2 0.8 copy-start.12
  7.2 1.3 copy-start.13
  7.2 10.5 %copy-start.1 = (f32[32,64,128]{2,1,0:T(8,128)S(1)}, f32[32,64,128]{2,1,0:T(8,128)}, u32[]{:S(2)}) copy-start(f32[32,64,128]{2,1,0:T(8,128)} %param.15) | copy-start | bytes 3145732
  7.2 22.1 %all-gather.2.cloned.1.call-start = ((), (), s32[]{:S(2)}) async-start(), calls=%async_computation.4 | async-start | bytes 9437184 | tf_op jit(solution)/shard_map/all_gather | solution.py:65
  7.9 11.8 %copy-start.14 = (s32[128]{0:T(128)S(1)}, s32[128]{0:T(128)}, u32[]{:S(2)}) copy-start(s32[128]{0:T(128)} %param.24) | copy-start | bytes 1540
  8.0 15.1 %copy-start.17 = (u32[32]{0:T(128)S(1)}, u32[32]{0:T(128)}, u32[]{:S(2)}) copy-start(u32[32]{0:T(128)} %constant.95) | copy-start | bytes 388
  8.0 16.3 %copy-start.15 = (s32[96]{0:T(128)S(1)}, s32[96]{0:T(128)}, u32[]{:S(2)}) copy-start(s32[96]{0:T(128)} %param.20) | copy-start | bytes 1156
  8.0 16.5 %copy-start.16 = (s32[96]{0:T(128)S(1)}, s32[96]{0:T(128)}, u32[]{:S(2)}) copy-start(s32[96]{0:T(128)} %param.19) | copy-start | bytes 1156
  8.5 110.5 %copy-start.10 = (s32[128]{0:T(128)}, s32[128]{0:T(128)S(1)}, u32[]{:S(2)}) copy-start(s32[128]{0:T(128)S(1)} %fusion.40) | copy-start | bytes 1540
  9.4 52.2 %all-to-all-start.1 = ((s32[16,1,16]{2,1,0:T(1,128)}), s32[16,1,16]{2,1,0:T(1,128)S(1)}, u32[]{:S(2)}, u32[]{:S(2)}) async-start(s32[16,1,16]{2,1,0:T(1,128)} %all_to_all.18), calls=%async_computation.1 | async-start | bytes 16384 | tf_op jit(solution)/shard_map/all_to_all | solution.py:88
  29.3 51.3 %copy-start.8 = (pred[192]{0:T(512)(128)(4,1)}, pred[192]{0:T(512)(128)(4,1)S(1)}, u32[]{:S(2)}) copy-start(pred[192]{0:T(512)(128)(4,1)S(1)} %compare_and_fusion) | copy-start | bytes 580
  37.7 29.4 %copy-start.7 = (f32[64,256]{1,0:T(8,128)S(1)}, f32[64,256]{1,0:T(8,128)}, u32[]{:S(2)}) copy-start(f32[64,256]{1,0:T(8,128)} %param.17) | copy-start | bytes 196612
  57.7 18.8 %copy-start.6 = (f32[32,128]{1,0:T(8,128)S(1)}, f32[32,128]{1,0:T(8,128)}, u32[]{:S(2)}) copy-start(f32[32,128]{1,0:T(8,128)} %param.23) | copy-start | bytes 49156
  57.7 18.6 %collective-permute-start = (f32[16,64,128]{2,1,0:T(8,128)S(1)}, f32[16,64,128]{2,1,0:T(8,128)S(1)}, u32[]{:S(2)}, u32[]{:S(2)}) collective-permute-start(f32[16,64,128]{2,1,0:T(8,128)S(1)} %slice.58), channel_id=1, source_target_pairs={{0,2},{2,4},{4,6},{1,3},{3,5},{5,7},{8,10},{10,12},{12,14},{9,11},... | collective-permute-start | bytes 1572872 | tf_op jit(solution)/shard_map/ppermute | solution.py:12
  61.6 13.0 %all-to-all-start = ((f32[16,1,1024]{2,1,0:T(1,128)}), f32[16,1,1024]{2,1,0:T(1,128)S(1)}, u32[]{:S(2)}, u32[]{:S(2)}) async-start(f32[16,1,1024]{2,1,0:T(1,128)} %reshape.164), calls=%async_computation | async-start | bytes 131072 | tf_op jit(solution)/shard_map/all_to_all | solution.py:81
  109.8 24.0 %collective-permute-start.1 = (f32[16,64,128]{2,1,0:T(8,128)}, f32[16,64,128]{2,1,0:T(8,128)S(1)}, u32[]{:S(2)}, u32[]{:S(2)}) collective-permute-start(f32[16,64,128]{2,1,0:T(8,128)} %slice.61), channel_id=1, source_target_pairs={{0,2},{2,4},{4,6},{1,3},{3,5},{5,7},{8,10},{10,12},{12,14},{9,11},... | collective-permute-start | bytes 1572872 | tf_op jit(solution)/shard_map/ppermute | solution.py:12
  120.1 11.8 %all-to-all-start.2 = ((f32[16,1,1024]{2,1,0:T(1,128)}), f32[16,1,1024]{2,1,0:T(1,128)S(1)}, u32[]{:S(2)}, u32[]{:S(2)}) async-start(f32[16,1,1024]{2,1,0:T(1,128)} %reshape.166), calls=%async_computation.2 | async-start | bytes 131072 | tf_op jit(solution)/shard_map/all_to_all | solution.py:81
  132.8 1.2 copy-start.2
  132.8 1.6 copy-start.4
  140.5 2.7 %copy-start.9 = (pred[192]{0:T(512)(128)(4,1)S(1)}, pred[192]{0:T(512)(128)(4,1)}, u32[]{:S(2)}) copy-start(pred[192]{0:T(512)(128)(4,1)} %copy-done.8) | copy-start | bytes 580
  151.6 23.7 %copy-start.11 = (s32[128]{0:T(128)S(1)}, s32[128]{0:T(128)}, u32[]{:S(2)}) copy-start(s32[128]{0:T(128)} %copy-done.10) | copy-start | bytes 1540
  172.4 16.8 %collective-permute-start.2 = (f32[16,64,128]{2,1,0:T(8,128)}, f32[16,64,128]{2,1,0:T(8,128)S(1)}, u32[]{:S(2)}, u32[]{:S(2)}) collective-permute-start(f32[16,64,128]{2,1,0:T(8,128)} %slice.64), channel_id=1, source_target_pairs={{0,2},{2,4},{4,6},{1,3},{3,5},{5,7},{8,10},{10,12},{12,14},{9,11},... | collective-permute-start | bytes 1572872 | tf_op jit(solution)/shard_map/ppermute | solution.py:12
  176.4 10.9 %all-to-all-start.3 = ((f32[16,1,1024]{2,1,0:T(1,128)}), f32[16,1,1024]{2,1,0:T(1,128)S(1)}, u32[]{:S(2)}, u32[]{:S(2)}) async-start(f32[16,1,1024]{2,1,0:T(1,128)} %reshape.168), calls=%async_computation.3 | async-start | bytes 131072 | tf_op jit(solution)/shard_map/all_to_all | solution.py:81
  188.2 1.2 copy-start.3
  188.2 1.6 copy-start.5
Sparse Core Ops, SparseCore 0:
  9.6 19.4 all-gather.1
where the time goes:
time: 201 us; the launch traced here: 199 us
  other arithmetic  69.3 us (34%)
  starting transfers between devices  33.9 us (17%)
  matrix products  29.3 us (15%)
  local copies, waits for them, and re-layouts  27.8 us (14%)
  waiting for transfers between devices  21.7 us (11%)
  between operations  15.2 us (8%)
    scatter-add x3, other arithmetic, block_terms(): return jax.ops.segment_sum(prods, col_ids, num_segments=targets)  59.9 us
    dot_general x3, matrix products, block_terms(): jnp.einsum('ecn,enm->ecm', picked, mats, preferred_element_type=jnp.float32)  24.6 us
    all_to_all x3, waiting for transfers between devices, local(): lax.all_to_all(send_vals.reshape(network, slots, cases_here), ('sec', 'bl...  21 us
    all_to_all x3, starting transfers between devices, local(): lax.all_to_all(send_vals.reshape(network, slots, cases_here), ('sec', 'bl...  13.4 us
    ppermute x3, starting transfers between devices, shifted(): return lax.ppermute(block, axis, route)  12.2 us
    all_to_all x1, starting transfers between devices, local(): lax.all_to_all(bus_sent.reshape(network, slots), ('sec', 'blk'), split_ax...  8.34 us
    gather x3, local copies, waits for them, and re-layouts, block_terms(): picked = jnp.take(lam_rows, row_ids, axis=0)  8.1 us
    unnamed x48, local copies, waits for them, and re-layouts  6.59 us
  transfers between devices with their start and end apart: 8, of which 3 were waited for; matrix products, arithmetic and copies ran while one was open for 25% of the time, Pallas kernels for 0%

commit v1 on v0

v1 whole, which is shorter than its diff:
```python
import jax
import jax.numpy as jnp
from jax import lax
from jax.experimental import pallas as pl
from jax.experimental.pallas import tpu as pltpu
from jax.sharding import PartitionSpec as P

STEPS = 3
UNROLL = 16
CLASSES = 4
VMEM_LIMIT = 24 << 20

F32 = jnp.float32
BF16 = jnp.bfloat16
VM = pl.BlockSpec(memory_space=pltpu.VMEM)
SM = pl.BlockSpec(memory_space=pltpu.SMEM)


def kernel(body, outs, ins, name, scratch=(), out_specs=None):
    return pl.pallas_call(
        body,
        out_shape=outs,
        in_specs=[spec for _, spec in ins],
        out_specs=out_specs or tuple(VM for _ in outs),
        scratch_shapes=list(scratch),
        compiler_params=pltpu.CompilerParams(vmem_limit_bytes=VMEM_LIMIT),
        name=name,
    )(*[array for array, _ in ins])


def array(shape, dtype):
    return jax.ShapeDtypeStruct(shape, dtype)


def heads_of(lam, vertex, heads, cases, nodes):
    lane = lax.broadcasted_iota(jnp.int32, (cases, nodes), 1)

    def pick(s, kept):
        where = vertex[s]
        row = lam[where // nodes]
        turned = pltpu.roll(row, lax.rem(s - lax.rem(where, nodes) + nodes, nodes), 1)
        return jnp.where(lane == s, turned, kept)

    return lax.fori_loop(0, heads, pick, jnp.zeros((cases, nodes), F32), unroll=8)


def local(
    vertex_costate,
    inverter_costate,
    highvoltage_costate,
    derivative_tiles,
    tile_source_index,
    tile_target_index,
    inverter_decay_factor,
    costate_to_inverter_factor,
    inverter_to_costate_factor,
    distribution_entry_vertex,
    distribution_entry_holder,
    distribution_entry_substation,
    highvoltage_derivative_matrix,
):
    blocks, cases, nodes = vertex_costate.shape
    rim = blocks // 2
    low = blocks // 2
    targets = blocks + rim
    stored = derivative_tiles.shape[0]
    sections = lax.axis_size("sec")
    owners = lax.axis_size("blk")
    network = sections * owners
    heads = distribution_entry_vertex.shape[0]
    slots = max(2, 2 * heads // network)
    buses = highvoltage_derivative_matrix.shape[1]
    span = stored + UNROLL
    rows_sent = network * 2 * slots

    state = (blocks, cases, nodes)
    half = (low, cases, nodes)
    padded = (low + 1, cases, nodes)
    swap = [(0, 1), (1, 0)]
    onward = [(i, (i + 1) % owners) for i in range(owners)]

    own_codes = tile_source_index | (tile_target_index << 8)
    other_codes = lax.ppermute(own_codes, "case", swap)
    own = derivative_tiles
    other = lax.ppermute(own, "case", swap)
    follows = (lax.axis_index("blk") > 0).astype(jnp.int32).reshape(1)

    def run(lists, counts, segment, lam, tiles, acc):
        start = segment * span

        def some(i, carry):
            codes = [lists[start + i * UNROLL + u] for u in range(UNROLL)]
            prods = [
                jnp.dot(lam[(c >> 8) & 255], tiles[c & 255], preferred_element_type=F32)
                for c in codes
            ]
            for c, prod in zip(codes, prods):
                acc[c >> 16] += prod
            return carry

        lax.fori_loop(0, (counts[segment] + UNROLL - 1) // UNROLL, some, 0)

    def first_body(
        codes, vertex, lam, icar, tiles, decay, inflow, outflow, acc, lo, hi, icar_next, head, lam_bf
    ):
        zero = jnp.zeros((cases, nodes), BF16)
        for b in range(blocks):
            row = lam[b]
            rounded = row.astype(BF16)
            lam_bf[b] = rounded
            if b < low:
                lo[b] = rounded
            else:
                hi[b - low] = rounded
            kept = icar[b]
            acc[b] = outflow[b : b + 1, :] * kept
            icar_next[b] = decay[b : b + 1, :] * kept + inflow[b : b + 1, :] * row
        lo[low] = zero
        hi[blocks - low] = zero
        for b in range(rim):
            acc[blocks + b] = jnp.zeros((cases, nodes), F32)

        def some(i, carry):
            codes_here = [codes[i * UNROLL + u] for u in range(UNROLL)]
            prods = [
                jnp.dot(lam_bf[c & 255], tiles[i * UNROLL + u], preferred_element_type=F32)
                for u, c in enumerate(codes_here)
            ]
            for c, prod in zip(codes_here, prods):
                acc[c >> 8] += prod
            return carry

        lax.fori_loop(0, stored // UNROLL, some, 0)
        head[...] = heads_of(lam, vertex, heads, cases, nodes).astype(BF16)

    acc, lo, hi, icar, head0 = kernel(
        first_body,
        (
            array((targets, cases, nodes), F32),
            array(padded, BF16),
            array(padded, BF16),
            array(state, F32),
            array((cases, heads), BF16),
        ),
        [
            (own_codes, SM),
            (distribution_entry_vertex, SM),
            (vertex_costate, VM),
            (inverter_costate, VM),
            (own, VM),
            (inverter_decay_factor, VM),
            (costate_to_inverter_factor, VM),
            (inverter_to_costate_factor, VM),
        ],
        "first",
        scratch=[pltpu.VMEM(state, BF16)],
    )

    def sort_body(own_code, other_code, lists, counts):
        for side, code in enumerate((own_code, other_code)):

            def place(e, used, code=code, side=side):
                c = code[e]
                row = c & 255
                target = c >> 8
                is_low = (row < low).astype(jnp.int32)
                is_own = (target < blocks).astype(jnp.int32)
                kind = 2 * is_own + is_low
                at = (used >> (8 * kind)) & 255
                lists[(side * CLASSES + kind) * span + at] = (
                    e | ((row - low * (1 - is_low)) << 8) | ((target - blocks * (1 - is_own)) << 16)
                )
                return used + (1 << (8 * kind))

            used = lax.fori_loop(0, stored, place, jnp.int32(0), unroll=8)
            for kind in range(CLASSES):
                at = (used >> (8 * kind)) & 255
                counts[side * CLASSES + kind] = at
                for u in range(UNROLL):
                    lists[(side * CLASSES + kind) * span + at + u] = low << 8

    lists, counts = kernel(
        sort_body,
        (array((2 * CLASSES * span,), jnp.int32), array((2 * CLASSES,), jnp.int32)),
        [(own_codes, SM), (other_codes, SM)],
        "sort",
        out_specs=(SM, SM),
    )

    def rim_first_body(lists, counts, acc, lo, hi, other, out, sums):
        sums[...] = acc[blocks:]
        run(lists, counts, CLASSES + 0, hi, other, sums)
        run(lists, counts, CLASSES + 1, lo, other, sums)
        out[...] = sums[...].astype(BF16)

    (leaving,) = kernel(
        rim_first_body,
        (array((rim, cases, nodes), BF16),),
        [(lists, SM), (counts, SM), (acc, VM), (lo, VM), (hi, VM), (other, VM)],
        "rim_first",
        scratch=[pltpu.VMEM((rim, cases, nodes), F32)],
    )

    def begin_next(lists, counts, lam, icar, outflow, own, other, acc, hi):
        for b in range(blocks):
            acc[b] = outflow[b : b + 1, :] * icar[b]
        for b in range(rim):
            acc[blocks + b] = jnp.zeros((cases, nodes), F32)
        for b in range(low, blocks):
            hi[b - low] = lam[b].astype(BF16)
        hi[blocks - low] = jnp.zeros((cases, nodes), BF16)
        for side, tiles in enumerate((own, other)):
            run(lists, counts, side * CLASSES + 0, hi, tiles, acc.at[pl.ds(blocks, rim)])
            run(lists, counts, side * CLASSES + 2, hi, tiles, acc)

    def main_first_body(
        lists, counts, acc, lo, hi, icar, own, other, outflow, lam_next, acc_next, hi_next
    ):
        lam_next[...] = acc[:blocks]
        run(lists, counts, CLASSES + 2, hi, other, lam_next)
        run(lists, counts, CLASSES + 3, lo, other, lam_next)
        begin_next(lists, counts, lam_next, icar, outflow, own, other, acc_next, hi_next)

    def rim_body(lists, counts, follows, arrived, lam, acc, own, other, out, full, lo, sums):
        keep = follows[0] > 0
        for b in range(low):
            came = jnp.where(keep, arrived[b].astype(F32), 0.0)
            row = lam[b] + came
            full[b] = row
            lo[b] = row.astype(BF16)
        lo[low] = jnp.zeros((cases, nodes), BF16)
        sums[...] = acc[blocks:]
        run(lists, counts, 1, lo, own, sums)
        run(lists, counts, CLASSES + 1, lo, other, sums)
        out[...] = sums[...].astype(BF16)
        full[low:] = lam[low:]

    def finish_step(lists, counts, lam, lo, acc, icar, decay, inflow, own, other, lam_next, icar_next):
        lam_next[...] = acc[:blocks]
        run(lists, counts, 3, lo, own, lam_next)
        run(lists, counts, CLASSES + 3, lo, other, lam_next)
        for b in range(blocks):
            icar_next[b] = decay[b : b + 1, :] * icar[b] + inflow[b : b + 1, :] * lam[b]

    def main_body(
        lists, counts, vertex, lam, lo, acc, icar, own, other, decay, inflow, outflow,
        lam_next, acc_next, hi_next, icar_next, head,
    ):
        finish_step(
            lists, counts, lam, lo, acc, icar, decay, inflow, own, other, lam_next, icar_next
        )
        begin_next(lists, counts, lam_next, icar_next, outflow, own, other, acc_next, hi_next)
        head[...] = heads_of(lam, vertex, heads, cases, nodes).astype(BF16)

    def main_last_body(
        lists, counts, lam, lo, acc, icar, own, other, decay, inflow, lam_next, icar_next
    ):
        finish_step(
            lists, counts, lam, lo, acc, icar, decay, inflow, own, other, lam_next, icar_next
        )

    def pack_body(vertex, owner_col, owner_row, bus_row, lam, head0, head1, out):
        head2 = heads_of(lam, vertex, heads, cases, nodes)
        before = lax.broadcasted_iota(jnp.int32, (heads, heads), 0)
        after = lax.broadcasted_iota(jnp.int32, (heads, heads), 1)
        same = jnp.logical_and(owner_col[...] == owner_row[...], before < after)
        slot = jnp.sum(same.astype(jnp.int32), axis=0, keepdims=True)
        dest = owner_row[...] * (2 * slots) + slot
        row = lax.broadcasted_iota(jnp.int32, (rows_sent, heads), 0)
        place_a = (row == dest).astype(F32).astype(BF16)
        place_b = (row == dest + slots).astype(F32).astype(BF16)
        bus = jnp.broadcast_to((bus_row[...] + 1).astype(F32), (nodes - cases, heads))
        pair_a = jnp.concatenate([head0[...], head1[...]], axis=0)
        pair_b = jnp.concatenate([head2, bus], axis=0).astype(BF16)
        dims = (((1,), (1,)), ((), ()))
        sent = lax.dot_general(place_a, pair_a, dims, preferred_element_type=F32)
        sent += lax.dot_general(place_b, pair_b, dims, preferred_element_type=F32)
        out[...] = sent.astype(BF16)

    def trans_body(received, trans, matrix, out):
        got = received[...].astype(F32)
        row = lax.broadcasted_iota(jnp.int32, (rows_sent, buses), 0)
        second = lax.rem(row, 2 * slots) >= slots
        column = lax.broadcasted_iota(jnp.int32, (rows_sent, buses), 1)
        label = got[:, cases : cases + 1].astype(jnp.int32) - 1
        hot_b = jnp.where(jnp.logical_and(label == column, second), 1.0, 0.0)
        hot_a = pltpu.roll(hot_b, rows_sent - slots, 0)
        dims = (((0,), (0,)), ((), ()))
        first = lax.dot_general(received[...], hot_a.astype(BF16), dims, preferred_element_type=F32)
        last = lax.dot_general(received[...], hot_b.astype(BF16), dims, preferred_element_type=F32)
        value = trans[...]
        for inj in (first[:cases], first[cases:], last[:cases]):
            value = jnp.dot(value.astype(BF16), matrix[...], preferred_element_type=F32) + inj
        out[...] = value

    def last_body(follows, arrived, lam, out):
        keep = follows[0] > 0
        for b in range(low):
            out[b] = lam[b] + jnp.where(keep, arrived[b].astype(F32), 0.0)

    listed = [(lists, SM), (counts, SM)]
    tiles = [(own, VM), (other, VM)]
    factors = [(inverter_decay_factor, VM), (costate_to_inverter_factor, VM)]
    outflow = (inverter_to_costate_factor, VM)
    acc_type = array((targets, cases, nodes), F32)

    arriving = lax.ppermute(leaving, "blk", onward)
    lam, acc, hi = kernel(
        main_first_body,
        (array(state, F32), acc_type, array(padded, BF16)),
        listed + [(acc, VM), (lo, VM), (hi, VM), (icar, VM)] + tiles + [outflow],
        "main_first",
    )
    for step in range(1, STEPS):
        leaving, full, lo = kernel(
            rim_body,
            (array((rim, cases, nodes), BF16), array(state, F32), array(padded, BF16)),
            listed + [(follows, SM), (arriving, VM), (lam, VM), (acc, VM)] + tiles,
            "rim",
            scratch=[pltpu.VMEM((rim, cases, nodes), F32)],
        )
        arriving = lax.ppermute(leaving, "blk", onward)
        if step < STEPS - 1:
            lam, acc, hi, icar, head1 = kernel(
                main_body,
                (
                    array(state, F32),
                    acc_type,
                    array(padded, BF16),
                    array(state, F32),
                    array((cases, heads), BF16),
                ),
                listed
                + [(distribution_entry_vertex, SM), (full, VM), (lo, VM), (acc, VM), (icar, VM)]
                + tiles
                + factors
                + [outflow],
                "main",
            )
        else:
            (sent,) = kernel(
                pack_body,
                (array((rows_sent, nodes), BF16),),
                [
                    (distribution_entry_vertex, SM),
                    (distribution_entry_holder, VM),
                    (distribution_entry_holder.reshape(1, heads), VM),
                    (distribution_entry_substation.reshape(1, heads), VM),
                    (full, VM),
                    (head0, VM),
                    (head1, VM),
                ],
                "pack",
            )
            received = lax.all_to_all(
                sent.reshape(network, 2 * slots, nodes),
                ("sec", "blk"),
                split_axis=0,
                concat_axis=0,
                tiled=True,
            ).reshape(rows_sent, nodes)
            lam, icar = kernel(
                main_last_body,
                (array(state, F32), array(state, F32)),
                listed + [(full, VM), (lo, VM), (acc, VM), (icar, VM)] + tiles + factors,
                "main_last",
            )
    (trans,) = kernel(
        trans_body,
        (array(highvoltage_costate.shape, F32),),
        [(received, VM), (highvoltage_costate, VM), (highvoltage_derivative_matrix, VM)],
        "trans",
    )
    lower = pl.BlockSpec(half, lambda i: (0, 0, 0))
    lam = pl.pallas_call(
        last_body,
        grid=(1,),
        out_shape=array(state, F32),
        in_specs=[SM, lower, lower],
        out_specs=lower,
        input_output_aliases={2: 0},
        name="last",
    )(follows, arriving, lam)
    return (lam, icar, trans)


def solution(mesh):
    placed = (
        P(("sec", "blk"), "case", None),
        P(("sec", "blk"), "case", None),
        P("case", ("sec", "blk")),
        P(("sec", "blk", "case"), None, None),
        P(("sec", "blk", "case")),
        P(("sec", "blk", "case")),
        P(("sec", "blk"), None),
        P(("sec", "blk"), None),
        P(("sec", "blk"), None),
        P(("sec", "blk")),
        P(("sec", "blk"), None),
        P(("sec", "blk")),
        P(("sec", "blk"), None),
    )
    return jax.shard_map(
        local,
        mesh=mesh,
        in_specs=placed,
        out_specs=(
            P(("sec", "blk"), "case", None),
            P(("sec", "blk"), "case", None),
            P("case", ("sec", "blk")),
        ),
        check_vma=False,
    )
```

time: 201 us -> 80.6 us (0.40)
  other arithmetic: 69.3 us -> 0.67 us
  Pallas kernels: 0 us -> 36.9 us
  matrix products: 29.3 us -> 0 us
  starting transfers between devices: 33.9 us -> 12.4 us
  waiting for transfers between devices: 21.7 us -> 0.91 us
  between operations: 15.2 us -> 0.86 us
    scatter-add x3 -> x0, other arithmetic: 59.9 us -> none  [block_terms(): return jax.ops.segment_sum(prods, col_ids, num_segments=targets)]
    pallas_call x0 -> x11, Pallas kernels: none -> 36.9 us  [the longest x10 34.9 us: kernel(): pl.pallas_call(body, out_shape=outs, in_specs=[spec for _, spec in ins],...]
    dot_general x13 -> x0, matrix products: 29.3 us -> none  [the longest x3 24.6 us: block_terms(): jnp.einsum('ecn,enm->ecm', picked, mats, preferred_element_type=jnp.float32)]
    all_to_all x4 -> x1, waiting for transfers between devices: 21 us -> 0.01 us  [local(): lax.all_to_all(sent.reshape(network, 2 * slots, nodes), ('sec', 'blk'), s...]
    unnamed x48 -> x89, local copies, waits for them, and re-layouts: 6.59 us -> 27.5 us
    all_to_all x4 -> x1, starting transfers between devices: 21.7 us -> 6.99 us  [local(): lax.all_to_all(sent.reshape(network, 2 * slots, nodes), ('sec', 'blk'), s...]
    gather x6 -> x0, local copies, waits for them, and re-layouts: 13.7 us -> none  [the longest x3 8.1 us: block_terms(): picked = jnp.take(lam_rows, row_ids, axis=0)]
    ppermute x3 -> x5, starting transfers between devices: 12.2 us -> 5.44 us  [the longest x3 4.86 us: local(): arriving = lax.ppermute(leaving, 'blk', onward)]
  transfers between devices with their start and end apart: 8 -> 6, of which waited for: 3 -> 1; matrix products, arithmetic and copies ran while one was open for 25% -> 1% of each run, Pallas kernels for 0% -> 35%
where the time goes in v1:
time: 80.6 us; the launch traced here: 79.3 us
  Pallas kernels  36.9 us (46%)
  local copies, waits for them, and re-layouts  27.5 us (34%)
  starting transfers between devices  12.4 us (15%)
  waiting for transfers between devices  0.91 us (1%)
  between operations  0.86 us (1%)
    pallas_call x10, Pallas kernels, kernel(): pl.pallas_call(body, out_shape=outs, in_specs=[spec for _, spec in ins],...  34.9 us
    unnamed x89, local copies, waits for them, and re-layouts  27.5 us
    all_to_all x1, starting transfers between devices, local(): lax.all_to_all(sent.reshape(network, 2 * slots, nodes), ('sec', 'blk'), s...  6.99 us
    ppermute x3, starting transfers between devices, local(): arriving = lax.ppermute(leaving, 'blk', onward)  4.86 us
    pallas_call x1, Pallas kernels, local(): pl.pallas_call(last_body, grid=(1,), out_shape=array(state, F32), in_spec...  1.97 us
  transfers between devices with their start and end apart: 6, of which 1 were waited for; matrix products, arithmetic and copies ran while one was open for 1% of the time, Pallas kernels for 35%

profile of v1, /device:TPU:0, one launch (start us, length us, event | category | flops | bytes accessed | tf_op | source)
XLA Modules:
  0.0 79.3 jit_solution(11270438147061414080)
XLA Ops:
  0.6 0.6 collective-permute-start.1
  1.2 0.7 shift-left_or_fusion.own_code.codes
  1.9 0.0 collective-permute-start
  1.9 1.9 %copy-done = bf16[96,128,128]{2,1,0:T(8,128)(2,1)S(1)} copy-done((bf16[96,128,128]{2,1,0:T(8,128)(2,1)S(1)}, bf16[96,128,128]{2,1,0:T(8,128)(2,1)}, u32[]{:S(2)}) %copy-start) | copy-done | bytes 3145752
  3.8 1.2 %copy-done.20 = f32[32,64,128]{2,1,0:T(8,128)S(1)} copy-done((f32[32,64,128]{2,1,0:T(8,128)S(1)}, f32[32,64,128]{2,1,0:T(8,128)}, u32[]{:S(2)}) %copy-start.20) | copy-done | bytes 1048600
  5.0 1.2 %copy-done.21 = f32[32,64,128]{2,1,0:T(8,128)S(1)} copy-done((f32[32,64,128]{2,1,0:T(8,128)S(1)}, f32[32,64,128]{2,1,0:T(8,128)}, u32[]{:S(2)}) %copy-start.21) | copy-done | bytes 1048600
  6.2 0.7 copy-done.25
  6.9 0.7 copy-done.27
  7.7 0.7 copy-done.30
  8.4 0.7 copy-done.40
  9.0 4.7 %first.1 = (f32[48,64,128]{2,1,0:T(8,128)S(1)}, bf16[17,64,128]{2,1,0:T(8,128)(2,1)S(1)}, bf16[17,64,128]{2,1,0:T(8,128)(2,1)S(1)}, f32[32,64,128]{2,1,0:T(8,128)S(1)}, bf16[64,128]{1,0:T(8,128)(2,1)S(1)}) custom-call(s32[96]{0:T(128)S(1)} %shift-left_or_fusion.own_code.codes, s32[128]{0:T(128)S(1)} %copy-done.40, f32[32,64,128]{2,1,0:T(8,128)S(1)} %copy-done.20, ...), custom_call_target="tpu_custom_call" | custom-call | tf_op jit(solution)/shard_map/first/pallas_call | solution.py:20
  13.7 0.0 copy-start.10
  13.7 1.0 %copy-done.10 = f32[32,64,128]{2,1,0:T(8,128)} copy-done((f32[32,64,128]{2,1,0:T(8,128)}, f32[32,64,128]{2,1,0:T(8,128)S(1)}, u32[]{:S(2)}) %copy-start.10) | copy-done | bytes 1048600
  14.7 0.0 collective-permute-done.other_code
  14.7 3.1 %sort.1 = (s32[896]{0:T(1024)S(1)}, s32[8]{0:T(128)S(1)}) custom-call(s32[96]{0:T(128)S(1)} %shift-left_or_fusion.own_code.codes, s32[96]{0:T(128)S(1)} %collective-permute-done.other_code), custom_call_target="tpu_custom_call" | custom-call | tf_op jit(solution)/shard_map/sort/pallas_call | solution.py:20
  17.8 0.0 copy-start.22
  17.8 0.0 copy-start.35
  17.8 0.0 collective-permute-done.1.other
  17.8 0.0 copy-start.2
  17.8 0.0 copy-start.1
  17.8 0.0 copy-start.26
  17.8 2.2 %rim_first.1 = bf16[16,64,128]{2,1,0:T(8,128)(2,1)} custom-call(s32[896]{0:T(1024)S(1)} %get-tuple-element.24.lists, s32[8]{0:T(128)S(1)} %get-tuple-element.25.counts, f32[48,64,128]{2,1,0:T(8,128)S(1)} %get-tuple-element.26.acc, bf16[17,64,128]{2,1,0:T(8,128)(2,1)S(1)} %get-tuple-element.27.lo, bf16[17,64,128]{2,1,0:T(8,128)(2,1)S(1)} %get-tuple-element.28.hi, ...), custom_call_target="tpu_custom_call" | custom-call | tf_op jit(solution)/shard_map/rim_first/pallas_call | solution.py:20
  20.1 0.0 copy-done.8
  20.1 0.0 copy-done.16
  20.1 3.1 %collective-permute-start.2 = (bf16[16,64,128]{2,1,0:T(8,128)(2,1)}, bf16[16,64,128]{2,1,0:T(8,128)(2,1)}, u32[]{:S(2)}, u32[]{:S(2)}) collective-permute-start(bf16[16,64,128]{2,1,0:T(8,128)(2,1)} %rim_first.1), channel_id=1, source_target_pairs={{0,2},{2,4},{4,6},{6,0},{1,3},{3,5},{5,7},{7,1},{8,10},{10,12},{12... | collective-permute-start | bytes 786440 | tf_op jit(solution)/shard_map/ppermute | solution.py:307
  23.2 0.0 copy-done.1
  23.2 1.9 %copy-done.3 = bf16[96,128,128]{2,1,0:T(8,128)(2,1)S(1)} copy-done((bf16[96,128,128]{2,1,0:T(8,128)(2,1)S(1)}, bf16[96,128,128]{2,1,0:T(8,128)(2,1)}, u32[]{:S(2)}) %copy-start.3) | copy-done | bytes 3145752
  25.1 1.4 %copy-done.9 = f32[48,64,128]{2,1,0:T(8,128)S(1)} copy-done((f32[48,64,128]{2,1,0:T(8,128)S(1)}, f32[48,64,128]{2,1,0:T(8,128)}, u32[]{:S(2)}) %copy-start.9) | copy-done | bytes 1572888
  26.5 1.2 %copy-done.11 = f32[32,64,128]{2,1,0:T(8,128)S(1)} copy-done((f32[32,64,128]{2,1,0:T(8,128)S(1)}, f32[32,64,128]{2,1,0:T(8,128)}, u32[]{:S(2)}) %copy-start.11) | copy-done | bytes 1048600
  27.7 1.0 %copy-done.17 = bf16[17,64,128]{2,1,0:T(8,128)(2,1)S(1)} copy-done((bf16[17,64,128]{2,1,0:T(8,128)(2,1)S(1)}, bf16[17,64,128]{2,1,0:T(8,128)(2,1)}, u32[]{:S(2)}) %copy-start.17) | copy-done | bytes 278552
  28.7 4.9 %main_first.1 = (f32[32,64,128]{2,1,0:T(8,128)S(1)}, f32[48,64,128]{2,1,0:T(8,128)S(1)}, bf16[17,64,128]{2,1,0:T(8,128)(2,1)}) custom-call(s32[896]{0:T(1024)S(1)} %get-tuple-element.24.lists, s32[8]{0:T(128)S(1)} %get-tuple-element.25.counts, f32[48,64,128]{2,1,0:T(8,128)S(1)} %copy-done.9, bf16[17,64,128]{2,1,0:T(8,128)(2,1)S(1)} %get-tuple-element.27.lo, ...), custom_call_target="tpu_custom_call" | custom-call | tf_op jit(solution)/shard_map/main_first/pallas_call | solution.py:20
  33.6 0.0 collective-permute-done.2.arrived
  33.6 0.0 copy-start.28
  33.6 0.0 copy-start.31
  33.6 0.0 copy-start.41
  33.6 2.4 %rim.2 = (bf16[16,64,128]{2,1,0:T(8,128)(2,1)S(1)}, f32[32,64,128]{2,1,0:T(8,128)S(1)}, bf16[17,64,128]{2,1,0:T(8,128)(2,1)S(1)}) custom-call(s32[896]{0:T(1024)S(1)} %get-tuple-element.24.lists, s32[8]{0:T(128)S(1)} %get-tuple-element.25.counts, s32[1]{0:T(128)} %bitcast.follows, bf16[16,64,128]{2,1,0:T(8,128)(2,1)} %collective-permute-done.2.arrived, ...), custom_call_target="tpu_custom_call" | custom-call | tf_op jit(solution)/shard_map/rim/pallas_call | solution.py:20
  36.1 1.6 %collective-permute-start.3 = (bf16[16,64,128]{2,1,0:T(8,128)(2,1)S(1)}, bf16[16,64,128]{2,1,0:T(8,128)(2,1)S(1)}, u32[]{:S(2)}, u32[]{:S(2)}) collective-permute-start(bf16[16,64,128]{2,1,0:T(8,128)(2,1)S(1)} %get-tuple-element.32), channel_id=1, source_target_pairs={{0,2},{2,4},{4,6},{6,0},{1,3},{3,5},{5,7},{7,1},{8,10},{10,12},{12... | collective-permute-start | bytes 786440 | tf_op jit(solution)/shard_map/ppermute | solution.py:322
  37.7 6.9 %main.1 = (f32[32,64,128]{2,1,0:T(8,128)S(1)}, f32[48,64,128]{2,1,0:T(8,128)S(1)}, bf16[17,64,128]{2,1,0:T(8,128)(2,1)}, f32[32,64,128]{2,1,0:T(8,128)S(1)}, bf16[64,128]{1,0:T(8,128)(2,1)S(1)}) custom-call(s32[896]{0:T(1024)S(1)} %get-tuple-element.24.lists, s32[8]{0:T(128)S(1)} %get-tuple-element.25.counts, s32[128]{0:T(128)S(1)} %copy-done.41, ...), custom_call_target="tpu_custom_call" | custom-call | tf_op jit(solution)/shard_map/main/pallas_call | solution.py:20
  44.7 0.9 %collective-permute-done.3.arrived = bf16[16,64,128]{2,1,0:T(8,128)(2,1)S(1)} collective-permute-done((bf16[16,64,128]{2,1,0:T(8,128)(2,1)S(1)}, bf16[16,64,128]{2,1,0:T(8,128)(2,1)S(1)}, u32[]{:S(2)}, u32[]{:S(2)}) %collective-permute-start.3) | collective-permute-done | bytes 262176 | tf_op jit(solution)/shard_map/ppermute | solution.py:322
  45.6 0.7 copy-done.23
  46.2 0.6 copy-done.36
  46.9 2.6 %rim.3 = (bf16[16,64,128]{2,1,0:T(8,128)(2,1)}, f32[32,64,128]{2,1,0:T(8,128)S(1)}, bf16[17,64,128]{2,1,0:T(8,128)(2,1)S(1)}) custom-call(s32[896]{0:T(1024)S(1)} %copy-done.23, s32[8]{0:T(128)S(1)} %copy-done.36, s32[1]{0:T(128)} %bitcast.follows, bf16[16,64,128]{2,1,0:T(8,128)(2,1)S(1)} %collective-permute-done.3.arrived, ...), custom_call_target="tpu_custom_call" | custom-call | tf_op jit(solution)/shard_map/rim/pallas_call | solution.py:20
  49.5 1.0 %copy-done.13 = f32[32,64,128]{2,1,0:T(8,128)} copy-done((f32[32,64,128]{2,1,0:T(8,128)}, f32[32,64,128]{2,1,0:T(8,128)S(1)}, u32[]{:S(2)}) %copy-start.13) | copy-done | bytes 1048600
  50.4 0.1 collective-permute-start.4
  50.6 0.1 copy.17.owner_col
  50.7 0.0 copy-start.14
  50.7 1.2 %copy-done.14 = f32[32,64,128]{2,1,0:T(8,128)S(1)} copy-done((f32[32,64,128]{2,1,0:T(8,128)S(1)}, f32[32,64,128]{2,1,0:T(8,128)}, u32[]{:S(2)}) %copy-start.14) | copy-done | bytes 1048600
  51.9 3.7 %pack.1 = bf16[512,128]{1,0:T(8,128)(2,1)} custom-call(s32[128]{0:T(128)S(1)} %copy-done.41, s32[128,1]{1,0:T(8,128)S(1)} %copy.17.owner_col, s32[1,128]{1,0:T(1,128)S(1)} %bitcast.6, s32[1,128]{1,0:T(1,128)S(1)} %bitcast.7, f32[32,64,128]{2,1,0:T(8,128)S(1)} %copy-done.14, bf16[64,128]{1,0:T(8,128)(2,1)S(1)} %copy-done.39, ...), custom_call_target="tpu_custom_call" | custom-call | tf_op jit(solution)/shard_map/pack/pallas_call | solution.py:20
  55.6 7.0 %all-to-all-start = ((bf16[16,32,128]{2,1,0:T(8,128)(2,1)}), bf16[16,32,128]{2,1,0:T(8,128)(2,1)S(1)}, u32[]{:S(2)}, u32[]{:S(2)}) async-start(bf16[16,32,128]{2,1,0:T(8,128)(2,1)} %bitcast.3), calls=%async_computation | async-start | bytes 262144 | tf_op jit(solution)/shard_map/all_to_all | solution.py:355
  62.6 1.9 %copy-done.5 = bf16[96,128,128]{2,1,0:T(8,128)(2,1)S(1)} copy-done((bf16[96,128,128]{2,1,0:T(8,128)(2,1)S(1)}, bf16[96,128,128]{2,1,0:T(8,128)(2,1)}, u32[]{:S(2)}) %copy-start.5) | copy-done | bytes 3145752
  64.5 1.4 %copy-done.7 = f32[48,64,128]{2,1,0:T(8,128)S(1)} copy-done((f32[48,64,128]{2,1,0:T(8,128)S(1)}, f32[48,64,128]{2,1,0:T(8,128)}, u32[]{:S(2)}) %copy-start.7) | copy-done | bytes 1572888
  65.9 1.2 %copy-done.15 = f32[32,64,128]{2,1,0:T(8,128)S(1)} copy-done((f32[32,64,128]{2,1,0:T(8,128)S(1)}, f32[32,64,128]{2,1,0:T(8,128)}, u32[]{:S(2)}) %copy-start.15) | copy-done | bytes 1048600
  67.1 1.2 %copy-done.19 = f32[32,64,128]{2,1,0:T(8,128)S(1)} copy-done((f32[32,64,128]{2,1,0:T(8,128)S(1)}, f32[32,64,128]{2,1,0:T(8,128)}, u32[]{:S(2)}) %copy-start.19) | copy-done | bytes 1048600
  68.4 0.7 copy-done.24
  69.0 0.7 copy-done.29
  69.8 0.7 copy-done.32
  70.5 0.6 copy-done.37
  71.1 3.2 %main_last.1 = (f32[32,64,128]{2,1,0:T(8,128)}, f32[32,64,128]{2,1,0:T(8,128)}) custom-call(s32[896]{0:T(1024)S(1)} %copy-done.24, s32[8]{0:T(128)S(1)} %copy-done.37, f32[32,64,128]{2,1,0:T(8,128)S(1)} %copy-done.15, bf16[17,64,128]{2,1,0:T(8,128)(2,1)S(1)} %get-tuple-element.39.lo, f32[48,64,128]{2,1,0:T(8,128)S(1)} %copy-done.7, ...), custom_call_target="tpu_custom_call" | custom-call | tf_op jit(solution)/shard_map/main_last/pallas_call | solution.py:20
  74.3 0.0 all-to-all-done
  74.3 0.9 %copy-done.33 = bf16[256,256]{1,0:T(8,128)(2,1)S(1)} copy-done((bf16[256,256]{1,0:T(8,128)(2,1)S(1)}, bf16[256,256]{1,0:T(8,128)(2,1)}, u32[]{:S(2)}) %copy-start.33) | copy-done | bytes 131096
  75.3 0.8 %copy-done.34 = f32[64,256]{1,0:T(8,128)S(1)} copy-done((f32[64,256]{1,0:T(8,128)S(1)}, f32[64,256]{1,0:T(8,128)}, u32[]{:S(2)}) %copy-start.34) | copy-done | bytes 65560
  76.1 1.2 %trans.2 = f32[64,256]{1,0:T(8,128)} custom-call(bf16[512,128]{1,0:T(8,128)(2,1)S(1)} %bitcast.5, f32[64,256]{1,0:T(8,128)S(1)} %copy-done.34, bf16[256,256]{1,0:T(8,128)(2,1)S(1)} %copy-done.33), custom_call_target="tpu_custom_call" | custom-call | tf_op jit(solution)/shard_map/trans/pallas_call | solution.py:20
  77.3 0.0 collective-permute-done.4.arrived
  77.3 2.0 %last.1 = f32[32,64,128]{2,1,0:T(8,128)} custom-call(s32[1]{0:T(128)} %bitcast.follows, bf16[16,64,128]{2,1,0:T(8,128)(2,1)} %collective-permute-done.4.arrived, f32[32,64,128]{2,1,0:T(8,128)} %get-tuple-element.41.lam), custom_call_target="tpu_custom_call", output_to_operand_aliasing={{}: (2, {})} | custom-call | tf_op jit(solution)/shard_map/last/pallas_call | solution.py:375
  (49 shorter events, 0.1 us)
Async XLA Ops:
  0.6 17.2 %collective-permute-start.1 = (bf16[96,128,128]{2,1,0:T(8,128)(2,1)}, bf16[96,128,128]{2,1,0:T(8,128)(2,1)S(1)}, u32[]{:S(2)}, u32[]{:S(2)}) collective-permute-start(bf16[96,128,128]{2,1,0:T(8,128)(2,1)} %own.9), channel_id=1, source_target_pairs={{0,1},{1,0},{2,3},{3,2},{4,5},{5,4},{6,7},{7,6},{8,9},{9,8},{10,11... | collective-permute-start | bytes 9437192 | tf_op jit(solution)/shard_map/ppermute | solution.py:85
  1.9 12.8 %collective-permute-start = (s32[96]{0:T(128)S(1)}, s32[96]{0:T(128)S(1)}, u32[]{:S(2)}, u32[]{:S(2)}) collective-permute-start(s32[96]{0:T(128)S(1)} %shift-left_or_fusion.own_code.codes), channel_id=1, source_target_pairs={{0,1},{1,0},{2,3},{3,2},{4,5},{5,4},{6,7},{7,6},{8,9},{9,8},{10,11... | collective-permute-start | bytes 1160 | tf_op jit(solution)/shard_map/ppermute | solution.py:83
  1.9 1.9 %copy-start = (bf16[96,128,128]{2,1,0:T(8,128)(2,1)S(1)}, bf16[96,128,128]{2,1,0:T(8,128)(2,1)}, u32[]{:S(2)}) copy-start(bf16[96,128,128]{2,1,0:T(8,128)(2,1)} %own.9) | copy-start | bytes 9437188
  3.8 1.2 %copy-start.20 = (f32[32,64,128]{2,1,0:T(8,128)S(1)}, f32[32,64,128]{2,1,0:T(8,128)}, u32[]{:S(2)}) copy-start(f32[32,64,128]{2,1,0:T(8,128)} %lam.1) | copy-start | bytes 3145732
  5.0 1.2 %copy-start.21 = (f32[32,64,128]{2,1,0:T(8,128)S(1)}, f32[32,64,128]{2,1,0:T(8,128)}, u32[]{:S(2)}) copy-start(f32[32,64,128]{2,1,0:T(8,128)} %icar.1) | copy-start | bytes 3145732
  6.2 0.7 copy-start.25
  6.9 0.7 copy-start.27
  7.7 0.7 copy-start.30
  8.4 0.7 copy-start.40
  13.7 1.0 %copy-start.10 = (f32[32,64,128]{2,1,0:T(8,128)}, f32[32,64,128]{2,1,0:T(8,128)S(1)}, u32[]{:S(2)}) copy-start(f32[32,64,128]{2,1,0:T(8,128)S(1)} %get-tuple-element.29.icar) | copy-start | bytes 3145732
  14.7 5.4 %copy-start.8 = (f32[48,64,128]{2,1,0:T(8,128)}, f32[48,64,128]{2,1,0:T(8,128)S(1)}, u32[]{:S(2)}) copy-start(f32[48,64,128]{2,1,0:T(8,128)S(1)} %get-tuple-element.26.acc) | copy-start | bytes 4718596
  14.7 5.4 %copy-start.16 = (bf16[17,64,128]{2,1,0:T(8,128)(2,1)}, bf16[17,64,128]{2,1,0:T(8,128)(2,1)S(1)}, u32[]{:S(2)}) copy-start(bf16[17,64,128]{2,1,0:T(8,128)(2,1)S(1)} %get-tuple-element.28.hi) | copy-start | bytes 835588
  14.7 5.4 %copy-start.38 = (bf16[64,128]{1,0:T(8,128)(2,1)}, bf16[64,128]{1,0:T(8,128)(2,1)S(1)}, u32[]{:S(2)}) copy-start(bf16[64,128]{1,0:T(8,128)(2,1)S(1)} %get-tuple-element.43.head0) | copy-start | bytes 49156
  17.8 19.9 %copy-start.22 = (s32[896]{0:T(1024)}, s32[896]{0:T(1024)S(1)}, u32[]{:S(2)}) copy-start(s32[896]{0:T(1024)S(1)} %get-tuple-element.24.lists) | copy-start | bytes 10756
  17.8 19.9 %copy-start.35 = (s32[8]{0:T(128)}, s32[8]{0:T(128)S(1)}, u32[]{:S(2)}) copy-start(s32[8]{0:T(128)S(1)} %get-tuple-element.25.counts) | copy-start | bytes 100
  17.8 2.3 %copy-start.2 = (bf16[96,128,128]{2,1,0:T(8,128)(2,1)}, bf16[96,128,128]{2,1,0:T(8,128)(2,1)S(1)}, u32[]{:S(2)}) copy-start(bf16[96,128,128]{2,1,0:T(8,128)(2,1)S(1)} %collective-permute-done.1.other) | copy-start | bytes 9437188
  17.8 5.4 %copy-start.1 = (bf16[96,128,128]{2,1,0:T(8,128)(2,1)S(1)}, bf16[96,128,128]{2,1,0:T(8,128)(2,1)}, u32[]{:S(2)}) copy-start(bf16[96,128,128]{2,1,0:T(8,128)(2,1)} %own.9) | copy-start | bytes 9437188
  17.8 5.4 %copy-start.26 = (f32[32,128]{1,0:T(8,128)S(1)}, f32[32,128]{1,0:T(8,128)}, u32[]{:S(2)}) copy-start(f32[32,128]{1,0:T(8,128)} %outflow.5) | copy-start | bytes 49156
  20.1 13.5 %collective-permute-start.2 = (bf16[16,64,128]{2,1,0:T(8,128)(2,1)}, bf16[16,64,128]{2,1,0:T(8,128)(2,1)}, u32[]{:S(2)}, u32[]{:S(2)}) collective-permute-start(bf16[16,64,128]{2,1,0:T(8,128)(2,1)} %rim_first.1), channel_id=1, source_target_pairs={{0,2},{2,4},{4,6},{6,0},{1,3},{3,5},{5,7},{7,1},{8,10},{10,12},{12... | collective-permute-start | bytes 786440 | tf_op jit(solution)/shard_map/ppermute | solution.py:307
  23.2 1.9 %copy-start.3 = (bf16[96,128,128]{2,1,0:T(8,128)(2,1)S(1)}, bf16[96,128,128]{2,1,0:T(8,128)(2,1)}, u32[]{:S(2)}) copy-start(bf16[96,128,128]{2,1,0:T(8,128)(2,1)} %copy-done.2) | copy-start | bytes 9437188
  25.1 1.4 %copy-start.9 = (f32[48,64,128]{2,1,0:T(8,128)S(1)}, f32[48,64,128]{2,1,0:T(8,128)}, u32[]{:S(2)}) copy-start(f32[48,64,128]{2,1,0:T(8,128)} %copy-done.8) | copy-start | bytes 4718596
  26.5 1.2 %copy-start.11 = (f32[32,64,128]{2,1,0:T(8,128)S(1)}, f32[32,64,128]{2,1,0:T(8,128)}, u32[]{:S(2)}) copy-start(f32[32,64,128]{2,1,0:T(8,128)} %copy-done.10) | copy-start | bytes 3145732
  27.7 1.0 %copy-start.17 = (bf16[17,64,128]{2,1,0:T(8,128)(2,1)S(1)}, bf16[17,64,128]{2,1,0:T(8,128)(2,1)}, u32[]{:S(2)}) copy-start(bf16[17,64,128]{2,1,0:T(8,128)(2,1)} %copy-done.16) | copy-start | bytes 835588
  33.6 4.1 %copy-start.4 = (bf16[96,128,128]{2,1,0:T(8,128)(2,1)S(1)}, bf16[96,128,128]{2,1,0:T(8,128)(2,1)}, u32[]{:S(2)}) copy-start(bf16[96,128,128]{2,1,0:T(8,128)(2,1)} %copy-done.2) | copy-start | bytes 9437188
  33.6 4.1 %copy-start.12 = (f32[32,64,128]{2,1,0:T(8,128)S(1)}, f32[32,64,128]{2,1,0:T(8,128)}, u32[]{:S(2)}) copy-start(f32[32,64,128]{2,1,0:T(8,128)} %copy-done.10) | copy-start | bytes 3145732
  33.6 4.1 %copy-start.28 = (f32[32,128]{1,0:T(8,128)S(1)}, f32[32,128]{1,0:T(8,128)}, u32[]{:S(2)}) copy-start(f32[32,128]{1,0:T(8,128)} %decay.5) | copy-start | bytes 49156
  33.6 4.1 %copy-start.31 = (f32[32,128]{1,0:T(8,128)S(1)}, f32[32,128]{1,0:T(8,128)}, u32[]{:S(2)}) copy-start(f32[32,128]{1,0:T(8,128)} %inflow.5) | copy-start | bytes 49156
  33.6 4.1 %copy-start.41 = (s32[128]{0:T(128)S(1)}, s32[128]{0:T(128)}, u32[]{:S(2)}) copy-start(s32[128]{0:T(128)} %vertex.5) | copy-start | bytes 1540
  36.1 9.5 %collective-permute-start.3 = (bf16[16,64,128]{2,1,0:T(8,128)(2,1)S(1)}, bf16[16,64,128]{2,1,0:T(8,128)(2,1)S(1)}, u32[]{:S(2)}, u32[]{:S(2)}) collective-permute-start(bf16[16,64,128]{2,1,0:T(8,128)(2,1)S(1)} %get-tuple-element.32), channel_id=1, source_target_pairs={{0,2},{2,4},{4,6},{6,0},{1,3},{3,5},{5,7},{7,1},{8,10},{10,12},{12... | collective-permute-start | bytes 786440 | tf_op jit(solution)/shard_map/ppermute | solution.py:322
  44.7 4.8 %copy-start.6 = (f32[48,64,128]{2,1,0:T(8,128)}, f32[48,64,128]{2,1,0:T(8,128)S(1)}, u32[]{:S(2)}) copy-start(f32[48,64,128]{2,1,0:T(8,128)S(1)} %get-tuple-element.36.acc) | copy-start | bytes 4718596
  44.7 4.8 %copy-start.18 = (f32[32,64,128]{2,1,0:T(8,128)}, f32[32,64,128]{2,1,0:T(8,128)S(1)}, u32[]{:S(2)}) copy-start(f32[32,64,128]{2,1,0:T(8,128)S(1)} %get-tuple-element.40.icar) | copy-start | bytes 3145732
  45.6 0.7 copy-start.23
  46.2 0.6 copy-start.36
  46.9 3.7 %copy-start.42 = (s32[128,1]{0,1:T(1,128)S(1)}, s32[128,1]{0,1:T(1,128)}, u32[]{:S(2)}) copy-start(s32[128,1]{0,1:T(1,128)} %param.23) | copy-start | bytes 1540
  46.9 3.8 %copy-start.39 = (bf16[64,128]{1,0:T(8,128)(2,1)S(1)}, bf16[64,128]{1,0:T(8,128)(2,1)}, u32[]{:S(2)}) copy-start(bf16[64,128]{1,0:T(8,128)(2,1)} %copy-done.38) | copy-start | bytes 49156
  46.9 3.8 %copy-start.43 = (s32[128]{0:T(128)S(1)}, s32[128]{0:T(128)}, u32[]{:S(2)}) copy-start(s32[128]{0:T(128)} %param.24) | copy-start | bytes 1540
  49.5 1.0 %copy-start.13 = (f32[32,64,128]{2,1,0:T(8,128)}, f32[32,64,128]{2,1,0:T(8,128)S(1)}, u32[]{:S(2)}) copy-start(f32[32,64,128]{2,1,0:T(8,128)S(1)} %get-tuple-element.38.lam) | copy-start | bytes 3145732
  50.4 26.9 %collective-permute-start.4 = (bf16[16,64,128]{2,1,0:T(8,128)(2,1)}, bf16[16,64,128]{2,1,0:T(8,128)(2,1)}, u32[]{:S(2)}, u32[]{:S(2)}) collective-permute-start(bf16[16,64,128]{2,1,0:T(8,128)(2,1)} %get-tuple-element.37), channel_id=1, source_target_pairs={{0,2},{2,4},{4,6},{6,0},{1,3},{3,5},{5,7},{7,1},{8,10},{10,12},{12... | collective-permute-start | bytes 786440 | tf_op jit(solution)/shard_map/ppermute | solution.py:322
  50.7 1.2 %copy-start.14 = (f32[32,64,128]{2,1,0:T(8,128)S(1)}, f32[32,64,128]{2,1,0:T(8,128)}, u32[]{:S(2)}) copy-start(f32[32,64,128]{2,1,0:T(8,128)} %copy-done.13) | copy-start | bytes 3145732
  55.6 18.7 %all-to-all-start = ((bf16[16,32,128]{2,1,0:T(8,128)(2,1)}), bf16[16,32,128]{2,1,0:T(8,128)(2,1)S(1)}, u32[]{:S(2)}, u32[]{:S(2)}) async-start(bf16[16,32,128]{2,1,0:T(8,128)(2,1)} %bitcast.3), calls=%async_computation | async-start | bytes 262144 | tf_op jit(solution)/shard_map/all_to_all | solution.py:355
  62.6 1.9 %copy-start.5 = (bf16[96,128,128]{2,1,0:T(8,128)(2,1)S(1)}, bf16[96,128,128]{2,1,0:T(8,128)(2,1)}, u32[]{:S(2)}) copy-start(bf16[96,128,128]{2,1,0:T(8,128)(2,1)} %copy-done.2) | copy-start | bytes 9437188
  64.5 1.4 %copy-start.7 = (f32[48,64,128]{2,1,0:T(8,128)S(1)}, f32[48,64,128]{2,1,0:T(8,128)}, u32[]{:S(2)}) copy-start(f32[48,64,128]{2,1,0:T(8,128)} %copy-done.6) | copy-start | bytes 4718596
  65.9 1.2 %copy-start.15 = (f32[32,64,128]{2,1,0:T(8,128)S(1)}, f32[32,64,128]{2,1,0:T(8,128)}, u32[]{:S(2)}) copy-start(f32[32,64,128]{2,1,0:T(8,128)} %copy-done.13) | copy-start | bytes 3145732
  67.1 1.2 %copy-start.19 = (f32[32,64,128]{2,1,0:T(8,128)S(1)}, f32[32,64,128]{2,1,0:T(8,128)}, u32[]{:S(2)}) copy-start(f32[32,64,128]{2,1,0:T(8,128)} %copy-done.18) | copy-start | bytes 3145732
  68.4 0.7 copy-start.24
  69.0 0.7 copy-start.29
  69.8 0.7 copy-start.32
  70.5 0.6 copy-start.37
  74.3 0.9 %copy-start.33 = (bf16[256,256]{1,0:T(8,128)(2,1)S(1)}, bf16[256,256]{1,0:T(8,128)(2,1)}, u32[]{:S(2)}) copy-start(bf16[256,256]{1,0:T(8,128)(2,1)} %matrix.1) | copy-start | bytes 393220
  75.3 0.8 %copy-start.34 = (f32[64,256]{1,0:T(8,128)S(1)}, f32[64,256]{1,0:T(8,128)}, u32[]{:S(2)}) copy-start(f32[64,256]{1,0:T(8,128)} %trans.3) | copy-start | bytes 196612

commit v2 on v0

v2 whole, which is shorter than its diff:
```python
import jax
import jax.numpy as jnp
from jax import lax
from jax.experimental import pallas as pl
from jax.experimental.pallas import tpu as pltpu
from jax.sharding import PartitionSpec as P

STEPS = 3
UNROLL = 16
CLASSES = 4
VMEM_LIMIT = 24 << 20

F32 = jnp.float32
BF16 = jnp.bfloat16
VM = pl.BlockSpec(memory_space=pltpu.VMEM)
SM = pl.BlockSpec(memory_space=pltpu.SMEM)
HB = pl.BlockSpec(memory_space=pltpu.HBM)
STRIDE = 128


def kernel(body, outs, ins, name, scratch=(), out_specs=None, aliases=None):
    return pl.pallas_call(
        body,
        out_shape=outs,
        in_specs=[spec for _, spec in ins],
        out_specs=out_specs or tuple(VM for _ in outs),
        scratch_shapes=list(scratch),
        input_output_aliases=aliases or {},
        compiler_params=pltpu.CompilerParams(vmem_limit_bytes=VMEM_LIMIT),
        name=name,
    )(*[in_hbm(array) if spec is HB else array for array, spec in ins])


def in_hbm(array):
    return pltpu.with_memory_space_constraint(array, pltpu.HBM)


def array(shape, dtype):
    return jax.ShapeDtypeStruct(shape, dtype)


def local(
    vertex_costate,
    inverter_costate,
    highvoltage_costate,
    derivative_tiles,
    tile_source_index,
    tile_target_index,
    inverter_decay_factor,
    costate_to_inverter_factor,
    inverter_to_costate_factor,
    distribution_entry_vertex,
    distribution_entry_holder,
    distribution_entry_substation,
    highvoltage_derivative_matrix,
):
    blocks, cases, nodes = vertex_costate.shape
    rim = blocks // 2
    low = blocks // 2
    targets = blocks + rim
    stored = derivative_tiles.shape[0]
    sections = lax.axis_size("sec")
    owners = lax.axis_size("blk")
    network = sections * owners
    heads = distribution_entry_vertex.shape[0]
    slots = max(2, 2 * heads // network)
    buses = highvoltage_derivative_matrix.shape[1]
    rows_sent = network * 2 * slots
    assert stored + UNROLL <= STRIDE and blocks <= 64

    state = (blocks, cases, nodes)
    half = (low, cases, nodes)
    padded = (low + 1, cases, nodes)
    acc_shape = (targets, cases, nodes)
    hot_shape = (blocks, nodes, heads)
    factor_shape = inverter_decay_factor.shape
    swap = [(0, 1), (1, 0)]
    onward = [(i, (i + 1) % owners) for i in range(owners)]

    own = derivative_tiles
    other = lax.ppermute(own, "case", swap)
    is_low = (tile_source_index < low).astype(jnp.int32)
    is_own = (tile_target_index < blocks).astype(jnp.int32)
    own_codes = (
        lax.iota(jnp.int32, stored)
        | ((tile_source_index - low * (1 - is_low)) << 8)
        | ((tile_target_index - blocks * (1 - is_own)) << 16)
        | ((16 * is_own + 8 * is_low) << 24)
    )
    other_codes = lax.ppermute(own_codes, "case", swap)

    def group(codes, lam, tiles, acc):
        prods = [
            jnp.dot(lam[(c >> 8) & 255], tiles[c & 255], preferred_element_type=F32) for c in codes
        ]
        for c, prod in zip(codes, prods):
            acc[(c >> 16) & 255] += prod

    def run(lists, counts, segment, lam, tiles, acc):
        def some(i, carry):
            start = segment * STRIDE + i * UNROLL
            group([lists[start + u] for u in range(UNROLL)], lam, tiles, acc)
            return carry

        lax.fori_loop(0, (counts[segment] + UNROLL - 1) // UNROLL, some, 0)

    def first_body(codes, lam_in, own_in, acc, lo, hi, own_kept, lam, lam_bf, sems):
        lam_copy = pltpu.make_async_copy(lam_in, lam, sems.at[0])
        lam_copy.start()
        copies = [
            pltpu.make_async_copy(
                own_in.at[pl.ds(i, UNROLL)], own_kept.at[pl.ds(i, UNROLL)], sems.at[1 + i // UNROLL]
            )
            for i in range(0, stored, UNROLL)
        ]
        for copy in copies:
            copy.start()
        for b in range(targets):
            acc[b] = jnp.zeros((cases, nodes), F32)
        zero = jnp.zeros((cases, nodes), BF16)
        lo[low] = zero
        hi[blocks - low] = zero
        lam_copy.wait()
        for b in range(blocks):
            rounded = lam[b].astype(BF16)
            lam_bf[b] = rounded
            if b < low:
                lo[b] = rounded
            else:
                hi[b - low] = rounded
        for i, copy in enumerate(copies):
            copy.wait()
            prods = []
            for u in range(UNROLL):
                c = codes[i * UNROLL + u]
                k = c >> 24
                row = ((c >> 8) & 255) + jnp.where((k & 8) > 0, 0, low)
                target = ((c >> 16) & 255) + jnp.where((k & 16) > 0, 0, blocks)
                prod = jnp.dot(
                    lam_bf[row], own_kept[i * UNROLL + u], preferred_element_type=F32
                )
                prods.append((target, prod))
            for target, prod in prods:
                acc[target] += prod

    acc, lo, hi, own = kernel(
        first_body,
        (
            array(acc_shape, F32),
            array(padded, BF16),
            array(padded, BF16),
            array(own.shape, BF16),
        ),
        [(own_codes, SM), (vertex_costate, HB), (own, HB)],
        "first",
        scratch=[
            pltpu.VMEM(state, F32),
            pltpu.VMEM(state, BF16),
            pltpu.SemaphoreType.DMA((1 + stored // UNROLL,)),
        ],
    )

    def sort_body(own_code, other_code, lists, counts):
        for side, code in enumerate((own_code, other_code)):
            base = side * CLASSES * STRIDE

            def place(e, used, code=code, base=base):
                c = code[e]
                shift = c >> 24
                lists[base + shift * (STRIDE // 8) + ((used >> shift) & 255)] = c
                return used + (1 << shift)

            used = lax.fori_loop(0, stored, place, jnp.int32(0), unroll=8)
            for kind in range(CLASSES):
                at = (used >> (8 * kind)) & 255
                counts[side * CLASSES + kind] = at
                for u in range(UNROLL):
                    lists[base + kind * STRIDE + at + u] = low << 8

    lists, counts = kernel(
        sort_body,
        (array((2 * CLASSES * STRIDE,), jnp.int32), array((2 * CLASSES,), jnp.int32)),
        [(own_codes, SM), (other_codes, SM)],
        "sort",
        out_specs=(SM, SM),
    )
    listed = [(lists, SM), (counts, SM)]

    def rim_first_body(lists, counts, acc, lo, hi, other, out, sums):
        sums[...] = acc[blocks:]
        run(lists, counts, CLASSES + 0, hi, other, sums)
        run(lists, counts, CLASSES + 1, lo, other, sums)
        out[...] = sums[...].astype(BF16)

    (leaving,) = kernel(
        rim_first_body,
        (array((rim, cases, nodes), BF16),),
        listed + [(acc, VM), (lo, VM), (hi, VM), (other, VM)],
        "rim_first",
        scratch=[pltpu.VMEM((rim, cases, nodes), F32)],
    )
    arriving = lax.ppermute(leaving, "blk", onward)

    def begin_next(lists, counts, lam, icar, outflow, own, other, acc, acc_rim, hi):
        for b in range(blocks):
            acc[b] = outflow[b : b + 1, :] * icar[b]
        for b in range(rim):
            acc_rim[b] = jnp.zeros((cases, nodes), F32)
        for b in range(low, blocks):
            hi[b - low] = lam[b].astype(BF16)
        hi[blocks - low] = jnp.zeros((cases, nodes), BF16)
        for side, tiles in enumerate((own, other)):
            run(lists, counts, side * CLASSES + 0, hi, tiles, acc_rim)
            run(lists, counts, side * CLASSES + 2, hi, tiles, acc)

    def head_values(lo, hi, hot):
        total = jnp.dot(lo[0], hot[0], preferred_element_type=F32)
        for b in range(1, blocks):
            row = lo[b] if b < low else hi[b - low]
            total += jnp.dot(row, hot[b], preferred_element_type=F32)
        return total.astype(BF16)

    def main_first_body(
        lists, counts, acc, lo, hi, own, other, vertex, lam_in, icar_in, decay_in, inflow_in, outflow_in,
        lam_next, acc_next, acc_rim, hi_next, icar_next, head, hot, decay, inflow, outflow, other_kept,
        lam, icar, sems,
    ):
        kept = pltpu.make_async_copy(other, other_kept, sems.at[5])
        kept.start()
        pairs = [
            (icar_in, icar), (outflow_in, outflow), (lam_in, lam), (decay_in, decay), (inflow_in, inflow)
        ]
        copies = [pltpu.make_async_copy(a, b, sems.at[i]) for i, (a, b) in enumerate(pairs)]
        for copy in copies:
            copy.start()
        for copy in copies:
            copy.wait()
        for b in range(blocks):
            lam_next[b] = acc[b] + outflow[b : b + 1, :] * icar[b]
            icar_next[b] = decay[b : b + 1, :] * icar[b] + inflow[b : b + 1, :] * lam[b]
        run(lists, counts, CLASSES + 2, hi, other, lam_next)
        run(lists, counts, CLASSES + 3, lo, other, lam_next)
        begin_next(
            lists, counts, lam_next, icar_next, outflow, own, other, acc_next, acc_rim, hi_next
        )
        node = lax.broadcasted_iota(jnp.int32, (nodes, heads), 0)
        for b in range(blocks):
            hot[b] = jnp.where(node + b * nodes == vertex[...], 1.0, 0.0).astype(BF16)
        head[...] = head_values(lo, hi, hot)
        kept.wait()

    factor = array(factor_shape, F32)
    lam, acc, acc_rim, hi_next, icar, head0, hot, decay, inflow, outflow, other_kept = kernel(
        main_first_body,
        (
            array(state, F32),
            array(state, F32),
            array((rim, cases, nodes), F32),
            array(padded, BF16),
            array(state, F32),
            array((cases, heads), BF16),
            array(hot_shape, BF16),
            factor,
            factor,
            factor,
            array(other.shape, BF16),
        ),
        listed
        + [(acc, VM), (lo, VM), (hi, VM), (own, VM), (other, VM)]
        + [(distribution_entry_vertex.reshape(1, heads), VM)]
        + [(vertex_costate, HB), (inverter_costate, HB), (inverter_decay_factor, HB)]
        + [(costate_to_inverter_factor, HB), (inverter_to_costate_factor, HB)],
        "main_first",
        scratch=[pltpu.VMEM(state, F32), pltpu.VMEM(state, F32), pltpu.SemaphoreType.DMA((6,))],
        out_specs=(VM,) * 10 + (HB,),
    )

    def take_arrived(arrived, lam, low_rows, lo):
        keep = lax.axis_index("blk") > 0
        for b in range(low):
            row = lam[b] + jnp.where(keep, arrived[b].astype(F32), 0.0)
            low_rows[b] = row
            lo[b] = row.astype(BF16)
        lo[low] = jnp.zeros((cases, nodes), BF16)

    def rim_sums(lists, counts, acc_rim, lo, own, other, out, sums):
        sums[...] = acc_rim[...]
        run(lists, counts, 1, lo, own, sums)
        run(lists, counts, CLASSES + 1, lo, other, sums)
        out[...] = sums[...].astype(BF16)

    def rim_body(lists, counts, arrived, lam, acc_rim, own, other, out, low_rows, lo, sums):
        take_arrived(arrived, lam, low_rows, lo)
        rim_sums(lists, counts, acc_rim, lo, own, other, out, sums)

    def rim_last_body(
        lists, counts, arrived, lam, acc_rim, hi, own, other, hot, begun, place,
        out, low_rows, lo, sent, sums,
    ):
        take_arrived(arrived, lam, low_rows, lo)
        rim_sums(lists, counts, acc_rim, lo, own, other, out, sums)
        head = jnp.concatenate(
            [head_values(lo, hi, hot), jnp.zeros((nodes - cases, heads), BF16)], axis=0
        )
        dims = (((1,), (1,)), ((), ()))
        sent[...] = (
            begun[...] + lax.dot_general(place[...], head, dims, preferred_element_type=F32)
        ).astype(BF16)

    def main_body(
        lists, counts, owner, bus, low_rows, lam, lo, hi, acc, icar, own, other, hot, head0,
        decay, inflow, outflow,
        lam_low, acc_next, acc_rim, hi_next, icar_low, begun, place, icar_out,
        lam_next, icar_next, sem,
    ):
        for b in range(blocks):
            row = low_rows[b] if b < low else lam[b]
            icar_next[b] = decay[b : b + 1, :] * icar[b] + inflow[b : b + 1, :] * row
        lam_next[...] = acc[...]
        run(lists, counts, 3, lo, own, lam_next)
        run(lists, counts, CLASSES + 3, lo, other, lam_next)
        begin_next(
            lists, counts, lam_next, icar_next, outflow, own, other, acc_next, acc_rim, hi_next
        )
        for b in range(low):
            lam_low[b] = lam_next[b]
            icar_low[b] = icar_next[b]
        for b in range(low, blocks):
            icar_next[b] = decay[b : b + 1, :] * icar_next[b] + inflow[b : b + 1, :] * lam_next[b]
        upper = pl.ds(low, blocks - low)
        copy = pltpu.make_async_copy(icar_next.at[upper], icar_out.at[upper], sem)
        copy.start()
        mine = jnp.broadcast_to(owner[...].astype(F32), (heads, heads))
        before = lax.broadcasted_iota(jnp.int32, (heads, heads), 0)
        after = lax.broadcasted_iota(jnp.int32, (heads, heads), 1)
        same = jnp.logical_and(mine.T == mine, before < after)
        slot = jnp.sum(jnp.where(same, 1.0, 0.0), axis=0, keepdims=True).astype(jnp.int32)
        dest = owner[...] * (2 * slots) + slot
        row = lax.broadcasted_iota(jnp.int32, (rows_sent, heads), 0)
        place_a = jnp.where(row == dest, 1.0, 0.0).astype(BF16)
        place_b = jnp.where(row == dest + slots, 1.0, 0.0).astype(BF16)
        place[...] = place_b
        label = jnp.broadcast_to((bus[...] + 1).astype(F32), (nodes - cases, heads)).astype(BF16)
        pair_a = jnp.concatenate([head0[...], head_values(lo, hi, hot)], axis=0)
        pair_b = jnp.concatenate([jnp.zeros((cases, heads), BF16), label], axis=0)
        dims = (((1,), (1,)), ((), ()))
        begun[...] = lax.dot_general(
            place_a, pair_a, dims, preferred_element_type=F32
        ) + lax.dot_general(place_b, pair_b, dims, preferred_element_type=F32)
        copy.wait()

    tiles = [(own, VM), (other, VM)]
    rim_type = array((rim, cases, nodes), BF16)
    low_type = array(half, F32)
    sums = pltpu.VMEM((rim, cases, nodes), F32)
    assert STEPS == 3
    hi = hi_next
    leaving, low_rows, lo = kernel(
        rim_body,
        (rim_type, low_type, array(padded, BF16)),
        listed + [(arriving, VM), (lam, VM), (acc_rim, VM)] + tiles,
        "rim",
        scratch=[sums],
    )
    arriving = lax.ppermute(leaving, "blk", onward)
    lam, acc, acc_rim, hi_next, icar_low, begun, place, icar = kernel(
        main_body,
        (
            low_type,
            array(state, F32),
            array((rim, cases, nodes), F32),
            array(padded, BF16),
            low_type,
            array((rows_sent, nodes), F32),
            array((rows_sent, heads), BF16),
            array(state, F32),
        ),
        listed
        + [(distribution_entry_holder.reshape(1, heads), VM)]
        + [(distribution_entry_substation.reshape(1, heads), VM)]
        + [(low_rows, VM), (lam, VM), (lo, VM), (hi, VM), (acc, VM), (icar, VM)]
        + tiles
        + [(hot, VM), (head0, VM), (decay, VM), (inflow, VM), (outflow, VM)],
        "main",
        scratch=[pltpu.VMEM(state, F32), pltpu.VMEM(state, F32), pltpu.SemaphoreType.DMA],
        out_specs=(VM,) * 7 + (HB,),
    )

    leaving, low_rows, lo, sent = kernel(
        rim_last_body,
        (rim_type, low_type, array(padded, BF16), array((rows_sent, nodes), BF16)),
        listed
        + [(arriving, VM), (lam, VM), (acc_rim, VM), (hi_next, VM)]
        + tiles
        + [(hot, VM), (begun, VM), (place, VM)],
        "rim_last",
        scratch=[sums],
    )
    arriving = lax.ppermute(leaving, "blk", onward)
    received = lax.all_to_all(
        sent.reshape(network, 2 * slots, nodes),
        ("sec", "blk"),
        split_axis=0,
        concat_axis=0,
        tiled=True,
    ).reshape(rows_sent, nodes)

    def main_last_body(
        lists, counts, low_rows, lo, acc, icar_low, decay, inflow, own_in, other_in, icar_in,
        lam_out, low_next, icar_out, lam_next, icar_next, fetched, sems,
    ):
        del icar_in

        def fetch(side, source):
            segment = side * CLASSES + 3

            def one(i, carry):
                c = lists[segment * STRIDE + i]
                pltpu.make_async_copy(
                    source.at[c & 255], fetched.at[side * stored + i], sems.at[side]
                ).start()
                return carry

            lax.fori_loop(0, counts[segment], one, 0)

        def fetched_all(side, source):
            def one(i, carry):
                pltpu.make_async_copy(source.at[0], fetched.at[side * stored], sems.at[side]).wait()
                return carry

            lax.fori_loop(0, counts[side * CLASSES + 3], one, 0)

        fetch(0, own_in)
        fetch(1, other_in)
        for b in range(low):
            icar_next[b] = decay[b : b + 1, :] * icar_low[b] + inflow[b : b + 1, :] * low_rows[b]
        lower = pl.ds(0, low)
        icar_copy = pltpu.make_async_copy(icar_next, icar_out.at[lower], sems.at[2])
        icar_copy.start()
        lam_next[...] = acc[...]
        for side, source in enumerate((own_in, other_in)):
            fetched_all(side, source)
            segment = side * CLASSES + 3

            def some(i, carry, side=side, segment=segment):
                start = i * UNROLL
                words = []
                for u in range(UNROLL):
                    at = jnp.minimum(start + u, counts[segment] - 1)
                    words.append((lists[segment * STRIDE + start + u], side * stored + at))
                prods = [
                    jnp.dot(lo[(c >> 8) & 255], fetched[at], preferred_element_type=F32)
                    for c, at in words
                ]
                for (c, _), prod in zip(words, prods):
                    lam_next[(c >> 16) & 255] += prod
                return carry

            lax.fori_loop(0, (counts[segment] + UNROLL - 1) // UNROLL, some, 0)
        upper = pl.ds(low, blocks - low)
        lam_copy = pltpu.make_async_copy(lam_next.at[upper], lam_out.at[upper], sems.at[3])
        lam_copy.start()
        low_next[...] = lam_next[:low]
        icar_copy.wait()
        lam_copy.wait()

    lam, low_next, icar = kernel(
        main_last_body,
        (array(state, F32), low_type, array(state, F32)),
        listed
        + [(low_rows, VM), (lo, VM), (acc, VM), (icar_low, VM), (decay, VM), (inflow, VM)]
        + [(derivative_tiles, HB), (other_kept, HB), (icar, HB)],
        "main_last",
        scratch=[
            pltpu.VMEM(state, F32),
            pltpu.VMEM(half, F32),
            pltpu.VMEM((2 * stored, nodes, nodes), BF16),
            pltpu.SemaphoreType.DMA((4,)),
        ],
        out_specs=(HB, VM, HB),
        aliases={10: 2},
    )

    def trans_body(received, trans_in, matrix_in, out, trans, matrix, sems):
        copies = [
            pltpu.make_async_copy(trans_in, trans, sems.at[0]),
            pltpu.make_async_copy(matrix_in, matrix, sems.at[1]),
        ]
        for copy in copies:
            copy.start()
        got = received[...].astype(F32)
        row = lax.broadcasted_iota(jnp.int32, (rows_sent, buses), 0)
        second = lax.rem(row, 2 * slots) >= slots
        column = lax.broadcasted_iota(jnp.int32, (rows_sent, buses), 1)
        label = got[:, cases : cases + 1].astype(jnp.int32) - 1
        hot_b = jnp.where(jnp.logical_and(label == column, second), 1.0, 0.0)
        hot_a = pltpu.roll(hot_b, rows_sent - slots, 0)
        dims = (((0,), (0,)), ((), ()))
        first = lax.dot_general(received[...], hot_a.astype(BF16), dims, preferred_element_type=F32)
        last = lax.dot_general(received[...], hot_b.astype(BF16), dims, preferred_element_type=F32)
        for copy in copies:
            copy.wait()
        value = trans[...]
        for inj in (first[:cases], first[cases:], last[:cases]):
            value = jnp.dot(value.astype(BF16), matrix[...], preferred_element_type=F32) + inj
        out[...] = value

    (trans,) = kernel(
        trans_body,
        (array(highvoltage_costate.shape, F32),),
        [(received, VM), (highvoltage_costate, HB), (highvoltage_derivative_matrix, HB)],
        "trans",
        scratch=[
            pltpu.VMEM(highvoltage_costate.shape, F32),
            pltpu.VMEM(highvoltage_derivative_matrix.shape, BF16),
            pltpu.SemaphoreType.DMA((2,)),
        ],
    )

    def last_body(arrived, low_next, lam_in, lam_out, rows, sems):
        del lam_in
        keep = lax.axis_index("blk") > 0
        copies = []
        part = low // 4
        for i in range(4):
            for b in range(i * part, (i + 1) * part):
                rows[b] = low_next[b] + jnp.where(keep, arrived[b].astype(F32), 0.0)
            here = pl.ds(i * part, part)
            copies.append(pltpu.make_async_copy(rows.at[here], lam_out.at[here], sems.at[i]))
            copies[-1].start()
        for copy in copies:
            copy.wait()

    (lam,) = kernel(
        last_body,
        (array(state, F32),),
        [(arriving, VM), (low_next, VM), (lam, HB)],
        "last",
        scratch=[pltpu.VMEM(half, F32), pltpu.SemaphoreType.DMA((4,))],
        out_specs=(HB,),
        aliases={2: 0},
    )
    return (lam, icar, trans)


def solution(mesh):
    placed = (
        P(("sec", "blk"), "case", None),
        P(("sec", "blk"), "case", None),
        P("case", ("sec", "blk")),
        P(("sec", "blk", "case"), None, None),
        P(("sec", "blk", "case")),
        P(("sec", "blk", "case")),
        P(("sec", "blk"), None),
        P(("sec", "blk"), None),
        P(("sec", "blk"), None),
        P(("sec", "blk")),
        P(("sec", "blk"), None),
        P(("sec", "blk")),
        P(("sec", "blk"), None),
    )
    return jax.shard_map(
        local,
        mesh=mesh,
        in_specs=placed,
        out_specs=(
            P(("sec", "blk"), "case", None),
            P(("sec", "blk"), "case", None),
            P("case", ("sec", "blk")),
        ),
        check_vma=False,
    )
```

time: 201 us -> 53.4 us (0.27)
  other arithmetic: 69.3 us -> 0.68 us
  Pallas kernels: 0 us -> 31.9 us
  matrix products: 29.3 us -> 0 us
  local copies, waits for them, and re-layouts: 27.8 us -> 0.02 us
  starting transfers between devices: 33.9 us -> 9.89 us
  between operations: 15.2 us -> 0.75 us
  waiting for transfers between devices: 21.7 us -> 9.68 us
    scatter-add x3 -> x0, other arithmetic: 59.9 us -> none  [block_terms(): return jax.ops.segment_sum(prods, col_ids, num_segments=targets)]
    pallas_call x0 -> x10, Pallas kernels: none -> 31.9 us  [kernel(): pl.pallas_call(body, out_shape=outs, in_specs=[spec for _, spec in ins],...]
    dot_general x13 -> x0, matrix products: 29.3 us -> none  [the longest x3 24.6 us: block_terms(): jnp.einsum('ecn,enm->ecm', picked, mats, preferred_element_type=jnp.float32)]
    all_to_all x4 -> x1, waiting for transfers between devices: 21 us -> 3.78 us  [local(): lax.all_to_all(sent.reshape(network, 2 * slots, nodes), ('sec', 'blk'), s...]
    all_to_all x4 -> x1, starting transfers between devices: 21.7 us -> 6.31 us  [local(): lax.all_to_all(sent.reshape(network, 2 * slots, nodes), ('sec', 'blk'), s...]
    gather x6 -> x0, local copies, waits for them, and re-layouts: 13.7 us -> none  [the longest x3 8.1 us: block_terms(): picked = jnp.take(lam_rows, row_ids, axis=0)]
    ppermute x3 -> x5, starting transfers between devices: 12.2 us -> 3.58 us  [the longest x3 3 us: local(): arriving = lax.ppermute(leaving, 'blk', onward)]
    unnamed x48 -> x8, local copies, waits for them, and re-layouts: 6.59 us -> 0.02 us
  transfers between devices with their start and end apart: 8 -> 6, of which waited for: 3 -> 4; matrix products, arithmetic and copies ran while one was open for 25% -> 1% of each run, Pallas kernels for 0% -> 46%
where the time goes in v2:
time: 53.4 us; the launch traced here: 52.9 us
  Pallas kernels  31.9 us (60%)
  starting transfers between devices  9.89 us (19%)
  waiting for transfers between devices  9.68 us (18%)
  between operations  0.75 us (1%)
  other arithmetic  0.68 us (1%)
    pallas_call x10, Pallas kernels, kernel(): pl.pallas_call(body, out_shape=outs, in_specs=[spec for _, spec in ins],...  31.9 us
    all_to_all x1, starting transfers between devices, local(): lax.all_to_all(sent.reshape(network, 2 * slots, nodes), ('sec', 'blk'), s...  6.31 us
    ppermute x3, waiting for transfers between devices, local(): arriving = lax.ppermute(leaving, 'blk', onward)  4.75 us
    all_to_all x1, waiting for transfers between devices, local(): lax.all_to_all(sent.reshape(network, 2 * slots, nodes), ('sec', 'blk'), s...  3.78 us
    ppermute x3, starting transfers between devices, local(): arriving = lax.ppermute(leaving, 'blk', onward)  3 us
    ppermute x1, waiting for transfers between devices, local(): other_codes = lax.ppermute(own_codes, 'case', swap)  1.15 us
  transfers between devices with their start and end apart: 6, of which 4 were waited for; matrix products, arithmetic and copies ran while one was open for 1% of the time, Pallas kernels for 46%

profile of v2, /device:TPU:0, one launch (start us, length us, event | category | flops | bytes accessed | tf_op | source)
XLA Modules:
  0.0 52.9 jit_solution(10190640635310083679)
XLA Ops:
  0.6 0.6 %collective-permute-start.1 = (bf16[96,128,128]{2,1,0:T(8,128)(2,1)}, bf16[96,128,128]{2,1,0:T(8,128)(2,1)S(1)}, u32[]{:S(2)}, u32[]{:S(2)}) collective-permute-start(bf16[96,128,128]{2,1,0:T(8,128)(2,1)} %own_in.3), channel_id=1, source_target_pairs={{0,1},{1,0},{2,3},{3,2},{4,5},{5,4},{6,7},{7,6},{8,9},{9,8},{10,11... | collective-permute-start | bytes 9437192 | tf_op jit(solution)/shard_map/ppermute | solution.py:81
  1.2 0.7 %shift-left_or_fusion.own_code.codes = s32[96]{0:T(128)S(1)} fusion(s32[96]{0:T(128)} %param.18, s32[96]{0:T(128)} %param.17), kind=kLoop, calls=%fused_computation.15 | loop fusion | flops 1824 | bytes 1152 | tf_op jit(solution)/shard_map/or | solution.py:85
  1.9 0.0 collective-permute-start
  1.9 3.6 %first.1 = (f32[48,64,128]{2,1,0:T(8,128)S(1)}, bf16[17,64,128]{2,1,0:T(8,128)(2,1)S(1)}, bf16[17,64,128]{2,1,0:T(8,128)(2,1)S(1)}, bf16[96,128,128]{2,1,0:T(8,128)(2,1)S(1)}) custom-call(s32[96]{0:T(128)S(1)} %shift-left_or_fusion.own_code.codes, f32[32,64,128]{2,1,0:T(8,128)} %lam_in.3, bf16[96,128,128]{2,1,0:T(8,128)(2,1)} %own_in.3), custom_call_target="tpu_custom_call" | custom-call | tf_op jit(solution)/shard_map/first/pallas_call | solution.py:22
  5.5 0.0 copy-start.1
  5.5 1.1 %collective-permute-done.other_code = s32[96]{0:T(128)S(1)} collective-permute-done((s32[96]{0:T(128)S(1)}, s32[96]{0:T(128)S(1)}, u32[]{:S(2)}, u32[]{:S(2)}) %collective-permute-start) | collective-permute-done | bytes 416 | tf_op jit(solution)/shard_map/ppermute | solution.py:90
  6.7 2.0 %sort.1 = (s32[1024]{0:T(1024)S(1)}, s32[8]{0:T(128)S(1)}) custom-call(s32[96]{0:T(128)S(1)} %shift-left_or_fusion.own_code.codes, s32[96]{0:T(128)S(1)} %collective-permute-done.other_code), custom_call_target="tpu_custom_call" | custom-call | tf_op jit(solution)/shard_map/sort/pallas_call | solution.py:22
  8.7 0.0 collective-permute-done.1.other
  8.7 1.8 %rim_first.1 = bf16[16,64,128]{2,1,0:T(8,128)(2,1)S(1)} custom-call(s32[1024]{0:T(1024)S(1)} %get-tuple-element.38.lists, s32[8]{0:T(128)S(1)} %get-tuple-element.39.counts, f32[48,64,128]{2,1,0:T(8,128)S(1)} %get-tuple-element.40.acc, bf16[17,64,128]{2,1,0:T(8,128)(2,1)S(1)} %get-tuple-element.41.lo, bf16[17,64,128]{2,1,0:T(8,128)(2,1)S(1)} %get-tuple-element.42.hi, ...), custom_call_target="tpu_custom_call" | custom-call | tf_op jit(solution)/shard_map/rim_first/pallas_call | solution.py:22
  10.5 2.7 %collective-permute-start.2 = (bf16[16,64,128]{2,1,0:T(8,128)(2,1)S(1)}, bf16[16,64,128]{2,1,0:T(8,128)(2,1)S(1)}, u32[]{:S(2)}, u32[]{:S(2)}) collective-permute-start(bf16[16,64,128]{2,1,0:T(8,128)(2,1)S(1)} %rim_first.1), channel_id=1, source_target_pairs={{0,2},{2,4},{4,6},{6,0},{1,3},{3,5},{5,7},{7,1},{8,10},{10,12},{12... | collective-permute-start | bytes 786440 | tf_op jit(solution)/shard_map/ppermute | solution.py:202
  13.2 0.0 copy-done.1
  13.2 6.7 %main_first.1 = (f32[32,64,128]{2,1,0:T(8,128)S(1)}, f32[32,64,128]{2,1,0:T(8,128)S(1)}, f32[16,64,128]{2,1,0:T(8,128)S(1)}, bf16[17,64,128]{2,1,0:T(8,128)(2,1)...) custom-call(s32[1024]{0:T(1024)S(1)} %get-tuple-element.38.lists, ...), custom_call_target="tpu_custom_call" | custom-call | tf_op jit(solution)/shard_map/main_first/pallas_call | solution.py:22
  19.9 0.0 copy-start
  20.0 1.6 %collective-permute-done.2.arrived = bf16[16,64,128]{2,1,0:T(8,128)(2,1)S(1)} collective-permute-done((bf16[16,64,128]{2,1,0:T(8,128)(2,1)S(1)}, bf16[16,64,128]{2,1,0:T(8,128)(2,1)S(1)}, u32[]{:S(2)}, u32[]{:S(2)}) %collective-permute-start.2) | collective-permute-done | bytes 262176 | tf_op jit(solution)/shard_map/ppermute | solution.py:202
  21.6 0.0 copy-start.2
  21.6 0.0 copy-start.3
  21.6 1.9 %rim.1 = (bf16[16,64,128]{2,1,0:T(8,128)(2,1)S(1)}, f32[16,64,128]{2,1,0:T(8,128)S(1)}, bf16[17,64,128]{2,1,0:T(8,128)(2,1)S(1)}) custom-call(s32[1024]{0:T(1024)S(1)} %get-tuple-element.38.lists, s32[8]{0:T(128)S(1)} %get-tuple-element.39.counts, bf16[16,64,128]{2,1,0:T(8,128)(2,1)S(1)} %collective-permute-done.2.arrived, ...), custom_call_target="tpu_custom_call" | custom-call | tf_op jit(solution)/shard_map/rim/pallas_call | solution.py:22
  23.4 0.0 copy-done
  23.4 0.3 collective-permute-start.3
  23.7 0.0 copy-done.2
  23.8 0.0 copy-done.3
  23.8 5.9 %main.1 = (f32[16,64,128]{2,1,0:T(8,128)S(1)}, f32[32,64,128]{2,1,0:T(8,128)S(1)}, f32[16,64,128]{2,1,0:T(8,128)S(1)}, bf16[17,64,128]{2,1,0:T(8,128)(2,1)S(1)},...) custom-call(s32[1024]{0:T(1024)S(1)} %get-tuple-element.38.lists, ...), custom_call_target="tpu_custom_call" | custom-call | tf_op jit(solution)/shard_map/main/pallas_call | solution.py:22
  29.6 3.1 %collective-permute-done.3.arrived = bf16[16,64,128]{2,1,0:T(8,128)(2,1)S(1)} collective-permute-done((bf16[16,64,128]{2,1,0:T(8,128)(2,1)S(1)}, bf16[16,64,128]{2,1,0:T(8,128)(2,1)S(1)}, u32[]{:S(2)}, u32[]{:S(2)}) %collective-permute-start.3) | collective-permute-done | bytes 262176 | tf_op jit(solution)/shard_map/ppermute | solution.py:365
  32.8 3.2 %rim_last.1 = (bf16[16,64,128]{2,1,0:T(8,128)(2,1)}, f32[16,64,128]{2,1,0:T(8,128)S(1)}, bf16[17,64,128]{2,1,0:T(8,128)(2,1)S(1)}, bf16[512,128]{1,0:T(8,128)(2,1)}) custom-call(s32[1024]{0:T(1024)S(1)} %get-tuple-element.38.lists, s32[8]{0:T(128)S(1)} %get-tuple-element.39.counts, bf16[16,64,128]{2,1,0:T(8,128)(2,1)S(1)} %collective-permute-done.3.arrived, ...), custom_call_target="tpu_custom_call" | custom-call | tf_op jit(solution)/shard_map/rim_last/pallas_call | solution.py:22
  36.0 0.0 collective-permute-start.4
  36.0 6.3 %all-to-all-start = ((bf16[16,32,128]{2,1,0:T(8,128)(2,1)}), bf16[16,32,128]{2,1,0:T(8,128)(2,1)S(1)}, u32[]{:S(2)}, u32[]{:S(2)}) async-start(bf16[16,32,128]{2,1,0:T(8,128)(2,1)} %bitcast.3), calls=%async_computation | async-start | bytes 262144 | tf_op jit(solution)/shard_map/all_to_all | solution.py:400
  42.3 3.8 %main_last.1 = (f32[32,64,128]{2,1,0:T(8,128)}, f32[16,64,128]{2,1,0:T(8,128)S(1)}, f32[32,64,128]{2,1,0:T(8,128)}) custom-call(s32[1024]{0:T(1024)S(1)} %get-tuple-element.38.lists, s32[8]{0:T(128)S(1)} %get-tuple-element.39.counts, f32[16,64,128]{2,1,0:T(8,128)S(1)} %get-tuple-element.63.low_rows, ...), custom_call_target="tpu_custom_call", output_to_operand_aliasing={{2}: (10, {})} | custom-call | tf_op jit(solution)/shard_map/main_last/pallas_call | solution.py:22
  46.1 3.8 %all-to-all-done = bf16[16,32,128]{2,1,0:T(8,128)(2,1)S(1)} async-done(((bf16[16,32,128]{2,1,0:T(8,128)(2,1)}), bf16[16,32,128]{2,1,0:T(8,128)(2,1)S(1)}, u32[]{:S(2)}, u32[]{:S(2)}) %all-to-all-start) | async-done | bytes 131104 | tf_op jit(solution)/shard_map/all_to_all | solution.py:400
  49.9 2.1 %trans.1 = f32[64,256]{1,0:T(8,128)} custom-call(bf16[512,128]{1,0:T(8,128)(2,1)S(1)} %bitcast.5, f32[64,256]{1,0:T(8,128)} %trans_in.1, bf16[256,256]{1,0:T(8,128)(2,1)} %matrix_in.1), custom_call_target="tpu_custom_call" | custom-call | tf_op jit(solution)/shard_map/trans/pallas_call | solution.py:22
  52.0 0.0 collective-permute-done.4.arrived
  52.0 0.8 %last.1 = f32[32,64,128]{2,1,0:T(8,128)} custom-call(bf16[16,64,128]{2,1,0:T(8,128)(2,1)S(1)} %collective-permute-done.4.arrived, f32[16,64,128]{2,1,0:T(8,128)S(1)} %get-tuple-element.69.low_next, f32[32,64,128]{2,1,0:T(8,128)} %get-tuple-element.70.lam_in), custom_call_target="tpu_custom_call", output_to_operand_aliasing={{}: (2, {})} | custom-call | tf_op jit(solution)/shard_map/last/pallas_call | solution.py:22
Async XLA Ops:
  0.6 8.0 %collective-permute-start.1 = (bf16[96,128,128]{2,1,0:T(8,128)(2,1)}, bf16[96,128,128]{2,1,0:T(8,128)(2,1)S(1)}, u32[]{:S(2)}, u32[]{:S(2)}) collective-permute-start(bf16[96,128,128]{2,1,0:T(8,128)(2,1)} %own_in.3), channel_id=1, source_target_pairs={{0,1},{1,0},{2,3},{3,2},{4,5},{5,4},{6,7},{7,6},{8,9},{9,8},{10,11... | collective-permute-start | bytes 9437192 | tf_op jit(solution)/shard_map/ppermute | solution.py:81
  1.9 4.8 %collective-permute-start = (s32[96]{0:T(128)S(1)}, s32[96]{0:T(128)S(1)}, u32[]{:S(2)}, u32[]{:S(2)}) collective-permute-start(s32[96]{0:T(128)S(1)} %shift-left_or_fusion.own_code.codes), channel_id=1, source_target_pairs={{0,1},{1,0},{2,3},{3,2},{4,5},{5,4},{6,7},{7,6},{8,9},{9,8},{10,11... | collective-permute-start | bytes 1160 | tf_op jit(solution)/shard_map/ppermute | solution.py:90
  5.5 7.7 %copy-start.1 = (s32[128]{0:T(128)S(1)}, s32[128]{0:T(128)}, u32[]{:S(2)}) copy-start(s32[128]{0:T(128)} %param.22) | copy-start | bytes 1540
  10.5 11.1 %collective-permute-start.2 = (bf16[16,64,128]{2,1,0:T(8,128)(2,1)S(1)}, bf16[16,64,128]{2,1,0:T(8,128)(2,1)S(1)}, u32[]{:S(2)}, u32[]{:S(2)}) collective-permute-start(bf16[16,64,128]{2,1,0:T(8,128)(2,1)S(1)} %rim_first.1), channel_id=1, source_target_pairs={{0,2},{2,4},{4,6},{6,0},{1,3},{3,5},{5,7},{7,1},{8,10},{10,12},{12... | collective-permute-start | bytes 786440 | tf_op jit(solution)/shard_map/ppermute | solution.py:202
  19.9 3.5 %copy-start = (bf16[96,128,128]{2,1,0:T(8,128)(2,1)}, bf16[96,128,128]{2,1,0:T(8,128)(2,1)S(1)}, u32[]{:S(2)}) copy-start(bf16[96,128,128]{2,1,0:T(8,128)(2,1)S(1)} %get-tuple-element.67.other_in) | copy-start | bytes 9437188
  21.6 2.2 %copy-start.2 = (s32[128,1]{0,1:T(1,128)S(1)}, s32[128,1]{0,1:T(1,128)}, u32[]{:S(2)}) copy-start(s32[128,1]{0,1:T(1,128)} %param.23) | copy-start | bytes 1540
  21.6 2.2 %copy-start.3 = (s32[128]{0:T(128)S(1)}, s32[128]{0:T(128)}, u32[]{:S(2)}) copy-start(s32[128]{0:T(128)} %param.24) | copy-start | bytes 1540
  23.4 9.3 %collective-permute-start.3 = (bf16[16,64,128]{2,1,0:T(8,128)(2,1)S(1)}, bf16[16,64,128]{2,1,0:T(8,128)(2,1)S(1)}, u32[]{:S(2)}, u32[]{:S(2)}) collective-permute-start(bf16[16,64,128]{2,1,0:T(8,128)(2,1)S(1)} %get-tuple-element.46), channel_id=1, source_target_pairs={{0,2},{2,4},{4,6},{6,0},{1,3},{3,5},{5,7},{7,1},{8,10},{10,12},{12... | collective-permute-start | bytes 786440 | tf_op jit(solution)/shard_map/ppermute | solution.py:365
  36.0 16.0 %collective-permute-start.4 = (bf16[16,64,128]{2,1,0:T(8,128)(2,1)}, bf16[16,64,128]{2,1,0:T(8,128)(2,1)S(1)}, u32[]{:S(2)}, u32[]{:S(2)}) collective-permute-start(bf16[16,64,128]{2,1,0:T(8,128)(2,1)} %get-tuple-element.62), channel_id=1, source_target_pairs={{0,2},{2,4},{4,6},{6,0},{1,3},{3,5},{5,7},{7,1},{8,10},{10,12},{12... | collective-permute-start | bytes 786440 | tf_op jit(solution)/shard_map/ppermute | solution.py:399
  36.0 13.9 %all-to-all-start = ((bf16[16,32,128]{2,1,0:T(8,128)(2,1)}), bf16[16,32,128]{2,1,0:T(8,128)(2,1)S(1)}, u32[]{:S(2)}, u32[]{:S(2)}) async-start(bf16[16,32,128]{2,1,0:T(8,128)(2,1)} %bitcast.3), calls=%async_computation | async-start | bytes 262144 | tf_op jit(solution)/shard_map/all_to_all | solution.py:400

commit v3 on v2

--- a/solution.py
+++ b/solution.py
@@ -5,8 +5,11 @@
 from jax.experimental.pallas import tpu as pltpu
 from jax.sharding import PartitionSpec as P
 
+
 STEPS = 3
 UNROLL = 16
+FEW = 24
+MANY = 40
 CLASSES = 4
 VMEM_LIMIT = 24 << 20
 
@@ -18,7 +21,7 @@
 STRIDE = 128
 
 
-def kernel(body, outs, ins, name, scratch=(), out_specs=None, aliases=None):
+def kernel(body, outs, ins, scratch=(), out_specs=None, aliases=None):
     return pl.pallas_call(
         body,
         out_shape=outs,
@@ -27,8 +30,14 @@
         scratch_shapes=list(scratch),
         input_output_aliases=aliases or {},
         compiler_params=pltpu.CompilerParams(vmem_limit_bytes=VMEM_LIMIT),
-        name=name,
     )(*[in_hbm(array) if spec is HB else array for array, spec in ins])
+
+
+def with_lists(body):
+    def whole(own_list, own_count, other_list, other_count, *refs):
+        return body((own_list, other_list), (own_count, other_count), *refs)
+
+    return whole
 
 
 def in_hbm(array):
@@ -66,7 +75,7 @@
     slots = max(2, 2 * heads // network)
     buses = highvoltage_derivative_matrix.shape[1]
     rows_sent = network * 2 * slots
-    assert stored + UNROLL <= STRIDE and blocks <= 64
+    assert -(-stored // MANY) * MANY <= STRIDE and -(-stored // FEW) * FEW <= STRIDE
 
     state = (blocks, cases, nodes)
     half = (low, cases, nodes)
@@ -77,8 +86,6 @@
     swap = [(0, 1), (1, 0)]
     onward = [(i, (i + 1) % owners) for i in range(owners)]
 
-    own = derivative_tiles
-    other = lax.ppermute(own, "case", swap)
     is_low = (tile_source_index < low).astype(jnp.int32)
     is_own = (tile_target_index < blocks).astype(jnp.int32)
     own_codes = (
@@ -87,24 +94,53 @@
         | ((tile_target_index - blocks * (1 - is_own)) << 16)
         | ((16 * is_own + 8 * is_low) << 24)
     )
+    own = derivative_tiles
     other_codes = lax.ppermute(own_codes, "case", swap)
-
-    def group(codes, lam, tiles, acc):
-        prods = [
-            jnp.dot(lam[(c >> 8) & 255], tiles[c & 255], preferred_element_type=F32) for c in codes
-        ]
-        for c, prod in zip(codes, prods):
-            acc[(c >> 16) & 255] += prod
-
-    def run(lists, counts, segment, lam, tiles, acc):
+    other = lax.ppermute(own, "case", swap)
+
+    def run(lists, counts, parts, width):
         def some(i, carry):
-            start = segment * STRIDE + i * UNROLL
-            group([lists[start + u] for u in range(UNROLL)], lam, tiles, acc)
+            words = [
+                (lists[side][kind * STRIDE + i * width + u], lam, tiles, acc)
+                for (side, kind), lam, tiles, acc in parts
+                for u in range(width)
+            ]
+            prods = [
+                jnp.dot(lam[(c >> 8) & 255], tiles[c & 255], preferred_element_type=F32)
+                for c, lam, tiles, _ in words
+            ]
+            for (c, _, _, acc), prod in zip(words, prods):
+                acc[(c >> 16) & 255] += prod
             return carry
 
-        lax.fori_loop(0, (counts[segment] + UNROLL - 1) // UNROLL, some, 0)
-
-    def first_body(codes, lam_in, own_in, acc, lo, hi, own_kept, lam, lam_bf, sems):
+        longest = 0
+        for (side, kind), _, _, _ in parts:
+            longest = jnp.maximum(longest, counts[side][kind])
+        lax.fori_loop(0, (longest + width - 1) // width, some, 0)
+
+    def sort(codes, lists, counts):
+        def place(e, used):
+            c = codes[e]
+            shift = c >> 24
+            lists[shift * (STRIDE // 8) + ((used >> shift) & 255)] = c
+            return used + (1 << shift)
+
+        used = lax.fori_loop(0, stored, place, jnp.int32(0), unroll=8)
+        for kind in range(CLASSES):
+            counts[kind] = (used >> (8 * kind)) & 255
+
+    list_shape = (CLASSES * STRIDE,)
+    list_types = (array(list_shape, jnp.int32), array((CLASSES,), jnp.int32))
+
+    def fill_idle(idle, lists, sem):
+        idle[...] = jnp.full(idle.shape, low << 8, jnp.int32)
+        fill = pltpu.make_async_copy(idle, lists, sem)
+        fill.start()
+        return fill
+
+    def first_body(
+        codes, lam_in, own_in, acc, lo, hi, own_kept, lists, counts, lam, lam_bf, idle, sems
+    ):
         lam_copy = pltpu.make_async_copy(lam_in, lam, sems.at[0])
         lam_copy.start()
         copies = [
@@ -115,11 +151,14 @@
         ]
         for copy in copies:
             copy.start()
+        fill = fill_idle(idle, lists, sems.at[1 + stored // UNROLL])
         for b in range(targets):
             acc[b] = jnp.zeros((cases, nodes), F32)
         zero = jnp.zeros((cases, nodes), BF16)
         lo[low] = zero
         hi[blocks - low] = zero
+        fill.wait()
+        sort(codes, lists, counts)
         lam_copy.wait()
         for b in range(blocks):
             rounded = lam[b].astype(BF16)
@@ -143,60 +182,52 @@
             for target, prod in prods:
                 acc[target] += prod
 
-    acc, lo, hi, own = kernel(
+    acc, lo, hi, own, own_lists, own_counts = kernel(
         first_body,
         (
             array(acc_shape, F32),
             array(padded, BF16),
             array(padded, BF16),
             array(own.shape, BF16),
-        ),
+        )
+        + list_types,
         [(own_codes, SM), (vertex_costate, HB), (own, HB)],
-        "first",
         scratch=[
             pltpu.VMEM(state, F32),
             pltpu.VMEM(state, BF16),
-            pltpu.SemaphoreType.DMA((1 + stored // UNROLL,)),
+            pltpu.VMEM(list_shape, jnp.int32),
+            pltpu.SemaphoreType.DMA((2 + stored // UNROLL,)),
         ],
-    )
-
-    def sort_body(own_code, other_code, lists, counts):
-        for side, code in enumerate((own_code, other_code)):
-            base = side * CLASSES * STRIDE
-
-            def place(e, used, code=code, base=base):
-                c = code[e]
-                shift = c >> 24
-                lists[base + shift * (STRIDE // 8) + ((used >> shift) & 255)] = c
-                return used + (1 << shift)
-
-            used = lax.fori_loop(0, stored, place, jnp.int32(0), unroll=8)
-            for kind in range(CLASSES):
-                at = (used >> (8 * kind)) & 255
-                counts[side * CLASSES + kind] = at
-                for u in range(UNROLL):
-                    lists[base + kind * STRIDE + at + u] = low << 8
-
-    lists, counts = kernel(
+        out_specs=(VM,) * 4 + (SM, SM),
+    )
+
+    def sort_body(codes, lists, counts, idle, sem):
+        fill_idle(idle, lists, sem).wait()
+        sort(codes, lists, counts)
+
+    other_lists, other_counts = kernel(
         sort_body,
-        (array((2 * CLASSES * STRIDE,), jnp.int32), array((2 * CLASSES,), jnp.int32)),
-        [(own_codes, SM), (other_codes, SM)],
-        "sort",
+        list_types,
+        [(other_codes, SM)],
+        scratch=[pltpu.VMEM(list_shape, jnp.int32), pltpu.SemaphoreType.DMA],
         out_specs=(SM, SM),
     )
-    listed = [(lists, SM), (counts, SM)]
+    listed = [(own_lists, SM), (own_counts, SM), (other_lists, SM), (other_counts, SM)]
 
     def rim_first_body(lists, counts, acc, lo, hi, other, out, sums):
         sums[...] = acc[blocks:]
-        run(lists, counts, CLASSES + 0, hi, other, sums)
-        run(lists, counts, CLASSES + 1, lo, other, sums)
+        run(
+            lists,
+            counts,
+            [((1, 0), hi, other, sums), ((1, 1), lo, other, sums)],
+            FEW,
+        )
         out[...] = sums[...].astype(BF16)
 
     (leaving,) = kernel(
-        rim_first_body,
+        with_lists(rim_first_body),
         (array((rim, cases, nodes), BF16),),
         listed + [(acc, VM), (lo, VM), (hi, VM), (other, VM)],
-        "rim_first",
         scratch=[pltpu.VMEM((rim, cases, nodes), F32)],
     )
     arriving = lax.ppermute(leaving, "blk", onward)
@@ -209,9 +240,8 @@
         for b in range(low, blocks):
             hi[b - low] = lam[b].astype(BF16)
         hi[blocks - low] = jnp.zeros((cases, nodes), BF16)
-        for side, tiles in enumerate((own, other)):
-            run(lists, counts, side * CLASSES + 0, hi, tiles, acc_rim)
-            run(lists, counts, side * CLASSES + 2, hi, tiles, acc)
+        run(lists, counts, [((0, 0), hi, own, acc_rim), ((1, 0), hi, other, acc_rim)], FEW)
+        run(lists, counts, [((0, 2), hi, own, acc), ((1, 2), hi, other, acc)], MANY)
 
     def head_values(lo, hi, hot):
         total = jnp.dot(lo[0], hot[0], preferred_element_type=F32)
@@ -233,13 +263,18 @@
         copies = [pltpu.make_async_copy(a, b, sems.at[i]) for i, (a, b) in enumerate(pairs)]
         for copy in copies:
             copy.start()
+        lam_next[...] = acc[:blocks]
+        run(
+            lists,
+            counts,
+            [((1, 2), hi, other, lam_next), ((1, 3), lo, other, lam_next)],
+            MANY,
+        )
         for copy in copies:
             copy.wait()
         for b in range(blocks):
-            lam_next[b] = acc[b] + outflow[b : b + 1, :] * icar[b]
+            lam_next[b] += outflow[b : b + 1, :] * icar[b]
             icar_next[b] = decay[b : b + 1, :] * icar[b] + inflow[b : b + 1, :] * lam[b]
-        run(lists, counts, CLASSES + 2, hi, other, lam_next)
-        run(lists, counts, CLASSES + 3, lo, other, lam_next)
         begin_next(
             lists, counts, lam_next, icar_next, outflow, own, other, acc_next, acc_rim, hi_next
         )
@@ -251,7 +286,7 @@
 
     factor = array(factor_shape, F32)
     lam, acc, acc_rim, hi_next, icar, head0, hot, decay, inflow, outflow, other_kept = kernel(
-        main_first_body,
+        with_lists(main_first_body),
         (
             array(state, F32),
             array(state, F32),
@@ -270,7 +305,6 @@
         + [(distribution_entry_vertex.reshape(1, heads), VM)]
         + [(vertex_costate, HB), (inverter_costate, HB), (inverter_decay_factor, HB)]
         + [(costate_to_inverter_factor, HB), (inverter_to_costate_factor, HB)],
-        "main_first",
         scratch=[pltpu.VMEM(state, F32), pltpu.VMEM(state, F32), pltpu.SemaphoreType.DMA((6,))],
         out_specs=(VM,) * 10 + (HB,),
     )
@@ -285,8 +319,7 @@
 
     def rim_sums(lists, counts, acc_rim, lo, own, other, out, sums):
         sums[...] = acc_rim[...]
-        run(lists, counts, 1, lo, own, sums)
-        run(lists, counts, CLASSES + 1, lo, other, sums)
+        run(lists, counts, [((0, 1), lo, own, sums), ((1, 1), lo, other, sums)], FEW)
         out[...] = sums[...].astype(BF16)
 
     def rim_body(lists, counts, arrived, lam, acc_rim, own, other, out, low_rows, lo, sums):
@@ -317,8 +350,7 @@
             row = low_rows[b] if b < low else lam[b]
             icar_next[b] = decay[b : b + 1, :] * icar[b] + inflow[b : b + 1, :] * row
         lam_next[...] = acc[...]
-        run(lists, counts, 3, lo, own, lam_next)
-        run(lists, counts, CLASSES + 3, lo, other, lam_next)
+        run(lists, counts, [((0, 3), lo, own, lam_next), ((1, 3), lo, other, lam_next)], MANY)
         begin_next(
             lists, counts, lam_next, icar_next, outflow, own, other, acc_next, acc_rim, hi_next
         )
@@ -356,15 +388,14 @@
     assert STEPS == 3
     hi = hi_next
     leaving, low_rows, lo = kernel(
-        rim_body,
+        with_lists(rim_body),
         (rim_type, low_type, array(padded, BF16)),
         listed + [(arriving, VM), (lam, VM), (acc_rim, VM)] + tiles,
-        "rim",
         scratch=[sums],
     )
     arriving = lax.ppermute(leaving, "blk", onward)
     lam, acc, acc_rim, hi_next, icar_low, begun, place, icar = kernel(
-        main_body,
+        with_lists(main_body),
         (
             low_type,
             array(state, F32),
@@ -381,19 +412,17 @@
         + [(low_rows, VM), (lam, VM), (lo, VM), (hi, VM), (acc, VM), (icar, VM)]
         + tiles
         + [(hot, VM), (head0, VM), (decay, VM), (inflow, VM), (outflow, VM)],
-        "main",
         scratch=[pltpu.VMEM(state, F32), pltpu.VMEM(state, F32), pltpu.SemaphoreType.DMA],
         out_specs=(VM,) * 7 + (HB,),
     )
 
     leaving, low_rows, lo, sent = kernel(
-        rim_last_body,
+        with_lists(rim_last_body),
         (rim_type, low_type, array(padded, BF16), array((rows_sent, nodes), BF16)),
         listed
         + [(arriving, VM), (lam, VM), (acc_rim, VM), (hi_next, VM)]
         + tiles
         + [(hot, VM), (begun, VM), (place, VM)],
-        "rim_last",
         scratch=[sums],
     )
     arriving = lax.ppermute(leaving, "blk", onward)
@@ -412,23 +441,21 @@
         del icar_in
 
         def fetch(side, source):
-            segment = side * CLASSES + 3
-
             def one(i, carry):
-                c = lists[segment * STRIDE + i]
+                c = lists[side][3 * STRIDE + i]
                 pltpu.make_async_copy(
                     source.at[c & 255], fetched.at[side * stored + i], sems.at[side]
                 ).start()
                 return carry
 
-            lax.fori_loop(0, counts[segment], one, 0)
+            lax.fori_loop(0, counts[side][3], one, 0)
 
         def fetched_all(side, source):
             def one(i, carry):
                 pltpu.make_async_copy(source.at[0], fetched.at[side * stored], sems.at[side]).wait()
                 return carry
 
-            lax.fori_loop(0, counts[side * CLASSES + 3], one, 0)
+            lax.fori_loop(0, counts[side][3], one, 0)
 
         fetch(0, own_in)
         fetch(1, other_in)
@@ -440,14 +467,13 @@
         lam_next[...] = acc[...]
         for side, source in enumerate((own_in, other_in)):
             fetched_all(side, source)
-            segment = side * CLASSES + 3
-
-            def some(i, carry, side=side, segment=segment):
-                start = i * UNROLL
+
+            def some(i, carry, side=side):
+                start = i * MANY
                 words = []
-                for u in range(UNROLL):
-                    at = jnp.minimum(start + u, counts[segment] - 1)
-                    words.append((lists[segment * STRIDE + start + u], side * stored + at))
+                for u in range(MANY):
+                    at = jnp.minimum(start + u, counts[side][3] - 1)
+                    words.append((lists[side][3 * STRIDE + start + u], side * stored + at))
                 prods = [
                     jnp.dot(lo[(c >> 8) & 255], fetched[at], preferred_element_type=F32)
                     for c, at in words
@@ -456,7 +482,7 @@
                     lam_next[(c >> 16) & 255] += prod
                 return carry
 
-            lax.fori_loop(0, (counts[segment] + UNROLL - 1) // UNROLL, some, 0)
+            lax.fori_loop(0, (counts[side][3] + MANY - 1) // MANY, some, 0)
         upper = pl.ds(low, blocks - low)
         lam_copy = pltpu.make_async_copy(lam_next.at[upper], lam_out.at[upper], sems.at[3])
         lam_copy.start()
@@ -465,12 +491,11 @@
         lam_copy.wait()
 
     lam, low_next, icar = kernel(
-        main_last_body,
+        with_lists(main_last_body),
         (array(state, F32), low_type, array(state, F32)),
         listed
         + [(low_rows, VM), (lo, VM), (acc, VM), (icar_low, VM), (decay, VM), (inflow, VM)]
         + [(derivative_tiles, HB), (other_kept, HB), (icar, HB)],
-        "main_last",
         scratch=[
             pltpu.VMEM(state, F32),
             pltpu.VMEM(half, F32),
@@ -478,7 +503,7 @@
             pltpu.SemaphoreType.DMA((4,)),
         ],
         out_specs=(HB, VM, HB),
-        aliases={10: 2},
+        aliases={12: 2},
     )
 
     def trans_body(received, trans_in, matrix_in, out, trans, matrix, sems):
@@ -488,16 +513,27 @@
         ]
         for copy in copies:
             copy.start()
-        got = received[...].astype(F32)
-        row = lax.broadcasted_iota(jnp.int32, (rows_sent, buses), 0)
-        second = lax.rem(row, 2 * slots) >= slots
-        column = lax.broadcasted_iota(jnp.int32, (rows_sent, buses), 1)
-        label = got[:, cases : cases + 1].astype(jnp.int32) - 1
-        hot_b = jnp.where(jnp.logical_and(label == column, second), 1.0, 0.0)
-        hot_a = pltpu.roll(hot_b, rows_sent - slots, 0)
         dims = (((0,), (0,)), ((), ()))
-        first = lax.dot_general(received[...], hot_a.astype(BF16), dims, preferred_element_type=F32)
-        last = lax.dot_general(received[...], hot_b.astype(BF16), dims, preferred_element_type=F32)
+        if slots % 16 == 0:
+            parts = received[...].reshape(network, 2, slots, nodes)
+            part_a = parts[:, 0].reshape(network * slots, nodes)
+            part_b = parts[:, 1].reshape(network * slots, nodes)
+            column = lax.broadcasted_iota(jnp.int32, (network * slots, buses), 1)
+            label = part_b[:, cases : cases + 1].astype(F32).astype(jnp.int32) - 1
+            hot = jnp.where(label == column, 1.0, 0.0).astype(BF16)
+            first = lax.dot_general(part_a, hot, dims, preferred_element_type=F32)
+            last = lax.dot_general(part_b, hot, dims, preferred_element_type=F32)
+        else:
+            got = received[...].astype(F32)
+            row = lax.broadcasted_iota(jnp.int32, (rows_sent, buses), 0)
+            second = lax.rem(row, 2 * slots) >= slots
+            column = lax.broadcasted_iota(jnp.int32, (rows_sent, buses), 1)
+            label = got[:, cases : cases + 1].astype(jnp.int32) - 1
+            hot_b = jnp.where(jnp.logical_and(label == column, second), 1.0, 0.0)
+            hot_a = pltpu.roll(hot_b, rows_sent - slots, 0).astype(BF16)
+            hot_b = hot_b.astype(BF16)
+            first = lax.dot_general(received[...], hot_a, dims, preferred_element_type=F32)
+            last = lax.dot_general(received[...], hot_b, dims, preferred_element_type=F32)
         for copy in copies:
             copy.wait()
         value = trans[...]
@@ -509,7 +545,6 @@
         trans_body,
         (array(highvoltage_costate.shape, F32),),
         [(received, VM), (highvoltage_costate, HB), (highvoltage_derivative_matrix, HB)],
-        "trans",
         scratch=[
             pltpu.VMEM(highvoltage_costate.shape, F32),
             pltpu.VMEM(highvoltage_derivative_matrix.shape, BF16),
@@ -535,7 +570,6 @@
         last_body,
         (array(state, F32),),
         [(arriving, VM), (low_next, VM), (lam, HB)],
-        "last",
         scratch=[pltpu.VMEM(half, F32), pltpu.SemaphoreType.DMA((4,))],
         out_specs=(HB,),
         aliases={2: 0},
@@ -559,6 +593,7 @@
         P(("sec", "blk")),
         P(("sec", "blk"), None),
     )
+
     return jax.shard_map(
         local,
         mesh=mesh,

time: 53.4 us -> 53.1 us (level)
  Pallas kernels: 31.9 us -> 29.5 us
  starting transfers between devices: 9.89 us -> 11.4 us
  waiting for transfers between devices: 9.68 us -> 10.4 us
    pallas_call x10, Pallas kernels: 31.9 us -> 29.5 us  [kernel(): pl.pallas_call(body, out_shape=outs, in_specs=[spec for _, spec in ins],...]
    ppermute x3, waiting for transfers between devices: 4.75 us -> 5.93 us  [local(): arriving = lax.ppermute(leaving, 'blk', onward)]
    ppermute x3, starting transfers between devices: 3 us -> 3.93 us  [local(): arriving = lax.ppermute(leaving, 'blk', onward)]
    all_to_all x1, starting transfers between devices: 6.31 us -> 6.86 us  [local(): lax.all_to_all(sent.reshape(network, 2 * slots, nodes), ('sec', 'blk'), s...]
  transfers between devices with their start and end apart: 6 -> 6, of which waited for: 4 -> 4; matrix products, arithmetic and copies ran while one was open for 1% -> 1% of each run, Pallas kernels for 46% -> 44%
where the time goes in v3:
time: 53.1 us; the launch traced here: 52.7 us
  Pallas kernels  29.5 us (56%)
  starting transfers between devices  11.4 us (21%)
  waiting for transfers between devices  10.4 us (20%)
  between operations  0.75 us (1%)
  other arithmetic  0.68 us (1%)
    pallas_call x10, Pallas kernels, kernel(): pl.pallas_call(body, out_shape=outs, in_specs=[spec for _, spec in ins],...  29.5 us
    all_to_all x1, starting transfers between devices, local(): lax.all_to_all(sent.reshape(network, 2 * slots, nodes), ('sec', 'blk'), s...  6.86 us
    ppermute x3, waiting for transfers between devices, local(): arriving = lax.ppermute(leaving, 'blk', onward)  5.93 us
    ppermute x3, starting transfers between devices, local(): arriving = lax.ppermute(leaving, 'blk', onward)  3.93 us
    all_to_all x1, waiting for transfers between devices, local(): lax.all_to_all(sent.reshape(network, 2 * slots, nodes), ('sec', 'blk'), s...  3.83 us
  transfers between devices with their start and end apart: 6, of which 4 were waited for; matrix products, arithmetic and copies ran while one was open for 1% of the time, Pallas kernels for 44%

profile of v3, /device:TPU:0, one launch (start us, length us, event | category | flops | bytes accessed | tf_op | source)
XLA Modules:
  0.0 52.7 jit_solution(4056749205935388429)
XLA Ops:
  0.6 0.6 %collective-permute-start.1 = (bf16[96,128,128]{2,1,0:T(8,128)(2,1)}, bf16[96,128,128]{2,1,0:T(8,128)(2,1)S(1)}, u32[]{:S(2)}, u32[]{:S(2)}) collective-permute-start(bf16[96,128,128]{2,1,0:T(8,128)(2,1)} %refs_6_.3), channel_id=1, source_target_pairs={{0,1},{1,0},{2,3},{3,2},{4,5},{5,4},{6,7},{7,6},{8,9},{9,8},{10,11... | collective-permute-start | bytes 9437192 | tf_op jit(solution)/shard_map/ppermute | solution.py:99
  1.2 0.7 %shift-left_or_fusion.codes = s32[96]{0:T(128)S(1)} fusion(s32[96]{0:T(128)} %param.18, s32[96]{0:T(128)} %param.17), kind=kLoop, calls=%fused_computation.15 | loop fusion | flops 1824 | bytes 1152 | tf_op jit(solution)/shard_map/or | solution.py:92
  1.9 0.0 collective-permute-start
  1.9 4.1 %shard_map.148 = (f32[48,64,128]{2,1,0:T(8,128)S(1)}, bf16[17,64,128]{2,1,0:T(8,128)(2,1)S(1)}, bf16[17,64,128]{2,1,0:T(8,128)(2,1)S(1)}, bf16[96,128,128]{2,1,0...) custom-call(s32[96]{0:T(128)S(1)} %shift-left_or_fusion.codes, f32[32,64,128]{2,1,0:T(8,128)} %refs_6_.2, ...), custom_call_target="tpu_custom_call" | custom-call | tf_op jit(solution)/shard_map/pallas_call | solution.py:25
  6.0 0.0 copy-start.3
  6.0 0.6 %collective-permute-done.codes = s32[96]{0:T(128)S(1)} collective-permute-done((s32[96]{0:T(128)S(1)}, s32[96]{0:T(128)S(1)}, u32[]{:S(2)}, u32[]{:S(2)}) %collective-permute-start) | collective-permute-done | bytes 416 | tf_op jit(solution)/shard_map/ppermute | solution.py:98
  6.7 2.1 %shard_map.149 = (s32[512]{0:T(512)S(1)}, s32[4]{0:T(128)S(1)}) custom-call(s32[96]{0:T(128)S(1)} %collective-permute-done.codes), custom_call_target="tpu_custom_call" | custom-call | tf_op jit(solution)/shard_map/pallas_call | solution.py:25
  8.8 0.0 collective-permute-done.1.refs_3_.refs_4_.refs_9_.refs_5_
  8.8 1.3 %shard_map.150 = bf16[16,64,128]{2,1,0:T(8,128)(2,1)S(1)} custom-call(s32[512]{0:T(512)S(1)} %get-tuple-element.40.own_list, s32[4]{0:T(128)S(1)} %get-tuple-element.41.own_count, s32[512]{0:T(512)S(1)} %get-tuple-element.42.other_list, s32[4]{0:T(128)S(1)} %get-tuple-element.43.other_count, f32[48,64,128]{2,1,0:T(8,128)S(1)} %get-tuple-element.44.refs_0_, ...), custom_call_target="tpu_custom_call" | custom-call | tf_op jit(solution)/shard_map/pallas_call | solution.py:25
  10.1 3.6 %collective-permute-start.2 = (bf16[16,64,128]{2,1,0:T(8,128)(2,1)S(1)}, bf16[16,64,128]{2,1,0:T(8,128)(2,1)S(1)}, u32[]{:S(2)}, u32[]{:S(2)}) collective-permute-start(bf16[16,64,128]{2,1,0:T(8,128)(2,1)S(1)} %shard_map.150), channel_id=1, source_target_pairs={{0,2},{2,4},{4,6},{6,0},{1,3},{3,5},{5,7},{7,1},{8,10},{10,12},{12... | collective-permute-start | bytes 786440 | tf_op jit(solution)/shard_map/ppermute | solution.py:233
  13.7 0.0 copy-done.3
  13.7 5.6 %shard_map.151 = (f32[32,64,128]{2,1,0:T(8,128)S(1)}, f32[32,64,128]{2,1,0:T(8,128)S(1)}, f32[16,64,128]{2,1,0:T(8,128)S(1)}, bf16[17,64,128]{2,1,0:T(8,128)(2,1...) custom-call(s32[512]{0:T(512)S(1)} %get-tuple-element.40.own_list, ...), custom_call_target="tpu_custom_call" | custom-call | tf_op jit(solution)/shard_map/pallas_call | solution.py:25
  19.3 0.0 copy-start
  19.3 2.4 %collective-permute-done.2.refs_0_ = bf16[16,64,128]{2,1,0:T(8,128)(2,1)S(1)} collective-permute-done((bf16[16,64,128]{2,1,0:T(8,128)(2,1)S(1)}, bf16[16,64,128]{2,1,0:T(8,128)(2,1)S(1)}, u32[]{:S(2)}, u32[]{:S(2)}) %collective-permute-start.2) | collective-permute-done | bytes 262176 | tf_op jit(solution)/shard_map/ppermute | solution.py:233
  21.7 0.0 copy-start.1
  21.7 0.0 copy-start.2
  21.7 1.3 %shard_map.152 = (bf16[16,64,128]{2,1,0:T(8,128)(2,1)S(1)}, f32[16,64,128]{2,1,0:T(8,128)S(1)}, bf16[17,64,128]{2,1,0:T(8,128)(2,1)S(1)}) custom-call(s32[512]{0:T(512)S(1)} %get-tuple-element.40.own_list, s32[4]{0:T(128)S(1)} %get-tuple-element.41.own_count, s32[512]{0:T(512)S(1)} %get-tuple-element.42.other_list, s32[4]{0:T(128)S(1)} %get-tuple-element.43.other_count, ...), custom_call_target="tpu_custom_call" | custom-call | tf_op jit(solution)/shard_map/pallas_call | solution.py:25
  23.0 0.0 copy-done
  23.0 0.3 collective-permute-start.3
  23.4 0.0 copy-done.1
  23.4 0.0 copy-done.2
  23.4 5.7 %shard_map.153 = (f32[16,64,128]{2,1,0:T(8,128)S(1)}, f32[32,64,128]{2,1,0:T(8,128)S(1)}, f32[16,64,128]{2,1,0:T(8,128)S(1)}, bf16[17,64,128]{2,1,0:T(8,128)(2,1...) custom-call(s32[512]{0:T(512)S(1)} %get-tuple-element.40.own_list, ...), custom_call_target="tpu_custom_call" | custom-call | tf_op jit(solution)/shard_map/pallas_call | solution.py:25
  29.1 3.5 %collective-permute-done.3.refs_0_ = bf16[16,64,128]{2,1,0:T(8,128)(2,1)S(1)} collective-permute-done((bf16[16,64,128]{2,1,0:T(8,128)(2,1)S(1)}, bf16[16,64,128]{2,1,0:T(8,128)(2,1)S(1)}, u32[]{:S(2)}, u32[]{:S(2)}) %collective-permute-start.3) | collective-permute-done | bytes 262176 | tf_op jit(solution)/shard_map/ppermute | solution.py:396
  32.6 2.6 %shard_map.154 = (bf16[16,64,128]{2,1,0:T(8,128)(2,1)}, f32[16,64,128]{2,1,0:T(8,128)S(1)}, bf16[17,64,128]{2,1,0:T(8,128)(2,1)S(1)}, bf16[512,128]{1,0:T(8,128)(2,1)}) custom-call(s32[512]{0:T(512)S(1)} %get-tuple-element.40.own_list, s32[4]{0:T(128)S(1)} %get-tuple-element.41.own_count, s32[512]{0:T(512)S(1)} %get-tuple-element.42.other_list, ...), custom_call_target="tpu_custom_call" | custom-call | tf_op jit(solution)/shard_map/pallas_call | solution.py:25
  35.3 0.0 collective-permute-start.4
  35.3 6.9 %all-to-all-start = ((bf16[16,32,128]{2,1,0:T(8,128)(2,1)}), bf16[16,32,128]{2,1,0:T(8,128)(2,1)S(1)}, u32[]{:S(2)}, u32[]{:S(2)}) async-start(bf16[16,32,128]{2,1,0:T(8,128)(2,1)} %bitcast.3), calls=%async_computation | async-start | bytes 262144 | tf_op jit(solution)/shard_map/all_to_all | solution.py:429
  42.2 3.8 %shard_map.155 = (f32[32,64,128]{2,1,0:T(8,128)}, f32[16,64,128]{2,1,0:T(8,128)S(1)}, f32[32,64,128]{2,1,0:T(8,128)}) custom-call(s32[512]{0:T(512)S(1)} %get-tuple-element.40.own_list, s32[4]{0:T(128)S(1)} %get-tuple-element.41.own_count, s32[512]{0:T(512)S(1)} %get-tuple-element.42.other_list, ...), custom_call_target="tpu_custom_call", output_to_operand_aliasing={{2}: (12, {})} | custom-call | tf_op jit(solution)/shard_map/pallas_call | solution.py:25
  46.0 3.8 %all-to-all-done = bf16[16,32,128]{2,1,0:T(8,128)(2,1)S(1)} async-done(((bf16[16,32,128]{2,1,0:T(8,128)(2,1)}), bf16[16,32,128]{2,1,0:T(8,128)(2,1)S(1)}, u32[]{:S(2)}, u32[]{:S(2)}) %all-to-all-start) | async-done | bytes 131104 | tf_op jit(solution)/shard_map/all_to_all | solution.py:429
  49.8 2.1 %shard_map.157 = f32[64,256]{1,0:T(8,128)} custom-call(bf16[512,128]{1,0:T(8,128)(2,1)S(1)} %bitcast.5, f32[64,256]{1,0:T(8,128)} %trans_in.1, bf16[256,256]{1,0:T(8,128)(2,1)} %matrix_in.1), custom_call_target="tpu_custom_call" | custom-call | tf_op jit(solution)/shard_map/pallas_call | solution.py:25
  51.8 0.0 collective-permute-done.4.arrived
  51.8 0.8 %shard_map.156 = f32[32,64,128]{2,1,0:T(8,128)} custom-call(bf16[16,64,128]{2,1,0:T(8,128)(2,1)S(1)} %collective-permute-done.4.arrived, f32[16,64,128]{2,1,0:T(8,128)S(1)} %get-tuple-element.73.low_next, f32[32,64,128]{2,1,0:T(8,128)} %get-tuple-element.74.lam_in), custom_call_target="tpu_custom_call", output_to_operand_aliasing={{}: (2, {})} | custom-call | tf_op jit(solution)/shard_map/pallas_call | solution.py:25
Async XLA Ops:
  0.6 8.1 %collective-permute-start.1 = (bf16[96,128,128]{2,1,0:T(8,128)(2,1)}, bf16[96,128,128]{2,1,0:T(8,128)(2,1)S(1)}, u32[]{:S(2)}, u32[]{:S(2)}) collective-permute-start(bf16[96,128,128]{2,1,0:T(8,128)(2,1)} %refs_6_.3), channel_id=1, source_target_pairs={{0,1},{1,0},{2,3},{3,2},{4,5},{5,4},{6,7},{7,6},{8,9},{9,8},{10,11... | collective-permute-start | bytes 9437192 | tf_op jit(solution)/shard_map/ppermute | solution.py:99
  1.9 4.8 %collective-permute-start = (s32[96]{0:T(128)S(1)}, s32[96]{0:T(128)S(1)}, u32[]{:S(2)}, u32[]{:S(2)}) collective-permute-start(s32[96]{0:T(128)S(1)} %shift-left_or_fusion.codes), channel_id=1, source_target_pairs={{0,1},{1,0},{2,3},{3,2},{4,5},{5,4},{6,7},{7,6},{8,9},{9,8},{10,11... | collective-permute-start | bytes 1160 | tf_op jit(solution)/shard_map/ppermute | solution.py:98
  6.0 7.6 %copy-start.3 = (s32[128]{0:T(128)S(1)}, s32[128]{0:T(128)}, u32[]{:S(2)}) copy-start(s32[128]{0:T(128)} %param.22) | copy-start | bytes 1540
  10.1 11.6 %collective-permute-start.2 = (bf16[16,64,128]{2,1,0:T(8,128)(2,1)S(1)}, bf16[16,64,128]{2,1,0:T(8,128)(2,1)S(1)}, u32[]{:S(2)}, u32[]{:S(2)}) collective-permute-start(bf16[16,64,128]{2,1,0:T(8,128)(2,1)S(1)} %shard_map.150), channel_id=1, source_target_pairs={{0,2},{2,4},{4,6},{6,0},{1,3},{3,5},{5,7},{7,1},{8,10},{10,12},{12... | collective-permute-start | bytes 786440 | tf_op jit(solution)/shard_map/ppermute | solution.py:233
  19.3 3.7 %copy-start = (bf16[96,128,128]{2,1,0:T(8,128)(2,1)}, bf16[96,128,128]{2,1,0:T(8,128)(2,1)S(1)}, u32[]{:S(2)}) copy-start(bf16[96,128,128]{2,1,0:T(8,128)(2,1)S(1)} %get-tuple-element.71.refs_7_) | copy-start | bytes 9437188
  21.7 1.7 %copy-start.1 = (s32[128,1]{0,1:T(1,128)S(1)}, s32[128,1]{0,1:T(1,128)}, u32[]{:S(2)}) copy-start(s32[128,1]{0,1:T(1,128)} %param.23) | copy-start | bytes 1540
  21.7 1.7 %copy-start.2 = (s32[128]{0:T(128)S(1)}, s32[128]{0:T(128)}, u32[]{:S(2)}) copy-start(s32[128]{0:T(128)} %param.24) | copy-start | bytes 1540
  23.0 9.6 %collective-permute-start.3 = (bf16[16,64,128]{2,1,0:T(8,128)(2,1)S(1)}, bf16[16,64,128]{2,1,0:T(8,128)(2,1)S(1)}, u32[]{:S(2)}, u32[]{:S(2)}) collective-permute-start(bf16[16,64,128]{2,1,0:T(8,128)(2,1)S(1)} %get-tuple-element.50), channel_id=1, source_target_pairs={{0,2},{2,4},{4,6},{6,0},{1,3},{3,5},{5,7},{7,1},{8,10},{10,12},{12... | collective-permute-start | bytes 786440 | tf_op jit(solution)/shard_map/ppermute | solution.py:396
  35.3 16.6 %collective-permute-start.4 = (bf16[16,64,128]{2,1,0:T(8,128)(2,1)}, bf16[16,64,128]{2,1,0:T(8,128)(2,1)S(1)}, u32[]{:S(2)}, u32[]{:S(2)}) collective-permute-start(bf16[16,64,128]{2,1,0:T(8,128)(2,1)} %get-tuple-element.66), channel_id=1, source_target_pairs={{0,2},{2,4},{4,6},{6,0},{1,3},{3,5},{5,7},{7,1},{8,10},{10,12},{12... | collective-permute-start | bytes 786440 | tf_op jit(solution)/shard_map/ppermute | solution.py:428
  35.3 14.5 %all-to-all-start = ((bf16[16,32,128]{2,1,0:T(8,128)(2,1)}), bf16[16,32,128]{2,1,0:T(8,128)(2,1)S(1)}, u32[]{:S(2)}, u32[]{:S(2)}) async-start(bf16[16,32,128]{2,1,0:T(8,128)(2,1)} %bitcast.3), calls=%async_computation | async-start | bytes 262144 | tf_op jit(solution)/shard_map/all_to_all | solution.py:429

commit v4 on v3

--- a/solution.py
+++ b/solution.py
@@ -74,7 +74,7 @@
     heads = distribution_entry_vertex.shape[0]
     slots = max(2, 2 * heads // network)
     buses = highvoltage_derivative_matrix.shape[1]
-    rows_sent = network * 2 * slots
+    rows_sent = network * 3 * slots
     assert -(-stored // MANY) * MANY <= STRIDE and -(-stored // FEW) * FEW <= STRIDE
 
     state = (blocks, cases, nodes)
@@ -85,6 +85,7 @@
     factor_shape = inverter_decay_factor.shape
     swap = [(0, 1), (1, 0)]
     onward = [(i, (i + 1) % owners) for i in range(owners)]
+    backward = [(j, i) for i, j in onward]
 
     is_low = (tile_source_index < low).astype(jnp.int32)
     is_own = (tile_target_index < blocks).astype(jnp.int32)
@@ -232,6 +233,11 @@
     )
     arriving = lax.ppermute(leaving, "blk", onward)
 
+    mine = jnp.concatenate(
+        [distribution_entry_vertex, distribution_entry_holder[:, 0], distribution_entry_substation]
+    )
+    theirs = lax.ppermute(mine, "blk", backward)
+
     def begin_next(lists, counts, lam, icar, outflow, own, other, acc, acc_rim, hi):
         for b in range(blocks):
             acc[b] = outflow[b : b + 1, :] * icar[b]
@@ -326,60 +332,132 @@
         take_arrived(arrived, lam, low_rows, lo)
         rim_sums(lists, counts, acc_rim, lo, own, other, out, sums)
 
-    def rim_last_body(
-        lists, counts, arrived, lam, acc_rim, hi, own, other, hot, begun, place,
-        out, low_rows, lo, sent, sums,
-    ):
+    def rim_last_body(lists, counts, arrived, lam, acc_rim, kept, out, low_rows, lo, sums):
         take_arrived(arrived, lam, low_rows, lo)
-        rim_sums(lists, counts, acc_rim, lo, own, other, out, sums)
-        head = jnp.concatenate(
-            [head_values(lo, hi, hot), jnp.zeros((nodes - cases, heads), BF16)], axis=0
-        )
-        dims = (((1,), (1,)), ((), ()))
-        sent[...] = (
-            begun[...] + lax.dot_general(place[...], head, dims, preferred_element_type=F32)
-        ).astype(BF16)
+        sums[...] = acc_rim[...]
+        for side in (0, 1):
+            run_fetched(lists, counts, side, 1, lo, kept, side * stored, sums, FEW)
+        out[...] = sums[...].astype(BF16)
+
+    def rows_of(owner):
+        names = jnp.broadcast_to(owner.astype(F32), (heads, heads))
+        before = lax.broadcasted_iota(jnp.int32, (heads, heads), 0)
+        after = lax.broadcasted_iota(jnp.int32, (heads, heads), 1)
+        same = jnp.logical_and(names.T == names, before < after)
+        slot = jnp.sum(jnp.where(same, 1.0, 0.0), axis=0, keepdims=True).astype(jnp.int32)
+        return owner * (3 * slots) + slot
 
     def main_body(
-        lists, counts, owner, bus, low_rows, lam, lo, hi, acc, icar, own, other, hot, head0,
-        decay, inflow, outflow,
-        lam_low, acc_next, acc_rim, hi_next, icar_low, begun, place, icar_out,
-        lam_next, icar_next, sem,
+        lists, counts, owner, bus, theirs, left,
+        low_rows, lam, lo, hi, acc, icar, own, other, hot, head0, decay, inflow, outflow,
+        lam_low, acc_next, hi_next, icar_low, sent, icar_out, lam_next, icar_next, lo_base, sem,
     ):
         for b in range(blocks):
             row = low_rows[b] if b < low else lam[b]
             icar_next[b] = decay[b : b + 1, :] * icar[b] + inflow[b : b + 1, :] * row
+            acc_next[b] = outflow[b : b + 1, :] * icar_next[b]
         lam_next[...] = acc[...]
         run(lists, counts, [((0, 3), lo, own, lam_next), ((1, 3), lo, other, lam_next)], MANY)
-        begin_next(
-            lists, counts, lam_next, icar_next, outflow, own, other, acc_next, acc_rim, hi_next
-        )
         for b in range(low):
             lam_low[b] = lam_next[b]
+            lo_base[b] = lam_next[b].astype(BF16)
             icar_low[b] = icar_next[b]
         for b in range(low, blocks):
+            hi_next[b - low] = lam_next[b].astype(BF16)
             icar_next[b] = decay[b : b + 1, :] * icar_next[b] + inflow[b : b + 1, :] * lam_next[b]
+        hi_next[blocks - low] = jnp.zeros((cases, nodes), BF16)
         upper = pl.ds(low, blocks - low)
         copy = pltpu.make_async_copy(icar_next.at[upper], icar_out.at[upper], sem)
         copy.start()
-        mine = jnp.broadcast_to(owner[...].astype(F32), (heads, heads))
-        before = lax.broadcasted_iota(jnp.int32, (heads, heads), 0)
-        after = lax.broadcasted_iota(jnp.int32, (heads, heads), 1)
-        same = jnp.logical_and(mine.T == mine, before < after)
-        slot = jnp.sum(jnp.where(same, 1.0, 0.0), axis=0, keepdims=True).astype(jnp.int32)
-        dest = owner[...] * (2 * slots) + slot
+        node = lax.broadcasted_iota(jnp.int32, (nodes, heads), 0)
+        vertex_next, owner_next, bus_next = (theirs[:, i * heads : (i + 1) * heads] for i in range(3))
+        head_next = jnp.zeros((cases, heads), F32)
+        for b in range(low):
+            hot_next = jnp.where(node + b * nodes == vertex_next, 1.0, 0.0).astype(BF16)
+            head_next += jnp.dot(left[b], hot_next, preferred_element_type=F32)
         row = lax.broadcasted_iota(jnp.int32, (rows_sent, heads), 0)
-        place_a = jnp.where(row == dest, 1.0, 0.0).astype(BF16)
-        place_b = jnp.where(row == dest + slots, 1.0, 0.0).astype(BF16)
-        place[...] = place_b
-        label = jnp.broadcast_to((bus[...] + 1).astype(F32), (nodes - cases, heads)).astype(BF16)
-        pair_a = jnp.concatenate([head0[...], head_values(lo, hi, hot)], axis=0)
-        pair_b = jnp.concatenate([jnp.zeros((cases, heads), BF16), label], axis=0)
-        dims = (((1,), (1,)), ((), ()))
-        begun[...] = lax.dot_general(
-            place_a, pair_a, dims, preferred_element_type=F32
-        ) + lax.dot_general(place_b, pair_b, dims, preferred_element_type=F32)
+        dest = rows_of(owner[...])
+        followed = lax.axis_index("blk") < owners - 1
+        dest_next = jnp.where(followed, rows_of(owner_next) + 2 * slots, -1)
+        width = (nodes - cases, heads)
+        pairs = [
+            (dest, head0[...], head_values(lo, hi, hot)),
+            (
+                dest + slots,
+                head_values(lo_base, hi_next, hot),
+                jnp.broadcast_to((bus[...] + 1).astype(F32), width).astype(BF16),
+            ),
+            (
+                dest_next,
+                head_next.astype(BF16),
+                jnp.broadcast_to((bus_next + 1).astype(F32), width).astype(BF16),
+            ),
+        ]
+        total = jnp.zeros((rows_sent, nodes), F32)
+        for where, upper_half, lower_half in pairs:
+            place = jnp.where(row == where, 1.0, 0.0).astype(BF16)
+            total += lax.dot_general(
+                place,
+                jnp.concatenate([upper_half, lower_half], axis=0),
+                (((1,), (1,)), ((), ())),
+                preferred_element_type=F32,
+            )
+        sent[...] = total.astype(BF16)
         copy.wait()
+
+    def fetch(lists, counts, side, kind, source, dest, first, sem):
+        def one(i, carry):
+            c = lists[side][kind * STRIDE + i]
+            pltpu.make_async_copy(source.at[c & 255], dest.at[first + i], sem).start()
+            return carry
+
+        lax.fori_loop(0, counts[side][kind], one, 0)
+
+    def fetched(counts, side, kind, source, dest, sem):
+        def one(i, carry):
+            pltpu.make_async_copy(source.at[0], dest.at[0], sem).wait()
+            return carry
+
+        lax.fori_loop(0, counts[side][kind], one, 0)
+
+    def run_fetched(lists, counts, side, kind, lam, source, first, acc, width):
+        def some(i, carry):
+            words = []
+            for u in range(width):
+                at = jnp.minimum(i * width + u, counts[side][kind] - 1)
+                words.append((lists[side][kind * STRIDE + i * width + u], first + at))
+            prods = [
+                jnp.dot(lam[(c >> 8) & 255], source[at], preferred_element_type=F32)
+                for c, at in words
+            ]
+            for (c, _), prod in zip(words, prods):
+                acc[(c >> 16) & 255] += prod
+            return carry
+
+        lax.fori_loop(0, (counts[side][kind] + width - 1) // width, some, 0)
+
+    def begin_last_body(
+        lists, counts, begun, hi, own_in, other_in, acc, acc_rim, kept, ready, sems
+    ):
+        sources = (own_in, other_in)
+        for side in (0, 1):
+            first = side * stored
+            fetch(lists, counts, side, 0, sources[side], ready, first, sems.at[side, 0])
+            fetch(
+                lists, counts, side, 2, sources[side], ready, first + counts[side][0], sems.at[side, 2]
+            )
+        for side in (0, 1):
+            fetch(lists, counts, side, 1, sources[side], kept, side * stored, sems.at[side, 1])
+        acc[...] = begun[...]
+        acc_rim[...] = jnp.zeros(acc_rim.shape, F32)
+        for side in (0, 1):
+            first = side * stored
+            fetched(counts, side, 0, sources[side], ready, sems.at[side, 0])
+            run_fetched(lists, counts, side, 0, hi, ready, first, acc_rim, FEW)
+            fetched(counts, side, 2, sources[side], ready, sems.at[side, 2])
+            run_fetched(lists, counts, side, 2, hi, ready, first + counts[side][0], acc, MANY)
+        for side in (0, 1):
+            fetched(counts, side, 1, sources[side], kept, sems.at[side, 1])
 
     tiles = [(own, VM), (other, VM)]
     rim_type = array((rim, cases, nodes), BF16)
@@ -394,95 +472,76 @@
         scratch=[sums],
     )
     arriving = lax.ppermute(leaving, "blk", onward)
-    lam, acc, acc_rim, hi_next, icar_low, begun, place, icar = kernel(
+    lam, acc, hi_next, icar_low, sent, icar = kernel(
         with_lists(main_body),
         (
             low_type,
             array(state, F32),
-            array((rim, cases, nodes), F32),
             array(padded, BF16),
             low_type,
-            array((rows_sent, nodes), F32),
-            array((rows_sent, heads), BF16),
+            array((rows_sent, nodes), BF16),
             array(state, F32),
         ),
         listed
-        + [(distribution_entry_holder.reshape(1, heads), VM)]
-        + [(distribution_entry_substation.reshape(1, heads), VM)]
+        + [
+            (distribution_entry_holder.reshape(1, heads), VM),
+            (distribution_entry_substation.reshape(1, heads), VM),
+            (theirs.reshape(1, 3 * heads), VM),
+            (leaving, VM),
+        ]
         + [(low_rows, VM), (lam, VM), (lo, VM), (hi, VM), (acc, VM), (icar, VM)]
         + tiles
         + [(hot, VM), (head0, VM), (decay, VM), (inflow, VM), (outflow, VM)],
-        scratch=[pltpu.VMEM(state, F32), pltpu.VMEM(state, F32), pltpu.SemaphoreType.DMA],
-        out_specs=(VM,) * 7 + (HB,),
-    )
-
-    leaving, low_rows, lo, sent = kernel(
-        with_lists(rim_last_body),
-        (rim_type, low_type, array(padded, BF16), array((rows_sent, nodes), BF16)),
-        listed
-        + [(arriving, VM), (lam, VM), (acc_rim, VM), (hi_next, VM)]
-        + tiles
-        + [(hot, VM), (begun, VM), (place, VM)],
-        scratch=[sums],
-    )
-    arriving = lax.ppermute(leaving, "blk", onward)
+        scratch=[
+            pltpu.VMEM(state, F32),
+            pltpu.VMEM(state, F32),
+            pltpu.VMEM(half, BF16),
+            pltpu.SemaphoreType.DMA,
+        ],
+        out_specs=(VM,) * 5 + (HB,),
+    )
     received = lax.all_to_all(
-        sent.reshape(network, 2 * slots, nodes),
+        sent.reshape(network, 3 * slots, nodes),
         ("sec", "blk"),
         split_axis=0,
         concat_axis=0,
         tiled=True,
-    ).reshape(rows_sent, nodes)
+    )
+    received = received.reshape(rows_sent, nodes)
+    stored_in = [(derivative_tiles, HB), (other_kept, HB)]
+    fetched_shape = (2 * stored, nodes, nodes)
+    acc, acc_rim, kept = kernel(
+        with_lists(begin_last_body),
+        (array(state, F32), array((rim, cases, nodes), F32), array(fetched_shape, BF16)),
+        listed + [(acc, VM), (hi_next, VM)] + stored_in,
+        scratch=[pltpu.VMEM(fetched_shape, BF16), pltpu.SemaphoreType.DMA((2, 3))],
+    )
+
+    leaving, low_rows, lo = kernel(
+        with_lists(rim_last_body),
+        (rim_type, low_type, array(padded, BF16)),
+        listed + [(arriving, VM), (lam, VM), (acc_rim, VM), (kept, VM)],
+        scratch=[sums],
+    )
+    arriving = lax.ppermute(leaving, "blk", onward)
 
     def main_last_body(
         lists, counts, low_rows, lo, acc, icar_low, decay, inflow, own_in, other_in, icar_in,
-        lam_out, low_next, icar_out, lam_next, icar_next, fetched, sems,
+        lam_out, low_next, icar_out, lam_next, icar_next, ready, sems,
     ):
         del icar_in
-
-        def fetch(side, source):
-            def one(i, carry):
-                c = lists[side][3 * STRIDE + i]
-                pltpu.make_async_copy(
-                    source.at[c & 255], fetched.at[side * stored + i], sems.at[side]
-                ).start()
-                return carry
-
-            lax.fori_loop(0, counts[side][3], one, 0)
-
-        def fetched_all(side, source):
-            def one(i, carry):
-                pltpu.make_async_copy(source.at[0], fetched.at[side * stored], sems.at[side]).wait()
-                return carry
-
-            lax.fori_loop(0, counts[side][3], one, 0)
-
-        fetch(0, own_in)
-        fetch(1, other_in)
+        sources = (own_in, other_in)
+        for side in (0, 1):
+            fetch(lists, counts, side, 3, sources[side], ready, side * stored, sems.at[side])
         for b in range(low):
             icar_next[b] = decay[b : b + 1, :] * icar_low[b] + inflow[b : b + 1, :] * low_rows[b]
         lower = pl.ds(0, low)
         icar_copy = pltpu.make_async_copy(icar_next, icar_out.at[lower], sems.at[2])
         icar_copy.start()
         lam_next[...] = acc[...]
-        for side, source in enumerate((own_in, other_in)):
-            fetched_all(side, source)
-
-            def some(i, carry, side=side):
-                start = i * MANY
-                words = []
-                for u in range(MANY):
-                    at = jnp.minimum(start + u, counts[side][3] - 1)
-                    words.append((lists[side][3 * STRIDE + start + u], side * stored + at))
-                prods = [
-                    jnp.dot(lo[(c >> 8) & 255], fetched[at], preferred_element_type=F32)
-                    for c, at in words
-                ]
-                for (c, _), prod in zip(words, prods):
-                    lam_next[(c >> 16) & 255] += prod
-                return carry
-
-            lax.fori_loop(0, (counts[side][3] + MANY - 1) // MANY, some, 0)
+        for side in (0, 1):
+            fetched(counts, side, 3, sources[side], ready, sems.at[side])
+            run_fetched(lists, counts, side, 3, lo, ready, side * stored, lam_next, MANY)
         upper = pl.ds(low, blocks - low)
         lam_copy = pltpu.make_async_copy(lam_next.at[upper], lam_out.at[upper], sems.at[3])
         lam_copy.start()
@@ -495,11 +554,12 @@
         (array(state, F32), low_type, array(state, F32)),
         listed
         + [(low_rows, VM), (lo, VM), (acc, VM), (icar_low, VM), (decay, VM), (inflow, VM)]
-        + [(derivative_tiles, HB), (other_kept, HB), (icar, HB)],
+        + stored_in
+        + [(icar, HB)],
         scratch=[
             pltpu.VMEM(state, F32),
             pltpu.VMEM(half, F32),
-            pltpu.VMEM((2 * stored, nodes, nodes), BF16),
+            pltpu.VMEM(fetched_shape, BF16),
             pltpu.SemaphoreType.DMA((4,)),
         ],
         out_specs=(HB, VM, HB),
@@ -515,25 +575,31 @@
             copy.start()
         dims = (((0,), (0,)), ((), ()))
         if slots % 16 == 0:
-            parts = received[...].reshape(network, 2, slots, nodes)
-            part_a = parts[:, 0].reshape(network * slots, nodes)
-            part_b = parts[:, 1].reshape(network * slots, nodes)
+            parts = received[...].reshape(network, 3, slots, nodes)
+            part = [parts[:, i].reshape(network * slots, nodes) for i in range(3)]
             column = lax.broadcasted_iota(jnp.int32, (network * slots, buses), 1)
-            label = part_b[:, cases : cases + 1].astype(F32).astype(jnp.int32) - 1
-            hot = jnp.where(label == column, 1.0, 0.0).astype(BF16)
-            first = lax.dot_general(part_a, hot, dims, preferred_element_type=F32)
-            last = lax.dot_general(part_b, hot, dims, preferred_element_type=F32)
+
+            def hot_of(rows):
+                label = rows[:, cases : cases + 1].astype(F32).astype(jnp.int32) - 1
+                return jnp.where(label == column, 1.0, 0.0).astype(BF16)
+
+            hot = hot_of(part[1])
+            first = lax.dot_general(part[0], hot, dims, preferred_element_type=F32)
+            last = lax.dot_general(part[1], hot, dims, preferred_element_type=F32)
+            last += lax.dot_general(part[2], hot_of(part[2]), dims, preferred_element_type=F32)
         else:
             got = received[...].astype(F32)
             row = lax.broadcasted_iota(jnp.int32, (rows_sent, buses), 0)
-            second = lax.rem(row, 2 * slots) >= slots
+            place = lax.rem(row, 3 * slots)
             column = lax.broadcasted_iota(jnp.int32, (rows_sent, buses), 1)
             label = got[:, cases : cases + 1].astype(jnp.int32) - 1
-            hot_b = jnp.where(jnp.logical_and(label == column, second), 1.0, 0.0)
-            hot_a = pltpu.roll(hot_b, rows_sent - slots, 0).astype(BF16)
-            hot_b = hot_b.astype(BF16)
+            hot = jnp.where(jnp.logical_and(label == column, place >= slots), 1.0, 0.0)
+            own_hot = jnp.where(place < 2 * slots, hot, 0.0)
+            hot_a = pltpu.roll(own_hot, rows_sent - slots, 0).astype(BF16)
             first = lax.dot_general(received[...], hot_a, dims, preferred_element_type=F32)
-            last = lax.dot_general(received[...], hot_b, dims, preferred_element_type=F32)
+            last = lax.dot_general(
+                received[...], hot.astype(BF16), dims, preferred_element_type=F32
+            )
         for copy in copies:
             copy.wait()
         value = trans[...]

time: 53.1 us -> 56.7 us (1.068)
  waiting for transfers between devices: 10.4 us -> 3.73 us
  starting transfers between devices: 11.4 us -> 17.5 us
  Pallas kernels: 29.5 us -> 32 us
  local copies, waits for them, and re-layouts: 0.02 us -> 1.65 us
    ppermute x3, waiting for transfers between devices: 5.93 us -> 1.35 us  [local(): arriving = lax.ppermute(leaving, 'blk', onward)]
    all_to_all x1, waiting for transfers between devices: 3.83 us -> 0.01 us  [local(): lax.all_to_all(sent.reshape(network, 3 * slots, nodes), ('sec', 'blk'), s...]
    ppermute x0 -> x1, starting transfers between devices: none -> 3.57 us  [local(): theirs = lax.ppermute(mine, 'blk', backward)]
    pallas_call x10 -> x11, Pallas kernels: 29.5 us -> 32 us  [kernel(): pl.pallas_call(body, out_shape=outs, in_specs=[spec for _, spec in ins],...]
    ppermute x3, starting transfers between devices: 3.93 us -> 5.7 us  [local(): arriving = lax.ppermute(leaving, 'blk', onward)]
    ppermute x0 -> x1, waiting for transfers between devices: none -> 1.73 us  [local(): theirs = lax.ppermute(mine, 'blk', backward)]
    unnamed x8, local copies, waits for them, and re-layouts: 0.02 us -> 1.65 us
    all_to_all x1, starting transfers between devices: 6.86 us -> 7.61 us  [local(): lax.all_to_all(sent.reshape(network, 3 * slots, nodes), ('sec', 'blk'), s...]
  transfers between devices with their start and end apart: 6 -> 7, of which waited for: 4 -> 4; matrix products, arithmetic and copies ran while one was open for 1% -> 1% of each run, Pallas kernels for 44% -> 51%
where the time goes in v4:
time: 56.7 us; the launch traced here: 56.3 us
  Pallas kernels  32 us (56%)
  starting transfers between devices  17.5 us (31%)
  waiting for transfers between devices  3.73 us (7%)
  local copies, waits for them, and re-layouts  1.65 us (3%)
  between operations  0.77 us (1%)
  other arithmetic  0.69 us (1%)
    pallas_call x11, Pallas kernels, kernel(): pl.pallas_call(body, out_shape=outs, in_specs=[spec for _, spec in ins],...  32 us
    all_to_all x1, starting transfers between devices, local(): lax.all_to_all(sent.reshape(network, 3 * slots, nodes), ('sec', 'blk'), s...  7.61 us
    ppermute x3, starting transfers between devices, local(): arriving = lax.ppermute(leaving, 'blk', onward)  5.7 us
    ppermute x1, starting transfers between devices, local(): theirs = lax.ppermute(mine, 'blk', backward)  3.57 us
    ppermute x1, waiting for transfers between devices, local(): theirs = lax.ppermute(mine, 'blk', backward)  1.73 us
    unnamed x8, local copies, waits for them, and re-layouts  1.65 us
    ppermute x3, waiting for transfers between devices, local(): arriving = lax.ppermute(leaving, 'blk', onward)  1.35 us
  transfers between devices with their start and end apart: 7, of which 4 were waited for; matrix products, arithmetic and copies ran while one was open for 1% of the time, Pallas kernels for 51%

profile of v4, /device:TPU:0, one launch (start us, length us, event | category | flops | bytes accessed | tf_op | source)
XLA Modules:
  0.0 56.3 jit_solution(8994958612993081693)
XLA Ops:
  0.6 0.6 collective-permute-start.1
  1.2 0.7 %shift-left_or_fusion.codes = s32[96]{0:T(128)S(1)} fusion(s32[96]{0:T(128)} %param.18, s32[96]{0:T(128)} %param.17), kind=kLoop, calls=%fused_computation.16 | loop fusion | flops 1824 | bytes 1152 | tf_op jit(solution)/shard_map/or | solution.py:93
  1.9 0.0 collective-permute-start
  1.9 4.1 %shard_map.148 = (f32[48,64,128]{2,1,0:T(8,128)S(1)}, bf16[17,64,128]{2,1,0:T(8,128)(2,1)S(1)}, bf16[17,64,128]{2,1,0:T(8,128)(2,1)S(1)}, bf16[96,128,128]{2,1,0...) custom-call(s32[96]{0:T(128)S(1)} %shift-left_or_fusion.codes, f32[32,64,128]{2,1,0:T(8,128)} %refs_6_.2, ...), custom_call_target="tpu_custom_call" | custom-call | tf_op jit(solution)/shard_map/pallas_call | solution.py:25
  6.0 0.0 copy-start.3
  6.0 0.6 %collective-permute-done.codes = s32[96]{0:T(128)S(1)} collective-permute-done((s32[96]{0:T(128)S(1)}, s32[96]{0:T(128)S(1)}, u32[]{:S(2)}, u32[]{:S(2)}) %collective-permute-start) | collective-permute-done | bytes 416 | tf_op jit(solution)/shard_map/ppermute | solution.py:99
  6.7 2.1 %shard_map.149 = (s32[512]{0:T(512)S(1)}, s32[4]{0:T(128)S(1)}) custom-call(s32[96]{0:T(128)S(1)} %collective-permute-done.codes), custom_call_target="tpu_custom_call" | custom-call | tf_op jit(solution)/shard_map/pallas_call | solution.py:25
  8.8 0.0 collective-permute-done.1.refs_3_.refs_4_.refs_11_
  8.8 1.3 %shard_map.150 = bf16[16,64,128]{2,1,0:T(8,128)(2,1)S(1)} custom-call(s32[512]{0:T(512)S(1)} %get-tuple-element.40.own_list, s32[4]{0:T(128)S(1)} %get-tuple-element.41.own_count, s32[512]{0:T(512)S(1)} %get-tuple-element.42.other_list, s32[4]{0:T(128)S(1)} %get-tuple-element.43.other_count, f32[48,64,128]{2,1,0:T(8,128)S(1)} %get-tuple-element.44.refs_0_, ...), custom_call_target="tpu_custom_call" | custom-call | tf_op jit(solution)/shard_map/pallas_call | solution.py:25
  10.1 3.6 %collective-permute-start.2 = (bf16[16,64,128]{2,1,0:T(8,128)(2,1)S(1)}, bf16[16,64,128]{2,1,0:T(8,128)(2,1)S(1)}, u32[]{:S(2)}, u32[]{:S(2)}) collective-permute-start(bf16[16,64,128]{2,1,0:T(8,128)(2,1)S(1)} %shard_map.150), channel_id=1, source_target_pairs={{0,2},{2,4},{4,6},{6,0},{1,3},{3,5},{5,7},{7,1},{8,10},{10,12},{12... | collective-permute-start | bytes 786440 | tf_op jit(solution)/shard_map/ppermute | solution.py:234
  13.7 0.0 copy-done.3
  13.7 5.6 %shard_map.151 = (f32[32,64,128]{2,1,0:T(8,128)S(1)}, f32[32,64,128]{2,1,0:T(8,128)S(1)}, f32[16,64,128]{2,1,0:T(8,128)S(1)}, bf16[17,64,128]{2,1,0:T(8,128)(2,1...) custom-call(s32[512]{0:T(512)S(1)} %get-tuple-element.40.own_list, ...), custom_call_target="tpu_custom_call" | custom-call | tf_op jit(solution)/shard_map/pallas_call | solution.py:25
  19.3 0.0 copy-start
  19.3 1.6 %copy-done = bf16[96,128,128]{2,1,0:T(8,128)(2,1)} copy-done((bf16[96,128,128]{2,1,0:T(8,128)(2,1)}, bf16[96,128,128]{2,1,0:T(8,128)(2,1)S(1)}, u32[]{:S(2)}) %copy-start) | copy-done | bytes 3145752
  20.9 0.8 %collective-permute-done.2.refs_0_ = bf16[16,64,128]{2,1,0:T(8,128)(2,1)S(1)} collective-permute-done((bf16[16,64,128]{2,1,0:T(8,128)(2,1)S(1)}, bf16[16,64,128]{2,1,0:T(8,128)(2,1)S(1)}, u32[]{:S(2)}, u32[]{:S(2)}) %collective-permute-start.2) | collective-permute-done | bytes 262176 | tf_op jit(solution)/shard_map/ppermute | solution.py:234
  21.7 0.0 copy-start.1
  21.7 0.0 copy-start.2
  21.7 1.3 %shard_map.152 = (bf16[16,64,128]{2,1,0:T(8,128)(2,1)S(1)}, f32[16,64,128]{2,1,0:T(8,128)S(1)}, bf16[17,64,128]{2,1,0:T(8,128)(2,1)S(1)}) custom-call(s32[512]{0:T(512)S(1)} %get-tuple-element.40.own_list, s32[4]{0:T(128)S(1)} %get-tuple-element.41.own_count, s32[512]{0:T(512)S(1)} %get-tuple-element.42.other_list, s32[4]{0:T(128)S(1)} %get-tuple-element.43.other_count, ...), custom_call_target="tpu_custom_call" | custom-call | tf_op jit(solution)/shard_map/pallas_call | solution.py:25
  23.0 0.4 collective-permute-start.3
  23.4 0.0 copy-done.1
  23.4 0.0 copy-done.2
  23.4 3.6 %collective-permute-start.4 = (s32[384]{0:T(512)S(1)}, s32[384]{0:T(512)S(1)}, u32[]{:S(2)}, u32[]{:S(2)}) collective-permute-start(s32[384]{0:T(512)S(1)} %pad_add_fusion), channel_id=1, source_target_pairs={{2,0},{4,2},{6,4},{0,6},{3,1},{5,3},{7,5},{1,7},{10,8},{12,10},{14... | collective-permute-start | bytes 4616 | tf_op jit(solution)/shard_map/ppermute | solution.py:239
  27.0 1.7 %collective-permute-done.4 = s32[384]{0:T(512)S(1)} collective-permute-done((s32[384]{0:T(512)S(1)}, s32[384]{0:T(512)S(1)}, u32[]{:S(2)}, u32[]{:S(2)}) %collective-permute-start.4) | collective-permute-done | bytes 1568 | tf_op jit(solution)/shard_map/ppermute | solution.py:239
  28.7 4.7 %shard_map.153 = (f32[16,64,128]{2,1,0:T(8,128)S(1)}, f32[32,64,128]{2,1,0:T(8,128)S(1)}, bf16[17,64,128]{2,1,0:T(8,128)(2,1)S(1)}, f32[16,64,128]{2,1,0:T(8,128...) custom-call(s32[512]{0:T(512)S(1)} %get-tuple-element.40.own_list, s32[4]{0:T(128)S(1)} %get-tuple-element.41.own_count, ...), custom_call_target="tpu_custom_call" | custom-call | tf_op jit(solution)/shard_map/pallas_call | solution.py:25
  33.4 7.6 %all-to-all-start = ((bf16[16,48,128]{2,1,0:T(8,128)(2,1)}), bf16[16,48,128]{2,1,0:T(8,128)(2,1)S(1)}, u32[]{:S(2)}, u32[]{:S(2)}) async-start(bf16[16,48,128]{2,1,0:T(8,128)(2,1)} %bitcast.4), calls=%async_computation | async-start | bytes 393216 | tf_op jit(solution)/shard_map/all_to_all | solution.py:503
  41.0 4.6 %shard_map.154 = (f32[32,64,128]{2,1,0:T(8,128)S(1)}, f32[16,64,128]{2,1,0:T(8,128)S(1)}, bf16[192,128,128]{2,1,0:T(8,128)(2,1)S(1)}) custom-call(s32[512]{0:T(512)S(1)} %get-tuple-element.40.own_list, s32[4]{0:T(128)S(1)} %get-tuple-element.41.own_count, s32[512]{0:T(512)S(1)} %get-tuple-element.42.other_list, s32[4]{0:T(128)S(1)} %get-tuple-element.43.other_count, ...), custom_call_target="tpu_custom_call" | custom-call | tf_op jit(solution)/shard_map/pallas_call | solution.py:25
  45.7 0.0 collective-permute-done.3.refs_0_
  45.7 1.5 %shard_map.155 = (bf16[16,64,128]{2,1,0:T(8,128)(2,1)S(1)}, f32[16,64,128]{2,1,0:T(8,128)S(1)}, bf16[17,64,128]{2,1,0:T(8,128)(2,1)S(1)}) custom-call(s32[512]{0:T(512)S(1)} %get-tuple-element.40.own_list, s32[4]{0:T(128)S(1)} %get-tuple-element.41.own_count, s32[512]{0:T(512)S(1)} %get-tuple-element.42.other_list, s32[4]{0:T(128)S(1)} %get-tuple-element.43.other_count, ...), custom_call_target="tpu_custom_call" | custom-call | tf_op jit(solution)/shard_map/pallas_call | solution.py:25
  47.2 1.8 %collective-permute-start.5 = (bf16[16,64,128]{2,1,0:T(8,128)(2,1)S(1)}, bf16[16,64,128]{2,1,0:T(8,128)(2,1)S(1)}, u32[]{:S(2)}, u32[]{:S(2)}) collective-permute-start(bf16[16,64,128]{2,1,0:T(8,128)(2,1)S(1)} %get-tuple-element.67), channel_id=1, source_target_pairs={{0,2},{2,4},{4,6},{6,0},{1,3},{3,5},{5,7},{7,1},{8,10},{10,12},{12... | collective-permute-start | bytes 786440 | tf_op jit(solution)/shard_map/ppermute | solution.py:526
  48.9 3.8 %shard_map.156 = (f32[32,64,128]{2,1,0:T(8,128)}, f32[16,64,128]{2,1,0:T(8,128)S(1)}, f32[32,64,128]{2,1,0:T(8,128)}) custom-call(s32[512]{0:T(512)S(1)} %get-tuple-element.40.own_list, s32[4]{0:T(128)S(1)} %get-tuple-element.41.own_count, s32[512]{0:T(512)S(1)} %get-tuple-element.42.other_list, ...), custom_call_target="tpu_custom_call", output_to_operand_aliasing={{2}: (12, {})} | custom-call | tf_op jit(solution)/shard_map/pallas_call | solution.py:25
  52.7 0.0 all-to-all-done
  52.7 2.1 %shard_map.158 = f32[64,256]{1,0:T(8,128)} custom-call(bf16[768,128]{1,0:T(8,128)(2,1)S(1)} %bitcast.6, f32[64,256]{1,0:T(8,128)} %trans_in.1, bf16[256,256]{1,0:T(8,128)(2,1)} %matrix_in.1), custom_call_target="tpu_custom_call" | custom-call | tf_op jit(solution)/shard_map/pallas_call | solution.py:25
  54.8 0.6 %collective-permute-done.5.arrived = bf16[16,64,128]{2,1,0:T(8,128)(2,1)S(1)} collective-permute-done((bf16[16,64,128]{2,1,0:T(8,128)(2,1)S(1)}, bf16[16,64,128]{2,1,0:T(8,128)(2,1)S(1)}, u32[]{:S(2)}, u32[]{:S(2)}) %collective-permute-start.5) | collective-permute-done | bytes 262176 | tf_op jit(solution)/shard_map/ppermute | solution.py:526
  55.4 0.8 %shard_map.157 = f32[32,64,128]{2,1,0:T(8,128)} custom-call(bf16[16,64,128]{2,1,0:T(8,128)(2,1)S(1)} %collective-permute-done.5.arrived, f32[16,64,128]{2,1,0:T(8,128)S(1)} %get-tuple-element.73.low_next, f32[32,64,128]{2,1,0:T(8,128)} %get-tuple-element.74.lam_in), custom_call_target="tpu_custom_call", output_to_operand_aliasing={{}: (2, {})} | custom-call | tf_op jit(solution)/shard_map/pallas_call | solution.py:25
  (2 shorter events, 0.0 us)
Async XLA Ops:
  0.6 8.1 %collective-permute-start.1 = (bf16[96,128,128]{2,1,0:T(8,128)(2,1)}, bf16[96,128,128]{2,1,0:T(8,128)(2,1)S(1)}, u32[]{:S(2)}, u32[]{:S(2)}) collective-permute-start(bf16[96,128,128]{2,1,0:T(8,128)(2,1)} %refs_6_.3), channel_id=1, source_target_pairs={{0,1},{1,0},{2,3},{3,2},{4,5},{5,4},{6,7},{7,6},{8,9},{9,8},{10,11... | collective-permute-start | bytes 9437192 | tf_op jit(solution)/shard_map/ppermute | solution.py:100
  1.9 4.8 %collective-permute-start = (s32[96]{0:T(128)S(1)}, s32[96]{0:T(128)S(1)}, u32[]{:S(2)}, u32[]{:S(2)}) collective-permute-start(s32[96]{0:T(128)S(1)} %shift-left_or_fusion.codes), channel_id=1, source_target_pairs={{0,1},{1,0},{2,3},{3,2},{4,5},{5,4},{6,7},{7,6},{8,9},{9,8},{10,11... | collective-permute-start | bytes 1160 | tf_op jit(solution)/shard_map/ppermute | solution.py:99
  6.0 7.6 %copy-start.3 = (s32[128]{0:T(128)S(1)}, s32[128]{0:T(128)}, u32[]{:S(2)}) copy-start(s32[128]{0:T(128)} %param.22) | copy-start | bytes 1540
  10.1 11.6 %collective-permute-start.2 = (bf16[16,64,128]{2,1,0:T(8,128)(2,1)S(1)}, bf16[16,64,128]{2,1,0:T(8,128)(2,1)S(1)}, u32[]{:S(2)}, u32[]{:S(2)}) collective-permute-start(bf16[16,64,128]{2,1,0:T(8,128)(2,1)S(1)} %shard_map.150), channel_id=1, source_target_pairs={{0,2},{2,4},{4,6},{6,0},{1,3},{3,5},{5,7},{7,1},{8,10},{10,12},{12... | collective-permute-start | bytes 786440 | tf_op jit(solution)/shard_map/ppermute | solution.py:234
  19.3 1.6 %copy-start = (bf16[96,128,128]{2,1,0:T(8,128)(2,1)}, bf16[96,128,128]{2,1,0:T(8,128)(2,1)S(1)}, u32[]{:S(2)}) copy-start(bf16[96,128,128]{2,1,0:T(8,128)(2,1)S(1)} %get-tuple-element.64.refs_3_.refs_7_) | copy-start | bytes 9437188
  21.7 1.7 %copy-start.1 = (s32[128,1]{0,1:T(1,128)S(1)}, s32[128,1]{0,1:T(1,128)}, u32[]{:S(2)}) copy-start(s32[128,1]{0,1:T(1,128)} %param.23) | copy-start | bytes 1540
  21.7 1.7 %copy-start.2 = (s32[128]{0:T(128)S(1)}, s32[128]{0:T(128)}, u32[]{:S(2)}) copy-start(s32[128]{0:T(128)} %param.24) | copy-start | bytes 1540
  23.0 22.7 %collective-permute-start.3 = (bf16[16,64,128]{2,1,0:T(8,128)(2,1)S(1)}, bf16[16,64,128]{2,1,0:T(8,128)(2,1)S(1)}, u32[]{:S(2)}, u32[]{:S(2)}) collective-permute-start(bf16[16,64,128]{2,1,0:T(8,128)(2,1)S(1)} %get-tuple-element.50.refs_3_), channel_id=1, source_target_pairs={{0,2},{2,4},{4,6},{6,0},{1,3},{3,5},{5,7},{7,1},{8,10},{10,12},{12... | collective-permute-start | bytes 786440 | tf_op jit(solution)/shard_map/ppermute | solution.py:474
  23.4 5.3 %collective-permute-start.4 = (s32[384]{0:T(512)S(1)}, s32[384]{0:T(512)S(1)}, u32[]{:S(2)}, u32[]{:S(2)}) collective-permute-start(s32[384]{0:T(512)S(1)} %pad_add_fusion), channel_id=1, source_target_pairs={{2,0},{4,2},{6,4},{0,6},{3,1},{5,3},{7,5},{1,7},{10,8},{12,10},{14... | collective-permute-start | bytes 4616 | tf_op jit(solution)/shard_map/ppermute | solution.py:239
  33.4 19.3 %all-to-all-start = ((bf16[16,48,128]{2,1,0:T(8,128)(2,1)}), bf16[16,48,128]{2,1,0:T(8,128)(2,1)S(1)}, u32[]{:S(2)}, u32[]{:S(2)}) async-start(bf16[16,48,128]{2,1,0:T(8,128)(2,1)} %bitcast.4), calls=%async_computation | async-start | bytes 393216 | tf_op jit(solution)/shard_map/all_to_all | solution.py:503
  47.2 8.3 %collective-permute-start.5 = (bf16[16,64,128]{2,1,0:T(8,128)(2,1)S(1)}, bf16[16,64,128]{2,1,0:T(8,128)(2,1)S(1)}, u32[]{:S(2)}, u32[]{:S(2)}) collective-permute-start(bf16[16,64,128]{2,1,0:T(8,128)(2,1)S(1)} %get-tuple-element.67), channel_id=1, source_target_pairs={{0,2},{2,4},{4,6},{6,0},{1,3},{3,5},{5,7},{7,1},{8,10},{10,12},{12... | collective-permute-start | bytes 786440 | tf_op jit(solution)/shard_map/ppermute | solution.py:526

commit v5 on v4

--- a/solution.py
+++ b/solution.py
@@ -46,6 +46,10 @@
 
 def array(shape, dtype):
     return jax.ShapeDtypeStruct(shape, dtype)
+
+
+def hbm_array(shape, dtype):
+    return pltpu.HBM(shape, dtype)
 
 
 def local(
@@ -234,7 +238,12 @@
     arriving = lax.ppermute(leaving, "blk", onward)
 
     mine = jnp.concatenate(
-        [distribution_entry_vertex, distribution_entry_holder[:, 0], distribution_entry_substation]
+        [
+            distribution_entry_vertex.reshape(1, heads),
+            distribution_entry_holder.reshape(1, heads),
+            distribution_entry_substation.reshape(1, heads),
+        ],
+        axis=1,
     )
     theirs = lax.ppermute(mine, "blk", backward)
 
@@ -304,7 +313,7 @@
             factor,
             factor,
             factor,
-            array(other.shape, BF16),
+            hbm_array(other.shape, BF16),
         ),
         listed
         + [(acc, VM), (lo, VM), (hi, VM), (own, VM), (other, VM)]
@@ -332,11 +341,17 @@
         take_arrived(arrived, lam, low_rows, lo)
         rim_sums(lists, counts, acc_rim, lo, own, other, out, sums)
 
-    def rim_last_body(lists, counts, arrived, lam, acc_rim, kept, out, low_rows, lo, sums):
+    def rim_last_body(
+        lists, counts, arrived, lam, acc_rim, own_in, other_in, out, low_rows, lo, sums, ready, sems
+    ):
+        sources = (own_in, other_in)
+        for side in (0, 1):
+            fetch(lists, counts, side, 1, sources[side], ready, side * stored, sems.at[side])
         take_arrived(arrived, lam, low_rows, lo)
         sums[...] = acc_rim[...]
         for side in (0, 1):
-            run_fetched(lists, counts, side, 1, lo, kept, side * stored, sums, FEW)
+            fetched(counts, side, 1, sources[side], ready, sems.at[side])
+            run_fetched(lists, counts, side, 1, lo, ready, side * stored, sums, FEW)
         out[...] = sums[...].astype(BF16)
 
     def rows_of(owner):
@@ -349,26 +364,23 @@
 
     def main_body(
         lists, counts, owner, bus, theirs, left,
-        low_rows, lam, lo, hi, acc, icar, own, other, hot, head0, decay, inflow, outflow,
-        lam_low, acc_next, hi_next, icar_low, sent, icar_out, lam_next, icar_next, lo_base, sem,
+        low_rows, lam, lo, hi, acc, icar, own, other, hot, head0, decay, inflow,
+        lam_next, acc_rim, hi_next, sent, icar_out, icar_next, lo_base, sem,
     ):
         for b in range(blocks):
             row = low_rows[b] if b < low else lam[b]
             icar_next[b] = decay[b : b + 1, :] * icar[b] + inflow[b : b + 1, :] * row
-            acc_next[b] = outflow[b : b + 1, :] * icar_next[b]
+        copy = pltpu.make_async_copy(icar_next, icar_out, sem)
+        copy.start()
         lam_next[...] = acc[...]
         run(lists, counts, [((0, 3), lo, own, lam_next), ((1, 3), lo, other, lam_next)], MANY)
         for b in range(low):
-            lam_low[b] = lam_next[b]
             lo_base[b] = lam_next[b].astype(BF16)
-            icar_low[b] = icar_next[b]
         for b in range(low, blocks):
             hi_next[b - low] = lam_next[b].astype(BF16)
-            icar_next[b] = decay[b : b + 1, :] * icar_next[b] + inflow[b : b + 1, :] * lam_next[b]
         hi_next[blocks - low] = jnp.zeros((cases, nodes), BF16)
-        upper = pl.ds(low, blocks - low)
-        copy = pltpu.make_async_copy(icar_next.at[upper], icar_out.at[upper], sem)
-        copy.start()
+        acc_rim[...] = jnp.zeros(acc_rim.shape, F32)
+        run(lists, counts, [((0, 0), hi_next, own, acc_rim), ((1, 0), hi_next, other, acc_rim)], FEW)
         node = lax.broadcasted_iota(jnp.int32, (nodes, heads), 0)
         vertex_next, owner_next, bus_next = (theirs[:, i * heads : (i + 1) * heads] for i in range(3))
         head_next = jnp.zeros((cases, heads), F32)
@@ -436,29 +448,6 @@
 
         lax.fori_loop(0, (counts[side][kind] + width - 1) // width, some, 0)
 
-    def begin_last_body(
-        lists, counts, begun, hi, own_in, other_in, acc, acc_rim, kept, ready, sems
-    ):
-        sources = (own_in, other_in)
-        for side in (0, 1):
-            first = side * stored
-            fetch(lists, counts, side, 0, sources[side], ready, first, sems.at[side, 0])
-            fetch(
-                lists, counts, side, 2, sources[side], ready, first + counts[side][0], sems.at[side, 2]
-            )
-        for side in (0, 1):
-            fetch(lists, counts, side, 1, sources[side], kept, side * stored, sems.at[side, 1])
-        acc[...] = begun[...]
-        acc_rim[...] = jnp.zeros(acc_rim.shape, F32)
-        for side in (0, 1):
-            first = side * stored
-            fetched(counts, side, 0, sources[side], ready, sems.at[side, 0])
-            run_fetched(lists, counts, side, 0, hi, ready, first, acc_rim, FEW)
-            fetched(counts, side, 2, sources[side], ready, sems.at[side, 2])
-            run_fetched(lists, counts, side, 2, hi, ready, first + counts[side][0], acc, MANY)
-        for side in (0, 1):
-            fetched(counts, side, 1, sources[side], kept, sems.at[side, 1])
-
     tiles = [(own, VM), (other, VM)]
     rim_type = array((rim, cases, nodes), BF16)
     low_type = array(half, F32)
@@ -472,33 +461,31 @@
         scratch=[sums],
     )
     arriving = lax.ppermute(leaving, "blk", onward)
-    lam, acc, hi_next, icar_low, sent, icar = kernel(
+    lam, acc_rim, hi_next, sent, icar = kernel(
         with_lists(main_body),
         (
-            low_type,
             array(state, F32),
+            array((rim, cases, nodes), F32),
             array(padded, BF16),
-            low_type,
             array((rows_sent, nodes), BF16),
-            array(state, F32),
+            hbm_array(state, F32),
         ),
         listed
         + [
             (distribution_entry_holder.reshape(1, heads), VM),
             (distribution_entry_substation.reshape(1, heads), VM),
-            (theirs.reshape(1, 3 * heads), VM),
+            (theirs, VM),
             (leaving, VM),
         ]
         + [(low_rows, VM), (lam, VM), (lo, VM), (hi, VM), (acc, VM), (icar, VM)]
         + tiles
-        + [(hot, VM), (head0, VM), (decay, VM), (inflow, VM), (outflow, VM)],
+        + [(hot, VM), (head0, VM), (decay, VM), (inflow, VM)],
         scratch=[
-            pltpu.VMEM(state, F32),
             pltpu.VMEM(state, F32),
             pltpu.VMEM(half, BF16),
             pltpu.SemaphoreType.DMA,
         ],
-        out_specs=(VM,) * 5 + (HB,),
+        out_specs=(VM,) * 4 + (HB,),
     )
     received = lax.all_to_all(
         sent.reshape(network, 3 * slots, nodes),
@@ -510,40 +497,39 @@
     received = received.reshape(rows_sent, nodes)
     stored_in = [(derivative_tiles, HB), (other_kept, HB)]
     fetched_shape = (2 * stored, nodes, nodes)
-    acc, acc_rim, kept = kernel(
-        with_lists(begin_last_body),
-        (array(state, F32), array((rim, cases, nodes), F32), array(fetched_shape, BF16)),
-        listed + [(acc, VM), (hi_next, VM)] + stored_in,
-        scratch=[pltpu.VMEM(fetched_shape, BF16), pltpu.SemaphoreType.DMA((2, 3))],
-    )
-
     leaving, low_rows, lo = kernel(
         with_lists(rim_last_body),
         (rim_type, low_type, array(padded, BF16)),
-        listed + [(arriving, VM), (lam, VM), (acc_rim, VM), (kept, VM)],
-        scratch=[sums],
+        listed + [(arriving, VM), (lam, VM), (acc_rim, VM)] + stored_in,
+        scratch=[sums, pltpu.VMEM(fetched_shape, BF16), pltpu.SemaphoreType.DMA((2,))],
     )
     arriving = lax.ppermute(leaving, "blk", onward)
 
     def main_last_body(
-        lists, counts, low_rows, lo, acc, icar_low, decay, inflow, own_in, other_in, icar_in,
-        lam_out, low_next, icar_out, lam_next, icar_next, ready, sems,
+        lists, counts, low_rows, lam, lo, hi, decay, inflow, outflow, own_in, other_in, icar_in,
+        lam_out, low_next, icar_out, lam_next, icar, own, other, sems,
     ):
-        del icar_in
-        sources = (own_in, other_in)
-        for side in (0, 1):
-            fetch(lists, counts, side, 3, sources[side], ready, side * stored, sems.at[side])
-        for b in range(low):
-            icar_next[b] = decay[b : b + 1, :] * icar_low[b] + inflow[b : b + 1, :] * low_rows[b]
-        lower = pl.ds(0, low)
-        icar_copy = pltpu.make_async_copy(icar_next, icar_out.at[lower], sems.at[2])
+        copies = [
+            pltpu.make_async_copy(icar_in, icar, sems.at[0]),
+            pltpu.make_async_copy(own_in, own, sems.at[1]),
+            pltpu.make_async_copy(other_in, other, sems.at[2]),
+        ]
+        for copy in copies:
+            copy.start()
+        copies[0].wait()
+        for b in range(blocks):
+            row = low_rows[b] if b < low else lam[b]
+            before = icar[b]
+            lam_next[b] = outflow[b : b + 1, :] * before
+            icar[b] = decay[b : b + 1, :] * before + inflow[b : b + 1, :] * row
+        icar_copy = pltpu.make_async_copy(icar, icar_out, sems.at[0])
         icar_copy.start()
-        lam_next[...] = acc[...]
-        for side in (0, 1):
-            fetched(counts, side, 3, sources[side], ready, sems.at[side])
-            run_fetched(lists, counts, side, 3, lo, ready, side * stored, lam_next, MANY)
+        copies[1].wait()
+        copies[2].wait()
+        run(lists, counts, [((0, 2), hi, own, lam_next), ((1, 2), hi, other, lam_next)], MANY)
+        run(lists, counts, [((0, 3), lo, own, lam_next), ((1, 3), lo, other, lam_next)], MANY)
         upper = pl.ds(low, blocks - low)
-        lam_copy = pltpu.make_async_copy(lam_next.at[upper], lam_out.at[upper], sems.at[3])
+        lam_copy = pltpu.make_async_copy(lam_next.at[upper], lam_out.at[upper], sems.at[1])
         lam_copy.start()
         low_next[...] = lam_next[:low]
         icar_copy.wait()
@@ -551,19 +537,20 @@
 
     lam, low_next, icar = kernel(
         with_lists(main_last_body),
-        (array(state, F32), low_type, array(state, F32)),
+        (hbm_array(state, F32), low_type, hbm_array(state, F32)),
         listed
-        + [(low_rows, VM), (lo, VM), (acc, VM), (icar_low, VM), (decay, VM), (inflow, VM)]
+        + [(low_rows, VM), (lam, VM), (lo, VM), (hi_next, VM)]
+        + [(decay, VM), (inflow, VM), (outflow, VM)]
         + stored_in
         + [(icar, HB)],
         scratch=[
             pltpu.VMEM(state, F32),
-            pltpu.VMEM(half, F32),
-            pltpu.VMEM(fetched_shape, BF16),
-            pltpu.SemaphoreType.DMA((4,)),
+            pltpu.VMEM(state, F32),
+            pltpu.VMEM(own.shape, BF16),
+            pltpu.VMEM(own.shape, BF16),
+            pltpu.SemaphoreType.DMA((3,)),
         ],
         out_specs=(HB, VM, HB),
-        aliases={12: 2},
     )
 
     def trans_body(received, trans_in, matrix_in, out, trans, matrix, sems):

time: 56.7 us -> 56.4 us (level)
  local copies, waits for them, and re-layouts: 1.65 us -> 0.01 us
  Pallas kernels: 32 us -> 32.7 us
  starting transfers between devices: 17.5 us -> 18.1 us
    unnamed x8 -> x6, local copies, waits for them, and re-layouts: 1.65 us -> 0.01 us
    pallas_call x11 -> x10, Pallas kernels: 32 us -> 32.7 us  [kernel(): pl.pallas_call(body, out_shape=outs, in_specs=[spec for _, spec in ins],...]
    ppermute x3, starting transfers between devices: 5.7 us -> 6.32 us  [local(): arriving = lax.ppermute(leaving, 'blk', onward)]
  transfers between devices with their start and end apart: 7 -> 7, of which waited for: 4 -> 3; matrix products, arithmetic and copies ran while one was open for 1% -> 1% of each run, Pallas kernels for 51% -> 52%
where the time goes in v5:
time: 56.4 us; the launch traced here: 56.1 us
  Pallas kernels  32.7 us (58%)
  starting transfers between devices  18.1 us (32%)
  waiting for transfers between devices  3.83 us (7%)
  between operations  0.76 us (1%)
  other arithmetic  0.68 us (1%)
    pallas_call x10, Pallas kernels, kernel(): pl.pallas_call(body, out_shape=outs, in_specs=[spec for _, spec in ins],...  32.7 us
    all_to_all x1, starting transfers between devices, local(): lax.all_to_all(sent.reshape(network, 3 * slots, nodes), ('sec', 'blk'), s...  7.59 us
    ppermute x3, starting transfers between devices, local(): arriving = lax.ppermute(leaving, 'blk', onward)  6.32 us
    ppermute x1, starting transfers between devices, local(): theirs = lax.ppermute(mine, 'blk', backward)  3.58 us
    ppermute x1, waiting for transfers between devices, local(): theirs = lax.ppermute(mine, 'blk', backward)  1.72 us
    ppermute x3, waiting for transfers between devices, local(): arriving = lax.ppermute(leaving, 'blk', onward)  1.48 us
  transfers between devices with their start and end apart: 7, of which 3 were waited for; matrix products, arithmetic and copies ran while one was open for 1% of the time, Pallas kernels for 52%

profile of v5, /device:TPU:0, one launch (start us, length us, event | category | flops | bytes accessed | tf_op | source)
XLA Modules:
  0.0 56.1 jit_solution(10713787933113864689)
XLA Ops:
  0.6 0.6 collective-permute-start.1
  1.2 0.7 %shift-left_or_fusion.codes = s32[96]{0:T(128)S(1)} fusion(s32[96]{0:T(128)} %param.18, s32[96]{0:T(128)} %param.17), kind=kLoop, calls=%fused_computation.16 | loop fusion | flops 1824 | bytes 1152 | tf_op jit(solution)/shard_map/or | solution.py:97
  1.9 0.0 collective-permute-start
  1.9 4.2 %shard_map.148 = (f32[48,64,128]{2,1,0:T(8,128)S(1)}, bf16[17,64,128]{2,1,0:T(8,128)(2,1)S(1)}, bf16[17,64,128]{2,1,0:T(8,128)(2,1)S(1)}, bf16[96,128,128]{2,1,0...) custom-call(s32[96]{0:T(128)S(1)} %shift-left_or_fusion.codes, f32[32,64,128]{2,1,0:T(8,128)} %refs_6_.1, ...), custom_call_target="tpu_custom_call" | custom-call | tf_op jit(solution)/shard_map/pallas_call | solution.py:25
  6.0 0.0 copy-start.2
  6.1 0.6 %collective-permute-done.codes = s32[96]{0:T(128)S(1)} collective-permute-done((s32[96]{0:T(128)S(1)}, s32[96]{0:T(128)S(1)}, u32[]{:S(2)}, u32[]{:S(2)}) %collective-permute-start) | collective-permute-done | bytes 416 | tf_op jit(solution)/shard_map/ppermute | solution.py:103
  6.7 2.1 %shard_map.149 = (s32[512]{0:T(512)S(1)}, s32[4]{0:T(128)S(1)}) custom-call(s32[96]{0:T(128)S(1)} %collective-permute-done.codes), custom_call_target="tpu_custom_call" | custom-call | tf_op jit(solution)/shard_map/pallas_call | solution.py:25
  8.8 0.0 collective-permute-done.1.refs_3_.refs_4_.refs_11_
  8.8 1.3 %shard_map.150 = bf16[16,64,128]{2,1,0:T(8,128)(2,1)S(1)} custom-call(s32[512]{0:T(512)S(1)} %get-tuple-element.36.own_list, s32[4]{0:T(128)S(1)} %get-tuple-element.37.own_count, s32[512]{0:T(512)S(1)} %get-tuple-element.38.other_list, s32[4]{0:T(128)S(1)} %get-tuple-element.39.other_count, f32[48,64,128]{2,1,0:T(8,128)S(1)} %get-tuple-element.40.refs_0_, ...), custom_call_target="tpu_custom_call" | custom-call | tf_op jit(solution)/shard_map/pallas_call | solution.py:25
  10.1 3.6 %collective-permute-start.2 = (bf16[16,64,128]{2,1,0:T(8,128)(2,1)S(1)}, bf16[16,64,128]{2,1,0:T(8,128)(2,1)S(1)}, u32[]{:S(2)}, u32[]{:S(2)}) collective-permute-start(bf16[16,64,128]{2,1,0:T(8,128)(2,1)S(1)} %shard_map.150), channel_id=1, source_target_pairs={{0,2},{2,4},{4,6},{6,0},{1,3},{3,5},{5,7},{7,1},{8,10},{10,12},{12... | collective-permute-start | bytes 786440 | tf_op jit(solution)/shard_map/ppermute | solution.py:238
  13.6 0.0 copy-done.2
  13.6 6.6 %shard_map.151 = (f32[32,64,128]{2,1,0:T(8,128)S(1)}, f32[32,64,128]{2,1,0:T(8,128)S(1)}, f32[16,64,128]{2,1,0:T(8,128)S(1)}, bf16[17,64,128]{2,1,0:T(8,128)(2,1...) custom-call(s32[512]{0:T(512)S(1)} %get-tuple-element.36.own_list, ...), custom_call_target="tpu_custom_call" | custom-call | tf_op jit(solution)/shard_map/pallas_call | solution.py:25
  20.2 1.5 %collective-permute-done.2.refs_0_ = bf16[16,64,128]{2,1,0:T(8,128)(2,1)S(1)} collective-permute-done((bf16[16,64,128]{2,1,0:T(8,128)(2,1)S(1)}, bf16[16,64,128]{2,1,0:T(8,128)(2,1)S(1)}, u32[]{:S(2)}, u32[]{:S(2)}) %collective-permute-start.2) | collective-permute-done | bytes 262176 | tf_op jit(solution)/shard_map/ppermute | solution.py:238
  21.7 0.0 copy-start
  21.7 0.0 copy-start.1
  21.7 1.3 %shard_map.152 = (bf16[16,64,128]{2,1,0:T(8,128)(2,1)S(1)}, f32[16,64,128]{2,1,0:T(8,128)S(1)}, bf16[17,64,128]{2,1,0:T(8,128)(2,1)S(1)}) custom-call(s32[512]{0:T(512)S(1)} %get-tuple-element.36.own_list, s32[4]{0:T(128)S(1)} %get-tuple-element.37.own_count, s32[512]{0:T(512)S(1)} %get-tuple-element.38.other_list, s32[4]{0:T(128)S(1)} %get-tuple-element.39.other_count, ...), custom_call_target="tpu_custom_call" | custom-call | tf_op jit(solution)/shard_map/pallas_call | solution.py:25
  23.0 0.3 collective-permute-start.3
  23.4 0.0 copy-done
  23.4 0.0 copy-done.1
  23.4 3.6 %collective-permute-start.4 = (s32[1,384]{1,0:T(1,128)S(1)}, s32[1,384]{1,0:T(1,128)S(1)}, u32[]{:S(2)}, u32[]{:S(2)}) collective-permute-start(s32[1,384]{1,0:T(1,128)S(1)} %pad_add_fusion), channel_id=1, source_target_pairs={{2,0},{4,2},{6,4},{0,6},{3,1},{5,3},{7,5},{1,7},{10,8},{12,10},{14... | collective-permute-start | bytes 4616 | tf_op jit(solution)/shard_map/ppermute | solution.py:248
  26.9 1.7 %collective-permute-done.4.refs_2_ = s32[1,384]{1,0:T(1,128)S(1)} collective-permute-done((s32[1,384]{1,0:T(1,128)S(1)}, s32[1,384]{1,0:T(1,128)S(1)}, u32[]{:S(2)}, u32[]{:S(2)}) %collective-permute-start.4) | collective-permute-done | bytes 1568 | tf_op jit(solution)/shard_map/ppermute | solution.py:248
  28.7 4.4 %shard_map.153 = (f32[32,64,128]{2,1,0:T(8,128)S(1)}, f32[16,64,128]{2,1,0:T(8,128)S(1)}, bf16[17,64,128]{2,1,0:T(8,128)(2,1)S(1)}, bf16[768,128]{1,0:T(8,128)(2,1)}, f32[32,64,128]{2,1,0:T(8,128)}) custom-call(s32[512]{0:T(512)S(1)} %get-tuple-element.36.own_list, s32[4]{0:T(128)S(1)} %get-tuple-element.37.own_count, s32[512]{0:T(512)S(1)} %get-tuple-element.38.other_list, ...), custom_call_target="tpu_custom_call" | custom-call | tf_op jit(solution)/shard_map/pallas_call | solution.py:25
  33.1 7.6 %all-to-all-start = ((bf16[16,48,128]{2,1,0:T(8,128)(2,1)}), bf16[16,48,128]{2,1,0:T(8,128)(2,1)S(1)}, u32[]{:S(2)}, u32[]{:S(2)}) async-start(bf16[16,48,128]{2,1,0:T(8,128)(2,1)} %bitcast.3), calls=%async_computation | async-start | bytes 393216 | tf_op jit(solution)/shard_map/all_to_all | solution.py:490
  40.7 0.0 collective-permute-done.3.refs_0_
  40.7 2.4 %shard_map.154 = (bf16[16,64,128]{2,1,0:T(8,128)(2,1)S(1)}, f32[16,64,128]{2,1,0:T(8,128)S(1)}, bf16[17,64,128]{2,1,0:T(8,128)(2,1)S(1)}) custom-call(s32[512]{0:T(512)S(1)} %get-tuple-element.36.own_list, s32[4]{0:T(128)S(1)} %get-tuple-element.37.own_count, s32[512]{0:T(512)S(1)} %get-tuple-element.38.other_list, s32[4]{0:T(128)S(1)} %get-tuple-element.39.other_count, ...), custom_call_target="tpu_custom_call" | custom-call | tf_op jit(solution)/shard_map/pallas_call | solution.py:25
  43.2 2.4 %collective-permute-start.5 = (bf16[16,64,128]{2,1,0:T(8,128)(2,1)S(1)}, bf16[16,64,128]{2,1,0:T(8,128)(2,1)S(1)}, u32[]{:S(2)}, u32[]{:S(2)}) collective-permute-start(bf16[16,64,128]{2,1,0:T(8,128)(2,1)S(1)} %get-tuple-element.59), channel_id=1, source_target_pairs={{0,2},{2,4},{4,6},{6,0},{1,3},{3,5},{5,7},{7,1},{8,10},{10,12},{12... | collective-permute-start | bytes 786440 | tf_op jit(solution)/shard_map/ppermute | solution.py:506
  45.6 7.5 %shard_map.155 = (f32[32,64,128]{2,1,0:T(8,128)}, f32[16,64,128]{2,1,0:T(8,128)S(1)}, f32[32,64,128]{2,1,0:T(8,128)}) custom-call(s32[512]{0:T(512)S(1)} %get-tuple-element.36.own_list, s32[4]{0:T(128)S(1)} %get-tuple-element.37.own_count, s32[512]{0:T(512)S(1)} %get-tuple-element.38.other_list, s32[4]{0:T(128)S(1)} %get-tuple-element.39.other_count, ...), custom_call_target="tpu_custom_call" | custom-call | tf_op jit(solution)/shard_map/pallas_call | solution.py:25
  53.1 0.0 all-to-all-done
  53.1 2.1 %shard_map.157 = f32[64,256]{1,0:T(8,128)} custom-call(bf16[768,128]{1,0:T(8,128)(2,1)S(1)} %bitcast.5, f32[64,256]{1,0:T(8,128)} %trans_in.1, bf16[256,256]{1,0:T(8,128)(2,1)} %matrix_in.1), custom_call_target="tpu_custom_call" | custom-call | tf_op jit(solution)/shard_map/pallas_call | solution.py:25
  55.2 0.0 collective-permute-done.5.arrived
  55.2 0.8 %shard_map.156 = f32[32,64,128]{2,1,0:T(8,128)} custom-call(bf16[16,64,128]{2,1,0:T(8,128)(2,1)S(1)} %collective-permute-done.5.arrived, f32[16,64,128]{2,1,0:T(8,128)S(1)} %get-tuple-element.65.low_next, f32[32,64,128]{2,1,0:T(8,128)} %get-tuple-element.66.lam_in), custom_call_target="tpu_custom_call", output_to_operand_aliasing={{}: (2, {})} | custom-call | tf_op jit(solution)/shard_map/pallas_call | solution.py:25
  (1 shorter events, 0.0 us)
Async XLA Ops:
  0.6 8.1 %collective-permute-start.1 = (bf16[96,128,128]{2,1,0:T(8,128)(2,1)}, bf16[96,128,128]{2,1,0:T(8,128)(2,1)S(1)}, u32[]{:S(2)}, u32[]{:S(2)}) collective-permute-start(bf16[96,128,128]{2,1,0:T(8,128)(2,1)} %refs_7_.3), channel_id=1, source_target_pairs={{0,1},{1,0},{2,3},{3,2},{4,5},{5,4},{6,7},{7,6},{8,9},{9,8},{10,11... | collective-permute-start | bytes 9437192 | tf_op jit(solution)/shard_map/ppermute | solution.py:104
  1.9 4.8 %collective-permute-start = (s32[96]{0:T(128)S(1)}, s32[96]{0:T(128)S(1)}, u32[]{:S(2)}, u32[]{:S(2)}) collective-permute-start(s32[96]{0:T(128)S(1)} %shift-left_or_fusion.codes), channel_id=1, source_target_pairs={{0,1},{1,0},{2,3},{3,2},{4,5},{5,4},{6,7},{7,6},{8,9},{9,8},{10,11... | collective-permute-start | bytes 1160 | tf_op jit(solution)/shard_map/ppermute | solution.py:103
  6.0 7.6 %copy-start.2 = (s32[128]{0:T(128)S(1)}, s32[128]{0:T(128)}, u32[]{:S(2)}) copy-start(s32[128]{0:T(128)} %param.22) | copy-start | bytes 1540
  10.1 11.6 %collective-permute-start.2 = (bf16[16,64,128]{2,1,0:T(8,128)(2,1)S(1)}, bf16[16,64,128]{2,1,0:T(8,128)(2,1)S(1)}, u32[]{:S(2)}, u32[]{:S(2)}) collective-permute-start(bf16[16,64,128]{2,1,0:T(8,128)(2,1)S(1)} %shard_map.150), channel_id=1, source_target_pairs={{0,2},{2,4},{4,6},{6,0},{1,3},{3,5},{5,7},{7,1},{8,10},{10,12},{12... | collective-permute-start | bytes 786440 | tf_op jit(solution)/shard_map/ppermute | solution.py:238
  21.7 1.7 %copy-start = (s32[128,1]{0,1:T(1,128)S(1)}, s32[128,1]{0,1:T(1,128)}, u32[]{:S(2)}) copy-start(s32[128,1]{0,1:T(1,128)} %param.23) | copy-start | bytes 1540
  21.7 1.7 %copy-start.1 = (s32[128]{0:T(128)S(1)}, s32[128]{0:T(128)}, u32[]{:S(2)}) copy-start(s32[128]{0:T(128)} %param.24) | copy-start | bytes 1540
  23.0 17.7 %collective-permute-start.3 = (bf16[16,64,128]{2,1,0:T(8,128)(2,1)S(1)}, bf16[16,64,128]{2,1,0:T(8,128)(2,1)S(1)}, u32[]{:S(2)}, u32[]{:S(2)}) collective-permute-start(bf16[16,64,128]{2,1,0:T(8,128)(2,1)S(1)} %get-tuple-element.46.refs_3_), channel_id=1, source_target_pairs={{0,2},{2,4},{4,6},{6,0},{1,3},{3,5},{5,7},{7,1},{8,10},{10,12},{12... | collective-permute-start | bytes 786440 | tf_op jit(solution)/shard_map/ppermute | solution.py:463
  23.4 5.3 %collective-permute-start.4 = (s32[1,384]{1,0:T(1,128)S(1)}, s32[1,384]{1,0:T(1,128)S(1)}, u32[]{:S(2)}, u32[]{:S(2)}) collective-permute-start(s32[1,384]{1,0:T(1,128)S(1)} %pad_add_fusion), channel_id=1, source_target_pairs={{2,0},{4,2},{6,4},{0,6},{3,1},{5,3},{7,5},{1,7},{10,8},{12,10},{14... | collective-permute-start | bytes 4616 | tf_op jit(solution)/shard_map/ppermute | solution.py:248
  33.1 20.0 %all-to-all-start = ((bf16[16,48,128]{2,1,0:T(8,128)(2,1)}), bf16[16,48,128]{2,1,0:T(8,128)(2,1)S(1)}, u32[]{:S(2)}, u32[]{:S(2)}) async-start(bf16[16,48,128]{2,1,0:T(8,128)(2,1)} %bitcast.3), calls=%async_computation | async-start | bytes 393216 | tf_op jit(solution)/shard_map/all_to_all | solution.py:490
  43.2 12.1 %collective-permute-start.5 = (bf16[16,64,128]{2,1,0:T(8,128)(2,1)S(1)}, bf16[16,64,128]{2,1,0:T(8,128)(2,1)S(1)}, u32[]{:S(2)}, u32[]{:S(2)}) collective-permute-start(bf16[16,64,128]{2,1,0:T(8,128)(2,1)S(1)} %get-tuple-element.59), channel_id=1, source_target_pairs={{0,2},{2,4},{4,6},{6,0},{1,3},{3,5},{5,7},{7,1},{8,10},{10,12},{12... | collective-permute-start | bytes 786440 | tf_op jit(solution)/shard_map/ppermute | solution.py:506

commit v6 on v5

--- a/solution.py
+++ b/solution.py
@@ -34,10 +34,7 @@
 
 
 def with_lists(body):
-    def whole(own_list, own_count, other_list, other_count, *refs):
-        return body((own_list, other_list), (own_count, other_count), *refs)
-
-    return whole
+    return lambda own, other, *refs: body((own, other), *refs)
 
 
 def in_hbm(array):
@@ -91,22 +88,48 @@
     onward = [(i, (i + 1) % owners) for i in range(owners)]
     backward = [(j, i) for i, j in onward]
 
-    is_low = (tile_source_index < low).astype(jnp.int32)
-    is_own = (tile_target_index < blocks).astype(jnp.int32)
-    own_codes = (
-        lax.iota(jnp.int32, stored)
-        | ((tile_source_index - low * (1 - is_low)) << 8)
-        | ((tile_target_index - blocks * (1 - is_own)) << 16)
-        | ((16 * is_own + 8 * is_low) << 24)
-    )
     own = derivative_tiles
-    other_codes = lax.ppermute(own_codes, "case", swap)
+    other_rows = lax.ppermute(tile_source_index, "case", swap)
+    other_columns = lax.ppermute(tile_target_index, "case", swap)
     other = lax.ppermute(own, "case", swap)
 
-    def run(lists, counts, parts, width):
+    def sorted_list(rows, columns):
+        is_low = jnp.where(rows < low, 1, 0)
+        is_own = jnp.where(columns < blocks, 1, 0)
+        kind = 2 * is_own + is_low
+        place = lax.broadcasted_iota(jnp.int32, (1, stored), 1)
+        word = place | ((rows - low * (1 - is_low)) << 8) | ((columns - blocks * (1 - is_own)) << 16)
+        kind_row = jnp.broadcast_to(kind.astype(F32), (stored, stored))
+        word_row = jnp.broadcast_to(word.astype(F32), (stored, stored))
+        earlier = lax.broadcasted_iota(jnp.int32, (stored, stored), 0) > lax.broadcasted_iota(
+            jnp.int32, (stored, stored), 1
+        )
+        kind_col = kind_row.T
+        same = jnp.logical_and(kind_col == kind_row, earlier)
+        rank = jnp.sum(jnp.where(same, 1.0, 0.0), axis=1, keepdims=True)
+        spot = (kind_col[:, :1] * STRIDE + rank).astype(jnp.int32)
+        hit = lax.broadcasted_iota(jnp.int32, (stored, CLASSES * STRIDE), 1) == spot
+        words = jnp.sum(jnp.where(hit, word_row.T[:, :1], 0.0), axis=0, keepdims=True)
+        taken = jnp.sum(jnp.where(hit, 1.0, 0.0), axis=0, keepdims=True)
+        idle = jnp.full((1, CLASSES * STRIDE), low << 8, jnp.int32)
+        lane = lax.broadcasted_iota(jnp.int32, (stored, 128), 1).astype(F32)
+        counts = jnp.sum(jnp.where(kind_col[:, :1] == lane, 1.0, 0.0), axis=0, keepdims=True)
+        return jnp.concatenate(
+            [jnp.where(taken > 0, words.astype(jnp.int32), idle), counts.astype(jnp.int32)], axis=1
+        )
+
+    def word_of(lists, side, kind, i):
+        return lists[side][0, kind * STRIDE + i]
+
+    def count_of(lists, side, kind):
+        return lists[side][0, CLASSES * STRIDE + kind]
+
+    list_type = array((1, CLASSES * STRIDE + 128), jnp.int32)
+
+    def run(lists, parts, width):
         def some(i, carry):
             words = [
-                (lists[side][kind * STRIDE + i * width + u], lam, tiles, acc)
+                (word_of(lists, side, kind, i * width + u), lam, tiles, acc)
                 for (side, kind), lam, tiles, acc in parts
                 for u in range(width)
             ]
@@ -115,56 +138,41 @@
                 for c, lam, tiles, _ in words
             ]
             for (c, _, _, acc), prod in zip(words, prods):
-                acc[(c >> 16) & 255] += prod
+                acc[c >> 16] += prod
             return carry
 
         longest = 0
         for (side, kind), _, _, _ in parts:
-            longest = jnp.maximum(longest, counts[side][kind])
+            longest = jnp.maximum(longest, count_of(lists, side, kind))
         lax.fori_loop(0, (longest + width - 1) // width, some, 0)
 
-    def sort(codes, lists, counts):
-        def place(e, used):
-            c = codes[e]
-            shift = c >> 24
-            lists[shift * (STRIDE // 8) + ((used >> shift) & 255)] = c
-            return used + (1 << shift)
-
-        used = lax.fori_loop(0, stored, place, jnp.int32(0), unroll=8)
-        for kind in range(CLASSES):
-            counts[kind] = (used >> (8 * kind)) & 255
-
-    list_shape = (CLASSES * STRIDE,)
-    list_types = (array(list_shape, jnp.int32), array((CLASSES,), jnp.int32))
-
-    def fill_idle(idle, lists, sem):
-        idle[...] = jnp.full(idle.shape, low << 8, jnp.int32)
-        fill = pltpu.make_async_copy(idle, lists, sem)
-        fill.start()
-        return fill
-
     def first_body(
-        codes, lam_in, own_in, acc, lo, hi, own_kept, lists, counts, lam, lam_bf, idle, sems
+        rows, columns, rows_in, columns_in, lam_in, own_in, acc, lo, hi, own_kept, listed,
+        lam, lam_bf, rows_kept, columns_kept, sems,
     ):
-        lam_copy = pltpu.make_async_copy(lam_in, lam, sems.at[0])
-        lam_copy.start()
+        chunks = stored // UNROLL
+        early = [
+            pltpu.make_async_copy(rows_in, rows_kept, sems.at[chunks]),
+            pltpu.make_async_copy(columns_in, columns_kept, sems.at[chunks + 1]),
+            pltpu.make_async_copy(lam_in, lam, sems.at[chunks + 2]),
+        ]
         copies = [
             pltpu.make_async_copy(
-                own_in.at[pl.ds(i, UNROLL)], own_kept.at[pl.ds(i, UNROLL)], sems.at[1 + i // UNROLL]
+                own_in.at[pl.ds(i * UNROLL, UNROLL)], own_kept.at[pl.ds(i * UNROLL, UNROLL)], sems.at[i]
             )
-            for i in range(0, stored, UNROLL)
+            for i in range(chunks)
         ]
-        for copy in copies:
+        for copy in early + copies:
             copy.start()
-        fill = fill_idle(idle, lists, sems.at[1 + stored // UNROLL])
         for b in range(targets):
             acc[b] = jnp.zeros((cases, nodes), F32)
         zero = jnp.zeros((cases, nodes), BF16)
         lo[low] = zero
         hi[blocks - low] = zero
-        fill.wait()
-        sort(codes, lists, counts)
-        lam_copy.wait()
+        early[0].wait()
+        early[1].wait()
+        listed[...] = sorted_list(rows_kept[...], columns_kept[...])
+        early[2].wait()
         for b in range(blocks):
             rounded = lam[b].astype(BF16)
             lam_bf[b] = rounded
@@ -174,56 +182,57 @@
                 hi[b - low] = rounded
         for i, copy in enumerate(copies):
             copy.wait()
-            prods = []
-            for u in range(UNROLL):
-                c = codes[i * UNROLL + u]
-                k = c >> 24
-                row = ((c >> 8) & 255) + jnp.where((k & 8) > 0, 0, low)
-                target = ((c >> 16) & 255) + jnp.where((k & 16) > 0, 0, blocks)
-                prod = jnp.dot(
-                    lam_bf[row], own_kept[i * UNROLL + u], preferred_element_type=F32
+            prods = [
+                jnp.dot(
+                    lam_bf[rows[i * UNROLL + u]],
+                    own_kept[i * UNROLL + u],
+                    preferred_element_type=F32,
                 )
-                prods.append((target, prod))
-            for target, prod in prods:
-                acc[target] += prod
-
-    acc, lo, hi, own, own_lists, own_counts = kernel(
+                for u in range(UNROLL)
+            ]
+            for u, prod in enumerate(prods):
+                acc[columns[i * UNROLL + u]] += prod
+
+    acc, lo, hi, own, own_list = kernel(
         first_body,
         (
             array(acc_shape, F32),
             array(padded, BF16),
             array(padded, BF16),
             array(own.shape, BF16),
-        )
-        + list_types,
-        [(own_codes, SM), (vertex_costate, HB), (own, HB)],
+            list_type,
+        ),
+        [
+            (tile_source_index, SM),
+            (tile_target_index, SM),
+            (tile_source_index.reshape(1, stored), HB),
+            (tile_target_index.reshape(1, stored), HB),
+            (vertex_costate, HB),
+            (own, HB),
+        ],
         scratch=[
             pltpu.VMEM(state, F32),
             pltpu.VMEM(state, BF16),
-            pltpu.VMEM(list_shape, jnp.int32),
-            pltpu.SemaphoreType.DMA((2 + stored // UNROLL,)),
+            pltpu.VMEM((1, stored), jnp.int32),
+            pltpu.VMEM((1, stored), jnp.int32),
+            pltpu.SemaphoreType.DMA((stored // UNROLL + 3,)),
         ],
-        out_specs=(VM,) * 4 + (SM, SM),
-    )
-
-    def sort_body(codes, lists, counts, idle, sem):
-        fill_idle(idle, lists, sem).wait()
-        sort(codes, lists, counts)
-
-    other_lists, other_counts = kernel(
+    )
+
+    def sort_body(rows, columns, listed):
+        listed[...] = sorted_list(rows[...], columns[...])
+
+    (other_list,) = kernel(
         sort_body,
-        list_types,
-        [(other_codes, SM)],
-        scratch=[pltpu.VMEM(list_shape, jnp.int32), pltpu.SemaphoreType.DMA],
-        out_specs=(SM, SM),
-    )
-    listed = [(own_lists, SM), (own_counts, SM), (other_lists, SM), (other_counts, SM)]
-
-    def rim_first_body(lists, counts, acc, lo, hi, other, out, sums):
+        (list_type,),
+        [(other_rows.reshape(1, stored), VM), (other_columns.reshape(1, stored), VM)],
+    )
+    listed = [(own_list, SM), (other_list, SM)]
+
+    def rim_first_body(lists, acc, lo, hi, other, out, sums):
         sums[...] = acc[blocks:]
         run(
             lists,
-            counts,
             [((1, 0), hi, other, sums), ((1, 1), lo, other, sums)],
             FEW,
         )
@@ -247,7 +256,7 @@
     )
     theirs = lax.ppermute(mine, "blk", backward)
 
-    def begin_next(lists, counts, lam, icar, outflow, own, other, acc, acc_rim, hi):
+    def begin_next(lists, lam, icar, outflow, own, other, acc, acc_rim, hi):
         for b in range(blocks):
             acc[b] = outflow[b : b + 1, :] * icar[b]
         for b in range(rim):
@@ -255,8 +264,8 @@
         for b in range(low, blocks):
             hi[b - low] = lam[b].astype(BF16)
         hi[blocks - low] = jnp.zeros((cases, nodes), BF16)
-        run(lists, counts, [((0, 0), hi, own, acc_rim), ((1, 0), hi, other, acc_rim)], FEW)
-        run(lists, counts, [((0, 2), hi, own, acc), ((1, 2), hi, other, acc)], MANY)
+        run(lists, [((0, 0), hi, own, acc_rim), ((1, 0), hi, other, acc_rim)], FEW)
+        run(lists, [((0, 2), hi, own, acc), ((1, 2), hi, other, acc)], MANY)
 
     def head_values(lo, hi, hot):
         total = jnp.dot(lo[0], hot[0], preferred_element_type=F32)
@@ -266,22 +275,20 @@
         return total.astype(BF16)
 
     def main_first_body(
-        lists, counts, acc, lo, hi, own, other, vertex, lam_in, icar_in, decay_in, inflow_in, outflow_in,
+        lists, acc, lo, hi, own, other, vertex, lam_in, icar_in, decay_in, inflow_in, outflow_in,
         lam_next, acc_next, acc_rim, hi_next, icar_next, head, hot, decay, inflow, outflow, other_kept,
         lam, icar, sems,
     ):
-        kept = pltpu.make_async_copy(other, other_kept, sems.at[5])
-        kept.start()
         pairs = [
             (icar_in, icar), (outflow_in, outflow), (lam_in, lam), (decay_in, decay), (inflow_in, inflow)
         ]
         copies = [pltpu.make_async_copy(a, b, sems.at[i]) for i, (a, b) in enumerate(pairs)]
-        for copy in copies:
+        kept = pltpu.make_async_copy(other, other_kept, sems.at[5])
+        for copy in copies + [kept]:
             copy.start()
         lam_next[...] = acc[:blocks]
         run(
             lists,
-            counts,
             [((1, 2), hi, other, lam_next), ((1, 3), lo, other, lam_next)],
             MANY,
         )
@@ -291,7 +298,7 @@
             lam_next[b] += outflow[b : b + 1, :] * icar[b]
             icar_next[b] = decay[b : b + 1, :] * icar[b] + inflow[b : b + 1, :] * lam[b]
         begin_next(
-            lists, counts, lam_next, icar_next, outflow, own, other, acc_next, acc_rim, hi_next
+            lists, lam_next, icar_next, outflow, own, other, acc_next, acc_rim, hi_next
         )
         node = lax.broadcasted_iota(jnp.int32, (nodes, heads), 0)
         for b in range(blocks):
@@ -332,26 +339,26 @@
             lo[b] = row.astype(BF16)
         lo[low] = jnp.zeros((cases, nodes), BF16)
 
-    def rim_sums(lists, counts, acc_rim, lo, own, other, out, sums):
+    def rim_sums(lists, acc_rim, lo, own, other, out, sums):
         sums[...] = acc_rim[...]
-        run(lists, counts, [((0, 1), lo, own, sums), ((1, 1), lo, other, sums)], FEW)
+        run(lists, [((0, 1), lo, own, sums), ((1, 1), lo, other, sums)], FEW)
         out[...] = sums[...].astype(BF16)
 
-    def rim_body(lists, counts, arrived, lam, acc_rim, own, other, out, low_rows, lo, sums):
+    def rim_body(lists, arrived, lam, acc_rim, own, other, out, low_rows, lo, sums):
         take_arrived(arrived, lam, low_rows, lo)
-        rim_sums(lists, counts, acc_rim, lo, own, other, out, sums)
+        rim_sums(lists, acc_rim, lo, own, other, out, sums)
 
     def rim_last_body(
-        lists, counts, arrived, lam, acc_rim, own_in, other_in, out, low_rows, lo, sums, ready, sems
+        lists, arrived, lam, acc_rim, own_in, other_in, out, low_rows, lo, sums, ready, sems
     ):
         sources = (own_in, other_in)
         for side in (0, 1):
-            fetch(lists, counts, side, 1, sources[side], ready, side * stored, sems.at[side])
+            fetch(lists, side, 1, sources[side], ready, side * stored, sems.at[side])
         take_arrived(arrived, lam, low_rows, lo)
         sums[...] = acc_rim[...]
         for side in (0, 1):
-            fetched(counts, side, 1, sources[side], ready, sems.at[side])
-            run_fetched(lists, counts, side, 1, lo, ready, side * stored, sums, FEW)
+            fetched(lists, side, 1, sources[side], ready, sems.at[side])
+            run_fetched(lists, side, 1, lo, ready, side * stored, sums, FEW)
         out[...] = sums[...].astype(BF16)
 
     def rows_of(owner):
@@ -360,10 +367,10 @@
         after = lax.broadcasted_iota(jnp.int32, (heads, heads), 1)
         same = jnp.logical_and(names.T == names, before < after)
         slot = jnp.sum(jnp.where(same, 1.0, 0.0), axis=0, keepdims=True).astype(jnp.int32)
-        return owner * (3 * slots) + slot
+        return owner * slots + slot
 
     def main_body(
-        lists, counts, owner, bus, theirs, left,
+        lists, owner, bus, theirs, left,
         low_rows, lam, lo, hi, acc, icar, own, other, hot, head0, decay, inflow,
         lam_next, acc_rim, hi_next, sent, icar_out, icar_next, lo_base, sem,
     ):
@@ -373,80 +380,73 @@
         copy = pltpu.make_async_copy(icar_next, icar_out, sem)
         copy.start()
         lam_next[...] = acc[...]
-        run(lists, counts, [((0, 3), lo, own, lam_next), ((1, 3), lo, other, lam_next)], MANY)
+        run(lists, [((0, 3), lo, own, lam_next), ((1, 3), lo, other, lam_next)], MANY)
         for b in range(low):
             lo_base[b] = lam_next[b].astype(BF16)
         for b in range(low, blocks):
             hi_next[b - low] = lam_next[b].astype(BF16)
         hi_next[blocks - low] = jnp.zeros((cases, nodes), BF16)
         acc_rim[...] = jnp.zeros(acc_rim.shape, F32)
-        run(lists, counts, [((0, 0), hi_next, own, acc_rim), ((1, 0), hi_next, other, acc_rim)], FEW)
+        run(lists, [((0, 0), hi_next, own, acc_rim), ((1, 0), hi_next, other, acc_rim)], FEW)
         node = lax.broadcasted_iota(jnp.int32, (nodes, heads), 0)
         vertex_next, owner_next, bus_next = (theirs[:, i * heads : (i + 1) * heads] for i in range(3))
         head_next = jnp.zeros((cases, heads), F32)
         for b in range(low):
             hot_next = jnp.where(node + b * nodes == vertex_next, 1.0, 0.0).astype(BF16)
             head_next += jnp.dot(left[b], hot_next, preferred_element_type=F32)
-        row = lax.broadcasted_iota(jnp.int32, (rows_sent, heads), 0)
         dest = rows_of(owner[...])
         followed = lax.axis_index("blk") < owners - 1
-        dest_next = jnp.where(followed, rows_of(owner_next) + 2 * slots, -1)
+        dest_next = jnp.where(followed, rows_of(owner_next), -1)
         width = (nodes - cases, heads)
+        label = jnp.broadcast_to((bus[...] + 1).astype(F32), width).astype(BF16)
+        label_next = jnp.broadcast_to((bus_next + 1).astype(F32), width).astype(BF16)
         pairs = [
             (dest, head0[...], head_values(lo, hi, hot)),
-            (
-                dest + slots,
-                head_values(lo_base, hi_next, hot),
-                jnp.broadcast_to((bus[...] + 1).astype(F32), width).astype(BF16),
-            ),
-            (
-                dest_next,
-                head_next.astype(BF16),
-                jnp.broadcast_to((bus_next + 1).astype(F32), width).astype(BF16),
-            ),
+            (dest, head_values(lo_base, hi_next, hot), label),
+            (dest_next, head_next.astype(BF16), label_next),
         ]
-        total = jnp.zeros((rows_sent, nodes), F32)
-        for where, upper_half, lower_half in pairs:
+        row = lax.broadcasted_iota(jnp.int32, (network * slots, heads), 0)
+        for i, (where, first_half, second_half) in enumerate(pairs):
             place = jnp.where(row == where, 1.0, 0.0).astype(BF16)
-            total += lax.dot_general(
+            part = lax.dot_general(
                 place,
-                jnp.concatenate([upper_half, lower_half], axis=0),
+                jnp.concatenate([first_half, second_half], axis=0),
                 (((1,), (1,)), ((), ())),
                 preferred_element_type=F32,
             )
-        sent[...] = total.astype(BF16)
+            sent[:, i] = part.astype(BF16).reshape(network, slots, nodes)
         copy.wait()
 
-    def fetch(lists, counts, side, kind, source, dest, first, sem):
+    def fetch(lists, side, kind, source, dest, first, sem):
         def one(i, carry):
-            c = lists[side][kind * STRIDE + i]
+            c = word_of(lists, side, kind, i)
             pltpu.make_async_copy(source.at[c & 255], dest.at[first + i], sem).start()
             return carry
 
-        lax.fori_loop(0, counts[side][kind], one, 0)
-
-    def fetched(counts, side, kind, source, dest, sem):
+        lax.fori_loop(0, count_of(lists, side, kind), one, 0)
+
+    def fetched(lists, side, kind, source, dest, sem):
         def one(i, carry):
             pltpu.make_async_copy(source.at[0], dest.at[0], sem).wait()
             return carry
 
-        lax.fori_loop(0, counts[side][kind], one, 0)
-
-    def run_fetched(lists, counts, side, kind, lam, source, first, acc, width):
+        lax.fori_loop(0, count_of(lists, side, kind), one, 0)
+
+    def run_fetched(lists, side, kind, lam, source, first, acc, width):
         def some(i, carry):
             words = []
             for u in range(width):
-                at = jnp.minimum(i * width + u, counts[side][kind] - 1)
-                words.append((lists[side][kind * STRIDE + i * width + u], first + at))
+                at = jnp.minimum(i * width + u, count_of(lists, side, kind) - 1)
+                words.append((word_of(lists, side, kind, i * width + u), first + at))
             prods = [
                 jnp.dot(lam[(c >> 8) & 255], source[at], preferred_element_type=F32)
                 for c, at in words
             ]
             for (c, _), prod in zip(words, prods):
-                acc[(c >> 16) & 255] += prod
+                acc[c >> 16] += prod
             return carry
 
-        lax.fori_loop(0, (counts[side][kind] + width - 1) // width, some, 0)
+        lax.fori_loop(0, (count_of(lists, side, kind) + width - 1) // width, some, 0)
 
     tiles = [(own, VM), (other, VM)]
     rim_type = array((rim, cases, nodes), BF16)
@@ -467,7 +467,7 @@
             array(state, F32),
             array((rim, cases, nodes), F32),
             array(padded, BF16),
-            array((rows_sent, nodes), BF16),
+            array((network, 3, slots, nodes), BF16),
             hbm_array(state, F32),
         ),
         listed
@@ -506,28 +506,18 @@
     arriving = lax.ppermute(leaving, "blk", onward)
 
     def main_last_body(
-        lists, counts, low_rows, lam, lo, hi, decay, inflow, outflow, own_in, other_in, icar_in,
-        lam_out, low_next, icar_out, lam_next, icar, own, other, sems,
+        lists, low_rows, lam, lo, hi, decay, inflow, outflow, own, other, icar,
+        lam_out, low_next, icar_out, lam_next, icar_next, sems,
     ):
-        copies = [
-            pltpu.make_async_copy(icar_in, icar, sems.at[0]),
-            pltpu.make_async_copy(own_in, own, sems.at[1]),
-            pltpu.make_async_copy(other_in, other, sems.at[2]),
-        ]
-        for copy in copies:
-            copy.start()
-        copies[0].wait()
         for b in range(blocks):
             row = low_rows[b] if b < low else lam[b]
             before = icar[b]
             lam_next[b] = outflow[b : b + 1, :] * before
-            icar[b] = decay[b : b + 1, :] * before + inflow[b : b + 1, :] * row
-        icar_copy = pltpu.make_async_copy(icar, icar_out, sems.at[0])
+            icar_next[b] = decay[b : b + 1, :] * before + inflow[b : b + 1, :] * row
+        icar_copy = pltpu.make_async_copy(icar_next, icar_out, sems.at[0])
         icar_copy.start()
-        copies[1].wait()
-        copies[2].wait()
-        run(lists, counts, [((0, 2), hi, own, lam_next), ((1, 2), hi, other, lam_next)], MANY)
-        run(lists, counts, [((0, 3), lo, own, lam_next), ((1, 3), lo, other, lam_next)], MANY)
+        run(lists, [((0, 2), hi, own, lam_next), ((1, 2), hi, other, lam_next)], MANY)
+        run(lists, [((0, 3), lo, own, lam_next), ((1, 3), lo, other, lam_next)], MANY)
         upper = pl.ds(low, blocks - low)
         lam_copy = pltpu.make_async_copy(lam_next.at[upper], lam_out.at[upper], sems.at[1])
         lam_copy.start()
@@ -541,14 +531,11 @@
         listed
         + [(low_rows, VM), (lam, VM), (lo, VM), (hi_next, VM)]
         + [(decay, VM), (inflow, VM), (outflow, VM)]
-        + stored_in
-        + [(icar, HB)],
+        + [(derivative_tiles, VM), (other_kept, VM), (icar, VM)],
         scratch=[
             pltpu.VMEM(state, F32),
             pltpu.VMEM(state, F32),
-            pltpu.VMEM(own.shape, BF16),
-            pltpu.VMEM(own.shape, BF16),
-            pltpu.SemaphoreType.DMA((3,)),
+            pltpu.SemaphoreType.DMA((2,)),
         ],
         out_specs=(HB, VM, HB),
     )

time: 56.4 us -> 52.5 us (0.931)
  Pallas kernels: 32.7 us -> 27.4 us
  waiting for transfers between devices: 3.83 us -> 5.44 us
  other arithmetic: 0.68 us -> 0.01 us
    pallas_call x10, Pallas kernels: 32.7 us -> 27.4 us  [kernel(): pl.pallas_call(body, out_shape=outs, in_specs=[spec for _, spec in ins],...]
    ppermute x3, waiting for transfers between devices: 1.48 us -> 2.57 us  [local(): arriving = lax.ppermute(leaving, 'blk', onward)]
    or x1 -> x0, other arithmetic: 0.68 us -> none  [local(): lax.iota(jnp.int32, stored) | tile_source_index - low * (1 - is_low) << 8]
    ppermute x1 -> x2, waiting for transfers between devices: 0.63 us -> 1.15 us  [the longest x1 1.14 us: local(): other_rows = lax.ppermute(tile_source_index, 'case', swap)]
  transfers between devices with their start and end apart: 7 -> 8, of which waited for: 3 -> 4; matrix products, arithmetic and copies ran while one was open for 1% -> 0% of each run, Pallas kernels for 52% -> 46%
where the time goes in v6:
time: 52.5 us; the launch traced here: 52.2 us
  Pallas kernels  27.4 us (52%)
  starting transfers between devices  18.6 us (35%)
  waiting for transfers between devices  5.44 us (10%)
  between operations  0.77 us (1%)
    pallas_call x10, Pallas kernels, kernel(): pl.pallas_call(body, out_shape=outs, in_specs=[spec for _, spec in ins],...  27.4 us
    all_to_all x1, starting transfers between devices, local(): lax.all_to_all(sent.reshape(network, 3 * slots, nodes), ('sec', 'blk'), s...  7.6 us
    ppermute x3, starting transfers between devices, local(): arriving = lax.ppermute(leaving, 'blk', onward)  6.35 us
    ppermute x1, starting transfers between devices, local(): theirs = lax.ppermute(mine, 'blk', backward)  3.56 us
    ppermute x3, waiting for transfers between devices, local(): arriving = lax.ppermute(leaving, 'blk', onward)  2.57 us
    ppermute x1, waiting for transfers between devices, local(): theirs = lax.ppermute(mine, 'blk', backward)  1.72 us
    ppermute x1, waiting for transfers between devices, local(): other_rows = lax.ppermute(tile_source_index, 'case', swap)  1.14 us
  transfers between devices with their start and end apart: 8, of which 4 were waited for; matrix products, arithmetic and copies ran while one was open for 0% of the time, Pallas kernels for 46%

profile of v6, /device:TPU:0, one launch (start us, length us, event | category | flops | bytes accessed | tf_op | source)
XLA Modules:
  0.0 52.2 jit_solution(3322454782325931360)
XLA Ops:
  0.6 0.6 %collective-permute-start.2 = (bf16[96,128,128]{2,1,0:T(8,128)(2,1)}, bf16[96,128,128]{2,1,0:T(8,128)(2,1)S(1)}, u32[]{:S(2)}, u32[]{:S(2)}) collective-permute-start(bf16[96,128,128]{2,1,0:T(8,128)(2,1)} %refs_7_.3), channel_id=1, source_target_pairs={{0,1},{1,0},{2,3},{3,2},{4,5},{5,4},{6,7},{7,6},{8,9},{9,8},{10,11... | collective-permute-start | bytes 9437192 | tf_op jit(solution)/shard_map/ppermute | solution.py:94
  1.2 0.1 collective-permute-start
  1.3 0.4 collective-permute-start.1
  1.7 3.8 %shard_map.148 = (f32[48,64,128]{2,1,0:T(8,128)S(1)}, bf16[17,64,128]{2,1,0:T(8,128)(2,1)S(1)}, bf16[17,64,128]{2,1,0:T(8,128)(2,1)S(1)}, bf16[96,128,128]{2,1,0:T(8,128)(2,1)S(1)}, s32[1,640]{1,0:T(1,128)S(1)}) custom-call(s32[96]{0:T(128)} %rows.1, s32[96]{0:T(128)} %columns.1, s32[1,96]{1,0:T(1,128)} %bitcast.18, s32[1,96]{1,0:T(1,128)} %bitcast.19, ...), custom_call_target="tpu_custom_call" | custom-call | tf_op jit(solution)/shard_map/pallas_call | solution.py:25
  5.5 0.0 copy-start.5
  5.5 1.1 %collective-permute-done = s32[96]{0:T(128)S(1)} collective-permute-done((s32[96]{0:T(128)}, s32[96]{0:T(128)S(1)}, u32[]{:S(2)}, u32[]{:S(2)}) %collective-permute-start) | collective-permute-done | bytes 416 | tf_op jit(solution)/shard_map/ppermute | solution.py:92
  6.7 0.0 collective-permute-done.1
  6.7 0.4 shard_map.149.other
  7.1 0.0 collective-permute-done.2.refs_3_.refs_4_.refs_11_
  7.1 1.3 %shard_map.150 = bf16[16,64,128]{2,1,0:T(8,128)(2,1)S(1)} custom-call(s32[1,640]{1,0:T(1,128)S(1)} %get-tuple-element.33.own, s32[1,640]{1,0:T(1,128)S(1)} %shard_map.149.other, f32[48,64,128]{2,1,0:T(8,128)S(1)} %get-tuple-element.34.refs_0_, bf16[17,64,128]{2,1,0:T(8,128)(2,1)S(1)} %get-tuple-element.35.refs_1_, ...), custom_call_target="tpu_custom_call" | custom-call | tf_op jit(solution)/shard_map/pallas_call | solution.py:25
  8.4 3.6 %collective-permute-start.3 = (bf16[16,64,128]{2,1,0:T(8,128)(2,1)S(1)}, bf16[16,64,128]{2,1,0:T(8,128)(2,1)S(1)}, u32[]{:S(2)}, u32[]{:S(2)}) collective-permute-start(bf16[16,64,128]{2,1,0:T(8,128)(2,1)S(1)} %shard_map.150), channel_id=1, source_target_pairs={{0,2},{2,4},{4,6},{6,0},{1,3},{3,5},{5,7},{7,1},{8,10},{10,12},{12... | collective-permute-start | bytes 786440 | tf_op jit(solution)/shard_map/ppermute | solution.py:247
  11.9 0.0 copy-done.5
  11.9 6.6 %shard_map.151 = (f32[32,64,128]{2,1,0:T(8,128)S(1)}, f32[32,64,128]{2,1,0:T(8,128)S(1)}, f32[16,64,128]{2,1,0:T(8,128)S(1)}, bf16[17,64,128]{2,1,0:T(8,128)(2,1...) custom-call(s32[1,640]{1,0:T(1,128)S(1)} %get-tuple-element.33.own, ...), custom_call_target="tpu_custom_call" | custom-call | tf_op jit(solution)/shard_map/pallas_call | solution.py:25
  18.5 1.5 %collective-permute-done.3.refs_0_ = bf16[16,64,128]{2,1,0:T(8,128)(2,1)S(1)} collective-permute-done((bf16[16,64,128]{2,1,0:T(8,128)(2,1)S(1)}, bf16[16,64,128]{2,1,0:T(8,128)(2,1)S(1)}, u32[]{:S(2)}, u32[]{:S(2)}) %collective-permute-start.3) | collective-permute-done | bytes 262176 | tf_op jit(solution)/shard_map/ppermute | solution.py:247
  20.0 0.0 copy-start.3
  20.0 0.0 copy-start.4
  20.0 1.3 %shard_map.152 = (bf16[16,64,128]{2,1,0:T(8,128)(2,1)S(1)}, f32[16,64,128]{2,1,0:T(8,128)S(1)}, bf16[17,64,128]{2,1,0:T(8,128)(2,1)S(1)}) custom-call(s32[1,640]{1,0:T(1,128)S(1)} %get-tuple-element.33.own, s32[1,640]{1,0:T(1,128)S(1)} %shard_map.149.other, bf16[16,64,128]{2,1,0:T(8,128)(2,1)S(1)} %collective-permute-done.3.refs_0_, ...), custom_call_target="tpu_custom_call" | custom-call | tf_op jit(solution)/shard_map/pallas_call | solution.py:25
  21.3 0.4 collective-permute-start.4
  21.7 0.0 copy-done.3
  21.7 0.0 copy-done.4
  21.7 3.6 %collective-permute-start.5 = (s32[1,384]{1,0:T(1,128)S(1)}, s32[1,384]{1,0:T(1,128)S(1)}, u32[]{:S(2)}, u32[]{:S(2)}) collective-permute-start(s32[1,384]{1,0:T(1,128)S(1)} %pad_add_fusion), channel_id=1, source_target_pairs={{2,0},{4,2},{6,4},{0,6},{3,1},{5,3},{7,5},{1,7},{10,8},{12,10},{14... | collective-permute-start | bytes 4616 | tf_op jit(solution)/shard_map/ppermute | solution.py:257
  25.3 1.7 %collective-permute-done.5.refs_2_ = s32[1,384]{1,0:T(1,128)S(1)} collective-permute-done((s32[1,384]{1,0:T(1,128)S(1)}, s32[1,384]{1,0:T(1,128)S(1)}, u32[]{:S(2)}, u32[]{:S(2)}) %collective-permute-start.5) | collective-permute-done | bytes 1568 | tf_op jit(solution)/shard_map/ppermute | solution.py:257
  27.0 4.2 %shard_map.153 = (f32[32,64,128]{2,1,0:T(8,128)S(1)}, f32[16,64,128]{2,1,0:T(8,128)S(1)}, bf16[17,64,128]{2,1,0:T(8,128)(2,1)S(1)}, bf16[16,3,16,128]{3,2,1,0:T(8,128)(2,1)}, f32[32,64,128]{2,1,0:T(8,128)}) custom-call(s32[1,640]{1,0:T(1,128)S(1)} %get-tuple-element.33.own, s32[1,640]{1,0:T(1,128)S(1)} %shard_map.149.other, s32[1,128]{1,0:T(1,128)S(1)} %bitcast.11, ...), custom_call_target="tpu_custom_call" | custom-call | tf_op jit(solution)/shard_map/pallas_call | solution.py:25
  31.2 7.6 %all-to-all-start = ((bf16[16,48,128]{2,1,0:T(8,128)(2,1)}), bf16[16,48,128]{2,1,0:T(8,128)(2,1)S(1)}, u32[]{:S(2)}, u32[]{:S(2)}) async-start(bf16[16,48,128]{2,1,0:T(8,128)(2,1)} %bitcast.7), calls=%async_computation | async-start | bytes 393216 | tf_op jit(solution)/shard_map/all_to_all | solution.py:490
  38.8 0.0 collective-permute-done.4.refs_0_
  38.8 0.0 copy-start
  38.8 0.0 copy-start.1
  38.8 0.0 copy-start.2
  38.8 2.7 %shard_map.154 = (bf16[16,64,128]{2,1,0:T(8,128)(2,1)S(1)}, f32[16,64,128]{2,1,0:T(8,128)S(1)}, bf16[17,64,128]{2,1,0:T(8,128)(2,1)S(1)}) custom-call(s32[1,640]{1,0:T(1,128)S(1)} %get-tuple-element.33.own, s32[1,640]{1,0:T(1,128)S(1)} %shard_map.149.other, bf16[16,64,128]{2,1,0:T(8,128)(2,1)S(1)} %collective-permute-done.4.refs_0_, ...), custom_call_target="tpu_custom_call" | custom-call | tf_op jit(solution)/shard_map/pallas_call | solution.py:25
  41.6 2.4 %collective-permute-start.6 = (bf16[16,64,128]{2,1,0:T(8,128)(2,1)S(1)}, bf16[16,64,128]{2,1,0:T(8,128)(2,1)S(1)}, u32[]{:S(2)}, u32[]{:S(2)}) collective-permute-start(bf16[16,64,128]{2,1,0:T(8,128)(2,1)S(1)} %get-tuple-element.53), channel_id=1, source_target_pairs={{0,2},{2,4},{4,6},{6,0},{1,3},{3,5},{5,7},{7,1},{8,10},{10,12},{12... | collective-permute-start | bytes 786440 | tf_op jit(solution)/shard_map/ppermute | solution.py:506
  44.0 0.0 copy-done
  44.0 0.0 copy-done.1
  44.0 0.0 copy-done.2
  44.0 4.2 %shard_map.155 = (f32[32,64,128]{2,1,0:T(8,128)}, f32[16,64,128]{2,1,0:T(8,128)S(1)}, f32[32,64,128]{2,1,0:T(8,128)}) custom-call(s32[1,640]{1,0:T(1,128)S(1)} %get-tuple-element.33.own, s32[1,640]{1,0:T(1,128)S(1)} %shard_map.149.other, f32[16,64,128]{2,1,0:T(8,128)S(1)} %get-tuple-element.54.refs_0_, f32[32,64,128]{2,1,0:T(8,128)S(1)} %get-tuple-element.50.refs_1_, ...), custom_call_target="tpu_custom_call" | custom-call | tf_op jit(solution)/shard_map/pallas_call | solution.py:25
  48.2 0.0 all-to-all-done
  48.2 2.1 %shard_map.157 = f32[64,256]{1,0:T(8,128)} custom-call(bf16[768,128]{1,0:T(8,128)(2,1)S(1)} %bitcast.9, f32[64,256]{1,0:T(8,128)} %trans_in.1, bf16[256,256]{1,0:T(8,128)(2,1)} %matrix_in.1), custom_call_target="tpu_custom_call" | custom-call | tf_op jit(solution)/shard_map/pallas_call | solution.py:25
  50.3 1.1 %collective-permute-done.6.arrived = bf16[16,64,128]{2,1,0:T(8,128)(2,1)S(1)} collective-permute-done((bf16[16,64,128]{2,1,0:T(8,128)(2,1)S(1)}, bf16[16,64,128]{2,1,0:T(8,128)(2,1)S(1)}, u32[]{:S(2)}, u32[]{:S(2)}) %collective-permute-start.6) | collective-permute-done | bytes 262176 | tf_op jit(solution)/shard_map/ppermute | solution.py:506
  51.4 0.8 %shard_map.156 = f32[32,64,128]{2,1,0:T(8,128)} custom-call(bf16[16,64,128]{2,1,0:T(8,128)(2,1)S(1)} %collective-permute-done.6.arrived, f32[16,64,128]{2,1,0:T(8,128)S(1)} %get-tuple-element.59.low_next, f32[32,64,128]{2,1,0:T(8,128)} %get-tuple-element.60.lam_in), custom_call_target="tpu_custom_call", output_to_operand_aliasing={{}: (2, {})} | custom-call | tf_op jit(solution)/shard_map/pallas_call | solution.py:25
  (1 shorter events, 0.0 us)
Async XLA Ops:
  0.6 6.5 %collective-permute-start.2 = (bf16[96,128,128]{2,1,0:T(8,128)(2,1)}, bf16[96,128,128]{2,1,0:T(8,128)(2,1)S(1)}, u32[]{:S(2)}, u32[]{:S(2)}) collective-permute-start(bf16[96,128,128]{2,1,0:T(8,128)(2,1)} %refs_7_.3), channel_id=1, source_target_pairs={{0,1},{1,0},{2,3},{3,2},{4,5},{5,4},{6,7},{7,6},{8,9},{9,8},{10,11... | collective-permute-start | bytes 9437192 | tf_op jit(solution)/shard_map/ppermute | solution.py:94
  1.2 5.5 %collective-permute-start = (s32[96]{0:T(128)}, s32[96]{0:T(128)S(1)}, u32[]{:S(2)}, u32[]{:S(2)}) collective-permute-start(s32[96]{0:T(128)} %rows.1), channel_id=1, source_target_pairs={{0,1},{1,0},{2,3},{3,2},{4,5},{5,4},{6,7},{7,6},{8,9},{9,8},{10,11... | collective-permute-start | bytes 1160 | tf_op jit(solution)/shard_map/ppermute | solution.py:92
  1.3 5.4 %collective-permute-start.1 = (s32[96]{0:T(128)}, s32[96]{0:T(128)S(1)}, u32[]{:S(2)}, u32[]{:S(2)}) collective-permute-start(s32[96]{0:T(128)} %columns.1), channel_id=1, source_target_pairs={{0,1},{1,0},{2,3},{3,2},{4,5},{5,4},{6,7},{7,6},{8,9},{9,8},{10,11... | collective-permute-start | bytes 1160 | tf_op jit(solution)/shard_map/ppermute | solution.py:93
  5.5 6.4 %copy-start.5 = (s32[128]{0:T(128)S(1)}, s32[128]{0:T(128)}, u32[]{:S(2)}) copy-start(s32[128]{0:T(128)} %param.22) | copy-start | bytes 1540
  8.4 11.6 %collective-permute-start.3 = (bf16[16,64,128]{2,1,0:T(8,128)(2,1)S(1)}, bf16[16,64,128]{2,1,0:T(8,128)(2,1)S(1)}, u32[]{:S(2)}, u32[]{:S(2)}) collective-permute-start(bf16[16,64,128]{2,1,0:T(8,128)(2,1)S(1)} %shard_map.150), channel_id=1, source_target_pairs={{0,2},{2,4},{4,6},{6,0},{1,3},{3,5},{5,7},{7,1},{8,10},{10,12},{12... | collective-permute-start | bytes 786440 | tf_op jit(solution)/shard_map/ppermute | solution.py:247
  20.0 1.7 %copy-start.3 = (s32[128,1]{0,1:T(1,128)S(1)}, s32[128,1]{0,1:T(1,128)}, u32[]{:S(2)}) copy-start(s32[128,1]{0,1:T(1,128)} %param.23) | copy-start | bytes 1540
  20.0 1.7 %copy-start.4 = (s32[128]{0:T(128)S(1)}, s32[128]{0:T(128)}, u32[]{:S(2)}) copy-start(s32[128]{0:T(128)} %param.24) | copy-start | bytes 1540
  21.3 17.4 %collective-permute-start.4 = (bf16[16,64,128]{2,1,0:T(8,128)(2,1)S(1)}, bf16[16,64,128]{2,1,0:T(8,128)(2,1)S(1)}, u32[]{:S(2)}, u32[]{:S(2)}) collective-permute-start(bf16[16,64,128]{2,1,0:T(8,128)(2,1)S(1)} %get-tuple-element.40.refs_3_), channel_id=1, source_target_pairs={{0,2},{2,4},{4,6},{6,0},{1,3},{3,5},{5,7},{7,1},{8,10},{10,12},{12... | collective-permute-start | bytes 786440 | tf_op jit(solution)/shard_map/ppermute | solution.py:463
  21.7 5.3 %collective-permute-start.5 = (s32[1,384]{1,0:T(1,128)S(1)}, s32[1,384]{1,0:T(1,128)S(1)}, u32[]{:S(2)}, u32[]{:S(2)}) collective-permute-start(s32[1,384]{1,0:T(1,128)S(1)} %pad_add_fusion), channel_id=1, source_target_pairs={{2,0},{4,2},{6,4},{0,6},{3,1},{5,3},{7,5},{1,7},{10,8},{12,10},{14... | collective-permute-start | bytes 4616 | tf_op jit(solution)/shard_map/ppermute | solution.py:257
  31.2 17.0 %all-to-all-start = ((bf16[16,48,128]{2,1,0:T(8,128)(2,1)}), bf16[16,48,128]{2,1,0:T(8,128)(2,1)S(1)}, u32[]{:S(2)}, u32[]{:S(2)}) async-start(bf16[16,48,128]{2,1,0:T(8,128)(2,1)} %bitcast.7), calls=%async_computation | async-start | bytes 393216 | tf_op jit(solution)/shard_map/all_to_all | solution.py:490
  38.8 5.2 %copy-start = (bf16[96,128,128]{2,1,0:T(8,128)(2,1)S(1)}, bf16[96,128,128]{2,1,0:T(8,128)(2,1)}, u32[]{:S(2)}) copy-start(bf16[96,128,128]{2,1,0:T(8,128)(2,1)} %refs_7_.3) | copy-start | bytes 9437188
  38.8 5.2 %copy-start.1 = (bf16[96,128,128]{2,1,0:T(8,128)(2,1)S(1)}, bf16[96,128,128]{2,1,0:T(8,128)(2,1)}, u32[]{:S(2)}) copy-start(bf16[96,128,128]{2,1,0:T(8,128)(2,1)} %get-tuple-element.52.refs_4_.refs_8_) | copy-start | bytes 9437188
  38.8 5.2 %copy-start.2 = (f32[32,64,128]{2,1,0:T(8,128)S(1)}, f32[32,64,128]{2,1,0:T(8,128)}, u32[]{:S(2)}) copy-start(f32[32,64,128]{2,1,0:T(8,128)} %get-tuple-element.58.refs_9_) | copy-start | bytes 3145732
  41.6 9.8 %collective-permute-start.6 = (bf16[16,64,128]{2,1,0:T(8,128)(2,1)S(1)}, bf16[16,64,128]{2,1,0:T(8,128)(2,1)S(1)}, u32[]{:S(2)}, u32[]{:S(2)}) collective-permute-start(bf16[16,64,128]{2,1,0:T(8,128)(2,1)S(1)} %get-tuple-element.53), channel_id=1, source_target_pairs={{0,2},{2,4},{4,6},{6,0},{1,3},{3,5},{5,7},{7,1},{8,10},{10,12},{12... | collective-permute-start | bytes 786440 | tf_op jit(solution)/shard_map/ppermute | solution.py:506

commit v7 on v6

--- a/solution.py
+++ b/solution.py
@@ -10,6 +10,7 @@
 UNROLL = 16
 FEW = 24
 MANY = 40
+KEEP = 44
 CLASSES = 4
 VMEM_LIMIT = 24 << 20
 
@@ -229,6 +230,53 @@
     )
     listed = [(own_list, SM), (other_list, SM)]
 
+    def head_values(lo, hi, hot):
+        total = jnp.dot(lo[0], hot[0], preferred_element_type=F32)
+        for b in range(1, blocks):
+            row = lo[b] if b < low else hi[b - low]
+            total += jnp.dot(row, hot[b], preferred_element_type=F32)
+        return total.astype(BF16)
+
+    def rows_of(owner):
+        names = jnp.broadcast_to(owner.astype(F32), (heads, heads))
+        before = lax.broadcasted_iota(jnp.int32, (heads, heads), 0)
+        after = lax.broadcasted_iota(jnp.int32, (heads, heads), 1)
+        same = jnp.logical_and(names.T == names, before < after)
+        slot = jnp.sum(jnp.where(same, 1.0, 0.0), axis=0, keepdims=True).astype(jnp.int32)
+        return owner * slots + slot
+
+    def one_hots(vertex, count, out):
+        node = lax.broadcasted_iota(jnp.int32, (nodes, heads), 0)
+        for b in range(count):
+            out[b] = jnp.where(node + b * nodes == vertex, 1.0, 0.0).astype(BF16)
+
+    def place_rows(owner, keep, out):
+        row = lax.broadcasted_iota(jnp.int32, (network * slots, heads), 0)
+        out[...] = jnp.where(row == jnp.where(keep, rows_of(owner), -1), 1.0, 0.0).astype(BF16)
+
+    place_type = array((network * slots, heads), BF16)
+
+    def prepare_body(vertex, owner, lo, hi, hot, head, place):
+        one_hots(vertex[...], blocks, hot)
+        head[...] = head_values(lo, hi, hot)
+        place_rows(owner[...], True, place)
+
+    own_owner = distribution_entry_holder.reshape(1, heads)
+    hot, head0, place = kernel(
+        prepare_body,
+        (array(hot_shape, BF16), array((cases, heads), BF16), place_type),
+        [(distribution_entry_vertex.reshape(1, heads), VM), (own_owner, VM), (lo, VM), (hi, VM)],
+    )
+    mine = jnp.concatenate(
+        [
+            distribution_entry_vertex.reshape(1, heads),
+            own_owner,
+            distribution_entry_substation.reshape(1, heads),
+        ],
+        axis=1,
+    )
+    theirs = lax.ppermute(mine, "blk", backward)
+
     def rim_first_body(lists, acc, lo, hi, other, out, sums):
         sums[...] = acc[blocks:]
         run(
@@ -245,16 +293,6 @@
         scratch=[pltpu.VMEM((rim, cases, nodes), F32)],
     )
     arriving = lax.ppermute(leaving, "blk", onward)
-
-    mine = jnp.concatenate(
-        [
-            distribution_entry_vertex.reshape(1, heads),
-            distribution_entry_holder.reshape(1, heads),
-            distribution_entry_substation.reshape(1, heads),
-        ],
-        axis=1,
-    )
-    theirs = lax.ppermute(mine, "blk", backward)
 
     def begin_next(lists, lam, icar, outflow, own, other, acc, acc_rim, hi):
         for b in range(blocks):
@@ -267,16 +305,9 @@
         run(lists, [((0, 0), hi, own, acc_rim), ((1, 0), hi, other, acc_rim)], FEW)
         run(lists, [((0, 2), hi, own, acc), ((1, 2), hi, other, acc)], MANY)
 
-    def head_values(lo, hi, hot):
-        total = jnp.dot(lo[0], hot[0], preferred_element_type=F32)
-        for b in range(1, blocks):
-            row = lo[b] if b < low else hi[b - low]
-            total += jnp.dot(row, hot[b], preferred_element_type=F32)
-        return total.astype(BF16)
-
     def main_first_body(
-        lists, acc, lo, hi, own, other, vertex, lam_in, icar_in, decay_in, inflow_in, outflow_in,
-        lam_next, acc_next, acc_rim, hi_next, icar_next, head, hot, decay, inflow, outflow, other_kept,
+        lists, acc, lo, hi, own, other, theirs, lam_in, icar_in, decay_in, inflow_in, outflow_in,
+        lam_next, acc_next, acc_rim, hi_next, icar_next, hot_next, place_next, decay, inflow, outflow, other_kept,
         lam, icar, sems,
     ):
         pairs = [
@@ -300,14 +331,15 @@
         begin_next(
             lists, lam_next, icar_next, outflow, own, other, acc_next, acc_rim, hi_next
         )
-        node = lax.broadcasted_iota(jnp.int32, (nodes, heads), 0)
-        for b in range(blocks):
-            hot[b] = jnp.where(node + b * nodes == vertex[...], 1.0, 0.0).astype(BF16)
-        head[...] = head_values(lo, hi, hot)
+        followed = lax.axis_index("blk") < owners - 1
+        one_hots(theirs[:, :heads], low, hot_next)
+        place_rows(theirs[:, heads : 2 * heads], followed, place_next)
         kept.wait()
 
     factor = array(factor_shape, F32)
-    lam, acc, acc_rim, hi_next, icar, head0, hot, decay, inflow, outflow, other_kept = kernel(
+    (
+        lam, acc, acc_rim, hi_next, icar, hot_next, place_next, decay, inflow, outflow, other_kept
+    ) = kernel(
         with_lists(main_first_body),
         (
             array(state, F32),
@@ -315,8 +347,8 @@
             array((rim, cases, nodes), F32),
             array(padded, BF16),
             array(state, F32),
-            array((cases, heads), BF16),
-            array(hot_shape, BF16),
+            array((low, nodes, heads), BF16),
+            place_type,
             factor,
             factor,
             factor,
@@ -324,7 +356,7 @@
         ),
         listed
         + [(acc, VM), (lo, VM), (hi, VM), (own, VM), (other, VM)]
-        + [(distribution_entry_vertex.reshape(1, heads), VM)]
+        + [(theirs, VM)]
         + [(vertex_costate, HB), (inverter_costate, HB), (inverter_decay_factor, HB)]
         + [(costate_to_inverter_factor, HB), (inverter_to_costate_factor, HB)],
         scratch=[pltpu.VMEM(state, F32), pltpu.VMEM(state, F32), pltpu.SemaphoreType.DMA((6,))],
@@ -348,105 +380,117 @@
         take_arrived(arrived, lam, low_rows, lo)
         rim_sums(lists, acc_rim, lo, own, other, out, sums)
 
+    def start_copies(lists, side, kind, first, count, source, dest, at, sem):
+        def one(i, carry):
+            c = word_of(lists, side, kind, first + i)
+            pltpu.make_async_copy(source.at[c & 255], dest.at[at + i], sem).start()
+            return carry
+
+        lax.fori_loop(0, count, one, 0)
+
+    def finish_copies(count, source, dest, sem):
+        def one(i, carry):
+            pltpu.make_async_copy(source.at[0], dest.at[0], sem).wait()
+            return carry
+
+        lax.fori_loop(0, count, one, 0)
+
+    def run_copied(lists, first, count, lam, source, acc, width):
+        total = count[0] + count[1]
+
+        def some(i, carry):
+            words = []
+            for u in range(width):
+                j = i * width + u
+                is_own = j < count[0]
+                at = jnp.where(is_own, first[0] + j, first[1] + j - count[0])
+                at = jnp.clip(at, 0, STRIDE - 1)
+                word = jnp.where(is_own, word_of(lists, 0, 1, at), word_of(lists, 1, 1, at))
+                words.append((jnp.where(j < total, word, low << 8), jnp.minimum(j, total - 1)))
+            prods = [
+                jnp.dot(lam[(c >> 8) & 255], source[j], preferred_element_type=F32)
+                for c, j in words
+            ]
+            for (c, _), prod in zip(words, prods):
+                acc[c >> 16] += prod
+            return carry
+
+        lax.fori_loop(0, (total + width - 1) // width, some, 0)
+
     def rim_last_body(
-        lists, arrived, lam, acc_rim, own_in, other_in, out, low_rows, lo, sums, ready, sems
+        lists, arrived, lam, acc_rim, kept, own_in, other_in, out, low_rows, lo, sums, rest, sem
     ):
-        sources = (own_in, other_in)
-        for side in (0, 1):
-            fetch(lists, side, 1, sources[side], ready, side * stored, sems.at[side])
+        count_own = count_of(lists, 0, 1)
+        count_other = count_of(lists, 1, 1)
+        keep_own = jnp.minimum(count_own, KEEP)
+        keep_other = jnp.minimum(count_other, KEEP - keep_own)
+        more_own = count_own - keep_own
+        more_other = count_other - keep_other
+        start_copies(lists, 0, 1, keep_own, more_own, own_in, rest, 0, sem)
+        start_copies(lists, 1, 1, keep_other, more_other, other_in, rest, more_own, sem)
         take_arrived(arrived, lam, low_rows, lo)
         sums[...] = acc_rim[...]
-        for side in (0, 1):
-            fetched(lists, side, 1, sources[side], ready, sems.at[side])
-            run_fetched(lists, side, 1, lo, ready, side * stored, sums, FEW)
+        run_copied(lists, (0, 0), (keep_own, keep_other), lo, kept, sums, MANY)
+        finish_copies(more_own + more_other, own_in, rest, sem)
+        run_copied(
+            lists, (keep_own, keep_other), (more_own, more_other), lo, rest, sums, FEW
+        )
         out[...] = sums[...].astype(BF16)
 
-    def rows_of(owner):
-        names = jnp.broadcast_to(owner.astype(F32), (heads, heads))
-        before = lax.broadcasted_iota(jnp.int32, (heads, heads), 0)
-        after = lax.broadcasted_iota(jnp.int32, (heads, heads), 1)
-        same = jnp.logical_and(names.T == names, before < after)
-        slot = jnp.sum(jnp.where(same, 1.0, 0.0), axis=0, keepdims=True).astype(jnp.int32)
-        return owner * slots + slot
-
     def main_body(
-        lists, owner, bus, theirs, left,
-        low_rows, lam, lo, hi, acc, icar, own, other, hot, head0, decay, inflow,
-        lam_next, acc_rim, hi_next, sent, icar_out, icar_next, lo_base, sem,
+        lists, bus, theirs, left, low_rows, lam, lo, hi, acc, icar, own, other,
+        hot, hot_next, head0, place, place_next, decay, inflow,
+        lam_low, acc_rim, sent, kept, icar_out, lam_out, hi_out,
+        icar_next, lo_base, lam_next, hi_next, sems,
     ):
+        keep_own = jnp.minimum(count_of(lists, 0, 1), KEEP)
+        keep_other = jnp.minimum(count_of(lists, 1, 1), KEEP - keep_own)
+        start_copies(lists, 0, 1, 0, keep_own, own, kept, 0, sems.at[0])
+        start_copies(lists, 1, 1, 0, keep_other, other, kept, keep_own, sems.at[0])
         for b in range(blocks):
             row = low_rows[b] if b < low else lam[b]
             icar_next[b] = decay[b : b + 1, :] * icar[b] + inflow[b : b + 1, :] * row
-        copy = pltpu.make_async_copy(icar_next, icar_out, sem)
-        copy.start()
+        icar_copy = pltpu.make_async_copy(icar_next, icar_out, sems.at[1])
+        icar_copy.start()
         lam_next[...] = acc[...]
         run(lists, [((0, 3), lo, own, lam_next), ((1, 3), lo, other, lam_next)], MANY)
+        upper = pl.ds(low, blocks - low)
+        lam_copy = pltpu.make_async_copy(lam_next.at[upper], lam_out, sems.at[2])
+        lam_copy.start()
         for b in range(low):
+            lam_low[b] = lam_next[b]
             lo_base[b] = lam_next[b].astype(BF16)
         for b in range(low, blocks):
             hi_next[b - low] = lam_next[b].astype(BF16)
         hi_next[blocks - low] = jnp.zeros((cases, nodes), BF16)
+        hi_copy = pltpu.make_async_copy(hi_next, hi_out, sems.at[3])
+        hi_copy.start()
         acc_rim[...] = jnp.zeros(acc_rim.shape, F32)
         run(lists, [((0, 0), hi_next, own, acc_rim), ((1, 0), hi_next, other, acc_rim)], FEW)
-        node = lax.broadcasted_iota(jnp.int32, (nodes, heads), 0)
-        vertex_next, owner_next, bus_next = (theirs[:, i * heads : (i + 1) * heads] for i in range(3))
-        head_next = jnp.zeros((cases, heads), F32)
-        for b in range(low):
-            hot_next = jnp.where(node + b * nodes == vertex_next, 1.0, 0.0).astype(BF16)
-            head_next += jnp.dot(left[b], hot_next, preferred_element_type=F32)
-        dest = rows_of(owner[...])
-        followed = lax.axis_index("blk") < owners - 1
-        dest_next = jnp.where(followed, rows_of(owner_next), -1)
+        head_next = jnp.dot(left[0], hot_next[0], preferred_element_type=F32)
+        for b in range(1, low):
+            head_next += jnp.dot(left[b], hot_next[b], preferred_element_type=F32)
         width = (nodes - cases, heads)
         label = jnp.broadcast_to((bus[...] + 1).astype(F32), width).astype(BF16)
+        bus_next = theirs[:, 2 * heads : 3 * heads]
         label_next = jnp.broadcast_to((bus_next + 1).astype(F32), width).astype(BF16)
         pairs = [
-            (dest, head0[...], head_values(lo, hi, hot)),
-            (dest, head_values(lo_base, hi_next, hot), label),
-            (dest_next, head_next.astype(BF16), label_next),
+            (place, head0[...], head_values(lo, hi, hot)),
+            (place, head_values(lo_base, hi_next, hot), label),
+            (place_next, head_next.astype(BF16), label_next),
         ]
-        row = lax.broadcasted_iota(jnp.int32, (network * slots, heads), 0)
         for i, (where, first_half, second_half) in enumerate(pairs):
-            place = jnp.where(row == where, 1.0, 0.0).astype(BF16)
             part = lax.dot_general(
-                place,
+                where[...],
                 jnp.concatenate([first_half, second_half], axis=0),
                 (((1,), (1,)), ((), ())),
                 preferred_element_type=F32,
             )
             sent[:, i] = part.astype(BF16).reshape(network, slots, nodes)
-        copy.wait()
-
-    def fetch(lists, side, kind, source, dest, first, sem):
-        def one(i, carry):
-            c = word_of(lists, side, kind, i)
-            pltpu.make_async_copy(source.at[c & 255], dest.at[first + i], sem).start()
-            return carry
-
-        lax.fori_loop(0, count_of(lists, side, kind), one, 0)
-
-    def fetched(lists, side, kind, source, dest, sem):
-        def one(i, carry):
-            pltpu.make_async_copy(source.at[0], dest.at[0], sem).wait()
-            return carry
-
-        lax.fori_loop(0, count_of(lists, side, kind), one, 0)
-
-    def run_fetched(lists, side, kind, lam, source, first, acc, width):
-        def some(i, carry):
-            words = []
-            for u in range(width):
-                at = jnp.minimum(i * width + u, count_of(lists, side, kind) - 1)
-                words.append((word_of(lists, side, kind, i * width + u), first + at))
-            prods = [
-                jnp.dot(lam[(c >> 8) & 255], source[at], preferred_element_type=F32)
-                for c, at in words
-            ]
-            for (c, _), prod in zip(words, prods):
-                acc[c >> 16] += prod
-            return carry
-
-        lax.fori_loop(0, (count_of(lists, side, kind) + width - 1) // width, some, 0)
+        finish_copies(keep_own + keep_other, own, kept, sems.at[0])
+        icar_copy.wait()
+        lam_copy.wait()
+        hi_copy.wait()
 
     tiles = [(own, VM), (other, VM)]
     rim_type = array((rim, cases, nodes), BF16)
@@ -461,31 +505,31 @@
         scratch=[sums],
     )
     arriving = lax.ppermute(leaving, "blk", onward)
-    lam, acc_rim, hi_next, sent, icar = kernel(
+    lam_low, acc_rim, sent, kept, icar, lam_high, hi_next = kernel(
         with_lists(main_body),
         (
-            array(state, F32),
+            low_type,
             array((rim, cases, nodes), F32),
-            array(padded, BF16),
             array((network, 3, slots, nodes), BF16),
+            array((KEEP, nodes, nodes), BF16),
             hbm_array(state, F32),
+            hbm_array((blocks - low, cases, nodes), F32),
+            hbm_array(padded, BF16),
         ),
         listed
-        + [
-            (distribution_entry_holder.reshape(1, heads), VM),
-            (distribution_entry_substation.reshape(1, heads), VM),
-            (theirs, VM),
-            (leaving, VM),
-        ]
+        + [(distribution_entry_substation.reshape(1, heads), VM), (theirs, VM), (leaving, VM)]
         + [(low_rows, VM), (lam, VM), (lo, VM), (hi, VM), (acc, VM), (icar, VM)]
         + tiles
-        + [(hot, VM), (head0, VM), (decay, VM), (inflow, VM)],
+        + [(hot, VM), (hot_next, VM), (head0, VM), (place, VM), (place_next, VM)]
+        + [(decay, VM), (inflow, VM)],
         scratch=[
             pltpu.VMEM(state, F32),
             pltpu.VMEM(half, BF16),
-            pltpu.SemaphoreType.DMA,
+            pltpu.VMEM(state, F32),
+            pltpu.VMEM(padded, BF16),
+            pltpu.SemaphoreType.DMA((4,)),
         ],
-        out_specs=(VM,) * 4 + (HB,),
+        out_specs=(VM,) * 4 + (HB,) * 3,
     )
     received = lax.all_to_all(
         sent.reshape(network, 3 * slots, nodes),
@@ -500,17 +544,17 @@
     leaving, low_rows, lo = kernel(
         with_lists(rim_last_body),
         (rim_type, low_type, array(padded, BF16)),
-        listed + [(arriving, VM), (lam, VM), (acc_rim, VM)] + stored_in,
-        scratch=[sums, pltpu.VMEM(fetched_shape, BF16), pltpu.SemaphoreType.DMA((2,))],
+        listed + [(arriving, VM), (lam_low, VM), (acc_rim, VM), (kept, VM)] + stored_in,
+        scratch=[sums, pltpu.VMEM(fetched_shape, BF16), pltpu.SemaphoreType.DMA],
     )
     arriving = lax.ppermute(leaving, "blk", onward)
 
     def main_last_body(
-        lists, low_rows, lam, lo, hi, decay, inflow, outflow, own, other, icar,
+        lists, low_rows, lam_high, lo, hi, decay, inflow, outflow, own, other, icar,
         lam_out, low_next, icar_out, lam_next, icar_next, sems,
     ):
         for b in range(blocks):
-            row = low_rows[b] if b < low else lam[b]
+            row = low_rows[b] if b < low else lam_high[b - low]
             before = icar[b]
             lam_next[b] = outflow[b : b + 1, :] * before
             icar_next[b] = decay[b : b + 1, :] * before + inflow[b : b + 1, :] * row
@@ -529,7 +573,7 @@
         with_lists(main_last_body),
         (hbm_array(state, F32), low_type, hbm_array(state, F32)),
         listed
-        + [(low_rows, VM), (lam, VM), (lo, VM), (hi_next, VM)]
+        + [(low_rows, VM), (lam_high, VM), (lo, VM), (hi_next, VM)]
         + [(decay, VM), (inflow, VM), (outflow, VM)]
         + [(derivative_tiles, VM), (other_kept, VM), (icar, VM)],
         scratch=[

time: 52.5 us -> 55.4 us (1.055)
  waiting for transfers between devices: 5.44 us -> 11.3 us
  starting transfers between devices: 18.6 us -> 15.3 us
    all_to_all x1, waiting for transfers between devices: 0.01 us -> 6.42 us  [local(): lax.all_to_all(sent.reshape(network, 3 * slots, nodes), ('sec', 'blk'), s...]
    ppermute x3, waiting for transfers between devices: 2.57 us -> 0.01 us  [local(): arriving = lax.ppermute(leaving, 'blk', onward)]
    ppermute x1, waiting for transfers between devices: 1.72 us -> 3.76 us  [local(): theirs = lax.ppermute(mine, 'blk', backward)]
    ppermute x1, starting transfers between devices: 3.56 us -> 1.54 us  [local(): theirs = lax.ppermute(mine, 'blk', backward)]
    ppermute x3, starting transfers between devices: 6.35 us -> 5.59 us  [local(): arriving = lax.ppermute(leaving, 'blk', onward)]
    pallas_call x10 -> x11, Pallas kernels: 27.4 us -> 27.6 us  [kernel(): pl.pallas_call(body, out_shape=outs, in_specs=[spec for _, spec in ins],...]
  transfers between devices with their start and end apart: 8 -> 8, of which waited for: 4 -> 3; matrix products, arithmetic and copies ran while one was open for 0% -> 0% of each run, Pallas kernels for 46% -> 44%
where the time goes in v7:
time: 55.4 us; the launch traced here: 55.1 us
  Pallas kernels  27.6 us (50%)
  starting transfers between devices  15.3 us (28%)
  waiting for transfers between devices  11.3 us (20%)
  between operations  0.84 us (2%)
    pallas_call x11, Pallas kernels, kernel(): pl.pallas_call(body, out_shape=outs, in_specs=[spec for _, spec in ins],...  27.6 us
    all_to_all x1, starting transfers between devices, local(): lax.all_to_all(sent.reshape(network, 3 * slots, nodes), ('sec', 'blk'), s...  7.14 us
    all_to_all x1, waiting for transfers between devices, local(): lax.all_to_all(sent.reshape(network, 3 * slots, nodes), ('sec', 'blk'), s...  6.42 us
    ppermute x3, starting transfers between devices, local(): arriving = lax.ppermute(leaving, 'blk', onward)  5.59 us
    ppermute x1, waiting for transfers between devices, local(): theirs = lax.ppermute(mine, 'blk', backward)  3.76 us
    ppermute x1, starting transfers between devices, local(): theirs = lax.ppermute(mine, 'blk', backward)  1.54 us
    ppermute x1, waiting for transfers between devices, local(): other_rows = lax.ppermute(tile_source_index, 'case', swap)  1.14 us
  transfers between devices with their start and end apart: 8, of which 3 were waited for; matrix products, arithmetic and copies ran while one was open for 0% of the time, Pallas kernels for 44%

profile of v7, /device:TPU:0, one launch (start us, length us, event | category | flops | bytes accessed | tf_op | source)
XLA Modules:
  0.0 55.1 jit_solution(2224592007705617888)
XLA Ops:
  0.6 0.6 %collective-permute-start.2 = (bf16[96,128,128]{2,1,0:T(8,128)(2,1)}, bf16[96,128,128]{2,1,0:T(8,128)(2,1)S(1)}, u32[]{:S(2)}, u32[]{:S(2)}) collective-permute-start(bf16[96,128,128]{2,1,0:T(8,128)(2,1)} %refs_7_.3), channel_id=1, source_target_pairs={{0,1},{1,0},{2,3},{3,2},{4,5},{5,4},{6,7},{7,6},{8,9},{9,8},{10,11... | collective-permute-start | bytes 9437192 | tf_op jit(solution)/shard_map/ppermute | solution.py:95
  1.2 0.1 collective-permute-start
  1.3 0.4 collective-permute-start.1
  1.7 3.8 %shard_map.148 = (f32[48,64,128]{2,1,0:T(8,128)S(1)}, bf16[17,64,128]{2,1,0:T(8,128)(2,1)S(1)}, bf16[17,64,128]{2,1,0:T(8,128)(2,1)S(1)}, bf16[96,128,128]{2,1,0:T(8,128)(2,1)S(1)}, s32[1,640]{1,0:T(1,128)S(1)}) custom-call(s32[96]{0:T(128)} %rows.1, s32[96]{0:T(128)} %columns.1, s32[1,96]{1,0:T(1,128)} %bitcast.18, s32[1,96]{1,0:T(1,128)} %bitcast.19, ...), custom_call_target="tpu_custom_call" | custom-call | tf_op jit(solution)/shard_map/pallas_call | solution.py:26
  5.5 0.0 copy-start.5
  5.5 0.0 copy-start.6
  5.5 0.0 copy-start.7
  5.5 1.1 %collective-permute-done = s32[96]{0:T(128)S(1)} collective-permute-done((s32[96]{0:T(128)}, s32[96]{0:T(128)S(1)}, u32[]{:S(2)}, u32[]{:S(2)}) %collective-permute-start) | collective-permute-done | bytes 416 | tf_op jit(solution)/shard_map/ppermute | solution.py:93
  6.7 0.0 collective-permute-done.1
  6.7 0.4 shard_map.149.other
  7.1 0.0 collective-permute-done.2.refs_3_.refs_4_.refs_10_
  7.1 1.2 %shard_map.150 = bf16[16,64,128]{2,1,0:T(8,128)(2,1)S(1)} custom-call(s32[1,640]{1,0:T(1,128)S(1)} %get-tuple-element.38.own, s32[1,640]{1,0:T(1,128)S(1)} %shard_map.149.other, f32[48,64,128]{2,1,0:T(8,128)S(1)} %get-tuple-element.39.refs_0_, bf16[17,64,128]{2,1,0:T(8,128)(2,1)S(1)} %get-tuple-element.40.refs_1_.lo, ...), custom_call_target="tpu_custom_call" | custom-call | tf_op jit(solution)/shard_map/pallas_call | solution.py:26
  8.4 3.6 %collective-permute-start.3 = (bf16[16,64,128]{2,1,0:T(8,128)(2,1)S(1)}, bf16[16,64,128]{2,1,0:T(8,128)(2,1)S(1)}, u32[]{:S(2)}, u32[]{:S(2)}) collective-permute-start(bf16[16,64,128]{2,1,0:T(8,128)(2,1)S(1)} %shard_map.150), channel_id=1, source_target_pairs={{0,2},{2,4},{4,6},{6,0},{1,3},{3,5},{5,7},{7,1},{8,10},{10,12},{12... | collective-permute-start | bytes 786440 | tf_op jit(solution)/shard_map/ppermute | solution.py:295
  11.9 0.0 copy-done.5
  11.9 0.0 copy-done.6
  11.9 0.0 copy-done.7
  11.9 1.5 %collective-permute-start.4 = (s32[1,384]{1,0:T(1,128)S(1)}, s32[1,384]{1,0:T(1,128)S(1)}, u32[]{:S(2)}, u32[]{:S(2)}) collective-permute-start(s32[1,384]{1,0:T(1,128)S(1)} %pad_add_fusion), channel_id=1, source_target_pairs={{2,0},{4,2},{6,4},{0,6},{3,1},{5,3},{7,5},{1,7},{10,8},{12,10},{14... | collective-permute-start | bytes 4616 | tf_op jit(solution)/shard_map/ppermute | solution.py:278
  13.5 3.8 %collective-permute-done.4.refs_5_.refs_1_ = s32[1,384]{1,0:T(1,128)S(1)} collective-permute-done((s32[1,384]{1,0:T(1,128)S(1)}, s32[1,384]{1,0:T(1,128)S(1)}, u32[]{:S(2)}, u32[]{:S(2)}) %collective-permute-start.4) | collective-permute-done | bytes 1568 | tf_op jit(solution)/shard_map/ppermute | solution.py:278
  17.2 6.1 %shard_map.151 = (f32[32,64,128]{2,1,0:T(8,128)S(1)}, f32[32,64,128]{2,1,0:T(8,128)S(1)}, f32[16,64,128]{2,1,0:T(8,128)S(1)}, bf16[17,64,128]{2,1,0:T(8,128)(2,1...) custom-call(s32[1,640]{1,0:T(1,128)S(1)} %get-tuple-element.38.own, ...), custom_call_target="tpu_custom_call" | custom-call | tf_op jit(solution)/shard_map/pallas_call | solution.py:26
  23.4 0.0 collective-permute-done.3.refs_0_
  23.4 1.3 %shard_map.152 = (bf16[16,64,128]{2,1,0:T(8,128)(2,1)S(1)}, f32[16,64,128]{2,1,0:T(8,128)S(1)}, bf16[17,64,128]{2,1,0:T(8,128)(2,1)S(1)}) custom-call(s32[1,640]{1,0:T(1,128)S(1)} %get-tuple-element.38.own, s32[1,640]{1,0:T(1,128)S(1)} %shard_map.149.other, bf16[16,64,128]{2,1,0:T(8,128)(2,1)S(1)} %collective-permute-done.3.refs_0_, ...), custom_call_target="tpu_custom_call" | custom-call | tf_op jit(solution)/shard_map/pallas_call | solution.py:26
  24.7 0.1 collective-permute-start.5
  24.8 0.5 shard_map.153
  25.3 5.7 %shard_map.154 = (f32[16,64,128]{2,1,0:T(8,128)S(1)}, f32[16,64,128]{2,1,0:T(8,128)S(1)}, bf16[16,3,16,128]{3,2,1,0:T(8,128)(2,1)}, bf16[44,128,128]{2,1,0:T(8,1...) custom-call(s32[1,640]{1,0:T(1,128)S(1)} %get-tuple-element.38.own, ...), custom_call_target="tpu_custom_call" | custom-call | tf_op jit(solution)/shard_map/pallas_call | solution.py:26
  31.1 7.1 %all-to-all-start = ((bf16[16,48,128]{2,1,0:T(8,128)(2,1)}), bf16[16,48,128]{2,1,0:T(8,128)(2,1)S(1)}, u32[]{:S(2)}, u32[]{:S(2)}) async-start(bf16[16,48,128]{2,1,0:T(8,128)(2,1)} %bitcast.7), calls=%async_computation | async-start | bytes 393216 | tf_op jit(solution)/shard_map/all_to_all | solution.py:534
  38.2 0.0 collective-permute-done.5.refs_0_
  38.2 0.0 copy-start
  38.2 0.0 copy-start.1
  38.3 0.0 copy-start.2
  38.3 0.0 copy-start.3
  38.3 0.0 copy-start.4
  38.3 1.3 %shard_map.155 = (bf16[16,64,128]{2,1,0:T(8,128)(2,1)S(1)}, f32[16,64,128]{2,1,0:T(8,128)S(1)}, bf16[17,64,128]{2,1,0:T(8,128)(2,1)S(1)}) custom-call(s32[1,640]{1,0:T(1,128)S(1)} %get-tuple-element.38.own, s32[1,640]{1,0:T(1,128)S(1)} %shard_map.149.other, bf16[16,64,128]{2,1,0:T(8,128)(2,1)S(1)} %collective-permute-done.5.refs_0_, ...), custom_call_target="tpu_custom_call" | custom-call | tf_op jit(solution)/shard_map/pallas_call | solution.py:26
  39.6 2.0 %collective-permute-start.6 = (bf16[16,64,128]{2,1,0:T(8,128)(2,1)S(1)}, bf16[16,64,128]{2,1,0:T(8,128)(2,1)S(1)}, u32[]{:S(2)}, u32[]{:S(2)}) collective-permute-start(bf16[16,64,128]{2,1,0:T(8,128)(2,1)S(1)} %get-tuple-element.62), channel_id=1, source_target_pairs={{0,2},{2,4},{4,6},{6,0},{1,3},{3,5},{5,7},{7,1},{8,10},{10,12},{12... | collective-permute-start | bytes 786440 | tf_op jit(solution)/shard_map/ppermute | solution.py:550
  41.5 0.0 copy-done
  41.5 0.0 copy-done.1
  41.5 0.0 copy-done.2
  41.5 0.0 copy-done.3
  41.6 0.0 copy-done.4
  41.6 4.2 %shard_map.156 = (f32[32,64,128]{2,1,0:T(8,128)}, f32[16,64,128]{2,1,0:T(8,128)S(1)}, f32[32,64,128]{2,1,0:T(8,128)}) custom-call(s32[1,640]{1,0:T(1,128)S(1)} %get-tuple-element.38.own, s32[1,640]{1,0:T(1,128)S(1)} %shard_map.149.other, f32[16,64,128]{2,1,0:T(8,128)S(1)} %get-tuple-element.63.refs_0_, f32[16,64,128]{2,1,0:T(8,128)S(1)} %copy-done.3, ...), custom_call_target="tpu_custom_call" | custom-call | tf_op jit(solution)/shard_map/pallas_call | solution.py:26
  45.7 6.4 %all-to-all-done = bf16[16,48,128]{2,1,0:T(8,128)(2,1)S(1)} async-done(((bf16[16,48,128]{2,1,0:T(8,128)(2,1)}), bf16[16,48,128]{2,1,0:T(8,128)(2,1)S(1)}, u32[]{:S(2)}, u32[]{:S(2)}) %all-to-all-start) | async-done | bytes 196640 | tf_op jit(solution)/shard_map/all_to_all | solution.py:534
  52.1 2.1 %shard_map.158 = f32[64,256]{1,0:T(8,128)} custom-call(bf16[768,128]{1,0:T(8,128)(2,1)S(1)} %bitcast.9, f32[64,256]{1,0:T(8,128)} %trans_in.1, bf16[256,256]{1,0:T(8,128)(2,1)} %matrix_in.1), custom_call_target="tpu_custom_call" | custom-call | tf_op jit(solution)/shard_map/pallas_call | solution.py:26
  54.3 0.0 collective-permute-done.6.arrived
  54.3 0.8 %shard_map.157 = f32[32,64,128]{2,1,0:T(8,128)} custom-call(bf16[16,64,128]{2,1,0:T(8,128)(2,1)S(1)} %collective-permute-done.6.arrived, f32[16,64,128]{2,1,0:T(8,128)S(1)} %get-tuple-element.69.low_next, f32[32,64,128]{2,1,0:T(8,128)} %get-tuple-element.70.lam_in), custom_call_target="tpu_custom_call", output_to_operand_aliasing={{}: (2, {})} | custom-call | tf_op jit(solution)/shard_map/pallas_call | solution.py:26
  (1 shorter events, 0.0 us)
Async XLA Ops:
  0.6 6.5 %collective-permute-start.2 = (bf16[96,128,128]{2,1,0:T(8,128)(2,1)}, bf16[96,128,128]{2,1,0:T(8,128)(2,1)S(1)}, u32[]{:S(2)}, u32[]{:S(2)}) collective-permute-start(bf16[96,128,128]{2,1,0:T(8,128)(2,1)} %refs_7_.3), channel_id=1, source_target_pairs={{0,1},{1,0},{2,3},{3,2},{4,5},{5,4},{6,7},{7,6},{8,9},{9,8},{10,11... | collective-permute-start | bytes 9437192 | tf_op jit(solution)/shard_map/ppermute | solution.py:95
  1.2 5.5 %collective-permute-start = (s32[96]{0:T(128)}, s32[96]{0:T(128)S(1)}, u32[]{:S(2)}, u32[]{:S(2)}) collective-permute-start(s32[96]{0:T(128)} %rows.1), channel_id=1, source_target_pairs={{0,1},{1,0},{2,3},{3,2},{4,5},{5,4},{6,7},{7,6},{8,9},{9,8},{10,11... | collective-permute-start | bytes 1160 | tf_op jit(solution)/shard_map/ppermute | solution.py:93
  1.3 5.4 %collective-permute-start.1 = (s32[96]{0:T(128)}, s32[96]{0:T(128)S(1)}, u32[]{:S(2)}, u32[]{:S(2)}) collective-permute-start(s32[96]{0:T(128)} %columns.1), channel_id=1, source_target_pairs={{0,1},{1,0},{2,3},{3,2},{4,5},{5,4},{6,7},{7,6},{8,9},{9,8},{10,11... | collective-permute-start | bytes 1160 | tf_op jit(solution)/shard_map/ppermute | solution.py:94
  5.5 6.4 %copy-start.5 = (s32[128]{0:T(128)S(1)}, s32[128]{0:T(128)}, u32[]{:S(2)}) copy-start(s32[128]{0:T(128)} %param.24) | copy-start | bytes 1540
  5.5 6.4 %copy-start.6 = (s32[128,1]{0,1:T(1,128)S(1)}, s32[128,1]{0,1:T(1,128)}, u32[]{:S(2)}) copy-start(s32[128,1]{0,1:T(1,128)} %param.23) | copy-start | bytes 1540
  5.5 6.4 %copy-start.7 = (s32[128]{0:T(128)S(1)}, s32[128]{0:T(128)}, u32[]{:S(2)}) copy-start(s32[128]{0:T(128)} %param.22) | copy-start | bytes 1540
  8.4 15.0 %collective-permute-start.3 = (bf16[16,64,128]{2,1,0:T(8,128)(2,1)S(1)}, bf16[16,64,128]{2,1,0:T(8,128)(2,1)S(1)}, u32[]{:S(2)}, u32[]{:S(2)}) collective-permute-start(bf16[16,64,128]{2,1,0:T(8,128)(2,1)S(1)} %shard_map.150), channel_id=1, source_target_pairs={{0,2},{2,4},{4,6},{6,0},{1,3},{3,5},{5,7},{7,1},{8,10},{10,12},{12... | collective-permute-start | bytes 786440 | tf_op jit(solution)/shard_map/ppermute | solution.py:295
  11.9 5.3 %collective-permute-start.4 = (s32[1,384]{1,0:T(1,128)S(1)}, s32[1,384]{1,0:T(1,128)S(1)}, u32[]{:S(2)}, u32[]{:S(2)}) collective-permute-start(s32[1,384]{1,0:T(1,128)S(1)} %pad_add_fusion), channel_id=1, source_target_pairs={{2,0},{4,2},{6,4},{0,6},{3,1},{5,3},{7,5},{1,7},{10,8},{12,10},{14... | collective-permute-start | bytes 4616 | tf_op jit(solution)/shard_map/ppermute | solution.py:278
  24.7 13.5 %collective-permute-start.5 = (bf16[16,64,128]{2,1,0:T(8,128)(2,1)S(1)}, bf16[16,64,128]{2,1,0:T(8,128)(2,1)S(1)}, u32[]{:S(2)}, u32[]{:S(2)}) collective-permute-start(bf16[16,64,128]{2,1,0:T(8,128)(2,1)S(1)} %get-tuple-element.45.refs_2_), channel_id=1, source_target_pairs={{0,2},{2,4},{4,6},{6,0},{1,3},{3,5},{5,7},{7,1},{8,10},{10,12},{12... | collective-permute-start | bytes 786440 | tf_op jit(solution)/shard_map/ppermute | solution.py:507
  31.1 21.1 %all-to-all-start = ((bf16[16,48,128]{2,1,0:T(8,128)(2,1)}), bf16[16,48,128]{2,1,0:T(8,128)(2,1)S(1)}, u32[]{:S(2)}, u32[]{:S(2)}) async-start(bf16[16,48,128]{2,1,0:T(8,128)(2,1)} %bitcast.7), calls=%async_computation | async-start | bytes 393216 | tf_op jit(solution)/shard_map/all_to_all | solution.py:534
  38.2 3.3 %copy-start = (bf16[96,128,128]{2,1,0:T(8,128)(2,1)S(1)}, bf16[96,128,128]{2,1,0:T(8,128)(2,1)}, u32[]{:S(2)}) copy-start(bf16[96,128,128]{2,1,0:T(8,128)(2,1)} %refs_7_.3) | copy-start | bytes 9437188
  38.2 3.3 %copy-start.1 = (bf16[96,128,128]{2,1,0:T(8,128)(2,1)S(1)}, bf16[96,128,128]{2,1,0:T(8,128)(2,1)}, u32[]{:S(2)}) copy-start(bf16[96,128,128]{2,1,0:T(8,128)(2,1)} %get-tuple-element.61.refs_5_.refs_8_) | copy-start | bytes 9437188
  38.3 3.3 %copy-start.2 = (f32[32,64,128]{2,1,0:T(8,128)S(1)}, f32[32,64,128]{2,1,0:T(8,128)}, u32[]{:S(2)}) copy-start(f32[32,64,128]{2,1,0:T(8,128)} %get-tuple-element.68.refs_9_) | copy-start | bytes 3145732
  38.3 3.3 %copy-start.3 = (f32[16,64,128]{2,1,0:T(8,128)S(1)}, f32[16,64,128]{2,1,0:T(8,128)}, u32[]{:S(2)}) copy-start(f32[16,64,128]{2,1,0:T(8,128)} %get-tuple-element.64.refs_1_) | copy-start | bytes 1572868
  38.3 3.3 %copy-start.4 = (bf16[17,64,128]{2,1,0:T(8,128)(2,1)S(1)}, bf16[17,64,128]{2,1,0:T(8,128)(2,1)}, u32[]{:S(2)}) copy-start(bf16[17,64,128]{2,1,0:T(8,128)(2,1)} %get-tuple-element.66.refs_3_) | copy-start | bytes 835588
  39.6 14.7 %collective-permute-start.6 = (bf16[16,64,128]{2,1,0:T(8,128)(2,1)S(1)}, bf16[16,64,128]{2,1,0:T(8,128)(2,1)S(1)}, u32[]{:S(2)}, u32[]{:S(2)}) collective-permute-start(bf16[16,64,128]{2,1,0:T(8,128)(2,1)S(1)} %get-tuple-element.62), channel_id=1, source_target_pairs={{0,2},{2,4},{4,6},{6,0},{1,3},{3,5},{5,7},{7,1},{8,10},{10,12},{12... | collective-permute-start | bytes 786440 | tf_op jit(solution)/shard_map/ppermute | solution.py:550

commit v8 on v7

--- a/solution.py
+++ b/solution.py
@@ -267,15 +267,6 @@
         (array(hot_shape, BF16), array((cases, heads), BF16), place_type),
         [(distribution_entry_vertex.reshape(1, heads), VM), (own_owner, VM), (lo, VM), (hi, VM)],
     )
-    mine = jnp.concatenate(
-        [
-            distribution_entry_vertex.reshape(1, heads),
-            own_owner,
-            distribution_entry_substation.reshape(1, heads),
-        ],
-        axis=1,
-    )
-    theirs = lax.ppermute(mine, "blk", backward)
 
     def rim_first_body(lists, acc, lo, hi, other, out, sums):
         sums[...] = acc[blocks:]
@@ -293,6 +284,16 @@
         scratch=[pltpu.VMEM((rim, cases, nodes), F32)],
     )
     arriving = lax.ppermute(leaving, "blk", onward)
+
+    mine = jnp.concatenate(
+        [
+            distribution_entry_vertex.reshape(1, heads),
+            own_owner,
+            distribution_entry_substation.reshape(1, heads),
+        ],
+        axis=1,
+    )
+    theirs = lax.ppermute(mine, "blk", backward)
 
     def begin_next(lists, lam, icar, outflow, own, other, acc, acc_rim, hi):
         for b in range(blocks):
@@ -306,8 +307,8 @@
         run(lists, [((0, 2), hi, own, acc), ((1, 2), hi, other, acc)], MANY)
 
     def main_first_body(
-        lists, acc, lo, hi, own, other, theirs, lam_in, icar_in, decay_in, inflow_in, outflow_in,
-        lam_next, acc_next, acc_rim, hi_next, icar_next, hot_next, place_next, decay, inflow, outflow, other_kept,
+        lists, acc, lo, hi, own, other, lam_in, icar_in, decay_in, inflow_in, outflow_in,
+        lam_next, acc_next, acc_rim, hi_next, icar_next, decay, inflow, outflow, other_kept,
         lam, icar, sems,
     ):
         pairs = [
@@ -331,15 +332,10 @@
         begin_next(
             lists, lam_next, icar_next, outflow, own, other, acc_next, acc_rim, hi_next
         )
-        followed = lax.axis_index("blk") < owners - 1
-        one_hots(theirs[:, :heads], low, hot_next)
-        place_rows(theirs[:, heads : 2 * heads], followed, place_next)
         kept.wait()
 
     factor = array(factor_shape, F32)
-    (
-        lam, acc, acc_rim, hi_next, icar, hot_next, place_next, decay, inflow, outflow, other_kept
-    ) = kernel(
+    lam, acc, acc_rim, hi_next, icar, decay, inflow, outflow, other_kept = kernel(
         with_lists(main_first_body),
         (
             array(state, F32),
@@ -347,8 +343,6 @@
             array((rim, cases, nodes), F32),
             array(padded, BF16),
             array(state, F32),
-            array((low, nodes, heads), BF16),
-            place_type,
             factor,
             factor,
             factor,
@@ -356,11 +350,10 @@
         ),
         listed
         + [(acc, VM), (lo, VM), (hi, VM), (own, VM), (other, VM)]
-        + [(theirs, VM)]
         + [(vertex_costate, HB), (inverter_costate, HB), (inverter_decay_factor, HB)]
         + [(costate_to_inverter_factor, HB), (inverter_to_costate_factor, HB)],
         scratch=[pltpu.VMEM(state, F32), pltpu.VMEM(state, F32), pltpu.SemaphoreType.DMA((6,))],
-        out_specs=(VM,) * 10 + (HB,),
+        out_specs=(VM,) * 8 + (HB,),
     )
 
     def take_arrived(arrived, lam, low_rows, lo):
@@ -439,23 +432,21 @@
 
     def main_body(
         lists, bus, theirs, left, low_rows, lam, lo, hi, acc, icar, own, other,
-        hot, hot_next, head0, place, place_next, decay, inflow,
+        hot, head0, place, decay, inflow,
         lam_low, acc_rim, sent, kept, icar_out, lam_out, hi_out,
-        icar_next, lo_base, lam_next, hi_next, sems,
+        icar_next, lo_base, lam_next, hi_next, hot_next, place_next, sems,
     ):
         keep_own = jnp.minimum(count_of(lists, 0, 1), KEEP)
         keep_other = jnp.minimum(count_of(lists, 1, 1), KEEP - keep_own)
-        start_copies(lists, 0, 1, 0, keep_own, own, kept, 0, sems.at[0])
-        start_copies(lists, 1, 1, 0, keep_other, other, kept, keep_own, sems.at[0])
         for b in range(blocks):
             row = low_rows[b] if b < low else lam[b]
             icar_next[b] = decay[b : b + 1, :] * icar[b] + inflow[b : b + 1, :] * row
-        icar_copy = pltpu.make_async_copy(icar_next, icar_out, sems.at[1])
+        icar_copy = pltpu.make_async_copy(icar_next, icar_out, sems.at[0])
         icar_copy.start()
         lam_next[...] = acc[...]
         run(lists, [((0, 3), lo, own, lam_next), ((1, 3), lo, other, lam_next)], MANY)
         upper = pl.ds(low, blocks - low)
-        lam_copy = pltpu.make_async_copy(lam_next.at[upper], lam_out, sems.at[2])
+        lam_copy = pltpu.make_async_copy(lam_next.at[upper], lam_out, sems.at[1])
         lam_copy.start()
         for b in range(low):
             lam_low[b] = lam_next[b]
@@ -463,10 +454,13 @@
         for b in range(low, blocks):
             hi_next[b - low] = lam_next[b].astype(BF16)
         hi_next[blocks - low] = jnp.zeros((cases, nodes), BF16)
-        hi_copy = pltpu.make_async_copy(hi_next, hi_out, sems.at[3])
+        hi_copy = pltpu.make_async_copy(hi_next, hi_out, sems.at[2])
         hi_copy.start()
         acc_rim[...] = jnp.zeros(acc_rim.shape, F32)
         run(lists, [((0, 0), hi_next, own, acc_rim), ((1, 0), hi_next, other, acc_rim)], FEW)
+        followed = lax.axis_index("blk") < owners - 1
+        one_hots(theirs[:, :heads], low, hot_next)
+        place_rows(theirs[:, heads : 2 * heads], followed, place_next)
         head_next = jnp.dot(left[0], hot_next[0], preferred_element_type=F32)
         for b in range(1, low):
             head_next += jnp.dot(left[b], hot_next[b], preferred_element_type=F32)
@@ -487,7 +481,17 @@
                 preferred_element_type=F32,
             )
             sent[:, i] = part.astype(BF16).reshape(network, slots, nodes)
-        finish_copies(keep_own + keep_other, own, kept, sems.at[0])
+
+        def keep_own_block(i, carry):
+            kept[i] = own[word_of(lists, 0, 1, i) & 255]
+            return carry
+
+        def keep_other_block(i, carry):
+            kept[keep_own + i] = other[word_of(lists, 1, 1, i) & 255]
+            return carry
+
+        lax.fori_loop(0, keep_own, keep_own_block, 0)
+        lax.fori_loop(0, keep_other, keep_other_block, 0)
         icar_copy.wait()
         lam_copy.wait()
         hi_copy.wait()
@@ -520,14 +524,16 @@
         + [(distribution_entry_substation.reshape(1, heads), VM), (theirs, VM), (leaving, VM)]
         + [(low_rows, VM), (lam, VM), (lo, VM), (hi, VM), (acc, VM), (icar, VM)]
         + tiles
-        + [(hot, VM), (hot_next, VM), (head0, VM), (place, VM), (place_next, VM)]
+        + [(hot, VM), (head0, VM), (place, VM)]
         + [(decay, VM), (inflow, VM)],
         scratch=[
             pltpu.VMEM(state, F32),
             pltpu.VMEM(half, BF16),
             pltpu.VMEM(state, F32),
             pltpu.VMEM(padded, BF16),
-            pltpu.SemaphoreType.DMA((4,)),
+            pltpu.VMEM((low, nodes, heads), BF16),
+            pltpu.VMEM(place_type.shape, BF16),
+            pltpu.SemaphoreType.DMA((3,)),
         ],
         out_specs=(VM,) * 4 + (HB,) * 3,
     )

time: 55.4 us -> 55.9 us (level)
  starting transfers between devices: 15.3 us -> 18.1 us
  Pallas kernels: 27.6 us -> 26.1 us
  waiting for transfers between devices: 11.3 us -> 10.6 us
    ppermute x1, waiting for transfers between devices: 3.76 us -> 1.19 us  [local(): theirs = lax.ppermute(mine, 'blk', backward)]
    ppermute x1, starting transfers between devices: 1.54 us -> 3.59 us  [local(): theirs = lax.ppermute(mine, 'blk', backward)]
    ppermute x3, waiting for transfers between devices: 0.01 us -> 2.04 us  [local(): arriving = lax.ppermute(leaving, 'blk', onward)]
    pallas_call x11, Pallas kernels: 27.6 us -> 26.1 us  [kernel(): pl.pallas_call(body, out_shape=outs, in_specs=[spec for _, spec in ins],...]
  transfers between devices with their start and end apart: 8 -> 8, of which waited for: 3 -> 4; matrix products, arithmetic and copies ran while one was open for 0% -> 0% of each run, Pallas kernels for 44% -> 41%
where the time goes in v8:
time: 55.9 us; the launch traced here: 55.6 us
  Pallas kernels  26.1 us (47%)
  starting transfers between devices  18.1 us (32%)
  waiting for transfers between devices  10.6 us (19%)
  between operations  0.8 us (1%)
    pallas_call x11, Pallas kernels, kernel(): pl.pallas_call(body, out_shape=outs, in_specs=[spec for _, spec in ins],...  26.1 us
    all_to_all x1, starting transfers between devices, local(): lax.all_to_all(sent.reshape(network, 3 * slots, nodes), ('sec', 'blk'), s...  7.56 us
    all_to_all x1, waiting for transfers between devices, local(): lax.all_to_all(sent.reshape(network, 3 * slots, nodes), ('sec', 'blk'), s...  6.23 us
    ppermute x3, starting transfers between devices, local(): arriving = lax.ppermute(leaving, 'blk', onward)  5.87 us
    ppermute x1, starting transfers between devices, local(): theirs = lax.ppermute(mine, 'blk', backward)  3.59 us
    ppermute x3, waiting for transfers between devices, local(): arriving = lax.ppermute(leaving, 'blk', onward)  2.04 us
    ppermute x1, waiting for transfers between devices, local(): theirs = lax.ppermute(mine, 'blk', backward)  1.19 us
    ppermute x1, waiting for transfers between devices, local(): other_rows = lax.ppermute(tile_source_index, 'case', swap)  1.18 us
  transfers between devices with their start and end apart: 8, of which 4 were waited for; matrix products, arithmetic and copies ran while one was open for 0% of the time, Pallas kernels for 41%

profile of v8, /device:TPU:0, one launch (start us, length us, event | category | flops | bytes accessed | tf_op | source)
XLA Modules:
  0.0 55.6 jit_solution(7072198197378035620)
XLA Ops:
  0.6 0.6 %collective-permute-start.2 = (bf16[96,128,128]{2,1,0:T(8,128)(2,1)}, bf16[96,128,128]{2,1,0:T(8,128)(2,1)S(1)}, u32[]{:S(2)}, u32[]{:S(2)}) collective-permute-start(bf16[96,128,128]{2,1,0:T(8,128)(2,1)} %refs_7_.3), channel_id=1, source_target_pairs={{0,1},{1,0},{2,3},{3,2},{4,5},{5,4},{6,7},{7,6},{8,9},{9,8},{10,11... | collective-permute-start | bytes 9437192 | tf_op jit(solution)/shard_map/ppermute | solution.py:95
  1.2 0.1 collective-permute-start
  1.3 0.4 collective-permute-start.1
  1.7 3.8 %shard_map.148 = (f32[48,64,128]{2,1,0:T(8,128)S(1)}, bf16[17,64,128]{2,1,0:T(8,128)(2,1)S(1)}, bf16[17,64,128]{2,1,0:T(8,128)(2,1)S(1)}, bf16[96,128,128]{2,1,0:T(8,128)(2,1)S(1)}, s32[1,640]{1,0:T(1,128)S(1)}) custom-call(s32[96]{0:T(128)} %rows.1, s32[96]{0:T(128)} %columns.1, s32[1,96]{1,0:T(1,128)} %bitcast.18, s32[1,96]{1,0:T(1,128)} %bitcast.19, ...), custom_call_target="tpu_custom_call" | custom-call | tf_op jit(solution)/shard_map/pallas_call | solution.py:26
  5.5 1.2 %collective-permute-done = s32[96]{0:T(128)S(1)} collective-permute-done((s32[96]{0:T(128)}, s32[96]{0:T(128)S(1)}, u32[]{:S(2)}, u32[]{:S(2)}) %collective-permute-start) | collective-permute-done | bytes 416 | tf_op jit(solution)/shard_map/ppermute | solution.py:93
  6.7 0.0 collective-permute-done.1
  6.7 0.4 shard_map.149.other
  7.1 0.0 collective-permute-done.2.refs_3_.refs_4_.refs_10_
  7.1 1.2 %shard_map.150 = bf16[16,64,128]{2,1,0:T(8,128)(2,1)S(1)} custom-call(s32[1,640]{1,0:T(1,128)S(1)} %get-tuple-element.36.own, s32[1,640]{1,0:T(1,128)S(1)} %shard_map.149.other, f32[48,64,128]{2,1,0:T(8,128)S(1)} %get-tuple-element.37.refs_0_, bf16[17,64,128]{2,1,0:T(8,128)(2,1)S(1)} %get-tuple-element.38.refs_1_.lo, ...), custom_call_target="tpu_custom_call" | custom-call | tf_op jit(solution)/shard_map/pallas_call | solution.py:26
  8.4 3.6 %collective-permute-start.3 = (bf16[16,64,128]{2,1,0:T(8,128)(2,1)S(1)}, bf16[16,64,128]{2,1,0:T(8,128)(2,1)S(1)}, u32[]{:S(2)}, u32[]{:S(2)}) collective-permute-start(bf16[16,64,128]{2,1,0:T(8,128)(2,1)S(1)} %shard_map.150), channel_id=1, source_target_pairs={{0,2},{2,4},{4,6},{6,0},{1,3},{3,5},{5,7},{7,1},{8,10},{10,12},{12... | collective-permute-start | bytes 786440 | tf_op jit(solution)/shard_map/ppermute | solution.py:286
  11.9 6.0 %shard_map.151 = (f32[32,64,128]{2,1,0:T(8,128)S(1)}, f32[32,64,128]{2,1,0:T(8,128)S(1)}, f32[16,64,128]{2,1,0:T(8,128)S(1)}, bf16[17,64,128]{2,1,0:T(8,128)(2,1...) custom-call(s32[1,640]{1,0:T(1,128)S(1)} %get-tuple-element.36.own, ...), custom_call_target="tpu_custom_call" | custom-call | tf_op jit(solution)/shard_map/pallas_call | solution.py:26
  17.9 2.0 %collective-permute-done.3.refs_0_ = bf16[16,64,128]{2,1,0:T(8,128)(2,1)S(1)} collective-permute-done((bf16[16,64,128]{2,1,0:T(8,128)(2,1)S(1)}, bf16[16,64,128]{2,1,0:T(8,128)(2,1)S(1)}, u32[]{:S(2)}, u32[]{:S(2)}) %collective-permute-start.3) | collective-permute-done | bytes 262176 | tf_op jit(solution)/shard_map/ppermute | solution.py:286
  20.0 0.0 copy-start.5
  20.0 0.0 copy-start.6
  20.0 0.0 copy-start.7
  20.0 1.3 %shard_map.152 = (bf16[16,64,128]{2,1,0:T(8,128)(2,1)S(1)}, f32[16,64,128]{2,1,0:T(8,128)S(1)}, bf16[17,64,128]{2,1,0:T(8,128)(2,1)S(1)}) custom-call(s32[1,640]{1,0:T(1,128)S(1)} %get-tuple-element.36.own, s32[1,640]{1,0:T(1,128)S(1)} %shard_map.149.other, bf16[16,64,128]{2,1,0:T(8,128)(2,1)S(1)} %collective-permute-done.3.refs_0_, ...), custom_call_target="tpu_custom_call" | custom-call | tf_op jit(solution)/shard_map/pallas_call | solution.py:26
  21.3 0.3 collective-permute-start.4
  21.6 0.0 copy-done.5
  21.6 0.0 copy-done.6
  21.6 0.0 copy-done.7
  21.6 3.6 %collective-permute-start.5 = (s32[1,384]{1,0:T(1,128)S(1)}, s32[1,384]{1,0:T(1,128)S(1)}, u32[]{:S(2)}, u32[]{:S(2)}) collective-permute-start(s32[1,384]{1,0:T(1,128)S(1)} %pad_add_fusion), channel_id=1, source_target_pairs={{2,0},{4,2},{6,4},{0,6},{3,1},{5,3},{7,5},{1,7},{10,8},{12,10},{14... | collective-permute-start | bytes 4616 | tf_op jit(solution)/shard_map/ppermute | solution.py:296
  25.2 0.5 shard_map.153
  25.8 1.2 %collective-permute-done.5.refs_1_ = s32[1,384]{1,0:T(1,128)S(1)} collective-permute-done((s32[1,384]{1,0:T(1,128)S(1)}, s32[1,384]{1,0:T(1,128)S(1)}, u32[]{:S(2)}, u32[]{:S(2)}) %collective-permute-start.5) | collective-permute-done | bytes 1568 | tf_op jit(solution)/shard_map/ppermute | solution.py:296
  27.0 4.4 %shard_map.154 = (f32[16,64,128]{2,1,0:T(8,128)S(1)}, f32[16,64,128]{2,1,0:T(8,128)S(1)}, bf16[16,3,16,128]{3,2,1,0:T(8,128)(2,1)}, bf16[44,128,128]{2,1,0:T(8,1...) custom-call(s32[1,640]{1,0:T(1,128)S(1)} %get-tuple-element.36.own, ...), custom_call_target="tpu_custom_call" | custom-call | tf_op jit(solution)/shard_map/pallas_call | solution.py:26
  31.4 7.6 %all-to-all-start = ((bf16[16,48,128]{2,1,0:T(8,128)(2,1)}), bf16[16,48,128]{2,1,0:T(8,128)(2,1)S(1)}, u32[]{:S(2)}, u32[]{:S(2)}) async-start(bf16[16,48,128]{2,1,0:T(8,128)(2,1)} %bitcast.7), calls=%async_computation | async-start | bytes 393216 | tf_op jit(solution)/shard_map/all_to_all | solution.py:540
  38.9 0.0 collective-permute-done.4.refs_0_
  38.9 0.0 copy-start
  39.0 0.0 copy-start.1
  39.0 0.0 copy-start.2
  39.0 0.0 copy-start.3
  39.0 0.0 copy-start.4
  39.0 1.3 %shard_map.155 = (bf16[16,64,128]{2,1,0:T(8,128)(2,1)S(1)}, f32[16,64,128]{2,1,0:T(8,128)S(1)}, bf16[17,64,128]{2,1,0:T(8,128)(2,1)S(1)}) custom-call(s32[1,640]{1,0:T(1,128)S(1)} %get-tuple-element.36.own, s32[1,640]{1,0:T(1,128)S(1)} %shard_map.149.other, bf16[16,64,128]{2,1,0:T(8,128)(2,1)S(1)} %collective-permute-done.4.refs_0_, ...), custom_call_target="tpu_custom_call" | custom-call | tf_op jit(solution)/shard_map/pallas_call | solution.py:26
  40.3 2.0 %collective-permute-start.6 = (bf16[16,64,128]{2,1,0:T(8,128)(2,1)S(1)}, bf16[16,64,128]{2,1,0:T(8,128)(2,1)S(1)}, u32[]{:S(2)}, u32[]{:S(2)}) collective-permute-start(bf16[16,64,128]{2,1,0:T(8,128)(2,1)S(1)} %get-tuple-element.58), channel_id=1, source_target_pairs={{0,2},{2,4},{4,6},{6,0},{1,3},{3,5},{5,7},{7,1},{8,10},{10,12},{12... | collective-permute-start | bytes 786440 | tf_op jit(solution)/shard_map/ppermute | solution.py:556
  42.3 0.0 copy-done
  42.3 0.0 copy-done.1
  42.3 0.0 copy-done.2
  42.3 0.0 copy-done.3
  42.3 0.0 copy-done.4
  42.3 4.2 %shard_map.156 = (f32[32,64,128]{2,1,0:T(8,128)}, f32[16,64,128]{2,1,0:T(8,128)S(1)}, f32[32,64,128]{2,1,0:T(8,128)}) custom-call(s32[1,640]{1,0:T(1,128)S(1)} %get-tuple-element.36.own, s32[1,640]{1,0:T(1,128)S(1)} %shard_map.149.other, f32[16,64,128]{2,1,0:T(8,128)S(1)} %get-tuple-element.59.refs_0_, f32[16,64,128]{2,1,0:T(8,128)S(1)} %copy-done.3, ...), custom_call_target="tpu_custom_call" | custom-call | tf_op jit(solution)/shard_map/pallas_call | solution.py:26
  46.4 6.2 %all-to-all-done = bf16[16,48,128]{2,1,0:T(8,128)(2,1)S(1)} async-done(((bf16[16,48,128]{2,1,0:T(8,128)(2,1)}), bf16[16,48,128]{2,1,0:T(8,128)(2,1)S(1)}, u32[]{:S(2)}, u32[]{:S(2)}) %all-to-all-start) | async-done | bytes 196640 | tf_op jit(solution)/shard_map/all_to_all | solution.py:540
  52.7 2.1 %shard_map.158 = f32[64,256]{1,0:T(8,128)} custom-call(bf16[768,128]{1,0:T(8,128)(2,1)S(1)} %bitcast.9, f32[64,256]{1,0:T(8,128)} %trans_in.1, bf16[256,256]{1,0:T(8,128)(2,1)} %matrix_in.1), custom_call_target="tpu_custom_call" | custom-call | tf_op jit(solution)/shard_map/pallas_call | solution.py:26
  54.8 0.0 collective-permute-done.6.arrived
  54.8 0.8 %shard_map.157 = f32[32,64,128]{2,1,0:T(8,128)} custom-call(bf16[16,64,128]{2,1,0:T(8,128)(2,1)S(1)} %collective-permute-done.6.arrived, f32[16,64,128]{2,1,0:T(8,128)S(1)} %get-tuple-element.65.low_next, f32[32,64,128]{2,1,0:T(8,128)} %get-tuple-element.66.lam_in), custom_call_target="tpu_custom_call", output_to_operand_aliasing={{}: (2, {})} | custom-call | tf_op jit(solution)/shard_map/pallas_call | solution.py:26
  (1 shorter events, 0.0 us)
Async XLA Ops:
  0.6 6.5 %collective-permute-start.2 = (bf16[96,128,128]{2,1,0:T(8,128)(2,1)}, bf16[96,128,128]{2,1,0:T(8,128)(2,1)S(1)}, u32[]{:S(2)}, u32[]{:S(2)}) collective-permute-start(bf16[96,128,128]{2,1,0:T(8,128)(2,1)} %refs_7_.3), channel_id=1, source_target_pairs={{0,1},{1,0},{2,3},{3,2},{4,5},{5,4},{6,7},{7,6},{8,9},{9,8},{10,11... | collective-permute-start | bytes 9437192 | tf_op jit(solution)/shard_map/ppermute | solution.py:95
  1.2 5.5 %collective-permute-start = (s32[96]{0:T(128)}, s32[96]{0:T(128)S(1)}, u32[]{:S(2)}, u32[]{:S(2)}) collective-permute-start(s32[96]{0:T(128)} %rows.1), channel_id=1, source_target_pairs={{0,1},{1,0},{2,3},{3,2},{4,5},{5,4},{6,7},{7,6},{8,9},{9,8},{10,11... | collective-permute-start | bytes 1160 | tf_op jit(solution)/shard_map/ppermute | solution.py:93
  1.3 5.4 %collective-permute-start.1 = (s32[96]{0:T(128)}, s32[96]{0:T(128)S(1)}, u32[]{:S(2)}, u32[]{:S(2)}) collective-permute-start(s32[96]{0:T(128)} %columns.1), channel_id=1, source_target_pairs={{0,1},{1,0},{2,3},{3,2},{4,5},{5,4},{6,7},{7,6},{8,9},{9,8},{10,11... | collective-permute-start | bytes 1160 | tf_op jit(solution)/shard_map/ppermute | solution.py:94
  8.4 11.6 %collective-permute-start.3 = (bf16[16,64,128]{2,1,0:T(8,128)(2,1)S(1)}, bf16[16,64,128]{2,1,0:T(8,128)(2,1)S(1)}, u32[]{:S(2)}, u32[]{:S(2)}) collective-permute-start(bf16[16,64,128]{2,1,0:T(8,128)(2,1)S(1)} %shard_map.150), channel_id=1, source_target_pairs={{0,2},{2,4},{4,6},{6,0},{1,3},{3,5},{5,7},{7,1},{8,10},{10,12},{12... | collective-permute-start | bytes 786440 | tf_op jit(solution)/shard_map/ppermute | solution.py:286
  20.0 1.7 %copy-start.5 = (s32[128]{0:T(128)S(1)}, s32[128]{0:T(128)}, u32[]{:S(2)}) copy-start(s32[128]{0:T(128)} %param.24) | copy-start | bytes 1540
  20.0 1.7 %copy-start.6 = (s32[128,1]{0,1:T(1,128)S(1)}, s32[128,1]{0,1:T(1,128)}, u32[]{:S(2)}) copy-start(s32[128,1]{0,1:T(1,128)} %param.23) | copy-start | bytes 1540
  20.0 1.7 %copy-start.7 = (s32[128]{0:T(128)S(1)}, s32[128]{0:T(128)}, u32[]{:S(2)}) copy-start(s32[128]{0:T(128)} %param.22) | copy-start | bytes 1540
  21.3 17.6 %collective-permute-start.4 = (bf16[16,64,128]{2,1,0:T(8,128)(2,1)S(1)}, bf16[16,64,128]{2,1,0:T(8,128)(2,1)S(1)}, u32[]{:S(2)}, u32[]{:S(2)}) collective-permute-start(bf16[16,64,128]{2,1,0:T(8,128)(2,1)S(1)} %get-tuple-element.43.refs_2_), channel_id=1, source_target_pairs={{0,2},{2,4},{4,6},{6,0},{1,3},{3,5},{5,7},{7,1},{8,10},{10,12},{12... | collective-permute-start | bytes 786440 | tf_op jit(solution)/shard_map/ppermute | solution.py:511
  21.6 5.3 %collective-permute-start.5 = (s32[1,384]{1,0:T(1,128)S(1)}, s32[1,384]{1,0:T(1,128)S(1)}, u32[]{:S(2)}, u32[]{:S(2)}) collective-permute-start(s32[1,384]{1,0:T(1,128)S(1)} %pad_add_fusion), channel_id=1, source_target_pairs={{2,0},{4,2},{6,4},{0,6},{3,1},{5,3},{7,5},{1,7},{10,8},{12,10},{14... | collective-permute-start | bytes 4616 | tf_op jit(solution)/shard_map/ppermute | solution.py:296
  31.4 21.3 %all-to-all-start = ((bf16[16,48,128]{2,1,0:T(8,128)(2,1)}), bf16[16,48,128]{2,1,0:T(8,128)(2,1)S(1)}, u32[]{:S(2)}, u32[]{:S(2)}) async-start(bf16[16,48,128]{2,1,0:T(8,128)(2,1)} %bitcast.7), calls=%async_computation | async-start | bytes 393216 | tf_op jit(solution)/shard_map/all_to_all | solution.py:540
  38.9 3.3 %copy-start = (bf16[96,128,128]{2,1,0:T(8,128)(2,1)S(1)}, bf16[96,128,128]{2,1,0:T(8,128)(2,1)}, u32[]{:S(2)}) copy-start(bf16[96,128,128]{2,1,0:T(8,128)(2,1)} %refs_7_.3) | copy-start | bytes 9437188
  39.0 3.3 %copy-start.1 = (bf16[96,128,128]{2,1,0:T(8,128)(2,1)S(1)}, bf16[96,128,128]{2,1,0:T(8,128)(2,1)}, u32[]{:S(2)}) copy-start(bf16[96,128,128]{2,1,0:T(8,128)(2,1)} %get-tuple-element.57.refs_5_.refs_8_) | copy-start | bytes 9437188
  39.0 3.3 %copy-start.2 = (f32[32,64,128]{2,1,0:T(8,128)S(1)}, f32[32,64,128]{2,1,0:T(8,128)}, u32[]{:S(2)}) copy-start(f32[32,64,128]{2,1,0:T(8,128)} %get-tuple-element.64.refs_9_) | copy-start | bytes 3145732
  39.0 3.3 %copy-start.3 = (f32[16,64,128]{2,1,0:T(8,128)S(1)}, f32[16,64,128]{2,1,0:T(8,128)}, u32[]{:S(2)}) copy-start(f32[16,64,128]{2,1,0:T(8,128)} %get-tuple-element.60.refs_1_) | copy-start | bytes 1572868
  39.0 3.3 %copy-start.4 = (bf16[17,64,128]{2,1,0:T(8,128)(2,1)S(1)}, bf16[17,64,128]{2,1,0:T(8,128)(2,1)}, u32[]{:S(2)}) copy-start(bf16[17,64,128]{2,1,0:T(8,128)(2,1)} %get-tuple-element.62.refs_3_) | copy-start | bytes 835588
  40.3 14.5 %collective-permute-start.6 = (bf16[16,64,128]{2,1,0:T(8,128)(2,1)S(1)}, bf16[16,64,128]{2,1,0:T(8,128)(2,1)S(1)}, u32[]{:S(2)}, u32[]{:S(2)}) collective-permute-start(bf16[16,64,128]{2,1,0:T(8,128)(2,1)S(1)} %get-tuple-element.58), channel_id=1, source_target_pairs={{0,2},{2,4},{4,6},{6,0},{1,3},{3,5},{5,7},{7,1},{8,10},{10,12},{12... | collective-permute-start | bytes 786440 | tf_op jit(solution)/shard_map/ppermute | solution.py:556

commit v9 on v8

--- a/solution.py
+++ b/solution.py
@@ -256,16 +256,25 @@
 
     place_type = array((network * slots, heads), BF16)
 
-    def prepare_body(vertex, owner, lo, hi, hot, head, place):
+    def prepare_body(vertex, owner, lo, hi, trans, matrix, hot, head, place, product):
         one_hots(vertex[...], blocks, hot)
         head[...] = head_values(lo, hi, hot)
         place_rows(owner[...], True, place)
+        product[...] = jnp.dot(
+            trans[...].astype(BF16), matrix[...], preferred_element_type=F32
+        )
 
     own_owner = distribution_entry_holder.reshape(1, heads)
-    hot, head0, place = kernel(
+    hot, head0, place, product = kernel(
         prepare_body,
-        (array(hot_shape, BF16), array((cases, heads), BF16), place_type),
-        [(distribution_entry_vertex.reshape(1, heads), VM), (own_owner, VM), (lo, VM), (hi, VM)],
+        (
+            array(hot_shape, BF16),
+            array((cases, heads), BF16),
+            place_type,
+            hbm_array(highvoltage_costate.shape, F32),
+        ),
+        [(distribution_entry_vertex.reshape(1, heads), VM), (own_owner, VM), (lo, VM), (hi, VM)]
+        + [(highvoltage_costate, VM), (highvoltage_derivative_matrix, VM)],
     )
 
     def rim_first_body(lists, acc, lo, hi, other, out, sums):
@@ -553,7 +562,7 @@
         listed + [(arriving, VM), (lam_low, VM), (acc_rim, VM), (kept, VM)] + stored_in,
         scratch=[sums, pltpu.VMEM(fetched_shape, BF16), pltpu.SemaphoreType.DMA],
     )
-    arriving = lax.ppermute(leaving, "blk", onward)
+    arriving = lax.ppermute(leaving, "blk", onward[:-1])
 
     def main_last_body(
         lists, low_rows, lam_high, lo, hi, decay, inflow, outflow, own, other, icar,
@@ -590,13 +599,7 @@
         out_specs=(HB, VM, HB),
     )
 
-    def trans_body(received, trans_in, matrix_in, out, trans, matrix, sems):
-        copies = [
-            pltpu.make_async_copy(trans_in, trans, sems.at[0]),
-            pltpu.make_async_copy(matrix_in, matrix, sems.at[1]),
-        ]
-        for copy in copies:
-            copy.start()
+    def trans_body(received, product, matrix, out):
         dims = (((0,), (0,)), ((), ()))
         if slots % 16 == 0:
             parts = received[...].reshape(network, 3, slots, nodes)
@@ -624,22 +627,15 @@
             last = lax.dot_general(
                 received[...], hot.astype(BF16), dims, preferred_element_type=F32
             )
-        for copy in copies:
-            copy.wait()
-        value = trans[...]
-        for inj in (first[:cases], first[cases:], last[:cases]):
+        value = product[...] + first[:cases]
+        for inj in (first[cases:], last[:cases]):
             value = jnp.dot(value.astype(BF16), matrix[...], preferred_element_type=F32) + inj
         out[...] = value
 
     (trans,) = kernel(
         trans_body,
         (array(highvoltage_costate.shape, F32),),
-        [(received, VM), (highvoltage_costate, HB), (highvoltage_derivative_matrix, HB)],
-        scratch=[
-            pltpu.VMEM(highvoltage_costate.shape, F32),
-            pltpu.VMEM(highvoltage_derivative_matrix.shape, BF16),
-            pltpu.SemaphoreType.DMA((2,)),
-        ],
+        [(received, VM), (product, VM), (highvoltage_derivative_matrix, VM)],
     )
 
     def last_body(arrived, low_next, lam_in, lam_out, rows, sems):

time: 55.9 us -> 50.9 us (0.911)
  waiting for transfers between devices: 10.6 us -> 3.75 us
  starting transfers between devices: 18.1 us -> 20.2 us
    all_to_all x1, waiting for transfers between devices: 6.23 us -> 0.01 us  [local(): lax.all_to_all(sent.reshape(network, 3 * slots, nodes), ('sec', 'blk'), s...]
    ppermute x0 -> x1, starting transfers between devices: none -> 4.1 us  [local(): arriving = lax.ppermute(leaving, 'blk', onward[:-1])]
    ppermute x3 -> x2, starting transfers between devices: 5.87 us -> 3.9 us  [local(): arriving = lax.ppermute(leaving, 'blk', onward)]
    ppermute x1, waiting for transfers between devices: 1.19 us -> 0.53 us  [local(): theirs = lax.ppermute(mine, 'blk', backward)]
    ppermute x3 -> x2, waiting for transfers between devices: 2.04 us -> 2.04 us  [local(): arriving = lax.ppermute(leaving, 'blk', onward)]
  transfers between devices with their start and end apart: 8 -> 8, of which waited for: 4 -> 3; matrix products, arithmetic and copies ran while one was open for 0% -> 0% of each run, Pallas kernels for 41% -> 44%
where the time goes in v9:
time: 50.9 us; the launch traced here: 50.6 us
  Pallas kernels  25.7 us (50%)
  starting transfers between devices  20.2 us (40%)
  waiting for transfers between devices  3.75 us (7%)
  between operations  0.85 us (2%)
    pallas_call x11, Pallas kernels, kernel(): pl.pallas_call(body, out_shape=outs, in_specs=[spec for _, spec in ins],...  25.7 us
    all_to_all x1, starting transfers between devices, local(): lax.all_to_all(sent.reshape(network, 3 * slots, nodes), ('sec', 'blk'), s...  7.56 us
    ppermute x1, starting transfers between devices, local(): arriving = lax.ppermute(leaving, 'blk', onward[:-1])  4.1 us
    ppermute x2, starting transfers between devices, local(): arriving = lax.ppermute(leaving, 'blk', onward)  3.9 us
    ppermute x1, starting transfers between devices, local(): theirs = lax.ppermute(mine, 'blk', backward)  3.59 us
    ppermute x2, waiting for transfers between devices, local(): arriving = lax.ppermute(leaving, 'blk', onward)  2.04 us
    ppermute x1, waiting for transfers between devices, local(): other_rows = lax.ppermute(tile_source_index, 'case', swap)  1.18 us
  transfers between devices with their start and end apart: 8, of which 3 were waited for; matrix products, arithmetic and copies ran while one was open for 0% of the time, Pallas kernels for 44%

profile of v9, /device:TPU:0, one launch (start us, length us, event | category | flops | bytes accessed | tf_op | source)
XLA Modules:
  0.0 50.6 jit_solution(692640985137775705)
XLA Ops:
  0.6 0.6 %collective-permute-start.2 = (bf16[96,128,128]{2,1,0:T(8,128)(2,1)}, bf16[96,128,128]{2,1,0:T(8,128)(2,1)S(1)}, u32[]{:S(2)}, u32[]{:S(2)}) collective-permute-start(bf16[96,128,128]{2,1,0:T(8,128)(2,1)} %refs_7_.3), channel_id=1, source_target_pairs={{0,1},{1,0},{2,3},{3,2},{4,5},{5,4},{6,7},{7,6},{8,9},{9,8},{10,11... | collective-permute-start | bytes 9437192 | tf_op jit(solution)/shard_map/ppermute | solution.py:95
  1.2 0.1 collective-permute-start
  1.3 0.4 collective-permute-start.1
  1.7 3.8 %shard_map.148 = (f32[48,64,128]{2,1,0:T(8,128)S(1)}, bf16[17,64,128]{2,1,0:T(8,128)(2,1)S(1)}, bf16[17,64,128]{2,1,0:T(8,128)(2,1)S(1)}, bf16[96,128,128]{2,1,0:T(8,128)(2,1)S(1)}, s32[1,640]{1,0:T(1,128)S(1)}) custom-call(s32[96]{0:T(128)} %rows.1, s32[96]{0:T(128)} %columns.1, s32[1,96]{1,0:T(1,128)} %bitcast.18, s32[1,96]{1,0:T(1,128)} %bitcast.19, ...), custom_call_target="tpu_custom_call" | custom-call | tf_op jit(solution)/shard_map/pallas_call | solution.py:26
  5.5 1.2 %collective-permute-done = s32[96]{0:T(128)S(1)} collective-permute-done((s32[96]{0:T(128)}, s32[96]{0:T(128)S(1)}, u32[]{:S(2)}, u32[]{:S(2)}) %collective-permute-start) | collective-permute-done | bytes 416 | tf_op jit(solution)/shard_map/ppermute | solution.py:93
  6.7 0.0 collective-permute-done.1
  6.7 0.4 shard_map.149.other
  7.1 0.0 collective-permute-done.2.refs_3_.refs_4_.refs_10_
  7.1 1.2 %shard_map.150 = bf16[16,64,128]{2,1,0:T(8,128)(2,1)S(1)} custom-call(s32[1,640]{1,0:T(1,128)S(1)} %get-tuple-element.37.own, s32[1,640]{1,0:T(1,128)S(1)} %shard_map.149.other, f32[48,64,128]{2,1,0:T(8,128)S(1)} %get-tuple-element.38.refs_0_, bf16[17,64,128]{2,1,0:T(8,128)(2,1)S(1)} %get-tuple-element.39.refs_1_.lo, ...), custom_call_target="tpu_custom_call" | custom-call | tf_op jit(solution)/shard_map/pallas_call | solution.py:26
  8.4 3.6 %collective-permute-start.3 = (bf16[16,64,128]{2,1,0:T(8,128)(2,1)S(1)}, bf16[16,64,128]{2,1,0:T(8,128)(2,1)S(1)}, u32[]{:S(2)}, u32[]{:S(2)}) collective-permute-start(bf16[16,64,128]{2,1,0:T(8,128)(2,1)S(1)} %shard_map.150), channel_id=1, source_target_pairs={{0,2},{2,4},{4,6},{6,0},{1,3},{3,5},{5,7},{7,1},{8,10},{10,12},{12... | collective-permute-start | bytes 786440 | tf_op jit(solution)/shard_map/ppermute | solution.py:295
  11.9 6.0 %shard_map.151 = (f32[32,64,128]{2,1,0:T(8,128)S(1)}, f32[32,64,128]{2,1,0:T(8,128)S(1)}, f32[16,64,128]{2,1,0:T(8,128)S(1)}, bf16[17,64,128]{2,1,0:T(8,128)(2,1...) custom-call(s32[1,640]{1,0:T(1,128)S(1)} %get-tuple-element.37.own, ...), custom_call_target="tpu_custom_call" | custom-call | tf_op jit(solution)/shard_map/pallas_call | solution.py:26
  17.9 2.0 %collective-permute-done.3.refs_0_ = bf16[16,64,128]{2,1,0:T(8,128)(2,1)S(1)} collective-permute-done((bf16[16,64,128]{2,1,0:T(8,128)(2,1)S(1)}, bf16[16,64,128]{2,1,0:T(8,128)(2,1)S(1)}, u32[]{:S(2)}, u32[]{:S(2)}) %collective-permute-start.3) | collective-permute-done | bytes 262176 | tf_op jit(solution)/shard_map/ppermute | solution.py:295
  20.0 0.0 copy-start.8
  20.0 0.0 copy-start.9
  20.0 0.0 copy-start.10
  20.0 0.0 copy-start.4
  20.0 0.0 copy-start.6
  20.0 1.3 %shard_map.152 = (bf16[16,64,128]{2,1,0:T(8,128)(2,1)S(1)}, f32[16,64,128]{2,1,0:T(8,128)S(1)}, bf16[17,64,128]{2,1,0:T(8,128)(2,1)S(1)}) custom-call(s32[1,640]{1,0:T(1,128)S(1)} %get-tuple-element.37.own, s32[1,640]{1,0:T(1,128)S(1)} %shard_map.149.other, bf16[16,64,128]{2,1,0:T(8,128)(2,1)S(1)} %collective-permute-done.3.refs_0_, ...), custom_call_target="tpu_custom_call" | custom-call | tf_op jit(solution)/shard_map/pallas_call | solution.py:26
  21.3 0.3 collective-permute-start.4
  21.6 0.0 copy-done.8
  21.7 0.0 copy-done.9
  21.7 0.0 copy-done.10
  21.7 3.6 %collective-permute-start.5 = (s32[1,384]{1,0:T(1,128)S(1)}, s32[1,384]{1,0:T(1,128)S(1)}, u32[]{:S(2)}, u32[]{:S(2)}) collective-permute-start(s32[1,384]{1,0:T(1,128)S(1)} %pad_add_fusion), channel_id=1, source_target_pairs={{2,0},{4,2},{6,4},{0,6},{3,1},{5,3},{7,5},{1,7},{10,8},{12,10},{14... | collective-permute-start | bytes 4616 | tf_op jit(solution)/shard_map/ppermute | solution.py:305
  25.3 0.0 copy-done.4
  25.3 0.0 copy-done.6
  25.3 1.2 %shard_map.153 = (bf16[32,128,128]{2,1,0:T(8,128)(2,1)S(1)}, bf16[64,128]{1,0:T(8,128)(2,1)S(1)}, bf16[256,128]{1,0:T(8,128)(2,1)S(1)}, f32[64,256]{1,0:T(8,128)}) custom-call(s32[1,128]{1,0:T(1,128)S(1)} %bitcast.15, s32[1,128]{1,0:T(1,128)S(1)} %bitcast.13, bf16[17,64,128]{2,1,0:T(8,128)(2,1)S(1)} %get-tuple-element.39.refs_1_.lo, ...), custom_call_target="tpu_custom_call" | custom-call | tf_op jit(solution)/shard_map/pallas_call | solution.py:26
  26.4 0.5 %collective-permute-done.5.refs_1_ = s32[1,384]{1,0:T(1,128)S(1)} collective-permute-done((s32[1,384]{1,0:T(1,128)S(1)}, s32[1,384]{1,0:T(1,128)S(1)}, u32[]{:S(2)}, u32[]{:S(2)}) %collective-permute-start.5) | collective-permute-done | bytes 1568 | tf_op jit(solution)/shard_map/ppermute | solution.py:305
  27.0 4.4 %shard_map.154 = (f32[16,64,128]{2,1,0:T(8,128)S(1)}, f32[16,64,128]{2,1,0:T(8,128)S(1)}, bf16[16,3,16,128]{3,2,1,0:T(8,128)(2,1)}, bf16[44,128,128]{2,1,0:T(8,1...) custom-call(s32[1,640]{1,0:T(1,128)S(1)} %get-tuple-element.37.own, ...), custom_call_target="tpu_custom_call" | custom-call | tf_op jit(solution)/shard_map/pallas_call | solution.py:26
  31.4 7.6 %all-to-all-start = ((bf16[16,48,128]{2,1,0:T(8,128)(2,1)}), bf16[16,48,128]{2,1,0:T(8,128)(2,1)S(1)}, u32[]{:S(2)}, u32[]{:S(2)}) async-start(bf16[16,48,128]{2,1,0:T(8,128)(2,1)} %bitcast.7), calls=%async_computation | async-start | bytes 393216 | tf_op jit(solution)/shard_map/all_to_all | solution.py:549
  39.0 0.0 collective-permute-done.4.refs_0_
  39.0 0.0 copy-start
  39.0 0.0 copy-start.1
  39.0 0.0 copy-start.2
  39.0 0.0 copy-start.3
  39.0 0.0 copy-start.5
  39.0 1.3 %shard_map.155 = (bf16[16,64,128]{2,1,0:T(8,128)(2,1)S(1)}, f32[16,64,128]{2,1,0:T(8,128)S(1)}, bf16[17,64,128]{2,1,0:T(8,128)(2,1)S(1)}) custom-call(s32[1,640]{1,0:T(1,128)S(1)} %get-tuple-element.37.own, s32[1,640]{1,0:T(1,128)S(1)} %shard_map.149.other, bf16[16,64,128]{2,1,0:T(8,128)(2,1)S(1)} %collective-permute-done.4.refs_0_, ...), custom_call_target="tpu_custom_call" | custom-call | tf_op jit(solution)/shard_map/pallas_call | solution.py:26
  40.3 4.1 %collective-permute-start.6 = (bf16[16,64,128]{2,1,0:T(8,128)(2,1)S(1)}, bf16[16,64,128]{2,1,0:T(8,128)(2,1)S(1)}, u32[]{:S(2)}, u32[]{:S(2)}) collective-permute-start(bf16[16,64,128]{2,1,0:T(8,128)(2,1)S(1)} %get-tuple-element.59), channel_id=1, source_target_pairs={{0,2},{2,4},{4,6},{1,3},{3,5},{5,7},{8,10},{10,12},{12,14},{9,11},... | collective-permute-start | bytes 786440 | tf_op jit(solution)/shard_map/ppermute | solution.py:565
  44.4 0.0 copy-done
  44.4 0.0 copy-done.1
  44.4 0.0 copy-done.2
  44.4 0.0 copy-done.3
  44.5 0.0 copy-done.5
  44.5 0.0 copy-start.7
  44.5 4.2 %shard_map.156 = (f32[32,64,128]{2,1,0:T(8,128)}, f32[16,64,128]{2,1,0:T(8,128)S(1)}, f32[32,64,128]{2,1,0:T(8,128)}) custom-call(s32[1,640]{1,0:T(1,128)S(1)} %get-tuple-element.37.own, s32[1,640]{1,0:T(1,128)S(1)} %shard_map.149.other, f32[16,64,128]{2,1,0:T(8,128)S(1)} %get-tuple-element.60.refs_0_, f32[16,64,128]{2,1,0:T(8,128)S(1)} %copy-done.3, ...), custom_call_target="tpu_custom_call" | custom-call | tf_op jit(solution)/shard_map/pallas_call | solution.py:26
  48.6 0.0 all-to-all-done
  48.7 0.0 copy-done.7
  48.7 1.1 %shard_map.158 = f32[64,256]{1,0:T(8,128)} custom-call(bf16[768,128]{1,0:T(8,128)(2,1)S(1)} %bitcast.9, f32[64,256]{1,0:T(8,128)S(1)} %copy-done.7, bf16[256,256]{1,0:T(8,128)(2,1)S(1)} %copy-done.4), custom_call_target="tpu_custom_call" | custom-call | tf_op jit(solution)/shard_map/pallas_call | solution.py:26
  49.8 0.0 collective-permute-done.6.arrived
  49.8 0.8 %shard_map.157 = f32[32,64,128]{2,1,0:T(8,128)} custom-call(bf16[16,64,128]{2,1,0:T(8,128)(2,1)S(1)} %collective-permute-done.6.arrived, f32[16,64,128]{2,1,0:T(8,128)S(1)} %get-tuple-element.66.low_next, f32[32,64,128]{2,1,0:T(8,128)} %get-tuple-element.67.lam_in), custom_call_target="tpu_custom_call", output_to_operand_aliasing={{}: (2, {})} | custom-call | tf_op jit(solution)/shard_map/pallas_call | solution.py:26
  (1 shorter events, 0.0 us)
Async XLA Ops:
  0.6 6.5 %collective-permute-start.2 = (bf16[96,128,128]{2,1,0:T(8,128)(2,1)}, bf16[96,128,128]{2,1,0:T(8,128)(2,1)S(1)}, u32[]{:S(2)}, u32[]{:S(2)}) collective-permute-start(bf16[96,128,128]{2,1,0:T(8,128)(2,1)} %refs_7_.3), channel_id=1, source_target_pairs={{0,1},{1,0},{2,3},{3,2},{4,5},{5,4},{6,7},{7,6},{8,9},{9,8},{10,11... | collective-permute-start | bytes 9437192 | tf_op jit(solution)/shard_map/ppermute | solution.py:95
  1.2 5.5 %collective-permute-start = (s32[96]{0:T(128)}, s32[96]{0:T(128)S(1)}, u32[]{:S(2)}, u32[]{:S(2)}) collective-permute-start(s32[96]{0:T(128)} %rows.1), channel_id=1, source_target_pairs={{0,1},{1,0},{2,3},{3,2},{4,5},{5,4},{6,7},{7,6},{8,9},{9,8},{10,11... | collective-permute-start | bytes 1160 | tf_op jit(solution)/shard_map/ppermute | solution.py:93
  1.3 5.4 %collective-permute-start.1 = (s32[96]{0:T(128)}, s32[96]{0:T(128)S(1)}, u32[]{:S(2)}, u32[]{:S(2)}) collective-permute-start(s32[96]{0:T(128)} %columns.1), channel_id=1, source_target_pairs={{0,1},{1,0},{2,3},{3,2},{4,5},{5,4},{6,7},{7,6},{8,9},{9,8},{10,11... | collective-permute-start | bytes 1160 | tf_op jit(solution)/shard_map/ppermute | solution.py:94
  8.4 11.6 %collective-permute-start.3 = (bf16[16,64,128]{2,1,0:T(8,128)(2,1)S(1)}, bf16[16,64,128]{2,1,0:T(8,128)(2,1)S(1)}, u32[]{:S(2)}, u32[]{:S(2)}) collective-permute-start(bf16[16,64,128]{2,1,0:T(8,128)(2,1)S(1)} %shard_map.150), channel_id=1, source_target_pairs={{0,2},{2,4},{4,6},{6,0},{1,3},{3,5},{5,7},{7,1},{8,10},{10,12},{12... | collective-permute-start | bytes 786440 | tf_op jit(solution)/shard_map/ppermute | solution.py:295
  20.0 1.7 %copy-start.8 = (s32[128]{0:T(128)S(1)}, s32[128]{0:T(128)}, u32[]{:S(2)}) copy-start(s32[128]{0:T(128)} %param.24) | copy-start | bytes 1540
  20.0 1.7 %copy-start.9 = (s32[128,1]{0,1:T(1,128)S(1)}, s32[128,1]{0,1:T(1,128)}, u32[]{:S(2)}) copy-start(s32[128,1]{0,1:T(1,128)} %param.23) | copy-start | bytes 1540
  20.0 1.7 %copy-start.10 = (s32[128]{0:T(128)S(1)}, s32[128]{0:T(128)}, u32[]{:S(2)}) copy-start(s32[128]{0:T(128)} %param.22) | copy-start | bytes 1540
  20.0 5.3 %copy-start.4 = (bf16[256,256]{1,0:T(8,128)(2,1)S(1)}, bf16[256,256]{1,0:T(8,128)(2,1)}, u32[]{:S(2)}) copy-start(bf16[256,256]{1,0:T(8,128)(2,1)} %matrix.3) | copy-start | bytes 393220
  20.0 5.3 %copy-start.6 = (f32[64,256]{1,0:T(8,128)S(1)}, f32[64,256]{1,0:T(8,128)}, u32[]{:S(2)}) copy-start(f32[64,256]{1,0:T(8,128)} %trans.1) | copy-start | bytes 196612
  21.3 17.6 %collective-permute-start.4 = (bf16[16,64,128]{2,1,0:T(8,128)(2,1)S(1)}, bf16[16,64,128]{2,1,0:T(8,128)(2,1)S(1)}, u32[]{:S(2)}, u32[]{:S(2)}) collective-permute-start(bf16[16,64,128]{2,1,0:T(8,128)(2,1)S(1)} %get-tuple-element.44.refs_2_), channel_id=1, source_target_pairs={{0,2},{2,4},{4,6},{6,0},{1,3},{3,5},{5,7},{7,1},{8,10},{10,12},{12... | collective-permute-start | bytes 786440 | tf_op jit(solution)/shard_map/ppermute | solution.py:520
  21.7 5.3 %collective-permute-start.5 = (s32[1,384]{1,0:T(1,128)S(1)}, s32[1,384]{1,0:T(1,128)S(1)}, u32[]{:S(2)}, u32[]{:S(2)}) collective-permute-start(s32[1,384]{1,0:T(1,128)S(1)} %pad_add_fusion), channel_id=1, source_target_pairs={{2,0},{4,2},{6,4},{0,6},{3,1},{5,3},{7,5},{1,7},{10,8},{12,10},{14... | collective-permute-start | bytes 4616 | tf_op jit(solution)/shard_map/ppermute | solution.py:305
  31.4 17.3 %all-to-all-start = ((bf16[16,48,128]{2,1,0:T(8,128)(2,1)}), bf16[16,48,128]{2,1,0:T(8,128)(2,1)S(1)}, u32[]{:S(2)}, u32[]{:S(2)}) async-start(bf16[16,48,128]{2,1,0:T(8,128)(2,1)} %bitcast.7), calls=%async_computation | async-start | bytes 393216 | tf_op jit(solution)/shard_map/all_to_all | solution.py:549
  39.0 5.5 %copy-start = (bf16[96,128,128]{2,1,0:T(8,128)(2,1)S(1)}, bf16[96,128,128]{2,1,0:T(8,128)(2,1)}, u32[]{:S(2)}) copy-start(bf16[96,128,128]{2,1,0:T(8,128)(2,1)} %refs_7_.3) | copy-start | bytes 9437188
  39.0 5.4 %copy-start.1 = (bf16[96,128,128]{2,1,0:T(8,128)(2,1)S(1)}, bf16[96,128,128]{2,1,0:T(8,128)(2,1)}, u32[]{:S(2)}) copy-start(bf16[96,128,128]{2,1,0:T(8,128)(2,1)} %get-tuple-element.58.refs_5_.refs_8_) | copy-start | bytes 9437188
  39.0 5.4 %copy-start.2 = (f32[32,64,128]{2,1,0:T(8,128)S(1)}, f32[32,64,128]{2,1,0:T(8,128)}, u32[]{:S(2)}) copy-start(f32[32,64,128]{2,1,0:T(8,128)} %get-tuple-element.65.refs_9_) | copy-start | bytes 3145732
  39.0 5.4 %copy-start.3 = (f32[16,64,128]{2,1,0:T(8,128)S(1)}, f32[16,64,128]{2,1,0:T(8,128)}, u32[]{:S(2)}) copy-start(f32[16,64,128]{2,1,0:T(8,128)} %get-tuple-element.61.refs_1_) | copy-start | bytes 1572868
  39.0 5.4 %copy-start.5 = (bf16[17,64,128]{2,1,0:T(8,128)(2,1)S(1)}, bf16[17,64,128]{2,1,0:T(8,128)(2,1)}, u32[]{:S(2)}) copy-start(bf16[17,64,128]{2,1,0:T(8,128)(2,1)} %get-tuple-element.63.refs_3_) | copy-start | bytes 835588
  40.3 9.5 %collective-permute-start.6 = (bf16[16,64,128]{2,1,0:T(8,128)(2,1)S(1)}, bf16[16,64,128]{2,1,0:T(8,128)(2,1)S(1)}, u32[]{:S(2)}, u32[]{:S(2)}) collective-permute-start(bf16[16,64,128]{2,1,0:T(8,128)(2,1)S(1)} %get-tuple-element.59), channel_id=1, source_target_pairs={{0,2},{2,4},{4,6},{1,3},{3,5},{5,7},{8,10},{10,12},{12,14},{9,11},... | collective-permute-start | bytes 786440 | tf_op jit(solution)/shard_map/ppermute | solution.py:565
  44.5 4.2 %copy-start.7 = (f32[64,256]{1,0:T(8,128)S(1)}, f32[64,256]{1,0:T(8,128)}, u32[]{:S(2)}) copy-start(f32[64,256]{1,0:T(8,128)} %get-tuple-element.70.product) | copy-start | bytes 196612

commit v10 on v9

--- a/solution.py
+++ b/solution.py
@@ -84,7 +84,6 @@
     padded = (low + 1, cases, nodes)
     acc_shape = (targets, cases, nodes)
     hot_shape = (blocks, nodes, heads)
-    factor_shape = inverter_decay_factor.shape
     swap = [(0, 1), (1, 0)]
     onward = [(i, (i + 1) % owners) for i in range(owners)]
     backward = [(j, i) for i, j in onward]
@@ -292,7 +291,7 @@
         listed + [(acc, VM), (lo, VM), (hi, VM), (other, VM)],
         scratch=[pltpu.VMEM((rim, cases, nodes), F32)],
     )
-    arriving = lax.ppermute(leaving, "blk", onward)
+    arriving = lax.ppermute(leaving, "blk", onward[:-1])
 
     mine = jnp.concatenate(
         [
@@ -316,35 +315,24 @@
         run(lists, [((0, 2), hi, own, acc), ((1, 2), hi, other, acc)], MANY)
 
     def main_first_body(
-        lists, acc, lo, hi, own, other, lam_in, icar_in, decay_in, inflow_in, outflow_in,
-        lam_next, acc_next, acc_rim, hi_next, icar_next, decay, inflow, outflow, other_kept,
-        lam, icar, sems,
+        lists, acc, lo, hi, own, other, lam, icar, decay, inflow, outflow,
+        lam_next, acc_next, acc_rim, hi_next, icar_next, other_kept, sem,
     ):
-        pairs = [
-            (icar_in, icar), (outflow_in, outflow), (lam_in, lam), (decay_in, decay), (inflow_in, inflow)
-        ]
-        copies = [pltpu.make_async_copy(a, b, sems.at[i]) for i, (a, b) in enumerate(pairs)]
-        kept = pltpu.make_async_copy(other, other_kept, sems.at[5])
-        for copy in copies + [kept]:
-            copy.start()
-        lam_next[...] = acc[:blocks]
-        run(
-            lists,
-            [((1, 2), hi, other, lam_next), ((1, 3), lo, other, lam_next)],
-            MANY,
-        )
-        for copy in copies:
-            copy.wait()
+        kept = pltpu.make_async_copy(other, other_kept, sem)
+        kept.start()
         for b in range(blocks):
-            lam_next[b] += outflow[b : b + 1, :] * icar[b]
+            lam_next[b] = acc[b] + outflow[b : b + 1, :] * icar[b]
             icar_next[b] = decay[b : b + 1, :] * icar[b] + inflow[b : b + 1, :] * lam[b]
+        run(lists, [((1, 2), hi, other, lam_next), ((1, 3), lo, other, lam_next)], MANY)
         begin_next(
             lists, lam_next, icar_next, outflow, own, other, acc_next, acc_rim, hi_next
         )
         kept.wait()
 
-    factor = array(factor_shape, F32)
-    lam, acc, acc_rim, hi_next, icar, decay, inflow, outflow, other_kept = kernel(
+    decay, inflow, outflow = (
+        inverter_decay_factor, costate_to_inverter_factor, inverter_to_costate_factor
+    )
+    lam, acc, acc_rim, hi_next, icar, other_kept = kernel(
         with_lists(main_first_body),
         (
             array(state, F32),
@@ -352,17 +340,13 @@
             array((rim, cases, nodes), F32),
             array(padded, BF16),
             array(state, F32),
-            factor,
-            factor,
-            factor,
             hbm_array(other.shape, BF16),
         ),
         listed
         + [(acc, VM), (lo, VM), (hi, VM), (own, VM), (other, VM)]
-        + [(vertex_costate, HB), (inverter_costate, HB), (inverter_decay_factor, HB)]
-        + [(costate_to_inverter_factor, HB), (inverter_to_costate_factor, HB)],
-        scratch=[pltpu.VMEM(state, F32), pltpu.VMEM(state, F32), pltpu.SemaphoreType.DMA((6,))],
-        out_specs=(VM,) * 8 + (HB,),
+        + [(vertex_costate, VM), (inverter_costate, VM), (decay, VM), (inflow, VM), (outflow, VM)],
+        scratch=[pltpu.SemaphoreType.DMA],
+        out_specs=(VM,) * 5 + (HB,),
     )
 
     def take_arrived(arrived, lam, low_rows, lo):

time: 50.9 us -> 52 us (1.022)
  starting transfers between devices: 20.2 us -> 22.9 us
  Pallas kernels: 25.7 us -> 23.9 us
    ppermute x1 -> x2, starting transfers between devices: 4.1 us -> 9.52 us  [local(): arriving = lax.ppermute(leaving, 'blk', onward[:-1])]
    ppermute x1, starting transfers between devices: 3.59 us -> 1.54 us  [local(): theirs = lax.ppermute(mine, 'blk', backward)]
    ppermute x2 -> x1, waiting for transfers between devices: 2.04 us -> 0.01 us  [local(): arriving = lax.ppermute(leaving, 'blk', onward)]
    pallas_call x11, Pallas kernels: 25.7 us -> 23.9 us  [kernel(): pl.pallas_call(body, out_shape=outs, in_specs=[spec for _, spec in ins],...]
    ppermute x1, waiting for transfers between devices: 0.53 us -> 1.73 us  [local(): theirs = lax.ppermute(mine, 'blk', backward)]
    ppermute x1 -> x2, waiting for transfers between devices: 0.01 us -> 1.05 us  [local(): arriving = lax.ppermute(leaving, 'blk', onward[:-1])]
    ppermute x2 -> x1, starting transfers between devices: 3.9 us -> 3.11 us  [local(): arriving = lax.ppermute(leaving, 'blk', onward)]
  transfers between devices with their start and end apart: 8 -> 8, of which waited for: 3 -> 3; matrix products, arithmetic and copies ran while one was open for 0% -> 0% of each run, Pallas kernels for 44% -> 40%
where the time goes in v10:
time: 52 us; the launch traced here: 51.7 us
  Pallas kernels  23.9 us (46%)
  starting transfers between devices  22.9 us (44%)
  waiting for transfers between devices  3.91 us (8%)
  between operations  0.93 us (2%)
    pallas_call x11, Pallas kernels, kernel(): pl.pallas_call(body, out_shape=outs, in_specs=[spec for _, spec in ins],...  23.9 us
    ppermute x2, starting transfers between devices, local(): arriving = lax.ppermute(leaving, 'blk', onward[:-1])  9.52 us
    all_to_all x1, starting transfers between devices, local(): lax.all_to_all(sent.reshape(network, 3 * slots, nodes), ('sec', 'blk'), s...  7.65 us
    ppermute x1, starting transfers between devices, local(): arriving = lax.ppermute(leaving, 'blk', onward)  3.11 us
    ppermute x1, waiting for transfers between devices, local(): theirs = lax.ppermute(mine, 'blk', backward)  1.73 us
    ppermute x1, starting transfers between devices, local(): theirs = lax.ppermute(mine, 'blk', backward)  1.54 us
    ppermute x1, waiting for transfers between devices, local(): other_rows = lax.ppermute(tile_source_index, 'case', swap)  1.12 us
    ppermute x2, waiting for transfers between devices, local(): arriving = lax.ppermute(leaving, 'blk', onward[:-1])  1.05 us
  transfers between devices with their start and end apart: 8, of which 3 were waited for; matrix products, arithmetic and copies ran while one was open for 0% of the time, Pallas kernels for 40%

profile of v10, /device:TPU:0, one launch (start us, length us, event | category | flops | bytes accessed | tf_op | source)
XLA Modules:
  0.0 51.7 jit_solution(1729435711654084036)
XLA Ops:
  0.6 0.6 %collective-permute-start.2 = (bf16[96,128,128]{2,1,0:T(8,128)(2,1)}, bf16[96,128,128]{2,1,0:T(8,128)(2,1)S(1)}, u32[]{:S(2)}, u32[]{:S(2)}) collective-permute-start(bf16[96,128,128]{2,1,0:T(8,128)(2,1)} %refs_7_.3), channel_id=1, source_target_pairs={{0,1},{1,0},{2,3},{3,2},{4,5},{5,4},{6,7},{7,6},{8,9},{9,8},{10,11... | collective-permute-start | bytes 9437192 | tf_op jit(solution)/shard_map/ppermute | solution.py:94
  1.2 0.1 collective-permute-start
  1.3 0.4 collective-permute-start.1
  1.7 3.8 %shard_map.148 = (f32[48,64,128]{2,1,0:T(8,128)S(1)}, bf16[17,64,128]{2,1,0:T(8,128)(2,1)S(1)}, bf16[17,64,128]{2,1,0:T(8,128)(2,1)S(1)}, bf16[96,128,128]{2,1,0:T(8,128)(2,1)S(1)}, s32[1,640]{1,0:T(1,128)S(1)}) custom-call(s32[96]{0:T(128)} %rows.1, s32[96]{0:T(128)} %columns.1, s32[1,96]{1,0:T(1,128)} %bitcast.18, s32[1,96]{1,0:T(1,128)} %bitcast.19, ...), custom_call_target="tpu_custom_call" | custom-call | tf_op jit(solution)/shard_map/pallas_call | solution.py:26
  5.5 0.0 copy-start.2
  5.5 0.0 copy-start.3
  5.5 0.0 copy-start.8
  5.5 0.0 copy-start.9
  5.6 0.0 copy-start.10
  5.6 1.1 %collective-permute-done = s32[96]{0:T(128)S(1)} collective-permute-done((s32[96]{0:T(128)}, s32[96]{0:T(128)S(1)}, u32[]{:S(2)}, u32[]{:S(2)}) %collective-permute-start) | collective-permute-done | bytes 416 | tf_op jit(solution)/shard_map/ppermute | solution.py:92
  6.7 0.0 collective-permute-done.1
  6.7 0.4 shard_map.149.other
  7.1 0.0 collective-permute-done.2.refs_3_.refs_4_.refs_10_
  7.1 1.2 %shard_map.150 = bf16[16,64,128]{2,1,0:T(8,128)(2,1)S(1)} custom-call(s32[1,640]{1,0:T(1,128)S(1)} %get-tuple-element.34.own, s32[1,640]{1,0:T(1,128)S(1)} %shard_map.149.other, f32[48,64,128]{2,1,0:T(8,128)S(1)} %get-tuple-element.35.refs_0_, bf16[17,64,128]{2,1,0:T(8,128)(2,1)S(1)} %get-tuple-element.36.refs_1_.lo, ...), custom_call_target="tpu_custom_call" | custom-call | tf_op jit(solution)/shard_map/pallas_call | solution.py:26
  8.3 5.4 %collective-permute-start.3 = (bf16[16,64,128]{2,1,0:T(8,128)(2,1)S(1)}, bf16[16,64,128]{2,1,0:T(8,128)(2,1)S(1)}, u32[]{:S(2)}, u32[]{:S(2)}) collective-permute-start(bf16[16,64,128]{2,1,0:T(8,128)(2,1)S(1)} %shard_map.150), channel_id=1, source_target_pairs={{0,2},{2,4},{4,6},{1,3},{3,5},{5,7},{8,10},{10,12},{12,14},{9,11},... | collective-permute-start | bytes 786440 | tf_op jit(solution)/shard_map/ppermute | solution.py:294
  13.8 0.0 copy-done.2
  13.8 0.0 copy-done.3
  13.8 0.0 copy-done.8
  13.8 0.0 copy-done.9
  13.8 0.0 copy-done.10
  13.8 4.2 %shard_map.151 = (f32[32,64,128]{2,1,0:T(8,128)S(1)}, f32[32,64,128]{2,1,0:T(8,128)S(1)}, f32[16,64,128]{2,1,0:T(8,128)S(1)}, bf16[17,64,128]{2,1,0:T(8,128)(2,1...) custom-call(s32[1,640]{1,0:T(1,128)S(1)} %get-tuple-element.34.own, s32[1,640]{1,0:T(1,128)S(1)} %shard_map.149.other, ...), custom_call_target="tpu_custom_call" | custom-call | tf_op jit(solution)/shard_map/pallas_call | solution.py:26
  18.0 1.0 %collective-permute-done.3.refs_0_ = bf16[16,64,128]{2,1,0:T(8,128)(2,1)S(1)} collective-permute-done((bf16[16,64,128]{2,1,0:T(8,128)(2,1)S(1)}, bf16[16,64,128]{2,1,0:T(8,128)(2,1)S(1)}, u32[]{:S(2)}, u32[]{:S(2)}) %collective-permute-start.3) | collective-permute-done | bytes 262176 | tf_op jit(solution)/shard_map/ppermute | solution.py:294
  19.0 0.0 copy-start.13
  19.0 0.0 copy-start.14
  19.0 0.0 copy-start.15
  19.0 0.0 copy-start.6
  19.0 0.0 copy-start.11
  19.1 1.3 %shard_map.152 = (bf16[16,64,128]{2,1,0:T(8,128)(2,1)S(1)}, f32[16,64,128]{2,1,0:T(8,128)S(1)}, bf16[17,64,128]{2,1,0:T(8,128)(2,1)S(1)}) custom-call(s32[1,640]{1,0:T(1,128)S(1)} %get-tuple-element.34.own, s32[1,640]{1,0:T(1,128)S(1)} %shard_map.149.other, bf16[16,64,128]{2,1,0:T(8,128)(2,1)S(1)} %collective-permute-done.3.refs_0_, ...), custom_call_target="tpu_custom_call" | custom-call | tf_op jit(solution)/shard_map/pallas_call | solution.py:26
  20.4 3.1 %collective-permute-start.4 = (bf16[16,64,128]{2,1,0:T(8,128)(2,1)S(1)}, bf16[16,64,128]{2,1,0:T(8,128)(2,1)S(1)}, u32[]{:S(2)}, u32[]{:S(2)}) collective-permute-start(bf16[16,64,128]{2,1,0:T(8,128)(2,1)S(1)} %get-tuple-element.41.refs_2_), channel_id=1, source_target_pairs={{0,2},{2,4},{4,6},{6,0},{1,3},{3,5},{5,7},{7,1},{8,10},{10,12},{12... | collective-permute-start | bytes 786440 | tf_op jit(solution)/shard_map/ppermute | solution.py:504
  23.5 0.0 copy-done.13
  23.5 0.0 copy-done.14
  23.5 0.0 copy-done.15
  23.5 1.5 %collective-permute-start.5 = (s32[1,384]{1,0:T(1,128)S(1)}, s32[1,384]{1,0:T(1,128)S(1)}, u32[]{:S(2)}, u32[]{:S(2)}) collective-permute-start(s32[1,384]{1,0:T(1,128)S(1)} %pad_add_fusion), channel_id=1, source_target_pairs={{2,0},{4,2},{6,4},{0,6},{3,1},{5,3},{7,5},{1,7},{10,8},{12,10},{14... | collective-permute-start | bytes 4616 | tf_op jit(solution)/shard_map/ppermute | solution.py:304
  25.0 0.0 copy-done.6
  25.0 0.0 copy-done.11
  25.0 1.2 %shard_map.153 = (bf16[32,128,128]{2,1,0:T(8,128)(2,1)S(1)}, bf16[64,128]{1,0:T(8,128)(2,1)S(1)}, bf16[256,128]{1,0:T(8,128)(2,1)S(1)}, f32[64,256]{1,0:T(8,128)}) custom-call(s32[1,128]{1,0:T(1,128)S(1)} %bitcast.15, s32[1,128]{1,0:T(1,128)S(1)} %bitcast.13, bf16[17,64,128]{2,1,0:T(8,128)(2,1)S(1)} %get-tuple-element.36.refs_1_.lo, ...), custom_call_target="tpu_custom_call" | custom-call | tf_op jit(solution)/shard_map/pallas_call | solution.py:26
  26.2 1.7 %collective-permute-done.5.refs_1_ = s32[1,384]{1,0:T(1,128)S(1)} collective-permute-done((s32[1,384]{1,0:T(1,128)S(1)}, s32[1,384]{1,0:T(1,128)S(1)}, u32[]{:S(2)}, u32[]{:S(2)}) %collective-permute-start.5) | collective-permute-done | bytes 1568 | tf_op jit(solution)/shard_map/ppermute | solution.py:304
  28.0 4.5 %shard_map.154 = (f32[16,64,128]{2,1,0:T(8,128)S(1)}, f32[16,64,128]{2,1,0:T(8,128)S(1)}, bf16[16,3,16,128]{3,2,1,0:T(8,128)(2,1)}, bf16[44,128,128]{2,1,0:T(8,1...) custom-call(s32[1,640]{1,0:T(1,128)S(1)} %get-tuple-element.34.own, ...), custom_call_target="tpu_custom_call" | custom-call | tf_op jit(solution)/shard_map/pallas_call | solution.py:26
  32.4 7.7 %all-to-all-start = ((bf16[16,48,128]{2,1,0:T(8,128)(2,1)}), bf16[16,48,128]{2,1,0:T(8,128)(2,1)S(1)}, u32[]{:S(2)}, u32[]{:S(2)}) async-start(bf16[16,48,128]{2,1,0:T(8,128)(2,1)} %bitcast.7), calls=%async_computation | async-start | bytes 393216 | tf_op jit(solution)/shard_map/all_to_all | solution.py:533
  40.1 0.0 collective-permute-done.4.refs_0_
  40.1 0.0 copy-start
  40.1 0.0 copy-start.1
  40.1 0.0 copy-start.4
  40.1 0.0 copy-start.5
  40.1 0.0 copy-start.7
  40.1 1.3 %shard_map.155 = (bf16[16,64,128]{2,1,0:T(8,128)(2,1)S(1)}, f32[16,64,128]{2,1,0:T(8,128)S(1)}, bf16[17,64,128]{2,1,0:T(8,128)(2,1)S(1)}) custom-call(s32[1,640]{1,0:T(1,128)S(1)} %get-tuple-element.34.own, s32[1,640]{1,0:T(1,128)S(1)} %shard_map.149.other, bf16[16,64,128]{2,1,0:T(8,128)(2,1)S(1)} %collective-permute-done.4.refs_0_, ...), custom_call_target="tpu_custom_call" | custom-call | tf_op jit(solution)/shard_map/pallas_call | solution.py:26
  41.4 4.1 %collective-permute-start.6 = (bf16[16,64,128]{2,1,0:T(8,128)(2,1)S(1)}, bf16[16,64,128]{2,1,0:T(8,128)(2,1)S(1)}, u32[]{:S(2)}, u32[]{:S(2)}) collective-permute-start(bf16[16,64,128]{2,1,0:T(8,128)(2,1)S(1)} %get-tuple-element.54), channel_id=1, source_target_pairs={{0,2},{2,4},{4,6},{1,3},{3,5},{5,7},{8,10},{10,12},{12,14},{9,11},... | collective-permute-start | bytes 786440 | tf_op jit(solution)/shard_map/ppermute | solution.py:549
  45.5 0.0 copy-done
  45.5 0.0 copy-done.1
  45.6 0.0 copy-done.4
  45.6 0.0 copy-done.5
  45.6 0.0 copy-done.7
  45.6 0.0 copy-start.12
  45.6 4.2 %shard_map.156 = (f32[32,64,128]{2,1,0:T(8,128)}, f32[16,64,128]{2,1,0:T(8,128)S(1)}, f32[32,64,128]{2,1,0:T(8,128)}) custom-call(s32[1,640]{1,0:T(1,128)S(1)} %get-tuple-element.34.own, s32[1,640]{1,0:T(1,128)S(1)} %shard_map.149.other, f32[16,64,128]{2,1,0:T(8,128)S(1)} %get-tuple-element.55.refs_0_, f32[16,64,128]{2,1,0:T(8,128)S(1)} %copy-done.5, ...), custom_call_target="tpu_custom_call" | custom-call | tf_op jit(solution)/shard_map/pallas_call | solution.py:26
  49.8 0.0 all-to-all-done
  49.8 0.0 copy-done.12
  49.8 1.1 %shard_map.158 = f32[64,256]{1,0:T(8,128)} custom-call(bf16[768,128]{1,0:T(8,128)(2,1)S(1)} %bitcast.9, f32[64,256]{1,0:T(8,128)S(1)} %copy-done.12, bf16[256,256]{1,0:T(8,128)(2,1)S(1)} %copy-done.6), custom_call_target="tpu_custom_call" | custom-call | tf_op jit(solution)/shard_map/pallas_call | solution.py:26
  50.9 0.0 collective-permute-done.6.arrived
  50.9 0.8 %shard_map.157 = f32[32,64,128]{2,1,0:T(8,128)} custom-call(bf16[16,64,128]{2,1,0:T(8,128)(2,1)S(1)} %collective-permute-done.6.arrived, f32[16,64,128]{2,1,0:T(8,128)S(1)} %get-tuple-element.60.low_next, f32[32,64,128]{2,1,0:T(8,128)} %get-tuple-element.61.lam_in), custom_call_target="tpu_custom_call", output_to_operand_aliasing={{}: (2, {})} | custom-call | tf_op jit(solution)/shard_map/pallas_call | solution.py:26
  (1 shorter events, 0.0 us)
Async XLA Ops:
  0.6 6.5 %collective-permute-start.2 = (bf16[96,128,128]{2,1,0:T(8,128)(2,1)}, bf16[96,128,128]{2,1,0:T(8,128)(2,1)S(1)}, u32[]{:S(2)}, u32[]{:S(2)}) collective-permute-start(bf16[96,128,128]{2,1,0:T(8,128)(2,1)} %refs_7_.3), channel_id=1, source_target_pairs={{0,1},{1,0},{2,3},{3,2},{4,5},{5,4},{6,7},{7,6},{8,9},{9,8},{10,11... | collective-permute-start | bytes 9437192 | tf_op jit(solution)/shard_map/ppermute | solution.py:94
  1.2 5.5 %collective-permute-start = (s32[96]{0:T(128)}, s32[96]{0:T(128)S(1)}, u32[]{:S(2)}, u32[]{:S(2)}) collective-permute-start(s32[96]{0:T(128)} %rows.1), channel_id=1, source_target_pairs={{0,1},{1,0},{2,3},{3,2},{4,5},{5,4},{6,7},{7,6},{8,9},{9,8},{10,11... | collective-permute-start | bytes 1160 | tf_op jit(solution)/shard_map/ppermute | solution.py:92
  1.3 5.4 %collective-permute-start.1 = (s32[96]{0:T(128)}, s32[96]{0:T(128)S(1)}, u32[]{:S(2)}, u32[]{:S(2)}) collective-permute-start(s32[96]{0:T(128)} %columns.1), channel_id=1, source_target_pairs={{0,1},{1,0},{2,3},{3,2},{4,5},{5,4},{6,7},{7,6},{8,9},{9,8},{10,11... | collective-permute-start | bytes 1160 | tf_op jit(solution)/shard_map/ppermute | solution.py:93
  5.5 8.3 %copy-start.2 = (f32[32,64,128]{2,1,0:T(8,128)S(1)}, f32[32,64,128]{2,1,0:T(8,128)}, u32[]{:S(2)}) copy-start(f32[32,64,128]{2,1,0:T(8,128)} %refs_5_.2) | copy-start | bytes 3145732
  5.5 8.3 %copy-start.3 = (f32[32,64,128]{2,1,0:T(8,128)S(1)}, f32[32,64,128]{2,1,0:T(8,128)}, u32[]{:S(2)}) copy-start(f32[32,64,128]{2,1,0:T(8,128)} %refs_6_.2) | copy-start | bytes 3145732
  5.5 8.3 %copy-start.8 = (f32[32,128]{1,0:T(8,128)S(1)}, f32[32,128]{1,0:T(8,128)}, u32[]{:S(2)}) copy-start(f32[32,128]{1,0:T(8,128)} %refs_4_.3) | copy-start | bytes 49156
  5.5 8.3 %copy-start.9 = (f32[32,128]{1,0:T(8,128)S(1)}, f32[32,128]{1,0:T(8,128)}, u32[]{:S(2)}) copy-start(f32[32,128]{1,0:T(8,128)} %refs_5_.3) | copy-start | bytes 49156
  5.6 8.3 %copy-start.10 = (f32[32,128]{1,0:T(8,128)S(1)}, f32[32,128]{1,0:T(8,128)}, u32[]{:S(2)}) copy-start(f32[32,128]{1,0:T(8,128)} %refs_6_.3) | copy-start | bytes 49156
  8.3 10.7 %collective-permute-start.3 = (bf16[16,64,128]{2,1,0:T(8,128)(2,1)S(1)}, bf16[16,64,128]{2,1,0:T(8,128)(2,1)S(1)}, u32[]{:S(2)}, u32[]{:S(2)}) collective-permute-start(bf16[16,64,128]{2,1,0:T(8,128)(2,1)S(1)} %shard_map.150), channel_id=1, source_target_pairs={{0,2},{2,4},{4,6},{1,3},{3,5},{5,7},{8,10},{10,12},{12,14},{9,11},... | collective-permute-start | bytes 786440 | tf_op jit(solution)/shard_map/ppermute | solution.py:294
  19.0 4.4 %copy-start.13 = (s32[128]{0:T(128)S(1)}, s32[128]{0:T(128)}, u32[]{:S(2)}) copy-start(s32[128]{0:T(128)} %param.24) | copy-start | bytes 1540
  19.0 4.4 %copy-start.14 = (s32[128,1]{0,1:T(1,128)S(1)}, s32[128,1]{0,1:T(1,128)}, u32[]{:S(2)}) copy-start(s32[128,1]{0,1:T(1,128)} %param.23) | copy-start | bytes 1540
  19.0 4.4 %copy-start.15 = (s32[128]{0:T(128)S(1)}, s32[128]{0:T(128)}, u32[]{:S(2)}) copy-start(s32[128]{0:T(128)} %param.22) | copy-start | bytes 1540
  19.0 6.0 %copy-start.6 = (bf16[256,256]{1,0:T(8,128)(2,1)S(1)}, bf16[256,256]{1,0:T(8,128)(2,1)}, u32[]{:S(2)}) copy-start(bf16[256,256]{1,0:T(8,128)(2,1)} %matrix.3) | copy-start | bytes 393220
  19.0 6.0 %copy-start.11 = (f32[64,256]{1,0:T(8,128)S(1)}, f32[64,256]{1,0:T(8,128)}, u32[]{:S(2)}) copy-start(f32[64,256]{1,0:T(8,128)} %trans.1) | copy-start | bytes 196612
  20.4 19.7 %collective-permute-start.4 = (bf16[16,64,128]{2,1,0:T(8,128)(2,1)S(1)}, bf16[16,64,128]{2,1,0:T(8,128)(2,1)S(1)}, u32[]{:S(2)}, u32[]{:S(2)}) collective-permute-start(bf16[16,64,128]{2,1,0:T(8,128)(2,1)S(1)} %get-tuple-element.41.refs_2_), channel_id=1, source_target_pairs={{0,2},{2,4},{4,6},{6,0},{1,3},{3,5},{5,7},{7,1},{8,10},{10,12},{12... | collective-permute-start | bytes 786440 | tf_op jit(solution)/shard_map/ppermute | solution.py:504
  23.5 4.5 %collective-permute-start.5 = (s32[1,384]{1,0:T(1,128)S(1)}, s32[1,384]{1,0:T(1,128)S(1)}, u32[]{:S(2)}, u32[]{:S(2)}) collective-permute-start(s32[1,384]{1,0:T(1,128)S(1)} %pad_add_fusion), channel_id=1, source_target_pairs={{2,0},{4,2},{6,4},{0,6},{3,1},{5,3},{7,5},{1,7},{10,8},{12,10},{14... | collective-permute-start | bytes 4616 | tf_op jit(solution)/shard_map/ppermute | solution.py:304
  32.4 17.4 %all-to-all-start = ((bf16[16,48,128]{2,1,0:T(8,128)(2,1)}), bf16[16,48,128]{2,1,0:T(8,128)(2,1)S(1)}, u32[]{:S(2)}, u32[]{:S(2)}) async-start(bf16[16,48,128]{2,1,0:T(8,128)(2,1)} %bitcast.7), calls=%async_computation | async-start | bytes 393216 | tf_op jit(solution)/shard_map/all_to_all | solution.py:533
  40.1 5.5 %copy-start = (bf16[96,128,128]{2,1,0:T(8,128)(2,1)S(1)}, bf16[96,128,128]{2,1,0:T(8,128)(2,1)}, u32[]{:S(2)}) copy-start(bf16[96,128,128]{2,1,0:T(8,128)(2,1)} %refs_7_.3) | copy-start | bytes 9437188
  40.1 5.4 %copy-start.1 = (bf16[96,128,128]{2,1,0:T(8,128)(2,1)S(1)}, bf16[96,128,128]{2,1,0:T(8,128)(2,1)}, u32[]{:S(2)}) copy-start(bf16[96,128,128]{2,1,0:T(8,128)(2,1)} %get-tuple-element.53.refs_5_.refs_8_) | copy-start | bytes 9437188
  40.1 5.4 %copy-start.4 = (f32[32,64,128]{2,1,0:T(8,128)S(1)}, f32[32,64,128]{2,1,0:T(8,128)}, u32[]{:S(2)}) copy-start(f32[32,64,128]{2,1,0:T(8,128)} %get-tuple-element.59.refs_9_) | copy-start | bytes 3145732
  40.1 5.4 %copy-start.5 = (f32[16,64,128]{2,1,0:T(8,128)S(1)}, f32[16,64,128]{2,1,0:T(8,128)}, u32[]{:S(2)}) copy-start(f32[16,64,128]{2,1,0:T(8,128)} %get-tuple-element.56.refs_1_) | copy-start | bytes 1572868
  40.1 5.4 %copy-start.7 = (bf16[17,64,128]{2,1,0:T(8,128)(2,1)S(1)}, bf16[17,64,128]{2,1,0:T(8,128)(2,1)}, u32[]{:S(2)}) copy-start(bf16[17,64,128]{2,1,0:T(8,128)(2,1)} %get-tuple-element.58.refs_3_) | copy-start | bytes 835588
  41.4 9.5 %collective-permute-start.6 = (bf16[16,64,128]{2,1,0:T(8,128)(2,1)S(1)}, bf16[16,64,128]{2,1,0:T(8,128)(2,1)S(1)}, u32[]{:S(2)}, u32[]{:S(2)}) collective-permute-start(bf16[16,64,128]{2,1,0:T(8,128)(2,1)S(1)} %get-tuple-element.54), channel_id=1, source_target_pairs={{0,2},{2,4},{4,6},{1,3},{3,5},{5,7},{8,10},{10,12},{12,14},{9,11},... | collective-permute-start | bytes 786440 | tf_op jit(solution)/shard_map/ppermute | solution.py:549
  45.6 4.2 %copy-start.12 = (f32[64,256]{1,0:T(8,128)S(1)}, f32[64,256]{1,0:T(8,128)}, u32[]{:S(2)}) copy-start(f32[64,256]{1,0:T(8,128)} %get-tuple-element.64.product) | copy-start | bytes 196612

commit v11 on v10

--- a/solution.py
+++ b/solution.py
@@ -8,8 +8,8 @@
 
 STEPS = 3
 UNROLL = 16
-FEW = 24
-MANY = 40
+FEW = 28
+MANY = 48
 KEEP = 44
 CLASSES = 4
 VMEM_LIMIT = 24 << 20
@@ -303,6 +303,19 @@
     )
     theirs = lax.ppermute(mine, "blk", backward)
 
+    def prepare_next_body(theirs, hot, place, label):
+        one_hots(theirs[:, :heads], low, hot)
+        followed = lax.axis_index("blk") < owners - 1
+        place_rows(theirs[:, heads : 2 * heads], followed, place)
+        bus = (theirs[:, 2 * heads : 3 * heads] + 1).astype(F32)
+        label[...] = jnp.broadcast_to(bus, (nodes - cases, heads)).astype(BF16)
+
+    hot_next, place_next, label_next = kernel(
+        prepare_next_body,
+        (array((low, nodes, heads), BF16), place_type, array((nodes - cases, heads), BF16)),
+        [(theirs, VM)],
+    )
+
     def begin_next(lists, lam, icar, outflow, own, other, acc, acc_rim, hi):
         for b in range(blocks):
             acc[b] = outflow[b : b + 1, :] * icar[b]
@@ -424,10 +437,10 @@
         out[...] = sums[...].astype(BF16)
 
     def main_body(
-        lists, bus, theirs, left, low_rows, lam, lo, hi, acc, icar, own, other,
-        hot, head0, place, decay, inflow,
+        lists, bus, left, low_rows, lam, lo, hi, acc, icar, own, other,
+        hot, hot_next, head0, place, place_next, label_next, decay, inflow,
         lam_low, acc_rim, sent, kept, icar_out, lam_out, hi_out,
-        icar_next, lo_base, lam_next, hi_next, hot_next, place_next, sems,
+        icar_next, lo_base, lam_next, hi_next, sems,
     ):
         keep_own = jnp.minimum(count_of(lists, 0, 1), KEEP)
         keep_other = jnp.minimum(count_of(lists, 1, 1), KEEP - keep_own)
@@ -451,20 +464,15 @@
         hi_copy.start()
         acc_rim[...] = jnp.zeros(acc_rim.shape, F32)
         run(lists, [((0, 0), hi_next, own, acc_rim), ((1, 0), hi_next, other, acc_rim)], FEW)
-        followed = lax.axis_index("blk") < owners - 1
-        one_hots(theirs[:, :heads], low, hot_next)
-        place_rows(theirs[:, heads : 2 * heads], followed, place_next)
         head_next = jnp.dot(left[0], hot_next[0], preferred_element_type=F32)
         for b in range(1, low):
             head_next += jnp.dot(left[b], hot_next[b], preferred_element_type=F32)
         width = (nodes - cases, heads)
         label = jnp.broadcast_to((bus[...] + 1).astype(F32), width).astype(BF16)
-        bus_next = theirs[:, 2 * heads : 3 * heads]
-        label_next = jnp.broadcast_to((bus_next + 1).astype(F32), width).astype(BF16)
         pairs = [
             (place, head0[...], head_values(lo, hi, hot)),
             (place, head_values(lo_base, hi_next, hot), label),
-            (place_next, head_next.astype(BF16), label_next),
+            (place_next, head_next.astype(BF16), label_next[...]),
         ]
         for i, (where, first_half, second_half) in enumerate(pairs):
             part = lax.dot_general(
@@ -514,18 +522,16 @@
             hbm_array(padded, BF16),
         ),
         listed
-        + [(distribution_entry_substation.reshape(1, heads), VM), (theirs, VM), (leaving, VM)]
+        + [(distribution_entry_substation.reshape(1, heads), VM), (leaving, VM)]
         + [(low_rows, VM), (lam, VM), (lo, VM), (hi, VM), (acc, VM), (icar, VM)]
         + tiles
-        + [(hot, VM), (head0, VM), (place, VM)]
+        + [(hot, VM), (hot_next, VM), (head0, VM), (place, VM), (place_next, VM), (label_next, VM)]
         + [(decay, VM), (inflow, VM)],
         scratch=[
             pltpu.VMEM(state, F32),
             pltpu.VMEM(half, BF16),
             pltpu.VMEM(state, F32),
             pltpu.VMEM(padded, BF16),
-            pltpu.VMEM((low, nodes, heads), BF16),
-            pltpu.VMEM(place_type.shape, BF16),
             pltpu.SemaphoreType.DMA((3,)),
         ],
         out_specs=(VM,) * 4 + (HB,) * 3,

time: 52 us -> 52.5 us (level)
  waiting for transfers between devices: 3.91 us -> 4.89 us
    ppermute x2, waiting for transfers between devices: 1.05 us -> 2.06 us  [local(): arriving = lax.ppermute(leaving, 'blk', onward[:-1])]
    ppermute x1, starting transfers between devices: 1.54 us -> 2.12 us  [local(): theirs = lax.ppermute(mine, 'blk', backward)]
    ppermute x1, starting transfers between devices: 3.11 us -> 2.54 us  [local(): arriving = lax.ppermute(leaving, 'blk', onward)]
    pallas_call x11 -> x12, Pallas kernels: 23.9 us -> 23.6 us  [kernel(): pl.pallas_call(body, out_shape=outs, in_specs=[spec for _, spec in ins],...]
  transfers between devices with their start and end apart: 8 -> 8, of which waited for: 3 -> 3; matrix products, arithmetic and copies ran while one was open for 0% -> 0% of each run, Pallas kernels for 40% -> 38%
where the time goes in v11:
time: 52.5 us; the launch traced here: 52.2 us
  Pallas kernels  23.6 us (45%)
  starting transfers between devices  22.5 us (43%)
  waiting for transfers between devices  4.89 us (9%)
  between operations  1.1 us (2%)
    pallas_call x12, Pallas kernels, kernel(): pl.pallas_call(body, out_shape=outs, in_specs=[spec for _, spec in ins],...  23.6 us
    ppermute x2, starting transfers between devices, local(): arriving = lax.ppermute(leaving, 'blk', onward[:-1])  9.14 us
    all_to_all x1, starting transfers between devices, local(): lax.all_to_all(sent.reshape(network, 3 * slots, nodes), ('sec', 'blk'), s...  7.67 us
    ppermute x1, starting transfers between devices, local(): arriving = lax.ppermute(leaving, 'blk', onward)  2.54 us
    ppermute x1, starting transfers between devices, local(): theirs = lax.ppermute(mine, 'blk', backward)  2.12 us
    ppermute x2, waiting for transfers between devices, local(): arriving = lax.ppermute(leaving, 'blk', onward[:-1])  2.06 us
    ppermute x1, waiting for transfers between devices, local(): theirs = lax.ppermute(mine, 'blk', backward)  1.72 us
    ppermute x1, waiting for transfers between devices, local(): other_rows = lax.ppermute(tile_source_index, 'case', swap)  1.1 us
  transfers between devices with their start and end apart: 8, of which 3 were waited for; matrix products, arithmetic and copies ran while one was open for 0% of the time, Pallas kernels for 38%

profile of v11, /device:TPU:0, one launch (start us, length us, event | category | flops | bytes accessed | tf_op | source)
XLA Modules:
  0.0 52.2 jit_solution(16970559940684257670)
XLA Ops:
  0.6 0.6 %collective-permute-start.2 = (bf16[96,128,128]{2,1,0:T(8,128)(2,1)}, bf16[96,128,128]{2,1,0:T(8,128)(2,1)S(1)}, u32[]{:S(2)}, u32[]{:S(2)}) collective-permute-start(bf16[96,128,128]{2,1,0:T(8,128)(2,1)} %refs_7_.3), channel_id=1, source_target_pairs={{0,1},{1,0},{2,3},{3,2},{4,5},{5,4},{6,7},{7,6},{8,9},{9,8},{10,11... | collective-permute-start | bytes 9437192 | tf_op jit(solution)/shard_map/ppermute | solution.py:94
  1.2 0.1 collective-permute-start
  1.3 0.4 collective-permute-start.1
  1.7 3.8 %shard_map.148 = (f32[48,64,128]{2,1,0:T(8,128)S(1)}, bf16[17,64,128]{2,1,0:T(8,128)(2,1)S(1)}, bf16[17,64,128]{2,1,0:T(8,128)(2,1)S(1)}, bf16[96,128,128]{2,1,0:T(8,128)(2,1)S(1)}, s32[1,640]{1,0:T(1,128)S(1)}) custom-call(s32[96]{0:T(128)} %rows.1, s32[96]{0:T(128)} %columns.1, s32[1,96]{1,0:T(1,128)} %bitcast.18, s32[1,96]{1,0:T(1,128)} %bitcast.19, ...), custom_call_target="tpu_custom_call" | custom-call | tf_op jit(solution)/shard_map/pallas_call | solution.py:26
  5.5 0.0 copy-start.2
  5.5 0.0 copy-start.3
  5.5 0.0 copy-start.8
  5.6 0.0 copy-start.9
  5.6 0.0 copy-start.10
  5.6 1.1 %collective-permute-done = s32[96]{0:T(128)S(1)} collective-permute-done((s32[96]{0:T(128)}, s32[96]{0:T(128)S(1)}, u32[]{:S(2)}, u32[]{:S(2)}) %collective-permute-start) | collective-permute-done | bytes 416 | tf_op jit(solution)/shard_map/ppermute | solution.py:92
  6.7 0.0 collective-permute-done.1
  6.7 0.4 shard_map.149.other
  7.1 0.0 collective-permute-done.2.refs_3_.refs_4_.refs_9_
  7.1 1.3 %shard_map.150 = bf16[16,64,128]{2,1,0:T(8,128)(2,1)S(1)} custom-call(s32[1,640]{1,0:T(1,128)S(1)} %get-tuple-element.37.own, s32[1,640]{1,0:T(1,128)S(1)} %shard_map.149.other, f32[48,64,128]{2,1,0:T(8,128)S(1)} %get-tuple-element.38.refs_0_, bf16[17,64,128]{2,1,0:T(8,128)(2,1)S(1)} %get-tuple-element.39.refs_1_.lo, ...), custom_call_target="tpu_custom_call" | custom-call | tf_op jit(solution)/shard_map/pallas_call | solution.py:26
  8.4 4.9 %collective-permute-start.3 = (bf16[16,64,128]{2,1,0:T(8,128)(2,1)S(1)}, bf16[16,64,128]{2,1,0:T(8,128)(2,1)S(1)}, u32[]{:S(2)}, u32[]{:S(2)}) collective-permute-start(bf16[16,64,128]{2,1,0:T(8,128)(2,1)S(1)} %shard_map.150), channel_id=1, source_target_pairs={{0,2},{2,4},{4,6},{1,3},{3,5},{5,7},{8,10},{10,12},{12,14},{9,11},... | collective-permute-start | bytes 786440 | tf_op jit(solution)/shard_map/ppermute | solution.py:294
  13.3 0.0 copy-done.2
  13.3 0.0 copy-done.3
  13.3 0.0 copy-done.8
  13.3 0.0 copy-done.9
  13.3 0.0 copy-done.10
  13.4 3.7 %shard_map.151 = (f32[32,64,128]{2,1,0:T(8,128)S(1)}, f32[32,64,128]{2,1,0:T(8,128)S(1)}, f32[16,64,128]{2,1,0:T(8,128)S(1)}, bf16[17,64,128]{2,1,0:T(8,128)(2,1...) custom-call(s32[1,640]{1,0:T(1,128)S(1)} %get-tuple-element.37.own, s32[1,640]{1,0:T(1,128)S(1)} %shard_map.149.other, ...), custom_call_target="tpu_custom_call" | custom-call | tf_op jit(solution)/shard_map/pallas_call | solution.py:26
  17.1 2.1 %collective-permute-done.3.refs_0_ = bf16[16,64,128]{2,1,0:T(8,128)(2,1)S(1)} collective-permute-done((bf16[16,64,128]{2,1,0:T(8,128)(2,1)S(1)}, bf16[16,64,128]{2,1,0:T(8,128)(2,1)S(1)}, u32[]{:S(2)}, u32[]{:S(2)}) %collective-permute-start.3) | collective-permute-done | bytes 262176 | tf_op jit(solution)/shard_map/ppermute | solution.py:294
  19.1 0.0 copy-start.13
  19.1 0.0 copy-start.14
  19.1 0.0 copy-start.15
  19.1 0.0 copy-start.6
  19.1 0.0 copy-start.11
  19.2 1.4 %shard_map.152 = (bf16[16,64,128]{2,1,0:T(8,128)(2,1)S(1)}, f32[16,64,128]{2,1,0:T(8,128)S(1)}, bf16[17,64,128]{2,1,0:T(8,128)(2,1)S(1)}) custom-call(s32[1,640]{1,0:T(1,128)S(1)} %get-tuple-element.37.own, s32[1,640]{1,0:T(1,128)S(1)} %shard_map.149.other, bf16[16,64,128]{2,1,0:T(8,128)(2,1)S(1)} %collective-permute-done.3.refs_0_, ...), custom_call_target="tpu_custom_call" | custom-call | tf_op jit(solution)/shard_map/pallas_call | solution.py:26
  20.6 2.5 %collective-permute-start.4 = (bf16[16,64,128]{2,1,0:T(8,128)(2,1)S(1)}, bf16[16,64,128]{2,1,0:T(8,128)(2,1)S(1)}, u32[]{:S(2)}, u32[]{:S(2)}) collective-permute-start(bf16[16,64,128]{2,1,0:T(8,128)(2,1)S(1)} %get-tuple-element.44.refs_1_), channel_id=1, source_target_pairs={{0,2},{2,4},{4,6},{6,0},{1,3},{3,5},{5,7},{7,1},{8,10},{10,12},{12... | collective-permute-start | bytes 786440 | tf_op jit(solution)/shard_map/ppermute | solution.py:512
  23.1 0.0 copy-done.13
  23.1 0.0 copy-done.14
  23.1 0.0 copy-done.15
  23.1 2.1 %collective-permute-start.5 = (s32[1,384]{1,0:T(1,128)S(1)}, s32[1,384]{1,0:T(1,128)S(1)}, u32[]{:S(2)}, u32[]{:S(2)}) collective-permute-start(s32[1,384]{1,0:T(1,128)S(1)} %pad_add_fusion), channel_id=1, source_target_pairs={{2,0},{4,2},{6,4},{0,6},{3,1},{5,3},{7,5},{1,7},{10,8},{12,10},{14... | collective-permute-start | bytes 4616 | tf_op jit(solution)/shard_map/ppermute | solution.py:304
  25.2 0.0 copy-done.6
  25.2 0.0 copy-done.11
  25.3 1.2 %shard_map.153 = (bf16[32,128,128]{2,1,0:T(8,128)(2,1)S(1)}, bf16[64,128]{1,0:T(8,128)(2,1)S(1)}, bf16[256,128]{1,0:T(8,128)(2,1)S(1)}, f32[64,256]{1,0:T(8,128)}) custom-call(s32[1,128]{1,0:T(1,128)S(1)} %bitcast.13, s32[1,128]{1,0:T(1,128)S(1)} %bitcast.15, bf16[17,64,128]{2,1,0:T(8,128)(2,1)S(1)} %get-tuple-element.39.refs_1_.lo, ...), custom_call_target="tpu_custom_call" | custom-call | tf_op jit(solution)/shard_map/pallas_call | solution.py:26
  26.4 1.7 %collective-permute-done.5.theirs = s32[1,384]{1,0:T(1,128)S(1)} collective-permute-done((s32[1,384]{1,0:T(1,128)S(1)}, s32[1,384]{1,0:T(1,128)S(1)}, u32[]{:S(2)}, u32[]{:S(2)}) %collective-permute-start.5) | collective-permute-done | bytes 1568 | tf_op jit(solution)/shard_map/ppermute | solution.py:304
  28.1 0.2 shard_map.154
  28.3 4.7 %shard_map.155 = (f32[16,64,128]{2,1,0:T(8,128)S(1)}, f32[16,64,128]{2,1,0:T(8,128)S(1)}, bf16[16,3,16,128]{3,2,1,0:T(8,128)(2,1)}, bf16[44,128,128]{2,1,0:T(8,1...) custom-call(s32[1,640]{1,0:T(1,128)S(1)} %get-tuple-element.37.own, ...), custom_call_target="tpu_custom_call" | custom-call | tf_op jit(solution)/shard_map/pallas_call | solution.py:26
  33.1 7.7 %all-to-all-start = ((bf16[16,48,128]{2,1,0:T(8,128)(2,1)}), bf16[16,48,128]{2,1,0:T(8,128)(2,1)S(1)}, u32[]{:S(2)}, u32[]{:S(2)}) async-start(bf16[16,48,128]{2,1,0:T(8,128)(2,1)} %bitcast.7), calls=%async_computation | async-start | bytes 393216 | tf_op jit(solution)/shard_map/all_to_all | solution.py:539
  40.7 0.0 collective-permute-done.4.refs_0_
  40.8 0.0 copy-start
  40.8 0.0 copy-start.1
  40.8 0.0 copy-start.4
  40.8 0.0 copy-start.5
  40.8 0.0 copy-start.7
  40.8 1.3 %shard_map.156 = (bf16[16,64,128]{2,1,0:T(8,128)(2,1)S(1)}, f32[16,64,128]{2,1,0:T(8,128)S(1)}, bf16[17,64,128]{2,1,0:T(8,128)(2,1)S(1)}) custom-call(s32[1,640]{1,0:T(1,128)S(1)} %get-tuple-element.37.own, s32[1,640]{1,0:T(1,128)S(1)} %shard_map.149.other, bf16[16,64,128]{2,1,0:T(8,128)(2,1)S(1)} %collective-permute-done.4.refs_0_, ...), custom_call_target="tpu_custom_call" | custom-call | tf_op jit(solution)/shard_map/pallas_call | solution.py:26
  42.2 4.3 %collective-permute-start.6 = (bf16[16,64,128]{2,1,0:T(8,128)(2,1)S(1)}, bf16[16,64,128]{2,1,0:T(8,128)(2,1)S(1)}, u32[]{:S(2)}, u32[]{:S(2)}) collective-permute-start(bf16[16,64,128]{2,1,0:T(8,128)(2,1)S(1)} %get-tuple-element.60), channel_id=1, source_target_pairs={{0,2},{2,4},{4,6},{1,3},{3,5},{5,7},{8,10},{10,12},{12,14},{9,11},... | collective-permute-start | bytes 786440 | tf_op jit(solution)/shard_map/ppermute | solution.py:555
  46.5 0.0 copy-done
  46.5 0.0 copy-done.1
  46.5 0.0 copy-done.4
  46.5 0.0 copy-done.5
  46.5 0.0 copy-done.7
  46.5 0.0 copy-start.12
  46.5 3.6 %shard_map.157 = (f32[32,64,128]{2,1,0:T(8,128)}, f32[16,64,128]{2,1,0:T(8,128)S(1)}, f32[32,64,128]{2,1,0:T(8,128)}) custom-call(s32[1,640]{1,0:T(1,128)S(1)} %get-tuple-element.37.own, s32[1,640]{1,0:T(1,128)S(1)} %shard_map.149.other, f32[16,64,128]{2,1,0:T(8,128)S(1)} %get-tuple-element.61.refs_0_, f32[16,64,128]{2,1,0:T(8,128)S(1)} %copy-done.5, ...), custom_call_target="tpu_custom_call" | custom-call | tf_op jit(solution)/shard_map/pallas_call | solution.py:26
  50.1 0.0 all-to-all-done
  50.1 0.0 copy-done.12
  50.1 1.1 %shard_map.159 = f32[64,256]{1,0:T(8,128)} custom-call(bf16[768,128]{1,0:T(8,128)(2,1)S(1)} %bitcast.9, f32[64,256]{1,0:T(8,128)S(1)} %copy-done.12, bf16[256,256]{1,0:T(8,128)(2,1)S(1)} %copy-done.6), custom_call_target="tpu_custom_call" | custom-call | tf_op jit(solution)/shard_map/pallas_call | solution.py:26
  51.2 0.0 collective-permute-done.6.arrived
  51.2 0.8 %shard_map.158 = f32[32,64,128]{2,1,0:T(8,128)} custom-call(bf16[16,64,128]{2,1,0:T(8,128)(2,1)S(1)} %collective-permute-done.6.arrived, f32[16,64,128]{2,1,0:T(8,128)S(1)} %get-tuple-element.66.low_next, f32[32,64,128]{2,1,0:T(8,128)} %get-tuple-element.67.lam_in), custom_call_target="tpu_custom_call", output_to_operand_aliasing={{}: (2, {})} | custom-call | tf_op jit(solution)/shard_map/pallas_call | solution.py:26
  (1 shorter events, 0.0 us)
Async XLA Ops:
  0.6 6.5 %collective-permute-start.2 = (bf16[96,128,128]{2,1,0:T(8,128)(2,1)}, bf16[96,128,128]{2,1,0:T(8,128)(2,1)S(1)}, u32[]{:S(2)}, u32[]{:S(2)}) collective-permute-start(bf16[96,128,128]{2,1,0:T(8,128)(2,1)} %refs_7_.3), channel_id=1, source_target_pairs={{0,1},{1,0},{2,3},{3,2},{4,5},{5,4},{6,7},{7,6},{8,9},{9,8},{10,11... | collective-permute-start | bytes 9437192 | tf_op jit(solution)/shard_map/ppermute | solution.py:94
  1.2 5.5 %collective-permute-start = (s32[96]{0:T(128)}, s32[96]{0:T(128)S(1)}, u32[]{:S(2)}, u32[]{:S(2)}) collective-permute-start(s32[96]{0:T(128)} %rows.1), channel_id=1, source_target_pairs={{0,1},{1,0},{2,3},{3,2},{4,5},{5,4},{6,7},{7,6},{8,9},{9,8},{10,11... | collective-permute-start | bytes 1160 | tf_op jit(solution)/shard_map/ppermute | solution.py:92
  1.3 5.4 %collective-permute-start.1 = (s32[96]{0:T(128)}, s32[96]{0:T(128)S(1)}, u32[]{:S(2)}, u32[]{:S(2)}) collective-permute-start(s32[96]{0:T(128)} %columns.1), channel_id=1, source_target_pairs={{0,1},{1,0},{2,3},{3,2},{4,5},{5,4},{6,7},{7,6},{8,9},{9,8},{10,11... | collective-permute-start | bytes 1160 | tf_op jit(solution)/shard_map/ppermute | solution.py:93
  5.5 7.8 %copy-start.2 = (f32[32,64,128]{2,1,0:T(8,128)S(1)}, f32[32,64,128]{2,1,0:T(8,128)}, u32[]{:S(2)}) copy-start(f32[32,64,128]{2,1,0:T(8,128)} %refs_5_.2) | copy-start | bytes 3145732
  5.5 7.8 %copy-start.3 = (f32[32,64,128]{2,1,0:T(8,128)S(1)}, f32[32,64,128]{2,1,0:T(8,128)}, u32[]{:S(2)}) copy-start(f32[32,64,128]{2,1,0:T(8,128)} %refs_6_.2) | copy-start | bytes 3145732
  5.5 7.8 %copy-start.8 = (f32[32,128]{1,0:T(8,128)S(1)}, f32[32,128]{1,0:T(8,128)}, u32[]{:S(2)}) copy-start(f32[32,128]{1,0:T(8,128)} %refs_4_.3) | copy-start | bytes 49156
  5.6 7.8 %copy-start.9 = (f32[32,128]{1,0:T(8,128)S(1)}, f32[32,128]{1,0:T(8,128)}, u32[]{:S(2)}) copy-start(f32[32,128]{1,0:T(8,128)} %refs_5_.3) | copy-start | bytes 49156
  5.6 7.8 %copy-start.10 = (f32[32,128]{1,0:T(8,128)S(1)}, f32[32,128]{1,0:T(8,128)}, u32[]{:S(2)}) copy-start(f32[32,128]{1,0:T(8,128)} %refs_6_.3) | copy-start | bytes 49156
  8.4 10.7 %collective-permute-start.3 = (bf16[16,64,128]{2,1,0:T(8,128)(2,1)S(1)}, bf16[16,64,128]{2,1,0:T(8,128)(2,1)S(1)}, u32[]{:S(2)}, u32[]{:S(2)}) collective-permute-start(bf16[16,64,128]{2,1,0:T(8,128)(2,1)S(1)} %shard_map.150), channel_id=1, source_target_pairs={{0,2},{2,4},{4,6},{1,3},{3,5},{5,7},{8,10},{10,12},{12,14},{9,11},... | collective-permute-start | bytes 786440 | tf_op jit(solution)/shard_map/ppermute | solution.py:294
  19.1 4.0 %copy-start.13 = (s32[128]{0:T(128)S(1)}, s32[128]{0:T(128)}, u32[]{:S(2)}) copy-start(s32[128]{0:T(128)} %param.24) | copy-start | bytes 1540
  19.1 4.0 %copy-start.14 = (s32[128]{0:T(128)S(1)}, s32[128]{0:T(128)}, u32[]{:S(2)}) copy-start(s32[128]{0:T(128)} %param.22) | copy-start | bytes 1540
  19.1 4.0 %copy-start.15 = (s32[128,1]{0,1:T(1,128)S(1)}, s32[128,1]{0,1:T(1,128)}, u32[]{:S(2)}) copy-start(s32[128,1]{0,1:T(1,128)} %param.23) | copy-start | bytes 1540
  19.1 6.1 %copy-start.6 = (bf16[256,256]{1,0:T(8,128)(2,1)S(1)}, bf16[256,256]{1,0:T(8,128)(2,1)}, u32[]{:S(2)}) copy-start(bf16[256,256]{1,0:T(8,128)(2,1)} %matrix.3) | copy-start | bytes 393220
  19.1 6.1 %copy-start.11 = (f32[64,256]{1,0:T(8,128)S(1)}, f32[64,256]{1,0:T(8,128)}, u32[]{:S(2)}) copy-start(f32[64,256]{1,0:T(8,128)} %trans.1) | copy-start | bytes 196612
  20.6 20.2 %collective-permute-start.4 = (bf16[16,64,128]{2,1,0:T(8,128)(2,1)S(1)}, bf16[16,64,128]{2,1,0:T(8,128)(2,1)S(1)}, u32[]{:S(2)}, u32[]{:S(2)}) collective-permute-start(bf16[16,64,128]{2,1,0:T(8,128)(2,1)S(1)} %get-tuple-element.44.refs_1_), channel_id=1, source_target_pairs={{0,2},{2,4},{4,6},{6,0},{1,3},{3,5},{5,7},{7,1},{8,10},{10,12},{12... | collective-permute-start | bytes 786440 | tf_op jit(solution)/shard_map/ppermute | solution.py:512
  23.1 5.0 %collective-permute-start.5 = (s32[1,384]{1,0:T(1,128)S(1)}, s32[1,384]{1,0:T(1,128)S(1)}, u32[]{:S(2)}, u32[]{:S(2)}) collective-permute-start(s32[1,384]{1,0:T(1,128)S(1)} %pad_add_fusion), channel_id=1, source_target_pairs={{2,0},{4,2},{6,4},{0,6},{3,1},{5,3},{7,5},{1,7},{10,8},{12,10},{14... | collective-permute-start | bytes 4616 | tf_op jit(solution)/shard_map/ppermute | solution.py:304
  33.1 17.1 %all-to-all-start = ((bf16[16,48,128]{2,1,0:T(8,128)(2,1)}), bf16[16,48,128]{2,1,0:T(8,128)(2,1)S(1)}, u32[]{:S(2)}, u32[]{:S(2)}) async-start(bf16[16,48,128]{2,1,0:T(8,128)(2,1)} %bitcast.7), calls=%async_computation | async-start | bytes 393216 | tf_op jit(solution)/shard_map/all_to_all | solution.py:539
  40.8 5.7 %copy-start = (bf16[96,128,128]{2,1,0:T(8,128)(2,1)S(1)}, bf16[96,128,128]{2,1,0:T(8,128)(2,1)}, u32[]{:S(2)}) copy-start(bf16[96,128,128]{2,1,0:T(8,128)(2,1)} %refs_7_.3) | copy-start | bytes 9437188
  40.8 5.7 %copy-start.1 = (bf16[96,128,128]{2,1,0:T(8,128)(2,1)S(1)}, bf16[96,128,128]{2,1,0:T(8,128)(2,1)}, u32[]{:S(2)}) copy-start(bf16[96,128,128]{2,1,0:T(8,128)(2,1)} %get-tuple-element.59.refs_5_.refs_8_) | copy-start | bytes 9437188
  40.8 5.7 %copy-start.4 = (f32[32,64,128]{2,1,0:T(8,128)S(1)}, f32[32,64,128]{2,1,0:T(8,128)}, u32[]{:S(2)}) copy-start(f32[32,64,128]{2,1,0:T(8,128)} %get-tuple-element.65.refs_9_) | copy-start | bytes 3145732
  40.8 5.7 %copy-start.5 = (f32[16,64,128]{2,1,0:T(8,128)S(1)}, f32[16,64,128]{2,1,0:T(8,128)}, u32[]{:S(2)}) copy-start(f32[16,64,128]{2,1,0:T(8,128)} %get-tuple-element.62.refs_1_) | copy-start | bytes 1572868
  40.8 5.7 %copy-start.7 = (bf16[17,64,128]{2,1,0:T(8,128)(2,1)S(1)}, bf16[17,64,128]{2,1,0:T(8,128)(2,1)}, u32[]{:S(2)}) copy-start(bf16[17,64,128]{2,1,0:T(8,128)(2,1)} %get-tuple-element.64.refs_3_) | copy-start | bytes 835588
  42.2 9.1 %collective-permute-start.6 = (bf16[16,64,128]{2,1,0:T(8,128)(2,1)S(1)}, bf16[16,64,128]{2,1,0:T(8,128)(2,1)S(1)}, u32[]{:S(2)}, u32[]{:S(2)}) collective-permute-start(bf16[16,64,128]{2,1,0:T(8,128)(2,1)S(1)} %get-tuple-element.60), channel_id=1, source_target_pairs={{0,2},{2,4},{4,6},{1,3},{3,5},{5,7},{8,10},{10,12},{12,14},{9,11},... | collective-permute-start | bytes 786440 | tf_op jit(solution)/shard_map/ppermute | solution.py:555
  46.5 3.6 %copy-start.12 = (f32[64,256]{1,0:T(8,128)S(1)}, f32[64,256]{1,0:T(8,128)}, u32[]{:S(2)}) copy-start(f32[64,256]{1,0:T(8,128)} %get-tuple-element.70.product) | copy-start | bytes 196612

commit v12 on v11

--- a/solution.py
+++ b/solution.py
@@ -8,8 +8,8 @@
 
 STEPS = 3
 UNROLL = 16
-FEW = 28
-MANY = 48
+FEW = 24
+MANY = 40
 KEEP = 44
 CLASSES = 4
 VMEM_LIMIT = 24 << 20
@@ -291,7 +291,7 @@
         listed + [(acc, VM), (lo, VM), (hi, VM), (other, VM)],
         scratch=[pltpu.VMEM((rim, cases, nodes), F32)],
     )
-    arriving = lax.ppermute(leaving, "blk", onward[:-1])
+    arriving = lax.ppermute(leaving, "blk", onward)
 
     mine = jnp.concatenate(
         [

time: 52.5 us -> 51.2 us (0.975)
  starting transfers between devices: 22.5 us -> 20.2 us
  Pallas kernels: 23.6 us -> 24.3 us
  waiting for transfers between devices: 4.89 us -> 5.44 us
    ppermute x2 -> x1, starting transfers between devices: 9.14 us -> 4.1 us  [local(): arriving = lax.ppermute(leaving, 'blk', onward[:-1])]
    ppermute x1 -> x2, waiting for transfers between devices: 0.01 us -> 3.79 us  [local(): arriving = lax.ppermute(leaving, 'blk', onward)]
    ppermute x2 -> x1, waiting for transfers between devices: 2.06 us -> 0.01 us  [local(): arriving = lax.ppermute(leaving, 'blk', onward[:-1])]
    ppermute x1, starting transfers between devices: 2.12 us -> 3.56 us  [local(): theirs = lax.ppermute(mine, 'blk', backward)]
    ppermute x1 -> x2, starting transfers between devices: 2.54 us -> 3.94 us  [local(): arriving = lax.ppermute(leaving, 'blk', onward)]
    ppermute x1, waiting for transfers between devices: 1.72 us -> 0.53 us  [local(): theirs = lax.ppermute(mine, 'blk', backward)]
    pallas_call x12, Pallas kernels: 23.6 us -> 24.3 us  [kernel(): pl.pallas_call(body, out_shape=outs, in_specs=[spec for _, spec in ins],...]
  transfers between devices with their start and end apart: 8 -> 8, of which waited for: 3 -> 3; matrix products, arithmetic and copies ran while one was open for 0% -> 0% of each run, Pallas kernels for 38% -> 41%
where the time goes in v12:
time: 51.2 us; the launch traced here: 50.9 us
  Pallas kernels  24.3 us (47%)
  starting transfers between devices  20.2 us (39%)
  waiting for transfers between devices  5.44 us (11%)
  between operations  0.91 us (2%)
    pallas_call x12, Pallas kernels, kernel(): pl.pallas_call(body, out_shape=outs, in_specs=[spec for _, spec in ins],...  24.3 us
    all_to_all x1, starting transfers between devices, local(): lax.all_to_all(sent.reshape(network, 3 * slots, nodes), ('sec', 'blk'), s...  7.56 us
    ppermute x1, starting transfers between devices, local(): arriving = lax.ppermute(leaving, 'blk', onward[:-1])  4.1 us
    ppermute x2, starting transfers between devices, local(): arriving = lax.ppermute(leaving, 'blk', onward)  3.94 us
    ppermute x2, waiting for transfers between devices, local(): arriving = lax.ppermute(leaving, 'blk', onward)  3.79 us
    ppermute x1, starting transfers between devices, local(): theirs = lax.ppermute(mine, 'blk', backward)  3.56 us
    ppermute x1, waiting for transfers between devices, local(): other_rows = lax.ppermute(tile_source_index, 'case', swap)  1.1 us
  transfers between devices with their start and end apart: 8, of which 3 were waited for; matrix products, arithmetic and copies ran while one was open for 0% of the time, Pallas kernels for 41%

profile of v12, /device:TPU:0, one launch (start us, length us, event | category | flops | bytes accessed | tf_op | source)
XLA Modules:
  0.0 50.9 jit_solution(13045876885647998988)
XLA Ops:
  0.6 0.6 %collective-permute-start.2 = (bf16[96,128,128]{2,1,0:T(8,128)(2,1)}, bf16[96,128,128]{2,1,0:T(8,128)(2,1)S(1)}, u32[]{:S(2)}, u32[]{:S(2)}) collective-permute-start(bf16[96,128,128]{2,1,0:T(8,128)(2,1)} %refs_7_.3), channel_id=1, source_target_pairs={{0,1},{1,0},{2,3},{3,2},{4,5},{5,4},{6,7},{7,6},{8,9},{9,8},{10,11... | collective-permute-start | bytes 9437192 | tf_op jit(solution)/shard_map/ppermute | solution.py:94
  1.2 0.1 collective-permute-start
  1.3 0.4 collective-permute-start.1
  1.7 3.8 %shard_map.148 = (f32[48,64,128]{2,1,0:T(8,128)S(1)}, bf16[17,64,128]{2,1,0:T(8,128)(2,1)S(1)}, bf16[17,64,128]{2,1,0:T(8,128)(2,1)S(1)}, bf16[96,128,128]{2,1,0:T(8,128)(2,1)S(1)}, s32[1,640]{1,0:T(1,128)S(1)}) custom-call(s32[96]{0:T(128)} %rows.1, s32[96]{0:T(128)} %columns.1, s32[1,96]{1,0:T(1,128)} %bitcast.18, s32[1,96]{1,0:T(1,128)} %bitcast.19, ...), custom_call_target="tpu_custom_call" | custom-call | tf_op jit(solution)/shard_map/pallas_call | solution.py:26
  5.5 0.0 copy-start.2
  5.5 0.0 copy-start.3
  5.5 0.0 copy-start.8
  5.6 0.0 copy-start.9
  5.6 0.0 copy-start.10
  5.6 1.1 %collective-permute-done = s32[96]{0:T(128)S(1)} collective-permute-done((s32[96]{0:T(128)}, s32[96]{0:T(128)S(1)}, u32[]{:S(2)}, u32[]{:S(2)}) %collective-permute-start) | collective-permute-done | bytes 416 | tf_op jit(solution)/shard_map/ppermute | solution.py:92
  6.7 0.0 collective-permute-done.1
  6.7 0.4 shard_map.149.other
  7.1 0.0 collective-permute-done.2.refs_3_.refs_4_.refs_9_
  7.1 1.3 %shard_map.150 = bf16[16,64,128]{2,1,0:T(8,128)(2,1)S(1)} custom-call(s32[1,640]{1,0:T(1,128)S(1)} %get-tuple-element.37.own, s32[1,640]{1,0:T(1,128)S(1)} %shard_map.149.other, f32[48,64,128]{2,1,0:T(8,128)S(1)} %get-tuple-element.38.refs_0_, bf16[17,64,128]{2,1,0:T(8,128)(2,1)S(1)} %get-tuple-element.39.refs_1_.lo, ...), custom_call_target="tpu_custom_call" | custom-call | tf_op jit(solution)/shard_map/pallas_call | solution.py:26
  8.4 3.6 %collective-permute-start.3 = (bf16[16,64,128]{2,1,0:T(8,128)(2,1)S(1)}, bf16[16,64,128]{2,1,0:T(8,128)(2,1)S(1)}, u32[]{:S(2)}, u32[]{:S(2)}) collective-permute-start(bf16[16,64,128]{2,1,0:T(8,128)(2,1)S(1)} %shard_map.150), channel_id=1, source_target_pairs={{0,2},{2,4},{4,6},{6,0},{1,3},{3,5},{5,7},{7,1},{8,10},{10,12},{12... | collective-permute-start | bytes 786440 | tf_op jit(solution)/shard_map/ppermute | solution.py:294
  11.9 0.0 copy-done.2
  11.9 0.0 copy-done.3
  11.9 0.0 copy-done.8
  12.0 0.0 copy-done.9
  12.0 0.0 copy-done.10
  12.0 4.2 %shard_map.151 = (f32[32,64,128]{2,1,0:T(8,128)S(1)}, f32[32,64,128]{2,1,0:T(8,128)S(1)}, f32[16,64,128]{2,1,0:T(8,128)S(1)}, bf16[17,64,128]{2,1,0:T(8,128)(2,1...) custom-call(s32[1,640]{1,0:T(1,128)S(1)} %get-tuple-element.37.own, s32[1,640]{1,0:T(1,128)S(1)} %shard_map.149.other, ...), custom_call_target="tpu_custom_call" | custom-call | tf_op jit(solution)/shard_map/pallas_call | solution.py:26
  16.2 3.8 %collective-permute-done.3.refs_0_ = bf16[16,64,128]{2,1,0:T(8,128)(2,1)S(1)} collective-permute-done((bf16[16,64,128]{2,1,0:T(8,128)(2,1)S(1)}, bf16[16,64,128]{2,1,0:T(8,128)(2,1)S(1)}, u32[]{:S(2)}, u32[]{:S(2)}) %collective-permute-start.3) | collective-permute-done | bytes 262176 | tf_op jit(solution)/shard_map/ppermute | solution.py:294
  20.0 0.0 copy-start.13
  20.0 0.0 copy-start.14
  20.0 0.0 copy-start.15
  20.0 0.0 copy-start.6
  20.0 0.0 copy-start.11
  20.0 1.3 %shard_map.152 = (bf16[16,64,128]{2,1,0:T(8,128)(2,1)S(1)}, f32[16,64,128]{2,1,0:T(8,128)S(1)}, bf16[17,64,128]{2,1,0:T(8,128)(2,1)S(1)}) custom-call(s32[1,640]{1,0:T(1,128)S(1)} %get-tuple-element.37.own, s32[1,640]{1,0:T(1,128)S(1)} %shard_map.149.other, bf16[16,64,128]{2,1,0:T(8,128)(2,1)S(1)} %collective-permute-done.3.refs_0_, ...), custom_call_target="tpu_custom_call" | custom-call | tf_op jit(solution)/shard_map/pallas_call | solution.py:26
  21.4 0.4 collective-permute-start.4
  21.7 0.0 copy-done.13
  21.7 0.0 copy-done.14
  21.7 0.0 copy-done.15
  21.7 3.6 %collective-permute-start.5 = (s32[1,384]{1,0:T(1,128)S(1)}, s32[1,384]{1,0:T(1,128)S(1)}, u32[]{:S(2)}, u32[]{:S(2)}) collective-permute-start(s32[1,384]{1,0:T(1,128)S(1)} %pad_add_fusion), channel_id=1, source_target_pairs={{2,0},{4,2},{6,4},{0,6},{3,1},{5,3},{7,5},{1,7},{10,8},{12,10},{14... | collective-permute-start | bytes 4616 | tf_op jit(solution)/shard_map/ppermute | solution.py:304
  25.3 0.0 copy-done.6
  25.3 0.0 copy-done.11
  25.3 1.2 %shard_map.153 = (bf16[32,128,128]{2,1,0:T(8,128)(2,1)S(1)}, bf16[64,128]{1,0:T(8,128)(2,1)S(1)}, bf16[256,128]{1,0:T(8,128)(2,1)S(1)}, f32[64,256]{1,0:T(8,128)}) custom-call(s32[1,128]{1,0:T(1,128)S(1)} %bitcast.13, s32[1,128]{1,0:T(1,128)S(1)} %bitcast.15, bf16[17,64,128]{2,1,0:T(8,128)(2,1)S(1)} %get-tuple-element.39.refs_1_.lo, ...), custom_call_target="tpu_custom_call" | custom-call | tf_op jit(solution)/shard_map/pallas_call | solution.py:26
  26.5 0.5 %collective-permute-done.5.theirs = s32[1,384]{1,0:T(1,128)S(1)} collective-permute-done((s32[1,384]{1,0:T(1,128)S(1)}, s32[1,384]{1,0:T(1,128)S(1)}, u32[]{:S(2)}, u32[]{:S(2)}) %collective-permute-start.5) | collective-permute-done | bytes 1568 | tf_op jit(solution)/shard_map/ppermute | solution.py:304
  27.0 0.2 shard_map.154
  27.2 4.5 %shard_map.155 = (f32[16,64,128]{2,1,0:T(8,128)S(1)}, f32[16,64,128]{2,1,0:T(8,128)S(1)}, bf16[16,3,16,128]{3,2,1,0:T(8,128)(2,1)}, bf16[44,128,128]{2,1,0:T(8,1...) custom-call(s32[1,640]{1,0:T(1,128)S(1)} %get-tuple-element.37.own, ...), custom_call_target="tpu_custom_call" | custom-call | tf_op jit(solution)/shard_map/pallas_call | solution.py:26
  31.7 7.6 %all-to-all-start = ((bf16[16,48,128]{2,1,0:T(8,128)(2,1)}), bf16[16,48,128]{2,1,0:T(8,128)(2,1)S(1)}, u32[]{:S(2)}, u32[]{:S(2)}) async-start(bf16[16,48,128]{2,1,0:T(8,128)(2,1)} %bitcast.7), calls=%async_computation | async-start | bytes 393216 | tf_op jit(solution)/shard_map/all_to_all | solution.py:539
  39.3 0.0 collective-permute-done.4.refs_0_
  39.3 0.0 copy-start
  39.3 0.0 copy-start.1
  39.3 0.0 copy-start.4
  39.3 0.0 copy-start.5
  39.3 0.0 copy-start.7
  39.3 1.3 %shard_map.156 = (bf16[16,64,128]{2,1,0:T(8,128)(2,1)S(1)}, f32[16,64,128]{2,1,0:T(8,128)S(1)}, bf16[17,64,128]{2,1,0:T(8,128)(2,1)S(1)}) custom-call(s32[1,640]{1,0:T(1,128)S(1)} %get-tuple-element.37.own, s32[1,640]{1,0:T(1,128)S(1)} %shard_map.149.other, bf16[16,64,128]{2,1,0:T(8,128)(2,1)S(1)} %collective-permute-done.4.refs_0_, ...), custom_call_target="tpu_custom_call" | custom-call | tf_op jit(solution)/shard_map/pallas_call | solution.py:26
  40.6 4.1 %collective-permute-start.6 = (bf16[16,64,128]{2,1,0:T(8,128)(2,1)S(1)}, bf16[16,64,128]{2,1,0:T(8,128)(2,1)S(1)}, u32[]{:S(2)}, u32[]{:S(2)}) collective-permute-start(bf16[16,64,128]{2,1,0:T(8,128)(2,1)S(1)} %get-tuple-element.60), channel_id=1, source_target_pairs={{0,2},{2,4},{4,6},{1,3},{3,5},{5,7},{8,10},{10,12},{12,14},{9,11},... | collective-permute-start | bytes 786440 | tf_op jit(solution)/shard_map/ppermute | solution.py:555
  44.7 0.0 copy-done
  44.7 0.0 copy-done.1
  44.8 0.0 copy-done.4
  44.8 0.0 copy-done.5
  44.8 0.0 copy-done.7
  44.8 0.0 copy-start.12
  44.8 4.2 %shard_map.157 = (f32[32,64,128]{2,1,0:T(8,128)}, f32[16,64,128]{2,1,0:T(8,128)S(1)}, f32[32,64,128]{2,1,0:T(8,128)}) custom-call(s32[1,640]{1,0:T(1,128)S(1)} %get-tuple-element.37.own, s32[1,640]{1,0:T(1,128)S(1)} %shard_map.149.other, f32[16,64,128]{2,1,0:T(8,128)S(1)} %get-tuple-element.61.refs_0_, f32[16,64,128]{2,1,0:T(8,128)S(1)} %copy-done.5, ...), custom_call_target="tpu_custom_call" | custom-call | tf_op jit(solution)/shard_map/pallas_call | solution.py:26
  49.0 0.0 all-to-all-done
  49.0 0.0 copy-done.12
  49.0 1.1 %shard_map.159 = f32[64,256]{1,0:T(8,128)} custom-call(bf16[768,128]{1,0:T(8,128)(2,1)S(1)} %bitcast.9, f32[64,256]{1,0:T(8,128)S(1)} %copy-done.12, bf16[256,256]{1,0:T(8,128)(2,1)S(1)} %copy-done.6), custom_call_target="tpu_custom_call" | custom-call | tf_op jit(solution)/shard_map/pallas_call | solution.py:26
  50.1 0.0 collective-permute-done.6.arrived
  50.1 0.8 %shard_map.158 = f32[32,64,128]{2,1,0:T(8,128)} custom-call(bf16[16,64,128]{2,1,0:T(8,128)(2,1)S(1)} %collective-permute-done.6.arrived, f32[16,64,128]{2,1,0:T(8,128)S(1)} %get-tuple-element.66.low_next, f32[32,64,128]{2,1,0:T(8,128)} %get-tuple-element.67.lam_in), custom_call_target="tpu_custom_call", output_to_operand_aliasing={{}: (2, {})} | custom-call | tf_op jit(solution)/shard_map/pallas_call | solution.py:26
  (1 shorter events, 0.0 us)
Async XLA Ops:
  0.6 6.5 %collective-permute-start.2 = (bf16[96,128,128]{2,1,0:T(8,128)(2,1)}, bf16[96,128,128]{2,1,0:T(8,128)(2,1)S(1)}, u32[]{:S(2)}, u32[]{:S(2)}) collective-permute-start(bf16[96,128,128]{2,1,0:T(8,128)(2,1)} %refs_7_.3), channel_id=1, source_target_pairs={{0,1},{1,0},{2,3},{3,2},{4,5},{5,4},{6,7},{7,6},{8,9},{9,8},{10,11... | collective-permute-start | bytes 9437192 | tf_op jit(solution)/shard_map/ppermute | solution.py:94
  1.2 5.5 %collective-permute-start = (s32[96]{0:T(128)}, s32[96]{0:T(128)S(1)}, u32[]{:S(2)}, u32[]{:S(2)}) collective-permute-start(s32[96]{0:T(128)} %rows.1), channel_id=1, source_target_pairs={{0,1},{1,0},{2,3},{3,2},{4,5},{5,4},{6,7},{7,6},{8,9},{9,8},{10,11... | collective-permute-start | bytes 1160 | tf_op jit(solution)/shard_map/ppermute | solution.py:92
  1.3 5.4 %collective-permute-start.1 = (s32[96]{0:T(128)}, s32[96]{0:T(128)S(1)}, u32[]{:S(2)}, u32[]{:S(2)}) collective-permute-start(s32[96]{0:T(128)} %columns.1), channel_id=1, source_target_pairs={{0,1},{1,0},{2,3},{3,2},{4,5},{5,4},{6,7},{7,6},{8,9},{9,8},{10,11... | collective-permute-start | bytes 1160 | tf_op jit(solution)/shard_map/ppermute | solution.py:93
  5.5 6.4 %copy-start.2 = (f32[32,64,128]{2,1,0:T(8,128)S(1)}, f32[32,64,128]{2,1,0:T(8,128)}, u32[]{:S(2)}) copy-start(f32[32,64,128]{2,1,0:T(8,128)} %refs_5_.2) | copy-start | bytes 3145732
  5.5 6.4 %copy-start.3 = (f32[32,64,128]{2,1,0:T(8,128)S(1)}, f32[32,64,128]{2,1,0:T(8,128)}, u32[]{:S(2)}) copy-start(f32[32,64,128]{2,1,0:T(8,128)} %refs_6_.2) | copy-start | bytes 3145732
  5.5 6.4 %copy-start.8 = (f32[32,128]{1,0:T(8,128)S(1)}, f32[32,128]{1,0:T(8,128)}, u32[]{:S(2)}) copy-start(f32[32,128]{1,0:T(8,128)} %refs_4_.3) | copy-start | bytes 49156
  5.6 6.4 %copy-start.9 = (f32[32,128]{1,0:T(8,128)S(1)}, f32[32,128]{1,0:T(8,128)}, u32[]{:S(2)}) copy-start(f32[32,128]{1,0:T(8,128)} %refs_5_.3) | copy-start | bytes 49156
  5.6 6.4 %copy-start.10 = (f32[32,128]{1,0:T(8,128)S(1)}, f32[32,128]{1,0:T(8,128)}, u32[]{:S(2)}) copy-start(f32[32,128]{1,0:T(8,128)} %refs_6_.3) | copy-start | bytes 49156
  8.4 11.6 %collective-permute-start.3 = (bf16[16,64,128]{2,1,0:T(8,128)(2,1)S(1)}, bf16[16,64,128]{2,1,0:T(8,128)(2,1)S(1)}, u32[]{:S(2)}, u32[]{:S(2)}) collective-permute-start(bf16[16,64,128]{2,1,0:T(8,128)(2,1)S(1)} %shard_map.150), channel_id=1, source_target_pairs={{0,2},{2,4},{4,6},{6,0},{1,3},{3,5},{5,7},{7,1},{8,10},{10,12},{12... | collective-permute-start | bytes 786440 | tf_op jit(solution)/shard_map/ppermute | solution.py:294
  20.0 1.7 %copy-start.13 = (s32[128]{0:T(128)S(1)}, s32[128]{0:T(128)}, u32[]{:S(2)}) copy-start(s32[128]{0:T(128)} %param.24) | copy-start | bytes 1540
  20.0 1.7 %copy-start.14 = (s32[128]{0:T(128)S(1)}, s32[128]{0:T(128)}, u32[]{:S(2)}) copy-start(s32[128]{0:T(128)} %param.22) | copy-start | bytes 1540
  20.0 1.7 %copy-start.15 = (s32[128,1]{0,1:T(1,128)S(1)}, s32[128,1]{0,1:T(1,128)}, u32[]{:S(2)}) copy-start(s32[128,1]{0,1:T(1,128)} %param.23) | copy-start | bytes 1540
  20.0 5.3 %copy-start.6 = (bf16[256,256]{1,0:T(8,128)(2,1)S(1)}, bf16[256,256]{1,0:T(8,128)(2,1)}, u32[]{:S(2)}) copy-start(bf16[256,256]{1,0:T(8,128)(2,1)} %matrix.3) | copy-start | bytes 393220
  20.0 5.3 %copy-start.11 = (f32[64,256]{1,0:T(8,128)S(1)}, f32[64,256]{1,0:T(8,128)}, u32[]{:S(2)}) copy-start(f32[64,256]{1,0:T(8,128)} %trans.1) | copy-start | bytes 196612
  21.4 17.9 %collective-permute-start.4 = (bf16[16,64,128]{2,1,0:T(8,128)(2,1)S(1)}, bf16[16,64,128]{2,1,0:T(8,128)(2,1)S(1)}, u32[]{:S(2)}, u32[]{:S(2)}) collective-permute-start(bf16[16,64,128]{2,1,0:T(8,128)(2,1)S(1)} %get-tuple-element.44.refs_1_), channel_id=1, source_target_pairs={{0,2},{2,4},{4,6},{6,0},{1,3},{3,5},{5,7},{7,1},{8,10},{10,12},{12... | collective-permute-start | bytes 786440 | tf_op jit(solution)/shard_map/ppermute | solution.py:512
  21.7 5.3 %collective-permute-start.5 = (s32[1,384]{1,0:T(1,128)S(1)}, s32[1,384]{1,0:T(1,128)S(1)}, u32[]{:S(2)}, u32[]{:S(2)}) collective-permute-start(s32[1,384]{1,0:T(1,128)S(1)} %pad_add_fusion), channel_id=1, source_target_pairs={{2,0},{4,2},{6,4},{0,6},{3,1},{5,3},{7,5},{1,7},{10,8},{12,10},{14... | collective-permute-start | bytes 4616 | tf_op jit(solution)/shard_map/ppermute | solution.py:304
  31.7 17.3 %all-to-all-start = ((bf16[16,48,128]{2,1,0:T(8,128)(2,1)}), bf16[16,48,128]{2,1,0:T(8,128)(2,1)S(1)}, u32[]{:S(2)}, u32[]{:S(2)}) async-start(bf16[16,48,128]{2,1,0:T(8,128)(2,1)} %bitcast.7), calls=%async_computation | async-start | bytes 393216 | tf_op jit(solution)/shard_map/all_to_all | solution.py:539
  39.3 5.5 %copy-start = (bf16[96,128,128]{2,1,0:T(8,128)(2,1)S(1)}, bf16[96,128,128]{2,1,0:T(8,128)(2,1)}, u32[]{:S(2)}) copy-start(bf16[96,128,128]{2,1,0:T(8,128)(2,1)} %refs_7_.3) | copy-start | bytes 9437188
  39.3 5.4 %copy-start.1 = (bf16[96,128,128]{2,1,0:T(8,128)(2,1)S(1)}, bf16[96,128,128]{2,1,0:T(8,128)(2,1)}, u32[]{:S(2)}) copy-start(bf16[96,128,128]{2,1,0:T(8,128)(2,1)} %get-tuple-element.59.refs_5_.refs_8_) | copy-start | bytes 9437188
  39.3 5.4 %copy-start.4 = (f32[32,64,128]{2,1,0:T(8,128)S(1)}, f32[32,64,128]{2,1,0:T(8,128)}, u32[]{:S(2)}) copy-start(f32[32,64,128]{2,1,0:T(8,128)} %get-tuple-element.65.refs_9_) | copy-start | bytes 3145732
  39.3 5.4 %copy-start.5 = (f32[16,64,128]{2,1,0:T(8,128)S(1)}, f32[16,64,128]{2,1,0:T(8,128)}, u32[]{:S(2)}) copy-start(f32[16,64,128]{2,1,0:T(8,128)} %get-tuple-element.62.refs_1_) | copy-start | bytes 1572868
  39.3 5.4 %copy-start.7 = (bf16[17,64,128]{2,1,0:T(8,128)(2,1)S(1)}, bf16[17,64,128]{2,1,0:T(8,128)(2,1)}, u32[]{:S(2)}) copy-start(bf16[17,64,128]{2,1,0:T(8,128)(2,1)} %get-tuple-element.64.refs_3_) | copy-start | bytes 835588
  40.6 9.5 %collective-permute-start.6 = (bf16[16,64,128]{2,1,0:T(8,128)(2,1)S(1)}, bf16[16,64,128]{2,1,0:T(8,128)(2,1)S(1)}, u32[]{:S(2)}, u32[]{:S(2)}) collective-permute-start(bf16[16,64,128]{2,1,0:T(8,128)(2,1)S(1)} %get-tuple-element.60), channel_id=1, source_target_pairs={{0,2},{2,4},{4,6},{1,3},{3,5},{5,7},{8,10},{10,12},{12,14},{9,11},... | collective-permute-start | bytes 786440 | tf_op jit(solution)/shard_map/ppermute | solution.py:555
  44.8 4.2 %copy-start.12 = (f32[64,256]{1,0:T(8,128)S(1)}, f32[64,256]{1,0:T(8,128)}, u32[]{:S(2)}) copy-start(f32[64,256]{1,0:T(8,128)} %get-tuple-element.70.product) | copy-start | bytes 196612
